TPU v7x, 32 devices: a whole 2x2x4 slice. The times are simulated.
32 devices in a mesh: section: 2 (over core), dp: 16 (over z, y, x).
Axes of the slice: x: 2, y: 2, z: 4, core: 2. Of those that a mesh axis runs over, the one named last changes fastest.
Arguments:
- inputs: bfloat16 [64, 160, 768], P('dp'), may hold values from -6 to 6
- cotangent: bfloat16 [64, 160, 768], P('dp'), may hold values from -6 to 6
- chain_tags: int32 [64], P('dp'), may hold values 0 or 1
- chain_lengths: int32 [64], P('dp'), may hold values from 1 to 160, 6400 in all
- attn_in: float32 [2, 2, 768, 2304], P('section', None, 'dp'), may hold values from -0.3125 to 0.3125
- attn_out: float32 [2, 2, 768, 768], P('section', None, 'dp'), may hold values from -0.625 to 0.625
- ffn_in: float32 [2, 2, 768, 3072], P('section', None, 'dp'), may hold values from -0.21875 to 0.21875
- ffn_out: float32 [2, 2, 3072, 768], P('section', None, None, 'dp'), may hold values from -0.109375 to 0.109375
- proj_bias: float32 [2, 2, 4, 768], P('section', None, None, 'dp'), may hold values from -1.5 to 1.5
- ffn_bias: float32 [2, 2, 3072], P('section', None, 'dp'), may hold values from -1.5 to 1.5
- norm_gain: float32 [2, 2, 2, 768], P('section', None, None, 'dp'), may hold values from 0.25 to 1.75
- norm_shift: float32 [2, 2, 2, 768], P('section', None, None, 'dp'), may hold values from -1.5 to 1.5
Outputs:
- activations: bfloat16 [2, 64, 160, 768], P('section', 'dp')
- input_grads: float32 [2, 64, 160, 768], P('section', 'dp')
- grad_attn_in: float32 [2, 2, 768, 2304], P('section', None, 'dp')
- grad_attn_out: float32 [2, 2, 768, 768], P('section', None, 'dp')
- grad_ffn_in: float32 [2, 2, 768, 3072], P('section', None, 'dp')
- grad_ffn_out: float32 [2, 2, 3072, 768], P('section', None, None, 'dp')
- grad_proj_bias: float32 [2, 2, 4, 768], P('section', None, None, 'dp')
- grad_ffn_bias: float32 [2, 2, 3072], P('section', None, 'dp')
- grad_norm_gain: float32 [2, 2, 2, 768], P('section', None, None, 'dp')
- grad_norm_shift: float32 [2, 2, 2, 768], P('section', None, None, 'dp')
Inputs may be any that keep to these rules, and one draw needn't show every extreme that they name: `chain_tags`: 1 marks a light chain, 0 a heavy one. `chain_lengths`: the longest chain has exactly 160 residues.
All inputs are finite; a program needn't handle non-finite values. No bound on the sum of `chain_tags` or of `chain_lengths` on one device may be relied on, other than what follows from the above.
Results may differ from a plain program's by a relative error of at most 0.035.
The roundings to bfloat16 on the way count: a program that leaves them out, or rounds other values in their place, can miss the bound.
Values may be sent and summed in bfloat16 or wider, within the bound.
No kernel may reach another device: no remote copies, remote signals or barrier semaphores. Data moves between devices by JAX's collectives and lax.ppermute only.
A program may use at most 384 MiB of HBM per device.

v0:
```python
from functools import partial

import jax
import jax.numpy as jnp
from jax import lax
from jax.sharding import PartitionSpec as P

D = 768
HEADS = 12
HEAD_DIM = 64
FF = 3072
SEQ = 160
MICRO = 2


EPS = 1e-05
NEG = -1e30
SQRT_HALF = 0.7071067811865476
INV_ROOT = 0.3989422804014327


def as_sent(array):

    def short(part):
        return part.astype(jnp.bfloat16) if part.dtype == jnp.float32 else part

    return jax.tree.map(short, array)


def passed_along(array, axis, by):
    count = lax.axis_size(axis)
    pairs = [(i, i + by) for i in range(count) if 0 <= i + by < count]
    return lax.ppermute(array, axis, pairs)


def matmul(left_op, right_op):
    return jnp.dot(left_op, right_op, preferred_element_type=jnp.float32)


def matmul_left(left_op, right_op):
    return lax.dot_general(
        left_op, right_op, (((0,), (0,)), ((), ())), preferred_element_type=jnp.float32
    )


def matmul_right(left_op, right_op):
    return lax.dot_general(
        left_op, right_op, (((1,), (1,)), ((), ())), preferred_element_type=jnp.float32
    )


def norm_fwd(summed, gain_row, shift_row):
    center = summed - jnp.mean(summed, axis=-1, keepdims=True)
    inverse = lax.rsqrt(jnp.mean(center * center, axis=-1, keepdims=True) + EPS)
    normed = center * inverse
    return (normed * gain_row + shift_row, normed, inverse)


def norm_back(grad_out, normed, inverse, gain_row):
    scaled = grad_out * gain_row
    return inverse * (
        scaled
        - jnp.mean(scaled, axis=-1, keepdims=True)
        - normed * jnp.mean(scaled * normed, axis=-1, keepdims=True)
    )


def gelu_slope(pre_gelu):
    return (
        0.5 * (1.0 + lax.erf(pre_gelu * SQRT_HALF))
        + pre_gelu * jnp.exp(-0.5 * pre_gelu * pre_gelu) * INV_ROOT
    )


def project(model_id, weights, chain_rows):
    biases = weights[4][model_id].astype(jnp.float32)
    joined = jnp.concatenate([biases[0], jnp.zeros_like(biases[0]), biases[1]])
    return (matmul(chain_rows, weights[0][model_id]) + joined).astype(jnp.bfloat16)


def project_all(weights, chains, chain_kind):
    branches = [partial(project, 0, weights), partial(project, 1, weights)]

    def project_single(pieces):
        return lax.switch(pieces[1], branches, pieces[0])

    return lax.map(project_single, (chains, chain_kind))


def attend(qkv_rows, chain_len):
    per_micro = qkv_rows.shape[0]
    queries = qkv_rows[:, :, :D].reshape(per_micro, SEQ, HEADS, HEAD_DIM)
    key_rows = qkv_rows[:, :, D : 2 * D].reshape(per_micro, SEQ, HEADS, HEAD_DIM)
    values = qkv_rows[:, :, 2 * D :].reshape(per_micro, SEQ, HEADS, HEAD_DIM)
    raw_scores = jnp.einsum(
        "cqhd,ckhd->chqk", queries, key_rows, preferred_element_type=jnp.float32
    )
    live_keys = lax.broadcasted_iota(jnp.int32, (per_micro, SEQ), 1) < chain_len[:, None]
    scores = jnp.where(live_keys[:, None, None, :], raw_scores * HEAD_DIM ** (-0.5), NEG)
    exponent = jnp.exp(scores - jnp.max(scores, axis=-1, keepdims=True))
    attn_probs = exponent / jnp.sum(exponent, axis=-1, keepdims=True)
    context = jnp.einsum(
        "chqk,ckhd->cqhd",
        attn_probs.astype(jnp.bfloat16),
        values,
        preferred_element_type=jnp.float32,
    )
    return (
        context.reshape(per_micro, SEQ, D).astype(jnp.bfloat16),
        attn_probs,
        (queries, key_rows, values),
    )


def post_fwd(model_id, weights, chain_rows, context):
    biases = weights[4][model_id].astype(jnp.float32)
    up_bias = weights[5][model_id].astype(jnp.float32)
    gain_rows = weights[6][model_id].astype(jnp.float32)
    shift_rows = weights[7][model_id].astype(jnp.float32)
    attn_branch = matmul(context, weights[1][model_id]) + biases[2]
    hidden, normed_one, inverse_one = norm_fwd(
        chain_rows.astype(jnp.float32) + attn_branch, gain_rows[0], shift_rows[0]
    )
    hidden_low = hidden.astype(jnp.bfloat16)
    pre_gelu = matmul(hidden_low, weights[2][model_id]) + up_bias
    act_low = jax.nn.gelu(pre_gelu, approximate=False).astype(jnp.bfloat16)
    ffn_branch = matmul(act_low, weights[3][model_id]) + biases[3]
    result, normed_two, inverse_two = norm_fwd(hidden + ffn_branch, gain_rows[1], shift_rows[1])
    return (
        result,
        (normed_one, inverse_one, hidden_low, pre_gelu, act_low, normed_two, inverse_two),
    )


def post_only(model_id, weights, chain_rows, context):
    return post_fwd(model_id, weights, chain_rows, context)[0].astype(jnp.bfloat16)


def post_back(model_id, weights, chain_rows, context, grad_out):
    result, stored = post_fwd(model_id, weights, chain_rows, context)
    normed_one, inverse_one, hidden_low, pre_gelu, act_low, normed_two, inverse_two = stored
    gain_rows = weights[6][model_id].astype(jnp.float32)
    grad_gain_two = jnp.sum(grad_out * normed_two, axis=0)
    grad_shift_two = jnp.sum(grad_out, axis=0)
    grad_res_two = norm_back(grad_out, normed_two, inverse_two, gain_rows[1])
    grad_ffn = grad_res_two.astype(jnp.bfloat16)
    grad_act = matmul_right(grad_ffn, weights[3][model_id])
    grad_pre = (grad_act * gelu_slope(pre_gelu)).astype(jnp.bfloat16)
    grad_hidden_low = lax.optimization_barrier(
        matmul_right(grad_pre, weights[2][model_id]).astype(jnp.bfloat16)
    )
    grad_hidden = grad_res_two + grad_hidden_low.astype(jnp.float32)
    grad_gain_one = jnp.sum(grad_hidden * normed_one, axis=0)
    grad_shift_one = jnp.sum(grad_hidden, axis=0)
    grad_res_one = norm_back(grad_hidden, normed_one, inverse_one, gain_rows[0])
    grad_attn = grad_res_one.astype(jnp.bfloat16)
    grad_context = matmul_right(grad_attn, weights[1][model_id]).astype(jnp.bfloat16)
    norm_rows = jnp.stack([grad_gain_one, grad_gain_two, grad_shift_one, grad_shift_two])
    return (
        grad_context,
        grad_res_one,
        (hidden_low, act_low, grad_ffn, grad_pre, grad_attn, norm_rows),
    )


def front_back(model_id, weights, grad_qkv_rows, grad_res):
    return matmul_right(grad_qkv_rows, weights[0][model_id]) + grad_res


def forward_micro(weights, chains, chain_kind, chain_len):
    qkv_rows = project_all(weights, chains, chain_kind)
    context, attn_probs, parts = attend(qkv_rows, chain_len)
    branches = [partial(post_only, 0, weights), partial(post_only, 1, weights)]

    def forward_single(pieces):
        return lax.switch(pieces[2], branches, pieces[0], pieces[1])

    return lax.map(forward_single, (chains, context, chain_kind))


def blank_saved(per_micro):
    lead_shape = (per_micro, SEQ)
    narrow = jnp.zeros(lead_shape + (D,), jnp.bfloat16)
    broad = jnp.zeros(lead_shape + (FF,), jnp.bfloat16)
    return (
        narrow,
        narrow,
        narrow,
        narrow,
        broad,
        broad,
        narrow,
        jnp.zeros(lead_shape + (3 * D,), jnp.bfloat16),
        jnp.zeros((per_micro, 4, D), jnp.float32),
        jnp.zeros((per_micro,), jnp.int32),
    )


def backward_inputs(weights, chains, chain_kind, chain_len, grad_rows):
    per_micro = chains.shape[0]
    qkv_rows = project_all(weights, chains, chain_kind)
    context, attn_probs, (queries, key_rows, values) = attend(qkv_rows, chain_len)
    post_branches = [partial(post_back, 0, weights), partial(post_back, 1, weights)]

    def post_step(pieces):
        return lax.switch(pieces[3], post_branches, pieces[0], pieces[1], pieces[2])

    grad_context, grad_res_one, kept_rows = lax.map(
        post_step, (chains, context, grad_rows, chain_kind)
    )
    grad_heads = grad_context.reshape(per_micro, SEQ, HEADS, HEAD_DIM)
    grad_probs = jnp.einsum(
        "cqhd,ckhd->chqk", grad_heads, values, preferred_element_type=jnp.float32
    )
    grad_values = jnp.einsum(
        "chqk,cqhd->ckhd",
        attn_probs.astype(jnp.bfloat16),
        grad_heads,
        preferred_element_type=jnp.float32,
    )
    grad_scores = attn_probs * (
        grad_probs - jnp.sum(attn_probs * grad_probs, axis=-1, keepdims=True)
    )
    grad_raw = (grad_scores * HEAD_DIM ** (-0.5)).astype(jnp.bfloat16)
    grad_queries = jnp.einsum(
        "chqk,ckhd->cqhd", grad_raw, key_rows, preferred_element_type=jnp.float32
    )
    grad_keys = jnp.einsum("chqk,cqhd->ckhd", grad_raw, queries, preferred_element_type=jnp.float32)
    grad_qkv = jnp.concatenate(
        [
            grad_queries.reshape(per_micro, SEQ, D),
            grad_keys.reshape(per_micro, SEQ, D),
            grad_values.reshape(per_micro, SEQ, D),
        ],
        axis=-1,
    ).astype(jnp.bfloat16)
    front_branches = [partial(front_back, 0, weights), partial(front_back, 1, weights)]

    def front_step(pieces):
        return lax.switch(pieces[2], front_branches, pieces[0], pieces[1])

    grad_in = lax.map(front_step, (grad_qkv, grad_res_one, chain_kind))
    hidden_low, act_low, grad_ffn, grad_pre, grad_attn, norm_rows = kept_rows
    return (
        grad_in,
        (
            chains,
            context,
            grad_attn,
            hidden_low,
            grad_pre,
            act_low,
            grad_ffn,
            grad_qkv,
            norm_rows,
            chain_kind,
        ),
    )


def flat_rows(array):
    return array.reshape(-1, array.shape[-1])


def masked_rows(select, grads):
    return flat_rows(jnp.where(select[:, None, None], grads, jnp.zeros_like(grads)))


def chain_total(weight_col, per_chain):
    return jnp.sum(weight_col * per_chain, axis=0)


def weight_pass(operands):
    saved, totals = operands
    (
        chains,
        context,
        grad_attn,
        hidden_low,
        grad_pre,
        act_low,
        grad_ffn,
        grad_qkv,
        norm_rows,
        chain_kind,
    ) = saved
    qkv_sums = jnp.sum(grad_qkv.astype(jnp.float32), axis=1)
    attn_sums = jnp.sum(grad_attn.astype(jnp.float32), axis=1)
    ffn_sums = jnp.sum(grad_ffn.astype(jnp.float32), axis=1)
    pre_sums = jnp.sum(grad_pre.astype(jnp.float32), axis=1)
    per_model = []
    for model_id in range(2):
        select = chain_kind == model_id
        weight_col = select.astype(jnp.float32)[:, None]
        entries = (
            matmul_left(flat_rows(chains), masked_rows(select, grad_qkv)),
            matmul_left(flat_rows(context), masked_rows(select, grad_attn)),
            matmul_left(flat_rows(hidden_low), masked_rows(select, grad_pre)),
            matmul_left(flat_rows(act_low), masked_rows(select, grad_ffn)),
            jnp.stack(
                [
                    chain_total(weight_col, qkv_sums[:, :D]),
                    chain_total(weight_col, qkv_sums[:, 2 * D :]),
                    chain_total(weight_col, attn_sums),
                    chain_total(weight_col, ffn_sums),
                ]
            ),
            chain_total(weight_col, pre_sums),
            chain_total(weight_col[:, :, None], norm_rows[:, 0:2]),
            chain_total(weight_col[:, :, None], norm_rows[:, 2:4]),
        )
        per_model.append(entries)
    return tuple(
        (
            total + jnp.stack([first_model, second_model])
            for total, first_model, second_model in zip(totals, per_model[0], per_model[1])
        )
    )


def keep_totals(operands):
    return operands[1]


def per_device(
    inputs,
    cotangent,
    chain_tags,
    chain_lengths,
    attn_in,
    attn_out,
    ffn_in,
    ffn_out,
    proj_bias,
    ffn_bias,
    norm_gain,
    norm_shift,
):
    masters = (attn_in, attn_out, ffn_in, ffn_out, proj_bias, ffn_bias, norm_gain, norm_shift)
    gathered = (
        lax.all_gather(attn_in.astype(jnp.bfloat16), "dp", axis=2, tiled=True),
        lax.all_gather(attn_out.astype(jnp.bfloat16), "dp", axis=2, tiled=True),
        lax.all_gather(ffn_in.astype(jnp.bfloat16), "dp", axis=2, tiled=True),
        lax.all_gather(ffn_out.astype(jnp.bfloat16), "dp", axis=3, tiled=True),
        lax.all_gather(proj_bias.astype(jnp.bfloat16), "dp", axis=3, tiled=True),
        lax.all_gather(ffn_bias.astype(jnp.bfloat16), "dp", axis=2, tiled=True),
        lax.all_gather(norm_gain.astype(jnp.bfloat16), "dp", axis=3, tiled=True),
        lax.all_gather(norm_shift.astype(jnp.bfloat16), "dp", axis=3, tiled=True),
    )
    weights = tuple((shard_full[0] for shard_full in gathered))
    segment_id = lax.axis_index("section")
    per_micro = inputs.shape[0] // MICRO
    layer_in = inputs.reshape(MICRO, per_micro, SEQ, D)
    cot_parts = cotangent.reshape(MICRO, per_micro, SEQ, D)
    kind_parts = chain_tags.reshape(MICRO, per_micro)
    len_parts = chain_lengths.reshape(MICRO, per_micro)

    def run_forward(operands):
        return forward_micro(weights, operands[0], operands[1], operands[2])

    def skip_forward(operands):
        return jnp.zeros_like(operands[0])

    def run_inputs(operands):
        return backward_inputs(weights, operands[0], operands[1], operands[2], operands[3])

    def skip_inputs(operands):
        return (jnp.zeros(operands[0].shape, jnp.float32), blank_saved(operands[0].shape[0]))

    kept_in = jnp.zeros((MICRO, per_micro, SEQ, D), jnp.bfloat16)
    kept_out = jnp.zeros((MICRO, per_micro, SEQ, D), jnp.bfloat16)
    received = jnp.zeros((per_micro, SEQ, D), jnp.bfloat16)
    outgoing = received
    for tick_no in range(MICRO + 1):
        if tick_no > 0:
            received = jax.tree.map(
                lambda part, own: part.astype(own.dtype),
                passed_along(as_sent(outgoing), "section", 1),
                outgoing,
            )
        micro_id = tick_no - segment_id
        active = (micro_id >= 0) & (micro_id < MICRO)
        slot_id = jnp.clip(micro_id, 0, MICRO - 1)
        chains = jnp.where(
            segment_id == 0,
            lax.dynamic_index_in_dim(layer_in, slot_id, 0, keepdims=False),
            received,
        )
        chain_kind = lax.dynamic_index_in_dim(kind_parts, slot_id, 0, keepdims=False)
        chain_len = lax.dynamic_index_in_dim(len_parts, slot_id, 0, keepdims=False)
        outgoing = lax.cond(active, run_forward, skip_forward, (chains, chain_kind, chain_len))
        old_in = lax.dynamic_index_in_dim(kept_in, slot_id, 0, keepdims=False)
        kept_in = lax.dynamic_update_index_in_dim(
            kept_in, jnp.where(active, chains, old_in), slot_id, 0
        )
        old_out = lax.dynamic_index_in_dim(kept_out, slot_id, 0, keepdims=False)
        kept_out = lax.dynamic_update_index_in_dim(
            kept_out, jnp.where(active, outgoing, old_out), slot_id, 0
        )
    zero_totals = tuple((jnp.zeros(shard_full.shape, jnp.float32) for shard_full in weights))
    totals = zero_totals
    grad_shards = tuple((jnp.zeros(master.shape, jnp.float32) for master in masters))
    grad_kept = jnp.zeros((MICRO, per_micro, SEQ, D), jnp.float32)
    returned = jnp.zeros((per_micro, SEQ, D), jnp.bfloat16)
    outgoing_grad = returned
    for tick_no in range(MICRO + 1):
        if tick_no > 0:
            returned = passed_along(outgoing_grad, "section", -1)
        micro_id = tick_no - (1 - segment_id)
        active = (micro_id >= 0) & (micro_id < MICRO)
        slot_id = jnp.clip(micro_id, 0, MICRO - 1)
        chains = lax.dynamic_index_in_dim(kept_in, slot_id, 0, keepdims=False)
        chain_kind = lax.dynamic_index_in_dim(kind_parts, slot_id, 0, keepdims=False)
        chain_len = lax.dynamic_index_in_dim(len_parts, slot_id, 0, keepdims=False)
        rows_live = (
            lax.broadcasted_iota(jnp.int32, (per_micro, SEQ), 1) < chain_len[:, None]
        ).astype(jnp.float32)
        top_grad = (
            lax.dynamic_index_in_dim(cot_parts, slot_id, 0, keepdims=False).astype(jnp.float32)
            * rows_live[:, :, None]
        )
        grad_rows = jnp.where(segment_id == 1, top_grad, returned.astype(jnp.float32))
        grad_in, saved = lax.cond(
            active, run_inputs, skip_inputs, (chains, chain_kind, chain_len, grad_rows)
        )
        totals = lax.cond(active, weight_pass, keep_totals, (saved, totals))
        old_grad = lax.dynamic_index_in_dim(grad_kept, slot_id, 0, keepdims=False)
        grad_kept = lax.dynamic_update_index_in_dim(
            grad_kept, jnp.where(active, grad_in, old_grad), slot_id, 0
        )
        outgoing_grad = grad_in.astype(jnp.bfloat16)
    grad_shards = (
        lax.psum_scatter(totals[0][None], "dp", scatter_dimension=2, tiled=True),
        lax.psum_scatter(totals[1][None], "dp", scatter_dimension=2, tiled=True),
        lax.psum_scatter(totals[2][None], "dp", scatter_dimension=2, tiled=True),
        lax.psum_scatter(totals[3][None], "dp", scatter_dimension=3, tiled=True),
        lax.psum_scatter(totals[4][None], "dp", scatter_dimension=3, tiled=True),
        lax.psum_scatter(totals[5][None], "dp", scatter_dimension=2, tiled=True),
        lax.psum_scatter(totals[6][None], "dp", scatter_dimension=3, tiled=True),
        lax.psum_scatter(totals[7][None], "dp", scatter_dimension=3, tiled=True),
    )
    return (
        kept_out.reshape(1, MICRO * per_micro, SEQ, D),
        grad_kept.reshape(1, MICRO * per_micro, SEQ, D),
        grad_shards[0],
        grad_shards[1],
        grad_shards[2],
        grad_shards[3],
        grad_shards[4],
        grad_shards[5],
        grad_shards[6],
        grad_shards[7],
    )


def solution(mesh):
    in_specs = (
        P("dp", None, None),
        P("dp", None, None),
        P("dp"),
        P("dp"),
        P("section", None, "dp", None),
        P("section", None, "dp", None),
        P("section", None, "dp", None),
        P("section", None, None, "dp"),
        P("section", None, None, "dp"),
        P("section", None, "dp"),
        P("section", None, None, "dp"),
        P("section", None, None, "dp"),
    )
    out_specs = (
        P("section", "dp", None, None),
        P("section", "dp", None, None),
        P("section", None, "dp", None),
        P("section", None, "dp", None),
        P("section", None, "dp", None),
        P("section", None, None, "dp"),
        P("section", None, None, "dp"),
        P("section", None, "dp"),
        P("section", None, None, "dp"),
        P("section", None, None, "dp"),
    )
    return jax.shard_map(
        per_device, mesh=mesh, in_specs=in_specs, out_specs=out_specs, check_vma=False
    )
```

profile of v0, /device:TPU:1, one launch (start us, length us, event | category | flops | bytes accessed | tf_op | source)
XLA Modules:
  0.0 2732.6 jit_solution(5450762245562991838)
XLA Ops:
  14.8 50.8 %all_gather.30 = bf16[1,2,3072]{1,0,2:T(2,128)(2,1)S(1)} all-gather(bf16[1,2,192]{1,0,2:T(2,128)(2,1)S(1)} %copy.479), channel_id=1, replica_groups=mesh['section'=2,'dp'=16] {'dp'}, dimensions={2}, use_global_device_ids=true | all-gather | bytes 13056 | tf_op jit(solution)/shard_map/all_gather | solution.py:346
  68.2 34.1 %all_gather.27 = bf16[1,2,2,768]{2,1,0,3:T(2,128)(2,1)S(1)} all-gather(bf16[1,2,2,48]{2,1,0,3:T(2,128)(2,1)S(1)} %copy.477), channel_id=1, replica_groups=mesh['section'=2,'dp'=16] {'dp'}, dimensions={3}, use_global_device_ids=true | all-gather | bytes 6528 | tf_op jit(solution)/shard_map/all_gather | solution.py:347
  102.3 33.8 %all_gather.28 = bf16[1,2,2,768]{2,1,0,3:T(2,128)(2,1)S(1)} all-gather(bf16[1,2,2,48]{2,1,0,3:T(2,128)(2,1)S(1)} %copy.478), channel_id=1, replica_groups=mesh['section'=2,'dp'=16] {'dp'}, dimensions={3}, use_global_device_ids=true | all-gather | bytes 6528 | tf_op jit(solution)/shard_map/all_gather | solution.py:348
  136.1 37.4 %all_gather.25 = bf16[1,2,4,768]{2,1,0,3:T(2,128)(2,1)S(1)} all-gather(bf16[1,2,4,48]{2,1,0,3:T(2,128)(2,1)S(1)} %copy.476), channel_id=1, replica_groups=mesh['section'=2,'dp'=16] {'dp'}, dimensions={3}, use_global_device_ids=true | all-gather | bytes 13056 | tf_op jit(solution)/shard_map/all_gather | solution.py:345
  177.3 21.4 all-gather.5.cloned.1.call-done
  198.7 125.2 %all-gather.9.cloned.1.call-done = bf16[1,2,768,3072]{3,2,1,0:T(8,128)(2,1)} async-done(((bf16[1,2,48,3072]{3,2,1,0:T(8,128)(2,1)}), bf16[1,2,768,3072]{3,2,1,0:T(8,128)(2,1)}) %all-gather.9.cloned.1.call-update) | async-done | bytes 9437200 | tf_op jit(solution)/shard_map/all_gather | solution.py:343
  323.9 123.9 %all-gather.11.cloned.1.call-done = bf16[1,2,3072,768]{2,1,0,3:T(2,128)(2,1)} async-done(((bf16[1,2,3072,48]{2,1,0,3:T(2,128)(2,1)}), bf16[1,2,3072,768]{2,1,0,3:T(2,128)(2,1)}) %all-gather.11.cloned.1.call-update) | async-done | bytes 9437200 | tf_op jit(solution)/shard_map/all_gather | solution.py:344
  458.8 69.3 %collective-permute-done = bf16[2,160,768]{2,1,0:T(8,128)(2,1)S(1)} collective-permute-done((bf16[2,160,768]{2,1,0:T(8,128)(2,1)}, bf16[2,160,768]{2,1,0:T(8,128)(2,1)S(1)}, u32[]{:S(2)}, u32[]{:S(2)}) %collective-permute-start) | collective-permute-done | bytes 491552 | tf_op jit(solution)/shard_map/ppermute | solution.py:33
  529.3 75.1 %conditional.25 = (bf16[2,160,768]{2,1,0:T(8,128)(2,1)}) conditional(s32[]{:T(128)} %convert_element_type.782, () %tuple.324, (s32[2,2]{1,0:T(2,128)S(1)}, s32[]{:T(128)}, bf16[2,160,768]{2,1,0:T(8,128)(2,1)}, bf16[2,768,2304]{2,1,0:T(8,128)(2,1)}, bf16[2,4,768]{1,0,2:T(2,128)(2,1)S(1)}, /*index=5*/s32[2,2]{1,0:T(2,128)S(1)}, ...), branch_computations={%region_20.21_spmd, %region_21.40_spmd} | conditional | flops 2462655744 | bytes 65172848 | solution.py:391
  529.3 23.7 copy.489
  575.8 28.6 %while.312 = (s32[]{:T(128)}, bf16[2,160,768]{2,1,0:T(8,128)(2,1)}, s32[2]{0:T(128)S(1)}, bf16[2,160,768]{2,1,0:T(8,128)(2,1)}, bf16[2,160,768]{2,1,0:T(8,128)(2...) while((s32[]{:T(128)}, bf16[2,160,768]{2,1,0:T(8,128)(2,1)}, ...), condition=%wide.region_39.39_spmd, body=%wide.region_28.38_spmd.sunk | while | flops 1734460672 | bytes 16419081 | solution.py:178
  578.5 11.0 conditional.60
  592.5 11.0 conditional.60
  612.8 149.0 %conditional.27 = (f32[2,160,768]{2,1,0:T(8,128)}, bf16[2,160,768]{2,1,0:T(8,128)(2,1)S(1)}, bf16[2,160,768]{1,2,0:T(8,128)(2,1)}, bf16[2,160,768]{2,1,0:T(8,128...) conditional(s32[]{:T(128)} %convert_element_type.784, ...), branch_computations={%region_60.61_spmd, %region_61.101_spmd} | conditional | flops 5067848704 | bytes 247787872 | solution.py:423
  612.8 23.6 copy.497
  666.1 55.5 %while.316 = (s32[]{:T(128)}, bf16[2,160,768]{2,1,0:T(8,128)(2,1)}, f32[2,160,768]{2,1,0:T(8,128)}, bf16[2,160,768]{2,1,0:T(8,128)(2,1)}, bf16[2,160,3072]{2,1,0...) while((s32[]{:T(128)}, bf16[2,160,768]{2,1,0:T(8,128)(2,1)}, ...), condition=%wide.region_95.95_spmd, body=%wide.region_68.94_spmd.sunk | while | flops 3442989824 | bytes 133392648 | solution.py:208
  670.4 16.8 conditional.55
  698.0 16.8 conditional.55
  746.7 14.6 while.317
  767.2 152.7 %conditional.28 = (f32[2,160,768]{2,1,0:T(8,128)}, bf16[2,160,768]{2,1,0:T(8,128)(2,1)S(1)}, bf16[2,160,768]{1,2,0:T(8,128)(2,1)S(1)}, bf16[2,160,768]{2,1,0:T(8...) conditional(s32[]{:T(128)} %convert_element_type.786, ...), branch_computations={%region_101.102_spmd, %region_102.142_spmd} | conditional | flops 5067848704 | bytes 241889600 | solution.py:423
  767.2 23.7 copy.501
  820.7 57.3 %while.319 = (s32[]{:T(128)}, bf16[2,160,768]{2,1,0:T(8,128)(2,1)}, f32[2,160,768]{2,1,0:T(8,128)}, bf16[2,160,768]{2,1,0:T(8,128)(2,1)}, bf16[2,160,3072]{2,1,0...) while((s32[]{:T(128)}, bf16[2,160,768]{2,1,0:T(8,128)(2,1)}, ...), condition=%wide.region_136.136_spmd, body=%wide.region_109.135_spmd.sunk | while | flops 3442989824 | bytes 125528264 | solution.py:208
  824.8 17.2 conditional.52
  853.4 16.9 conditional.52
  903.0 16.9 while.320
  924.0 69.7 %conditional.30 = (f32[2,768,2304]{1,2,0:T(8,128)}, f32[2,768,768]{1,2,0:T(8,128)}, f32[2,768,3072]{1,2,0:T(8,128)}, f32[2,3072,768]{1,2,0:T(8,128)}, f32[2,4,76...) conditional(s32[]{:T(128)} %convert_element_type.784, ...), branch_computations={%region_183.184_spmd, %region_184.203_spmd} | conditional | flops 9082777600 | bytes 192436400 | solution.py:426
  950.7 11.0 pad_maximum_fusion.2
  993.8 82.0 %conditional.31 = ((f32[2,768,2304]{1,2,0:T(8,128)}, f32[2,768,768]{1,2,0:T(8,128)}, f32[2,768,3072]{1,2,0:T(8,128)}, f32[2,3072,768]{1,2,0:T(8,128)}, f32[2,4,7...) conditional(s32[]{:T(128)} %convert_element_type.786, ...), branch_computations={%region_203.204_spmd, %region_204.223_spmd} | conditional | flops 9096951808 | bytes 247167136 | solution.py:426
  1016.9 10.7 maximum_add_fusion.2
  1036.4 14.9 maximum_add_fusion.1
  1060.1 15.7 maximum_add_fusion
  1076.4 26.4 conditional.29
  1102.8 14.9 conditional.32
  1132.8 15.3 copy.509
  1149.0 18.7 copy.511
  1168.9 74.9 %conditional.26 = (bf16[2,160,768]{2,1,0:T(8,128)(2,1)}) conditional(s32[]{:T(128)} %convert_element_type.783, () %tuple.326, (s32[2,2]{1,0:T(2,128)S(1)}, s32[]{:T(128)}, bf16[2,160,768]{2,1,0:T(8,128)(2,1)}, bf16[2,768,2304]{2,1,0:T(8,128)(2,1)}, bf16[2,4,768]{1,0,2:T(2,128)(2,1)S(1)}, /*index=5*/s32[2,2]{1,0:T(2,128)S(1)}, ...), branch_computations={%region_40.41_spmd, %region_41.60_spmd} | conditional | flops 2462655744 | bytes 65172848 | solution.py:391
  1168.9 23.7 copy.493
  1215.4 28.2 %while.314 = (s32[]{:T(128)}, bf16[2,160,768]{2,1,0:T(8,128)(2,1)}, s32[2]{0:T(128)S(1)}, bf16[2,160,768]{2,1,0:T(8,128)(2,1)}, bf16[2,160,768]{2,1,0:T(8,128)(2...) while((s32[]{:T(128)}, bf16[2,160,768]{2,1,0:T(8,128)(2,1)}, ...), condition=%wide.region_59.59_spmd, body=%wide.region_48.58_spmd.sunk | while | flops 1734460672 | bytes 16419081 | solution.py:178
  1217.9 11.0 conditional.58
  1231.9 11.0 conditional.58
  1248.9 142.1 %reduce-scatter.29.cloned.1.call-done = f32[48,4]{1,0:T(8,128)} async-done(((f32[768,4]{1,0:T(8,128)}), f32[48,4]{1,0:T(8,128)}) %reduce-scatter.29.cloned.1.call-update) | async-done | bytes 784
  1392.5 124.5 %reduce-scatter.31.cloned.1.call-done = f32[48,4]{1,0:T(8,128)} async-done(((f32[768,4]{1,0:T(8,128)}), f32[48,4]{1,0:T(8,128)}) %reduce-scatter.31.cloned.1.call-update) | async-done | bytes 784
  1518.4 123.9 %reduce-scatter.25.cloned.1.call-done = f32[48,8]{1,0:T(8,128)} async-done(((f32[768,8]{1,0:T(8,128)}), f32[48,8]{1,0:T(8,128)}) %reduce-scatter.25.cloned.1.call-update) | async-done | bytes 1552
  1643.9 127.5 %reduce-scatter.27.cloned.1.call-done = f32[192,2]{1,0:T(8,128)} async-done(((f32[3072,2]{1,0:T(8,128)}), f32[192,2]{1,0:T(8,128)}) %reduce-scatter.27.cloned.1.call-update) | async-done | bytes 1552
  1772.9 140.9 %reduce-scatter.19.cloned.1.call-done = f32[1,2,48,768]{3,2,1,0:T(8,128)} async-done(((f32[1,2,768,768]{3,2,1,0:T(8,128)}), f32[1,2,48,768]{3,2,1,0:T(8,128)}) %reduce-scatter.19.cloned.1.call-update) | async-done | bytes 294928 | tf_op jit(solution)/shard_map/reduce_scatter | solution.py:434
  1913.8 228.2 %reduce-scatter.17.cloned.1.call-done = f32[1,2,48,2304]{3,2,1,0:T(8,128)} async-done(((f32[1,2,768,2304]{3,2,1,0:T(8,128)}), f32[1,2,48,2304]{3,2,1,0:T(8,128)}) %reduce-scatter.17.cloned.1.call-update) | async-done | bytes 884752 | tf_op jit(solution)/shard_map/reduce_scatter | solution.py:433
  2142.0 292.0 %reduce-scatter.23.cloned.1.call-done = f32[1,2,3072,48]{2,3,1,0:T(8,128)} async-done(((f32[1,2,3072,768]{2,3,1,0:T(8,128)}), f32[1,2,3072,48]{2,3,1,0:T(8,128)}) %reduce-scatter.23.cloned.1.call-update) | async-done | bytes 1179664 | tf_op jit(solution)/shard_map/reduce_scatter | solution.py:436
  2434.0 291.5 %reduce-scatter.21.cloned.1.call-done = f32[1,2,48,3072]{3,2,1,0:T(8,128)} async-done(((f32[1,2,768,3072]{3,2,1,0:T(8,128)}), f32[1,2,48,3072]{3,2,1,0:T(8,128)}) %reduce-scatter.21.cloned.1.call-update) | async-done | bytes 1179664 | tf_op jit(solution)/shard_map/reduce_scatter | solution.py:435
  (864 shorter events, 596.2 us)
Async XLA Ops:
  7.2 170.1 %all-gather.7.cloned.1.call-start = ((), (), s32[]{:S(2)}) async-start(), calls=%async_computation.9 | async-start | bytes 2506752 | tf_op jit(solution)/shard_map/all_gather | solution.py:342
  9.0 189.7 %all-gather.5.cloned.1.call-start = ((), (), s32[]{:S(2)}) async-start(), calls=%async_computation.8 | async-start | bytes 7520256 | tf_op jit(solution)/shard_map/all_gather | solution.py:341
  11.2 312.6 %all-gather.9.cloned.1.call-start = ((), (), s32[]{:S(2)}) async-start(), calls=%async_computation.10 | async-start | bytes 10027008 | tf_op jit(solution)/shard_map/all_gather | solution.py:343
  12.2 435.6 %all-gather.11.cloned.1.call-start = ((), (), s32[]{:S(2)}) async-start(), calls=%async_computation.11 | async-start | bytes 10027008 | tf_op jit(solution)/shard_map/all_gather | solution.py:344
  14.0 1377.0 %reduce-scatter.29.cloned.1.call-start = ((), (), s32[]{:S(2)}) async-start(), calls=%async_computation.18 | async-start | bytes 417792
  14.1 433.7 %copy-start.112 = (s32[2,2]{1,0:T(2,128)}, s32[2,2]{1,0:T(2,128)S(1)}, u32[]{:S(2)}) copy-start(s32[2,2]{1,0:T(2,128)S(1)} %reshape.1182) | copy-start | bytes 52
  14.2 433.7 %copy-start.107 = (s32[2,2]{1,0:T(2,128)}, s32[2,2]{1,0:T(2,128)S(1)}, u32[]{:S(2)}) copy-start(s32[2,2]{1,0:T(2,128)S(1)} %reshape.1183) | copy-start | bytes 52
  65.7 108.9 %copy-start.71 = (bf16[4,160,768]{2,1,0:T(8,128)(2,1)S(1)}, bf16[4,160,768]{2,1,0:T(8,128)(2,1)}, u32[]{:S(2)}) copy-start(bf16[4,160,768]{2,1,0:T(8,128)(2,1)} %param.90) | copy-start | bytes 2949124
  102.3 345.6 %copy-start.24 = (bf16[1,2,2,768]{2,1,0,3:T(2,128)(2,1)}, bf16[1,2,2,768]{2,1,0,3:T(2,128)(2,1)S(1)}, u32[]{:S(2)}) copy-start(bf16[1,2,2,768]{2,1,0,3:T(2,128)(2,1)S(1)} %all_gather.27) | copy-start | bytes 18436
  136.1 311.8 %copy-start.30 = (bf16[1,2,2,768]{2,1,0,3:T(2,128)(2,1)}, bf16[1,2,2,768]{2,1,0,3:T(2,128)(2,1)S(1)}, u32[]{:S(2)}) copy-start(bf16[1,2,2,768]{2,1,0,3:T(2,128)(2,1)S(1)} %all_gather.28) | copy-start | bytes 18436
  173.5 274.4 %copy-start.36 = (bf16[1,2,4,768]{2,1,0,3:T(2,128)(2,1)}, bf16[1,2,4,768]{2,1,0,3:T(2,128)(2,1)S(1)}, u32[]{:S(2)}) copy-start(bf16[1,2,4,768]{2,1,0,3:T(2,128)(2,1)S(1)} %all_gather.25) | copy-start | bytes 36868
  453.4 74.7 %copy-start.72 = (bf16[4,160,768]{2,1,0:T(8,128)(2,1)S(1)}, bf16[4,160,768]{2,1,0:T(8,128)(2,1)}, u32[]{:S(2)}) copy-start(bf16[4,160,768]{2,1,0:T(8,128)(2,1)} %param.90) | copy-start | bytes 2949124
  453.4 74.7 %copy-start.74 = (bf16[1,2,160,768]{3,2,1,0:T(8,128)(2,1)S(1)}, bf16[1,2,160,768]{3,2,1,0:T(8,128)(2,1)}, u32[]{:S(2)}) copy-start(bf16[1,2,160,768]{3,2,1,0:T(8,128)(2,1)} %constant_dynamic-slice_fusion.9) | copy-start | bytes 1474564
  453.4 74.7 %collective-permute-start = (bf16[2,160,768]{2,1,0:T(8,128)(2,1)}, bf16[2,160,768]{2,1,0:T(8,128)(2,1)S(1)}, u32[]{:S(2)}, u32[]{:S(2)}) collective-permute-start(bf16[2,160,768]{2,1,0:T(8,128)(2,1)} %get-tuple-element.6230), channel_id=1, source_target_pairs={{0,16},{1,17},{2,18},{3,19},{4,20},{5,21},{6,22},{7,23},{8,24},{9,... | collective-permute-start | bytes 1474568 | tf_op jit(solution)/shard_map/ppermute | solution.py:33
  457.9 71.3 %copy-start.25 = (bf16[1,2,2,768]{2,1,0,3:T(2,128)(2,1)S(1)}, bf16[1,2,2,768]{2,1,0,3:T(2,128)(2,1)}, u32[]{:S(2)}) copy-start(bf16[1,2,2,768]{2,1,0,3:T(2,128)(2,1)} %copy-done.24) | copy-start | bytes 18436
  457.9 71.3 %copy-start.31 = (bf16[1,2,2,768]{2,1,0,3:T(2,128)(2,1)S(1)}, bf16[1,2,2,768]{2,1,0,3:T(2,128)(2,1)}, u32[]{:S(2)}) copy-start(bf16[1,2,2,768]{2,1,0,3:T(2,128)(2,1)} %copy-done.30) | copy-start | bytes 18436
  457.9 71.3 %copy-start.37 = (bf16[1,2,4,768]{2,1,0,3:T(2,128)(2,1)S(1)}, bf16[1,2,4,768]{2,1,0,3:T(2,128)(2,1)}, u32[]{:S(2)}) copy-start(bf16[1,2,4,768]{2,1,0,3:T(2,128)(2,1)} %copy-done.36) | copy-start | bytes 36868
  457.9 71.3 %copy-start.108 = (s32[2,2]{1,0:T(2,128)S(1)}, s32[2,2]{1,0:T(2,128)}, u32[]{:S(2)}) copy-start(s32[2,2]{1,0:T(2,128)} %copy-done.107) | copy-start | bytes 52
  457.9 71.3 %copy-start.113 = (s32[2,2]{1,0:T(2,128)S(1)}, s32[2,2]{1,0:T(2,128)}, u32[]{:S(2)}) copy-start(s32[2,2]{1,0:T(2,128)} %copy-done.112) | copy-start | bytes 52
  604.3 6.5 collective-permute-start.1
  612.2 152.4 %copy-start.119 = (s32[2]{0:T(128)S(1)}, s32[2]{0:T(128)}, u32[]{:S(2)}) copy-start(s32[2]{0:T(128)} %get-tuple-element.4492) | copy-start | bytes 28
  666.1 57.0 %copy-start.128 = (f32[2,12,160]{2,1,0:T(8,128)S(1)}, f32[2,12,160]{2,1,0:T(8,128)}, u32[]{:S(2)}) copy-start(f32[2,12,160]{2,1,0:T(8,128)} %copy-done.127) | copy-start | bytes 46084 | tf_op jit(solution)/shard_map/cond
  670.6 7.9 slice-start
  698.1 7.9 slice-start
  729.1 7.9 copy-start.88
  746.7 14.6 copy-start.45
  763.3 2.8 collective-permute-start.2
  767.1 156.8 %copy-start.118 = (s32[2]{0:T(128)S(1)}, s32[2]{0:T(128)}, u32[]{:S(2)}) copy-start(s32[2]{0:T(128)} %get-tuple-element.4491) | copy-start | bytes 28
  820.7 58.8 %copy-start.130 = (f32[2,12,160]{2,1,0:T(8,128)S(1)}, f32[2,12,160]{2,1,0:T(8,128)}, u32[]{:S(2)}) copy-start(f32[2,12,160]{2,1,0:T(8,128)} %copy-done.129) | copy-start | bytes 46084 | tf_op jit(solution)/shard_map/cond
  824.9 8.0 slice-start.9
  853.5 7.9 slice-start.6
  885.3 7.9 copy-start.90
  903.0 16.9 copy-start.51
  903.0 16.9 copy-start.56
  921.9 153.9 %collective-permute-start.3 = (bf16[2,160,768]{2,1,0:T(8,128)(2,1)}, bf16[2,160,768]{2,1,0:T(8,128)(2,1)S(1)}, u32[]{:S(2)}, u32[]{:S(2)}) collective-permute-start(bf16[2,160,768]{2,1,0:T(8,128)(2,1)} %convert_element_type.792), channel_id=1, source_target_pairs={{16,0},{17,1},{18,2},{19,3},{20,4},{21,5},{22,6},{23,7},{24,8},{25... | collective-permute-start | bytes 1474568 | tf_op jit(solution)/shard_map/ppermute | solution.py:33
  993.7 82.2 %copy-start.28 = (bf16[1,2,2,768]{2,1,0,3:T(2,128)(2,1)S(1)}, bf16[1,2,2,768]{2,1,0,3:T(2,128)(2,1)}, u32[]{:S(2)}) copy-start(bf16[1,2,2,768]{2,1,0,3:T(2,128)(2,1)} %copy-done.24) | copy-start | bytes 18436
  993.7 82.2 %copy-start.34 = (bf16[1,2,2,768]{2,1,0,3:T(2,128)(2,1)S(1)}, bf16[1,2,2,768]{2,1,0,3:T(2,128)(2,1)}, u32[]{:S(2)}) copy-start(bf16[1,2,2,768]{2,1,0,3:T(2,128)(2,1)} %copy-done.30) | copy-start | bytes 18436
  993.7 82.2 %copy-start.40 = (bf16[1,2,4,768]{2,1,0,3:T(2,128)(2,1)S(1)}, bf16[1,2,4,768]{2,1,0,3:T(2,128)(2,1)}, u32[]{:S(2)}) copy-start(bf16[1,2,4,768]{2,1,0,3:T(2,128)(2,1)} %copy-done.36) | copy-start | bytes 36868
  993.8 82.2 %copy-start.67 = (pred[2,160,768]{2,1,0:T(8,128)(4,1)S(1)}, pred[2,160,768]{2,1,0:T(8,128)(4,1)}, u32[]{:S(2)}) copy-start(pred[2,160,768]{2,1,0:T(8,128)(4,1)} %copy-done.65) | copy-start | bytes 737284
  993.8 82.2 %copy-start.116 = (s32[2,2]{1,0:T(2,128)S(1)}, s32[2,2]{1,0:T(2,128)}, u32[]{:S(2)}) copy-start(s32[2,2]{1,0:T(2,128)} %copy-done.112) | copy-start | bytes 52
  1120.2 396.8 %reduce-scatter.31.cloned.1.call-start = ((), (), s32[]{:S(2)}) async-start(), calls=%async_computation.19 | async-start | bytes 417792
  1122.0 520.4 %reduce-scatter.25.cloned.1.call-start = ((), (), s32[]{:S(2)}) async-start(), calls=%async_computation.16 | async-start | bytes 417792
  1123.7 647.6 %reduce-scatter.27.cloned.1.call-start = ((), (), s32[]{:S(2)}) async-start(), calls=%async_computation.17 | async-start | bytes 1671168
  1126.6 787.2 %reduce-scatter.19.cloned.1.call-start = ((), (), s32[]{:S(2)}) async-start(), calls=%async_computation.13 | async-start | bytes 5013504 | tf_op jit(solution)/shard_map/reduce_scatter | solution.py:434
  1132.8 1009.3 %reduce-scatter.17.cloned.1.call-start = ((), (), s32[]{:S(2)}) async-start(), calls=%async_computation.12 | async-start | bytes 15040512 | tf_op jit(solution)/shard_map/reduce_scatter | solution.py:433
  1148.2 1285.9 %reduce-scatter.23.cloned.1.call-start = ((), (), s32[]{:S(2)}) async-start(), calls=%async_computation.15 | async-start | bytes 20054016 | tf_op jit(solution)/shard_map/reduce_scatter | solution.py:436
  1148.9 1576.6 %reduce-scatter.21.cloned.1.call-start = ((), (), s32[]{:S(2)}) async-start(), calls=%async_computation.14 | async-start | bytes 20054016 | tf_op jit(solution)/shard_map/reduce_scatter | solution.py:435
  1248.9 1476.6 %copy-start.63 = (f32[2,2,160,768]{3,2,1,0:T(8,128)}, f32[2,2,160,768]{3,2,1,0:T(8,128)S(1)}, u32[]{:S(2)}) copy-start(f32[2,2,160,768]{3,2,1,0:T(8,128)S(1)} %bitcast_dynamic-update-slice_fusion) | copy-start | bytes 5898244
  (99 other events, 345.2 us)
Sparse Core Ops, SparseCore 0:
  11.3 74.2 all-gather.6
  88.8 109.8 all-gather.4
  202.0 121.8 all-gather.8
  327.1 120.6 all-gather.10
  1120.3 270.6 reduce-scatter.28
  1396.2 120.6 reduce-scatter.30
  1521.6 120.7 reduce-scatter.24
  1647.9 123.4 reduce-scatter.26
  1777.9 135.8 reduce-scatter.18
  1920.0 221.9 reduce-scatter.16
  2149.4 284.6 reduce-scatter.22
  2441.2 284.2 reduce-scatter.20
where the time goes:
time: 2750 us; the launch traced here: 2730 us
  waiting for transfers between devices  1810 us (66%)
  local copies, waits for them, and re-layouts  293 us (11%)
  matrix products  266 us (10%)
  blocking collectives  156 us (6%)
  other arithmetic  128 us (5%)
  loops' own time  55.3 us (2%)
    unnamed x16, waiting for transfers between devices  519 us
    reduce_scatter x1, waiting for transfers between devices, per_device(): lax.psum_scatter(totals[3][None], 'dp', scatter_dimension=3, tiled=True)  292 us
    reduce_scatter x1, waiting for transfers between devices, per_device(): lax.psum_scatter(totals[2][None], 'dp', scatter_dimension=2, tiled=True)  291 us
    reduce_scatter x1, waiting for transfers between devices, per_device(): lax.psum_scatter(totals[0][None], 'dp', scatter_dimension=2, tiled=True)  228 us
    reduce_scatter x1, waiting for transfers between devices, per_device(): lax.psum_scatter(totals[1][None], 'dp', scatter_dimension=2, tiled=True)  141 us
    all_gather x1, waiting for transfers between devices, per_device(): lax.all_gather(ffn_in.astype(jnp.bfloat16), 'dp', axis=2, tiled=True)  125 us
    all_gather x1, waiting for transfers between devices, per_device(): lax.all_gather(ffn_out.astype(jnp.bfloat16), 'dp', axis=3, tiled=True)  124 us
    another operation x44, local copies, waits for them, and re-layouts  116 us
  transfers between devices with their start and end apart: 16, of which 13 were waited for; matrix products, arithmetic and copies ran while one was open for 11% of the time, Pallas kernels for 0%

commit v1 on v0

v1 whole, which is shorter than its diff:
```python
import functools

import jax
import jax.numpy as jnp
from jax import lax
from jax.experimental import pallas as pl
from jax.experimental.pallas import tpu as pltpu
from jax.sharding import PartitionSpec as P

D = 768
HEADS = 12
HEAD_DIM = 64
FF = 3072
SEQ = 160
PAIRS = HEADS // 2
BLOCKS = 16
ROWS = D // BLOCKS
WIDE = 3072
EXTRA = 128
CHUNK = 768

EPS = 1e-05
NEG = -1e30
SQRT_HALF = 0.7071067811865476
INV_ROOT = 0.3989422804014327
SCALE = HEAD_DIM**-0.5

ROTATIONS = ((0, 1, 2), (1, 2, 0), (2, 0, 1))
F32 = jnp.float32
BF16 = jnp.bfloat16


def unit_masks(unit):
    one, two, three = (1 << bit for bit in ROTATIONS[unit])
    base = [0, one, two, two | one]
    return [side | far | mask for side in (0, 8) for far in (0, three) for mask in base]


def grad_masks(unit):
    one, two, three = (1 << bit for bit in ROTATIONS[unit])
    return [
        (8 if p & 8 else 0) | (one if p & 4 else 0) | (two if p & 2 else 0) | (three if p & 1 else 0)
        for p in range(BLOCKS)
    ]


def dot_nn(a, b):
    return jnp.dot(a, b, preferred_element_type=F32)


def dot_nt(a, b):
    return lax.dot_general(a, b, (((1,), (1,)), ((), ())), preferred_element_type=F32)


def dot_tn(a, b):
    return lax.dot_general(a, b, (((0,), (0,)), ((), ())), preferred_element_type=F32)


def row_mean(a):
    return jnp.sum(a, axis=-1, keepdims=True) * (1.0 / D)


def norm(summed):
    center = summed - row_mean(summed)
    inverse = lax.rsqrt(row_mean(center * center) + EPS)
    return center * inverse, inverse


def norm_back(grad, normed, inverse, gain):
    scaled = grad * gain
    return inverse * (scaled - row_mean(scaled) - normed * row_mean(scaled * normed))


def col_sum(a):
    return jnp.sum(a.astype(F32), axis=0, keepdims=True)


def lanes(start, width):
    return pl.ds(pl.multiple_of(start, 128), width)


def layer_kernel(back, half, index, x_index, gy_index, masked, count, *refs):
    refs = list(refs)
    take = lambda n: [refs.pop(0) for _ in range(n)]
    (meta,) = take(1)
    rows_ref, fbias_ref = take(2)
    pieces = take(24)
    (x_hbm,) = take(1)
    if back:
        (gy_hbm,) = take(1)
    n_alias = len(refs)
    n_out = 11 if back else 2
    n_scratch = 23 if back else 12
    take(n_alias - n_out - n_scratch)
    outs = take(n_out)
    scr = take(n_scratch)
    win, wout, wfi, wfo, x_s, qkv, ctx, act, hl, y_s, acc, sems = scr[:12]
    if back:
        (gx16_o, y_o, gx_o, sum_o, fsum_o, sx_o, sctx_o, shid_o, sdf_o, sr0_o, sr1_o) = outs[:11]
        gy_s, probs, slope, n1_s, n2_s, dr0, dpre, dfn, gx_s, sum_s, fsum_s = scr[12:]
    else:
        y1_o, y_o = outs

    @pl.when(meta[0] == half)
    def _():
        tag = meta[1 + index]
        length = meta[1 + count + index]
        cp_x = pltpu.make_async_copy(x_hbm.at[x_index], x_s, sems.at[4, 0])
        cp_x.start()
        if back:
            cp_g = pltpu.make_async_copy(gy_hbm.at[gy_index], gy_s, sems.at[4, 1])
            cp_g.start()

        def load_from(model):
            def one(unit, col, width, dst, group):
                for q in range(4):
                    src = pieces[(model * 3 + unit) * 4 + q]

                    def body(e, carry):
                        k = q * 4 + e
                        row = pl.multiple_of(meta[1 + 2 * count + unit * BLOCKS + k] * ROWS, 16)
                        pltpu.make_async_copy(
                            src.at[e, :, col : col + width],
                            dst.at[pl.ds(row, ROWS)],
                            sems.at[group, k],
                        ).start()
                        return carry

                    lax.fori_loop(0, 4, body, 0)

            one(0, 0, 3 * D, win, 0)
            one(0, 3 * D, D, wout, 1)
            one(1, 0, FF, wfi, 2)
            one(2, 0, FF, wfo, 3)

        pl.when(tag == 0)(lambda: load_from(0))
        pl.when(tag != 0)(lambda: load_from(1))

        def landed(dst, group):
            def body(k, carry):
                part = dst.at[pl.ds(0, ROWS)]
                pltpu.make_async_copy(part, part, sems.at[group, k]).wait()
                return carry

            lax.fori_loop(0, BLOCKS, body, 0)

        def small(row):
            return rows_ref[tag, row : row + 1, :]

        cp_x.wait()
        landed(win, 0)
        x = x_s[...]
        zero_row = jnp.zeros((1, D), F32)
        for n, bias in enumerate((small(0), zero_row, small(1))):
            cols = slice(n * D, (n + 1) * D)
            qkv[:, cols] = (dot_nn(x, win[:, cols]) + bias).astype(BF16)

        low_half = lax.broadcasted_iota(jnp.int32, (1, 2 * HEAD_DIM), 1) < HEAD_DIM
        head_mask = (low_half.astype(F32).astype(BF16), (1 - low_half.astype(F32)).astype(BF16))
        live = lax.broadcasted_iota(jnp.int32, (SEQ, SEQ), 1) < length

        def heads_fwd(pair, carry):
            off = pair * 2 * HEAD_DIM
            q2 = qkv[:, lanes(off, 128)]
            k2 = qkv[:, lanes(D + off, 128)]
            v2 = qkv[:, lanes(2 * D + off, 128)]
            joined = None
            for side in range(2):
                raw = dot_nt(q2 * head_mask[side], k2)
                scores = jnp.where(live, raw * SCALE, NEG)
                expo = jnp.exp(scores - jnp.max(scores, axis=-1, keepdims=True))
                prob = expo * (1.0 / jnp.sum(expo, axis=-1, keepdims=True))
                if back:
                    probs[2 * pair + side] = prob
                part = dot_nn(prob.astype(BF16), v2 * head_mask[side])
                joined = part if joined is None else joined + part
            ctx[:, lanes(off, 128)] = joined.astype(BF16)
            return carry

        lax.fori_loop(0, PAIRS, heads_fwd, 0)

        landed(wout, 1)
        branch = dot_nn(ctx[...], wout[...]) + small(2)
        n1, i1 = norm(x.astype(F32) + branch)
        hidden = n1 * small(4) + small(6)
        if back:
            n1_s[...] = n1
        hl[...] = hidden.astype(BF16)
        acc[...] = hidden
        landed(wfi, 2)
        landed(wfo, 3)

        def ffn_fwd(n, carry):
            cols = lanes(n * CHUNK, CHUNK)
            pre = dot_nn(hl[...], wfi[:, cols]) + fbias_ref[tag, :, cols]
            phi = 0.5 * (1.0 + lax.erf(pre * SQRT_HALF))
            act[:, cols] = (pre * phi).astype(BF16)
            if back:
                slope[:, cols] = phi + pre * jnp.exp(-0.5 * pre * pre) * INV_ROOT
            return carry

        lax.fori_loop(0, FF // CHUNK, ffn_fwd, 0)
        branch = dot_nt(act[...], wfo[...]) + small(3)
        n2, i2 = norm(acc[...] + branch)
        y_s[...] = (n2 * small(5) + small(7)).astype(BF16)
        copies = []

        def put(src, dst, sem):
            copy = pltpu.make_async_copy(src, dst, sem)
            copy.start()
            copies.append(copy)

        put(y_s, y_o.at[index], sems.at[5, 0])
        if not back:
            put(y_s, y1_o.at[0], sems.at[5, 1])
        else:
            put(x_s, sx_o.at[index], sems.at[5, 2])
            put(ctx, sctx_o.at[index], sems.at[5, 3])
            put(hl, shid_o.at[index], sems.at[5, 4])
            put(act, sr1_o.at[1, index], sems.at[5, 5])
            cp_g.wait()
            gy = gy_s[...].astype(F32)
            if masked:
                alive = lax.broadcasted_iota(jnp.int32, (SEQ, D), 0) < length
                gy = jnp.where(alive, gy, 0.0)
            sum_s[5:6, :] = col_sum(gy * n2)
            sum_s[7:8, :] = col_sum(gy)
            gr2 = norm_back(gy, n2, i2, small(5))
            dfn[...] = gr2.astype(BF16)
            sum_s[3:4, :] = col_sum(dfn[...])
            put(dfn, sdf_o.at[index], sems.at[5, 6])
            n2_s[...] = gr2

            def ffn_back(n, carry):
                cols = lanes(n * CHUNK, CHUNK)
                d_act = dot_nn(dfn[...], wfo[:, cols])
                d_pre = (d_act * slope[:, cols]).astype(BF16)
                dpre[:, cols] = d_pre
                fsum_s[:, cols] = col_sum(d_pre)
                return carry

            lax.fori_loop(0, FF // CHUNK, ffn_back, 0)
            put(dpre, sr1_o.at[0, index], sems.at[5, 7])
            gh = n2_s[...] + dot_nt(dpre[...], wfi[...]).astype(BF16).astype(F32)
            n1 = n1_s[...]
            sum_s[4:5, :] = col_sum(gh * n1)
            sum_s[6:7, :] = col_sum(gh)
            gr1 = norm_back(gh, n1, i1, small(4))
            acc[...] = gr1
            d_attn = gr1.astype(BF16)
            dr0[:, 3 * D :] = d_attn
            sum_s[2:3, :] = col_sum(d_attn)
            gx_s[...] = dot_nt(d_attn, wout[...]).astype(BF16)

            def heads_back(pair, carry):
                off = pair * 2 * HEAD_DIM
                q2 = qkv[:, lanes(off, 128)]
                k2 = qkv[:, lanes(D + off, 128)]
                v2 = qkv[:, lanes(2 * D + off, 128)]
                dc2 = gx_s[:, lanes(off, 128)]
                dq = dk = dv = None
                for side in range(2):
                    prob = probs[2 * pair + side]
                    dch = dc2 * head_mask[side]
                    d_prob = dot_nt(dch, v2)
                    inner = jnp.sum(prob * d_prob, axis=-1, keepdims=True)
                    d_raw = (prob * (d_prob - inner) * SCALE).astype(BF16)
                    a = dot_nn(d_raw, k2 * head_mask[side])
                    b = dot_tn(d_raw, q2 * head_mask[side])
                    c = dot_tn(prob.astype(BF16), dch)
                    dq, dk, dv = (a, b, c) if dq is None else (dq + a, dk + b, dv + c)
                dr0[:, lanes(off, 128)] = dq.astype(BF16)
                dr0[:, lanes(D + off, 128)] = dk.astype(BF16)
                dr0[:, lanes(2 * D + off, 128)] = dv.astype(BF16)
                return carry

            lax.fori_loop(0, PAIRS, heads_back, 0)
            put(dr0, sr0_o.at[index], sems.at[5, 8])
            sum_s[0:1, :] = col_sum(dr0[:, :D])
            sum_s[1:2, :] = col_sum(dr0[:, 2 * D : 3 * D])
            grad_a = dot_nt(dr0[:, : 3 * D], win[...]) + acc[...]
            n1_s[...] = grad_a
            hl_out = grad_a.astype(BF16)
            gy_s[...] = hl_out
            put(sum_s, sum_o.at[index], sems.at[5, 11])
            put(fsum_s, fsum_o.at[index], sems.at[5, 12])
            put(n1_s, gx_o.at[index], sems.at[5, 9])
            put(gy_s, gx16_o.at[0], sems.at[5, 10])
        for copy in copies:
            copy.wait()


def grad_kernel(unit, meta, *refs):
    n_left = 2 if unit == 0 else 1
    left, (right,), outs, (turned, acc) = refs[:n_left], refs[n_left : n_left + 1], refs[n_left + 1 : n_left + 5], refs[-2:]
    n = pl.program_id(0)

    @pl.when(n == 0)
    def _():
        for i in range(n_left):
            for c in range(left[i].shape[0]):
                turned[i, c] = left[i][c].T

    pick = jnp.where(n == 3, 1, 0) if unit == 0 else 0
    acc[...] = jnp.zeros_like(acc)

    def add_chain(c, carry):
        tag = jnp.where(meta[1 + c] == 0, 0, 1)
        acc[tag] += dot_nn(turned[pick, c], right[c])
        return carry

    lax.fori_loop(0, right.shape[0], add_chain, 0)
    for model in range(2):
        for p in range(BLOCKS):
            row = pl.multiple_of(meta[1 + 2 * right.shape[0] + (3 + unit) * BLOCKS + p] * ROWS, 16)
            outs[2 * model + p // 8][p % 8] = acc[model, pl.ds(row, ROWS), :].astype(BF16)


ANY = pl.BlockSpec(memory_space=pl.ANY)
SMEM = pl.BlockSpec(memory_space=pltpu.SMEM)
VMEM = pl.BlockSpec(memory_space=pltpu.VMEM)


def shaped(shape, dtype):
    return jax.ShapeDtypeStruct(shape, dtype)


def saved_shapes(count):
    narrow = shaped((count, SEQ, D), BF16)
    return [
        narrow,
        shaped((count, SEQ, D), F32),
        shaped((count, 8, D), F32),
        shaped((count, 1, FF), F32),
        narrow,
        narrow,
        narrow,
        narrow,
        shaped((count, SEQ, WIDE), BF16),
        shaped((2, count, SEQ, WIDE), BF16),
    ]


def layer_call(back, half, index, masked, count, meta, rows, fbias, pieces, x, x_index, gy, gy_index, held):
    scratch = [
        pltpu.VMEM((D, 3 * D), BF16),
        pltpu.VMEM((D, D), BF16),
        pltpu.VMEM((D, FF), BF16),
        pltpu.VMEM((D, FF), BF16),
        pltpu.VMEM((SEQ, D), BF16),
        pltpu.VMEM((SEQ, 3 * D), BF16),
        pltpu.VMEM((SEQ, D), BF16),
        pltpu.VMEM((SEQ, FF), BF16),
        pltpu.VMEM((SEQ, D), BF16),
        pltpu.VMEM((SEQ, D), BF16),
        pltpu.VMEM((SEQ, D), F32),
        pltpu.SemaphoreType.DMA((6, BLOCKS)),
    ]
    if back:
        scratch += [
            pltpu.VMEM((SEQ, D), BF16),
            pltpu.VMEM((HEADS, SEQ, SEQ), F32),
            pltpu.VMEM((SEQ, FF), F32),
            pltpu.VMEM((SEQ, D), F32),
            pltpu.VMEM((SEQ, D), F32),
            pltpu.VMEM((SEQ, WIDE), BF16),
            pltpu.VMEM((SEQ, FF), BF16),
            pltpu.VMEM((SEQ, D), BF16),
            pltpu.VMEM((SEQ, D), BF16),
            pltpu.VMEM((8, D), F32),
            pltpu.VMEM((1, FF), F32),
        ]
    operands = [meta, rows, fbias, *pieces, x]
    specs = [SMEM, VMEM, VMEM] + [ANY] * (len(pieces) + 1)
    if back:
        operands.append(gy)
        specs.append(ANY)
    first = [shaped((1, SEQ, D), BF16)]
    kept = saved_shapes(count) if back else [shaped((count, SEQ, D), BF16)]
    aliases = {}
    for at, array in enumerate(held):
        if array is not None:
            aliases[len(operands)] = at + 1
            operands.append(array)
            specs.append(ANY)
    scale = 3 if back else 1
    outs = pl.pallas_call(
        functools.partial(layer_kernel, back, half, index, x_index, gy_index, masked, count),
        out_shape=first + kept,
        in_specs=specs,
        out_specs=[ANY] * (1 + len(kept)),
        scratch_shapes=scratch,
        input_output_aliases=aliases,
        compiler_params=pltpu.CompilerParams(vmem_limit_bytes=50 * 1024 * 1024),
        cost_estimate=pl.CostEstimate(
            flops=scale * 2 * SEQ * D * 9216, bytes_accessed=scale * D * 9216 * 2, transcendentals=0
        ),
        name="layer_back" if back else "layer_fwd",
    )(*operands)
    return outs[0], list(outs[1:])


def grad_call(unit, meta, left, right, which):
    count = left[0].shape[0]
    block = (count, SEQ, CHUNK)
    if right.ndim == 4:
        right_spec = pl.BlockSpec((None,) + block, lambda n, m: (which, 0, 0, n))
    else:
        right_spec = pl.BlockSpec(block, lambda n, m: (0, 0, n))
    out = shaped((8, ROWS, WIDE), BF16)
    return pl.pallas_call(
        functools.partial(grad_kernel, unit),
        out_shape=[out] * 4,
        grid_spec=pltpu.PrefetchScalarGridSpec(
            num_scalar_prefetch=1,
            grid=(WIDE // CHUNK,),
            in_specs=[pl.BlockSpec((count, SEQ, D), lambda n, m: (0, 0, 0))] * len(left) + [right_spec],
            out_specs=[pl.BlockSpec((8, ROWS, CHUNK), lambda n, m: (0, 0, n))] * 4,
            scratch_shapes=[
                pltpu.VMEM((len(left), count, D, SEQ), BF16),
                pltpu.VMEM((2, D, CHUNK), F32),
            ],
        ),
        compiler_params=pltpu.CompilerParams(vmem_limit_bytes=50 * 1024 * 1024),
        cost_estimate=pl.CostEstimate(
            flops=2 * count * SEQ * D * WIDE * 2, bytes_accessed=4 * 8 * ROWS * WIDE * 2, transcendentals=0
        ),
        name="layer_grad",
    )(meta, *left, right)


def swap_bit(array, bit):
    count = lax.axis_size("dp")
    return lax.ppermute(array, "dp", [(i, i ^ (1 << bit)) for i in range(count)])


def swap_section(array):
    return lax.ppermute(array, "section", [(0, 1), (1, 0)])


def along(array, pairs):
    count = lax.axis_size("dp")
    flat = [(s * count + i, t * count + k) for (s, i), (t, k) in pairs]
    return lax.ppermute(array, ("section", "dp"), flat)


def swap_crossed(array):
    near = lax.axis_size("dp") // 2
    pairs = []
    for j in range(near):
        pairs += [((1, j), (0, near + j)), ((0, near + j), (1, j))]
    return along(array, pairs)


def gather_pieces(own, unit):
    one, two, three = ROTATIONS[unit]
    pair = jnp.concatenate([own, swap_bit(own, one)], 0)
    four = jnp.concatenate([pair, swap_bit(pair, two)], 0)
    far = swap_bit(four, three)
    return [four, far, swap_section(four), swap_section(far)]


def both(first, second):
    return (first.astype(F32) + second.astype(F32)).astype(BF16)


def scatter_sums(keep, send, unit):
    got = swap_section(send)
    for step, bit in enumerate(ROTATIONS[unit]):
        width = 4 >> step
        send = both(keep[width:], got[width:])
        keep = both(keep[:width], got[:width])
        got = swap_bit(send, bit)
    return keep.astype(F32) + got.astype(F32)


def per_device(
    inputs,
    cotangent,
    chain_tags,
    chain_lengths,
    attn_in,
    attn_out,
    ffn_in,
    ffn_out,
    proj_bias,
    ffn_bias,
    norm_gain,
    norm_shift,
):
    n_dp = lax.axis_size("dp")
    near = n_dp // 2
    rows = attn_in.shape[2]
    count = inputs.shape[0]
    fast = near == 8 and rows == ROWS
    section = lax.axis_index("section")
    place = lax.axis_index("dp")
    half = place // near
    spot = place % near
    at_home = section == half
    crossing = []
    for j in range(near):
        crossing += [((1, near + j), (1, j)), ((0, j), (0, near + j))]

    moved = along(jnp.where(half == 1, inputs, cotangent), crossing)
    numbers = jnp.concatenate([chain_tags, chain_lengths])
    numbers = jnp.where(at_home, numbers, along(numbers, crossing))
    chains = jnp.where(at_home, inputs, moved)
    top_grad = jnp.where(at_home, cotangent, moved)

    gap = jnp.zeros((2, rows, EXTRA - 12), BF16)
    small = jnp.concatenate(
        [
            jnp.swapaxes(proj_bias[0], 1, 2),
            jnp.swapaxes(norm_gain[0], 1, 2),
            jnp.swapaxes(norm_shift[0], 1, 2),
            ffn_bias[0].reshape(2, rows, 4),
        ],
        -1,
    ).astype(BF16)
    units = [
        jnp.concatenate([attn_in[0].astype(BF16), attn_out[0].astype(BF16), small, gap], -1),
        ffn_in[0].astype(BF16),
        jnp.swapaxes(ffn_out[0].astype(BF16), 1, 2),
    ]
    shard = spot + section * near
    if fast:
        gathered = []
        for model in range(2):
            for unit in range(3):
                own = units[unit][model : model + 1]
                own = jnp.where(at_home, own, swap_crossed(own))
                gathered.append(gather_pieces(own, unit))
        tables = [shard ^ jnp.asarray(unit_masks(unit), jnp.int32) for unit in range(3)]
        tables += [shard ^ jnp.asarray(grad_masks(unit), jnp.int32) for unit in range(3)]
    else:
        order = jnp.arange(BLOCKS, dtype=jnp.int32)
        tables = [order] * 6
        whole = []
        for unit in range(3):
            full = lax.all_gather(units[unit], ("section", "dp"), axis=0)
            full = full.reshape((2, n_dp) + full.shape[1:])
            full = lax.dynamic_index_in_dim(full, half, 0, keepdims=False)
            full = jnp.swapaxes(full, 0, 1).reshape(2, BLOCKS, ROWS, full.shape[-1])
            whole.append(full)
        gathered = [
            [whole[unit][model, 4 * q : 4 * q + 4] for q in range(4)] for model in range(2) for unit in range(3)
        ]
    meta = jnp.concatenate([half[None].astype(jnp.int32), numbers] + tables)
    pieces = [array for group in gathered for array in group]

    pick = (tables[0][None, :] == jnp.arange(BLOCKS, dtype=jnp.int32)[:, None]).astype(BF16)
    row_list, fbias_list = [], []
    for model in range(2):
        cols = jnp.concatenate([array[:, :, WIDE : WIDE + 12] for array in gathered[3 * model]], 0)
        cols = dot_nn(pick, cols.reshape(BLOCKS, ROWS * 12)).reshape(D, 12)
        row_list.append(cols[:, :8].T)
        fbias_list.append(cols[:, 8:].reshape(1, FF))
    rows_all = jnp.stack(row_list)
    fbias_all = jnp.stack(fbias_list)

    call = functools.partial(layer_call, count=count, meta=meta, rows=rows_all, fbias=fbias_all, pieces=pieces)
    forward = [((0, j), (0, near + j)) for j in range(near)] + [((1, j), (1, near + j)) for j in range(near)]
    backward = [(b, a) for a, b in forward]
    acts, act_all = [], [None]
    for c in range(count):
        out, act_all = call(False, 0, c, False, x=chains, x_index=c, gy=None, gy_index=0, held=act_all)
        acts.append(along(out, forward))
    held = act_all + [None] * 9
    grads = []
    for c in range(count):
        out, held = call(True, 1, c, True, x=acts[c], x_index=0, gy=top_grad, gy_index=c, held=held)
        grads.append(along(out, backward))
    for c in range(count):
        out, held = call(True, 0, c, False, x=chains, x_index=c, gy=grads[c], gy_index=0, held=held)
    act_all, grad_all, sums, fsums, s_x, s_ctx, s_hid, s_dffn, s_r0, s_r1 = held

    totals = [
        grad_call(2, meta, [s_dffn], s_r1, 1),
        grad_call(1, meta, [s_hid], s_r1, 0),
        grad_call(0, meta, [s_x, s_ctx], s_r0, 0),
    ]
    chosen = (numbers[None, :count] == jnp.arange(2, dtype=jnp.int32)[:, None]).astype(F32)
    row_sums = jnp.sum(chosen[:, :, None, None] * sums[None], axis=1)
    fbias_sums = jnp.sum(chosen[:, :, None] * fsums[None, :, 0], axis=1)
    small_grads = jnp.concatenate([jnp.swapaxes(row_sums, 1, 2), fbias_sums.reshape(2, D, 4)], -1)

    results = {}
    if fast:
        for at, unit in enumerate((2, 1, 0)):
            for model in range(2):
                keep, send = totals[at][2 * model : 2 * model + 2]
                results[unit, model] = scatter_sums(keep, send, unit)[0]
        laid = jnp.concatenate([small_grads, jnp.zeros((2, D, EXTRA - 12), F32)], -1).astype(BF16)
        laid = jnp.swapaxes(laid.reshape(2, BLOCKS, ROWS, EXTRA), 0, 1)
        pick = (tables[3][:, None] == jnp.arange(BLOCKS, dtype=jnp.int32)[None, :]).astype(BF16)
        laid = dot_nn(pick, laid.reshape(BLOCKS, -1)).astype(BF16).reshape(BLOCKS, 2 * ROWS, EXTRA)
        small_out = scatter_sums(laid[:8], laid[8:], 0)[0].reshape(2, ROWS, EXTRA)

        def home(array):
            return jnp.where(at_home, array, swap_crossed(array.astype(BF16)).astype(F32))

        unit_out = [jnp.stack([home(results[unit, model]) for model in range(2)]) for unit in range(3)]
        small_out = home(small_out)
    else:

        def summed(array):
            layers = jnp.stack([jnp.where(half == layer, array, jnp.zeros_like(array)) for layer in range(2)])
            layers = jnp.swapaxes(layers, 1, 2).reshape(2 * n_dp, rows, 2, array.shape[-1])
            out = lax.psum_scatter(layers, ("section", "dp"), scatter_dimension=0, tiled=True)
            return jnp.swapaxes(out[0], 0, 1)

        unit_out = [None] * 3
        for at, unit in enumerate((2, 1, 0)):
            group = [
                jnp.concatenate(totals[at][2 * model : 2 * model + 2], 0).reshape(D, WIDE) for model in range(2)
            ]
            unit_out[unit] = summed(jnp.stack(group).astype(F32))
        small_out = summed(small_grads)

    pairs = []
    for j in range(near):
        pairs += [((1, near + j), (0, near + j)), ((0, near + j), (1, j))]
    other = along(jnp.where(section == 1, jnp.concatenate(acts, 0), act_all), pairs)
    act_out = jnp.where(at_home, act_all, other)
    pairs = []
    for j in range(near):
        pairs += [((0, j), (1, j)), ((1, j), (0, near + j))]
    other = along(jnp.where(section == 0, jnp.concatenate(grads, 0), grad_all.astype(BF16)), pairs)
    grad_out = jnp.where(at_home, grad_all, other.astype(F32))

    turned = jnp.swapaxes(small_out[:, :, :8], 1, 2)
    return (
        act_out[None],
        grad_out[None],
        unit_out[0][None, :, :, : 3 * D],
        unit_out[0][None, :, :, 3 * D :],
        unit_out[1][None],
        jnp.swapaxes(unit_out[2], 1, 2)[None],
        turned[None, :, 0:4],
        small_out[:, :, 8:12].reshape(1, 2, 4 * rows),
        turned[None, :, 4:6],
        turned[None, :, 6:8],
    )


def solution(mesh):
    in_specs = (
        P("dp", None, None),
        P("dp", None, None),
        P("dp"),
        P("dp"),
        P("section", None, "dp", None),
        P("section", None, "dp", None),
        P("section", None, "dp", None),
        P("section", None, None, "dp"),
        P("section", None, None, "dp"),
        P("section", None, "dp"),
        P("section", None, None, "dp"),
        P("section", None, None, "dp"),
    )
    out_specs = (
        P("section", "dp", None, None),
        P("section", "dp", None, None),
        P("section", None, "dp", None),
        P("section", None, "dp", None),
        P("section", None, "dp", None),
        P("section", None, None, "dp"),
        P("section", None, None, "dp"),
        P("section", None, "dp"),
        P("section", None, None, "dp"),
        P("section", None, None, "dp"),
    )
    return jax.shard_map(
        per_device, mesh=mesh, in_specs=in_specs, out_specs=out_specs, check_vma=False
    )
```

time: 2750 us -> 667 us (0.24)
  waiting for transfers between devices: 1810 us -> 271 us
  local copies, waits for them, and re-layouts: 293 us -> 21.3 us
  matrix products: 266 us -> 0.56 us
  Pallas kernels: 0 us -> 212 us
  blocking collectives: 156 us -> 0 us
  starting transfers between devices: 6.54 us -> 111 us
  other arithmetic: 128 us -> 39 us
  loops' own time: 55.3 us -> 0 us
    reduce_scatter x4 -> x0, waiting for transfers between devices: 953 us -> none  [the longest x1 292 us: per_device(): lax.psum_scatter(totals[3][None], 'dp', scatter_dimension=3, tiled=True)]
    unnamed x16 -> x0, waiting for transfers between devices: 519 us -> none
    all_gather x4 -> x0, waiting for transfers between devices: 270 us -> none  [the longest x1 125 us: per_device(): lax.all_gather(ffn_in.astype(jnp.bfloat16), 'dp', axis=2, tiled=True)]
    dot_general x72 -> x3, matrix products: 252 us -> 0.56 us  [dot_nn(): return jnp.dot(a, b, preferred_element_type=F32)]
    pallas_call x0 -> x15, Pallas kernels: none -> 212 us  [the longest x12 172 us: layer_call(): pl.pallas_call(functools.partial(layer_kernel, back, half, index, x_index...]
    ppermute x4 -> x83, waiting for transfers between devices: 70.7 us -> 271 us  [the longest x39 188 us: swap_bit(): return lax.ppermute(array, 'dp', [(i, i ^ 1 << bit) for i in range(count)])]
    all_gather x4 -> x0, blocking collectives: 156 us -> none  [the longest x1 50.8 us: per_device(): lax.all_gather(ffn_bias.astype(jnp.bfloat16), 'dp', axis=2, tiled=True)]
    another operation x76 -> x4, local copies, waits for them, and re-layouts: 116 us -> 0.63 us  [the longest x3 0.52 us: per_device(): fbias_all = jnp.stack(fbias_list)]
  transfers between devices with their start and end apart: 16 -> 83, of which waited for: 13 -> 36; matrix products, arithmetic and copies ran while one was open for 11% -> 7% of each run, Pallas kernels for 0% -> 26%
where the time goes in v1:
time: 667 us; the launch traced here: 658 us
  waiting for transfers between devices  271 us (41%)
  Pallas kernels  212 us (32%)
  starting transfers between devices  111 us (17%)
  other arithmetic  39 us (6%)
  local copies, waits for them, and re-layouts  21.3 us (3%)
    ppermute x39, waiting for transfers between devices, swap_bit(): return lax.ppermute(array, 'dp', [(i, i ^ 1 << bit) for i in range(count)])  188 us
    pallas_call x12, Pallas kernels, layer_call(): pl.pallas_call(functools.partial(layer_kernel, back, half, index, x_index...  172 us
    ppermute x25, waiting for transfers between devices, along(): return lax.ppermute(array, ('section', 'dp'), flat)  79.8 us
    ppermute x25, starting transfers between devices, along(): return lax.ppermute(array, ('section', 'dp'), flat)  63.8 us
    pallas_call x3, Pallas kernels, grad_call(): pl.pallas_call(functools.partial(grad_kernel, unit), out_shape=[out] * 4,...  40.7 us
    ppermute x39, starting transfers between devices, swap_bit(): return lax.ppermute(array, 'dp', [(i, i ^ 1 << bit) for i in range(count)])  40.1 us
    convert_element_type x21, other arithmetic, both(): return (first.astype(F32) + second.astype(F32)).astype(BF16)  13.6 us
  transfers between devices with their start and end apart: 83, of which 36 were waited for; matrix products, arithmetic and copies ran while one was open for 7% of the time, Pallas kernels for 26%

profile of v1, /device:TPU:1, one launch (start us, length us, event | category | flops | bytes accessed | tf_op | source)
XLA Modules:
  0.0 657.7 jit_solution(2110016487697693988)
XLA Ops:
  2.9 5.6 collective-permute-start.13
  11.5 4.5 collective-permute-start.31
  24.0 6.1 collective-permute-done.25
  32.6 14.5 %collective-permute-done.31 = bf16[1,48,3072]{2,1,0:T(8,128)(2,1)} collective-permute-done((bf16[1,48,3072]{2,1,0:T(8,128)(2,1)}, bf16[1,48,3072]{2,1,0:T(8,128)(2,1)}, u32[]{:S(2)}, u32[]{:S(2)}) %collective-permute-start.31) | collective-permute-done | bytes 294944 | tf_op jit(solution)/shard_map/ppermute | solution.py:444
  49.3 4.2 collective-permute-done.1
  55.5 10.2 %collective-permute-done.19 = bf16[1,48,3072]{2,1,0:T(8,128)(2,1)S(1)} collective-permute-done((bf16[1,48,3072]{2,1,0:T(8,128)(2,1)S(1)}, bf16[1,48,3072]{2,1,0:T(8,128)(2,1)S(1)}, u32[]{:S(2)}, u32[]{:S(2)}) %collective-permute-start.19) | collective-permute-done | bytes 294944 | tf_op jit(solution)/shard_map/ppermute | solution.py:444
  67.1 4.6 collective-permute-start.7
  71.8 7.8 %collective-permute-done.7 = bf16[1,48,3200]{2,1,0:T(8,128)(2,1)S(1)} collective-permute-done((bf16[1,48,3200]{2,1,0:T(8,128)(2,1)S(1)}, bf16[1,48,3200]{2,1,0:T(8,128)(2,1)S(1)}, u32[]{:S(2)}, u32[]{:S(2)}) %collective-permute-start.7) | collective-permute-done | bytes 307232 | tf_op jit(solution)/shard_map/ppermute | solution.py:444
  80.2 6.3 collective-permute-done.8
  87.7 3.8 collective-permute-done.15
  92.9 11.3 %collective-permute-done.27 = bf16[2,48,3072]{2,1,0:T(8,128)(2,1)S(1)} collective-permute-done((bf16[2,48,3072]{2,1,0:T(8,128)(2,1)S(1)}, bf16[2,48,3072]{2,1,0:T(8,128)(2,1)S(1)}, u32[]{:S(2)}, u32[]{:S(2)}) %collective-permute-start.27) | collective-permute-done | bytes 589856 | tf_op jit(solution)/shard_map/ppermute | solution.py:434
  108.3 4.4 collective-permute-done.20
  116.2 38.8 %collective-permute-done.33 = bf16[2,48,3072]{2,1,0:T(8,128)(2,1)S(1)} collective-permute-done((bf16[2,48,3072]{2,1,0:T(8,128)(2,1)S(1)}, bf16[2,48,3072]{2,1,0:T(8,128)(2,1)S(1)}, u32[]{:S(2)}, u32[]{:S(2)}) %collective-permute-start.33) | collective-permute-done | bytes 589856 | tf_op jit(solution)/shard_map/ppermute | solution.py:434
  155.0 6.7 %collective-permute-done.21 = bf16[2,48,3072]{2,1,0:T(8,128)(2,1)S(1)} collective-permute-done((bf16[2,48,3072]{2,1,0:T(8,128)(2,1)S(1)}, bf16[2,48,3072]{2,1,0:T(8,128)(2,1)S(1)}, u32[]{:S(2)}, u32[]{:S(2)}) %collective-permute-start.21) | collective-permute-done | bytes 589856 | tf_op jit(solution)/shard_map/ppermute | solution.py:434
  171.0 14.3 %collective-permute-done.10.refs_16_ = bf16[4,48,3200]{2,1,0:T(8,128)(2,1)} collective-permute-done((bf16[4,48,3200]{2,1,0:T(8,128)(2,1)}, bf16[4,48,3200]{2,1,0:T(8,128)(2,1)}, u32[]{:S(2)}, u32[]{:S(2)}) %collective-permute-start.10) | collective-permute-done | bytes 1228832 | tf_op jit(solution)/shard_map/ppermute | solution.py:434
  199.2 23.3 %collective-permute-done.22.refs_12_ = bf16[4,48,3072]{2,1,0:T(8,128)(2,1)} collective-permute-done((bf16[4,48,3072]{2,1,0:T(8,128)(2,1)}, bf16[4,48,3072]{2,1,0:T(8,128)(2,1)}, u32[]{:S(2)}, u32[]{:S(2)}) %collective-permute-start.22) | collective-permute-done | bytes 1179680 | tf_op jit(solution)/shard_map/ppermute | solution.py:434
  228.2 13.4 %layer_fwd.4 = (bf16[1,160,768]{2,1,0:T(8,128)(2,1)S(1)}, bf16[4,160,768]{2,1,0:T(8,128)(2,1)S(1)}) custom-call(s32[105]{0:T(128)S(1)} %concatenate.76.refs_0_.meta, f32[2,8,768]{2,1,0:T(8,128)S(1)} %pad_maximum_fusion.15.refs_1_, f32[2,1,3072]{2,1,0:T(1,128)S(1)} %constant_dynamic-update-slice_fusion.refs_2_, bf16[4,48,3200]{2,1,0:T(8,128)(2,1)} %copy-done.22, ...), custom_call_target="tpu_custom_call" | custom-call | flops 2264924160 | bytes 14155776 | tf_op jit(solution)/shard_map/layer_fwd/pallas_call | solution.py:387
  243.0 13.7 %layer_fwd.5 = (bf16[1,160,768]{2,1,0:T(8,128)(2,1)S(1)}, bf16[4,160,768]{2,1,0:T(8,128)(2,1)S(1)}) custom-call(s32[105]{0:T(128)S(1)} %concatenate.76.refs_0_.meta, f32[2,8,768]{2,1,0:T(8,128)S(1)} %pad_maximum_fusion.15.refs_1_, f32[2,1,3072]{2,1,0:T(1,128)S(1)} %constant_dynamic-update-slice_fusion.refs_2_, ...), custom_call_target="tpu_custom_call", output_to_operand_aliasing={{1}: (28, {})} | custom-call | flops 2264924160 | bytes 14155776 | tf_op jit(solution)/shard_map/layer_fwd/pallas_call | solution.py:387
  258.0 13.5 %layer_fwd.6 = (bf16[1,160,768]{2,1,0:T(8,128)(2,1)S(1)}, bf16[4,160,768]{2,1,0:T(8,128)(2,1)S(1)}) custom-call(s32[105]{0:T(128)S(1)} %concatenate.76.refs_0_.meta, f32[2,8,768]{2,1,0:T(8,128)S(1)} %pad_maximum_fusion.15.refs_1_, f32[2,1,3072]{2,1,0:T(1,128)S(1)} %constant_dynamic-update-slice_fusion.refs_2_, ...), custom_call_target="tpu_custom_call", output_to_operand_aliasing={{1}: (28, {})} | custom-call | flops 2264924160 | bytes 14155776 | tf_op jit(solution)/shard_map/layer_fwd/pallas_call | solution.py:387
  272.9 13.5 %layer_fwd.7 = (bf16[1,160,768]{2,1,0:T(8,128)(2,1)S(1)}, bf16[4,160,768]{2,1,0:T(8,128)(2,1)S(1)}) custom-call(s32[105]{0:T(128)S(1)} %concatenate.76.refs_0_.meta, f32[2,8,768]{2,1,0:T(8,128)S(1)} %pad_maximum_fusion.15.refs_1_, f32[2,1,3072]{2,1,0:T(1,128)S(1)} %constant_dynamic-update-slice_fusion.refs_2_, ...), custom_call_target="tpu_custom_call", output_to_operand_aliasing={{1}: (28, {})} | custom-call | flops 2264924160 | bytes 14155776 | tf_op jit(solution)/shard_map/layer_fwd/pallas_call | solution.py:387
  287.7 7.6 %layer_back.8 = (bf16[1,160,768]{2,1,0:T(8,128)(2,1)S(1)}, bf16[4,160,768]{2,1,0:T(8,128)(2,1)S(1)}, f32[4,160,768]{2,1,0:T(8,128)}, f32[4,8,768]{2,1,0:T(8,128)...) custom-call(s32[105]{0:T(128)S(1)} %concatenate.76.refs_0_.meta, ...), custom_call_target="tpu_custom_call", output_to_operand_aliasing={{1}: (29, {})} | custom-call | flops 6794772480 | bytes 42467328 | tf_op jit(solution)/shard_map/layer_back/pallas_call | solution.py:387
  299.4 7.4 %layer_back.10 = (bf16[1,160,768]{2,1,0:T(8,128)(2,1)S(1)}, bf16[4,160,768]{2,1,0:T(8,128)(2,1)S(1)}, f32[4,160,768]{2,1,0:T(8,128)}, f32[4,8,768]{2,1,0:T(8,128...) custom-call(s32[105]{0:T(128)S(1)} %concatenate.76.refs_0_.meta, ...), custom_call_target="tpu_custom_call", output_to_operand_aliasing={{1}: (29, {}), {2}: (30, {}), {3}: (31, {}), {4}: (32, {}),... | custom-call | flops 6794772480 | bytes 42467328 | tf_op jit(solution)/shard_map/layer_back/pallas_call | solution.py:387
  311.0 25.2 %layer_back.12 = (bf16[1,160,768]{2,1,0:T(8,128)(2,1)}, bf16[4,160,768]{2,1,0:T(8,128)(2,1)S(1)}, f32[4,160,768]{2,1,0:T(8,128)}, f32[4,8,768]{2,1,0:T(8,128)S(1...) custom-call(s32[105]{0:T(128)S(1)} %concatenate.76.refs_0_.meta, ...), custom_call_target="tpu_custom_call", output_to_operand_aliasing={{1}: (29, {}), {2}: (30, {}), {3}: (31, {}), {4}: (32, {}),... | custom-call | flops 6794772480 | bytes 42467328 | tf_op jit(solution)/shard_map/layer_back/pallas_call | solution.py:387
  337.2 24.7 %layer_back.13 = (bf16[1,160,768]{2,1,0:T(8,128)(2,1)}, bf16[4,160,768]{2,1,0:T(8,128)(2,1)S(1)}, f32[4,160,768]{2,1,0:T(8,128)}, f32[4,8,768]{2,1,0:T(8,128)S(1...) custom-call(s32[105]{0:T(128)S(1)} %concatenate.76.refs_0_.meta, ...), custom_call_target="tpu_custom_call", output_to_operand_aliasing={{1}: (29, {}), {2}: (30, {}), {3}: (31, {}), {4}: (32, {}),... | custom-call | flops 6794772480 | bytes 42467328 | tf_op jit(solution)/shard_map/layer_back/pallas_call | solution.py:387
  363.6 24.9 %layer_back.14 = (bf16[1,160,768]{2,1,0:T(8,128)(2,1)}, bf16[4,160,768]{2,1,0:T(8,128)(2,1)S(1)}, f32[4,160,768]{2,1,0:T(8,128)}, f32[4,8,768]{2,1,0:T(8,128)S(1...) custom-call(s32[105]{0:T(128)S(1)} %concatenate.76.refs_0_.meta, ...), custom_call_target="tpu_custom_call", output_to_operand_aliasing={{1}: (29, {}), {2}: (30, {}), {3}: (31, {}), {4}: (32, {}),... | custom-call | flops 6794772480 | bytes 42467328 | tf_op jit(solution)/shard_map/layer_back/pallas_call | solution.py:387
  389.8 24.7 %layer_back.15 = (bf16[1,160,768]{2,1,0:T(8,128)(2,1)}, bf16[4,160,768]{2,1,0:T(8,128)(2,1)S(1)}, f32[4,160,768]{2,1,0:T(8,128)}, f32[4,8,768]{2,1,0:T(8,128)S(1...) custom-call(s32[105]{0:T(128)S(1)} %concatenate.76.refs_0_.meta, ...), custom_call_target="tpu_custom_call", output_to_operand_aliasing={{1}: (29, {}), {2}: (30, {}), {3}: (31, {}), {4}: (32, {}),... | custom-call | flops 6794772480 | bytes 42467328 | tf_op jit(solution)/shard_map/layer_back/pallas_call | solution.py:387
  419.9 13.3 %layer_grad.5 = (bf16[8,48,3072]{2,1,0:T(8,128)(2,1)S(1)}, bf16[8,48,3072]{2,1,0:T(8,128)(2,1)}, bf16[8,48,3072]{2,1,0:T(8,128)(2,1)}, bf16[8,48,3072]{2,1,0:T(8,128)(2,1)}) custom-call(s32[105]{0:T(128)S(1)} %concatenate.76.refs_0_.meta, bf16[4,160,768]{2,1,0:T(8,128)(2,1)S(1)} %copy-done.3, bf16[2,4,160,3072]{3,2,1,0:T(8,128)(2,1)} %get-tuple-element.206.refs_1_), custom_call_target="tpu_custom_call" | custom-call | flops 6039797760 | bytes 9437184 | tf_op jit(solution)/shard_map/layer_grad/pallas_call | solution.py:411
  436.7 13.3 %layer_grad.4 = (bf16[8,48,3072]{2,1,0:T(8,128)(2,1)S(1)}, bf16[8,48,3072]{2,1,0:T(8,128)(2,1)}, bf16[8,48,3072]{2,1,0:T(8,128)(2,1)}, bf16[8,48,3072]{2,1,0:T(8,128)(2,1)}) custom-call(s32[105]{0:T(128)S(1)} %concatenate.76.refs_0_.meta, bf16[4,160,768]{2,1,0:T(8,128)(2,1)S(1)} %copy-done.2, bf16[2,4,160,3072]{3,2,1,0:T(8,128)(2,1)} %get-tuple-element.206.refs_1_), custom_call_target="tpu_custom_call" | custom-call | flops 6039797760 | bytes 9437184 | tf_op jit(solution)/shard_map/layer_grad/pallas_call | solution.py:411
  453.5 14.1 %layer_grad.3 = (bf16[8,48,3072]{2,1,0:T(8,128)(2,1)}, bf16[8,48,3072]{2,1,0:T(8,128)(2,1)}, bf16[8,48,3072]{2,1,0:T(8,128)(2,1)}, bf16[8,48,3072]{2,1,0:T(8,128)(2,1)}) custom-call(s32[105]{0:T(128)S(1)} %concatenate.76.refs_0_.meta, bf16[4,160,768]{2,1,0:T(8,128)(2,1)S(1)} %get-tuple-element.198.refs_0_, ...), custom_call_target="tpu_custom_call" | custom-call | flops 6039797760 | bytes 9437184 | tf_op jit(solution)/shard_map/layer_grad/pallas_call | solution.py:411
  467.6 4.9 collective-permute-start.82
  475.2 3.6 collective-permute-start.47
  484.0 5.5 collective-permute-done.47
  492.7 2.7 add_convert_fusion.3
  495.3 11.7 %collective-permute-start.69 = (bf16[4,48,3072]{2,1,0:T(8,128)(2,1)S(1)}, bf16[4,48,3072]{2,1,0:T(8,128)(2,1)S(1)}, u32[]{:S(2)}, u32[]{:S(2)}) collective-permute-start(bf16[4,48,3072]{2,1,0:T(8,128)(2,1)S(1)} %get-tuple-element.259), channel_id=1, source_target_pairs={{0,4},{1,5},{2,6},{3,7},{4,0},{5,1},{6,2},{7,3},{8,12},{9,13},{10,... | collective-permute-start | bytes 3538952 | tf_op jit(solution)/shard_map/ppermute | solution.py:434
  507.1 2.7 add_convert_fusion.1
  509.9 2.7 add_convert_fusion.7
  518.2 15.4 %collective-permute-done.69 = bf16[4,48,3072]{2,1,0:T(8,128)(2,1)S(1)} collective-permute-done((bf16[4,48,3072]{2,1,0:T(8,128)(2,1)S(1)}, bf16[4,48,3072]{2,1,0:T(8,128)(2,1)S(1)}, u32[]{:S(2)}, u32[]{:S(2)}) %collective-permute-start.69) | collective-permute-done | bytes 1179680 | tf_op jit(solution)/shard_map/ppermute | solution.py:434
  535.1 23.8 %collective-permute-done.74 = bf16[4,48,3072]{2,1,0:T(8,128)(2,1)S(1)} collective-permute-done((bf16[4,48,3072]{2,1,0:T(8,128)(2,1)S(1)}, bf16[4,48,3072]{2,1,0:T(8,128)(2,1)S(1)}, u32[]{:S(2)}, u32[]{:S(2)}) %collective-permute-start.74) | collective-permute-done | bytes 1179680 | tf_op jit(solution)/shard_map/ppermute | solution.py:434
  561.2 4.3 collective-permute-done.64
  569.9 11.8 %collective-permute-done.70 = bf16[2,48,3072]{2,1,0:T(8,128)(2,1)S(1)} collective-permute-done((bf16[2,48,3072]{2,1,0:T(8,128)(2,1)S(1)}, bf16[2,48,3072]{2,1,0:T(8,128)(2,1)S(1)}, u32[]{:S(2)}, u32[]{:S(2)}) %collective-permute-start.70) | collective-permute-done | bytes 589856 | tf_op jit(solution)/shard_map/ppermute | solution.py:434
  582.3 12.1 %collective-permute-done.75 = bf16[2,48,3072]{2,1,0:T(8,128)(2,1)S(1)} collective-permute-done((bf16[2,48,3072]{2,1,0:T(8,128)(2,1)S(1)}, bf16[2,48,3072]{2,1,0:T(8,128)(2,1)S(1)}, u32[]{:S(2)}, u32[]{:S(2)}) %collective-permute-start.75) | collective-permute-done | bytes 589856 | tf_op jit(solution)/shard_map/ppermute | solution.py:434
  602.5 5.4 collective-permute-done.76
  607.9 5.6 collective-permute-start.72
  615.8 4.5 collective-permute-start.62
  622.5 4.5 collective-permute-start.57
  627.2 6.6 %collective-permute-done.72 = bf16[48,3072]{1,0:T(8,128)(2,1)S(1)} collective-permute-done((bf16[48,3072]{1,0:T(8,128)(2,1)S(1)}, bf16[48,3072]{1,0:T(8,128)(2,1)S(1)}, u32[]{:S(2)}, u32[]{:S(2)}) %collective-permute-start.72) | collective-permute-done | bytes 294944 | tf_op jit(solution)/shard_map/ppermute | solution.py:444
  635.9 13.7 %collective-permute-done.57 = bf16[48,3072]{1,0:T(8,128)(2,1)S(1)} collective-permute-done((bf16[48,3072]{1,0:T(8,128)(2,1)S(1)}, bf16[48,3072]{1,0:T(8,128)(2,1)S(1)}, u32[]{:S(2)}, u32[]{:S(2)}) %collective-permute-start.57) | collective-permute-done | bytes 294944 | tf_op jit(solution)/shard_map/ppermute | solution.py:444
  649.7 3.0 collective-permute-done.52
  (365 shorter events, 134.7 us)
Async XLA Ops:
  11.5 35.6 %collective-permute-start.31 = (bf16[1,48,3072]{2,1,0:T(8,128)(2,1)}, bf16[1,48,3072]{2,1,0:T(8,128)(2,1)}, u32[]{:S(2)}, u32[]{:S(2)}) collective-permute-start(bf16[1,48,3072]{2,1,0:T(8,128)(2,1)} %slice.479), channel_id=1, source_target_pairs={{16,8},{8,16},{17,9},{9,17},{18,10},{10,18},{19,11},{11,19},{20,12... | collective-permute-start | bytes 884744 | tf_op jit(solution)/shard_map/ppermute | solution.py:444
  17.7 35.8 %collective-permute-start.1 = (bf16[1,48,3200]{2,1,0:T(8,128)(2,1)}, bf16[1,48,3200]{2,1,0:T(8,128)(2,1)S(1)}, u32[]{:S(2)}, u32[]{:S(2)}) collective-permute-start(bf16[1,48,3200]{2,1,0:T(8,128)(2,1)} %slice.462), channel_id=1, source_target_pairs={{16,8},{8,16},{17,9},{9,17},{18,10},{10,18},{19,11},{11,19},{20,12... | collective-permute-start | bytes 921608 | tf_op jit(solution)/shard_map/ppermute | solution.py:444
  19.7 87.0 %collective-permute-start = (s32[8]{0:T(128)S(1)}, s32[8]{0:T(128)S(1)}, u32[]{:S(2)}, u32[]{:S(2)}) collective-permute-start(s32[8]{0:T(128)S(1)} %pad_add_fusion), channel_id=1, source_target_pairs={{24,16},{0,8},{25,17},{1,9},{26,18},{2,10},{27,19},{3,11},{28,20},... | collective-permute-start | bytes 104 | tf_op jit(solution)/shard_map/ppermute | solution.py:444
  22.7 90.7 %collective-permute-start.37 = (bf16[4,160,768]{2,1,0:T(8,128)(2,1)S(1)}, bf16[4,160,768]{2,1,0:T(8,128)(2,1)S(1)}, u32[]{:S(2)}, u32[]{:S(2)}) collective-permute-start(bf16[4,160,768]{2,1,0:T(8,128)(2,1)S(1)} %broadcast_select_fusion), channel_id=1, source_target_pairs={{24,16},{0,8},{25,17},{1,9},{26,18},{2,10},{27,19},{3,11},{28,20},... | collective-permute-start | bytes 2949128 | tf_op jit(solution)/shard_map/ppermute | solution.py:444
  31.2 34.5 %collective-permute-start.14 = (bf16[1,48,3072]{2,1,0:T(8,128)(2,1)S(1)}, bf16[1,48,3072]{2,1,0:T(8,128)(2,1)S(1)}, u32[]{:S(2)}, u32[]{:S(2)}) collective-permute-start(bf16[1,48,3072]{2,1,0:T(8,128)(2,1)S(1)} %get-tuple-element.289), channel_id=1, source_target_pairs={{0,2},{1,3},{2,0},{3,1},{4,6},{5,7},{6,4},{7,5},{8,10},{9,11},{10,... | collective-permute-start | bytes 884744 | tf_op jit(solution)/shard_map/ppermute | solution.py:434
  65.7 41.1 %collective-permute-start.32 = (bf16[1,48,3072]{2,1,0:T(8,128)(2,1)S(1)}, bf16[1,48,3072]{2,1,0:T(8,128)(2,1)S(1)}, u32[]{:S(2)}, u32[]{:S(2)}) collective-permute-start(bf16[1,48,3072]{2,1,0:T(8,128)(2,1)S(1)} %get-tuple-element.286), channel_id=1, source_target_pairs={{0,4},{1,5},{2,6},{3,7},{4,0},{5,1},{6,2},{7,3},{8,12},{9,13},{10,... | collective-permute-start | bytes 884744 | tf_op jit(solution)/shard_map/ppermute | solution.py:434
  106.7 56.4 %collective-permute-start.16 = (bf16[4,48,3072]{2,1,0:T(8,128)(2,1)S(1)}, bf16[4,48,3072]{2,1,0:T(8,128)(2,1)}, u32[]{:S(2)}, u32[]{:S(2)}) collective-permute-start(bf16[4,48,3072]{2,1,0:T(8,128)(2,1)S(1)} %pad_maximum_fusion.2.refs_7_), channel_id=1, source_target_pairs={{0,1},{1,0},{2,3},{3,2},{4,5},{5,4},{6,7},{7,6},{8,9},{9,8},{10,11... | collective-permute-start | bytes 3538952 | tf_op jit(solution)/shard_map/ppermute | solution.py:434
  106.8 56.9 %collective-permute-start.28 = (bf16[4,48,3072]{2,1,0:T(8,128)(2,1)}, bf16[4,48,3072]{2,1,0:T(8,128)(2,1)}, u32[]{:S(2)}, u32[]{:S(2)}) collective-permute-start(bf16[4,48,3072]{2,1,0:T(8,128)(2,1)} %pad_maximum_fusion.4.refs_19_), channel_id=1, source_target_pairs={{0,1},{1,0},{2,3},{3,2},{4,5},{5,4},{6,7},{7,6},{8,9},{9,8},{10,11... | collective-permute-start | bytes 3538952 | tf_op jit(solution)/shard_map/ppermute | solution.py:434
  112.7 50.5 %collective-permute-start.4 = (bf16[4,48,3200]{2,1,0:T(8,128)(2,1)S(1)}, bf16[4,48,3200]{2,1,0:T(8,128)(2,1)}, u32[]{:S(2)}, u32[]{:S(2)}) collective-permute-start(bf16[4,48,3200]{2,1,0:T(8,128)(2,1)S(1)} %pad_maximum_fusion.refs_3_), channel_id=1, source_target_pairs={{0,4},{1,5},{2,6},{3,7},{4,0},{5,1},{6,2},{7,3},{8,12},{9,13},{10,... | collective-permute-start | bytes 3686408 | tf_op jit(solution)/shard_map/ppermute | solution.py:434
  113.4 41.6 %collective-permute-start.33 = (bf16[2,48,3072]{2,1,0:T(8,128)(2,1)S(1)}, bf16[2,48,3072]{2,1,0:T(8,128)(2,1)S(1)}, u32[]{:S(2)}, u32[]{:S(2)}) collective-permute-start(bf16[2,48,3072]{2,1,0:T(8,128)(2,1)S(1)} %pad_maximum_fusion.11), channel_id=1, source_target_pairs={{0,1},{1,0},{2,3},{3,2},{4,5},{5,4},{6,7},{7,6},{8,9},{9,8},{10,11... | collective-permute-start | bytes 1769480 | tf_op jit(solution)/shard_map/ppermute | solution.py:434
  114.6 47.1 %collective-permute-start.21 = (bf16[2,48,3072]{2,1,0:T(8,128)(2,1)S(1)}, bf16[2,48,3072]{2,1,0:T(8,128)(2,1)S(1)}, u32[]{:S(2)}, u32[]{:S(2)}) collective-permute-start(bf16[2,48,3072]{2,1,0:T(8,128)(2,1)S(1)} %pad_maximum_fusion.9), channel_id=1, source_target_pairs={{0,1},{1,0},{2,3},{3,2},{4,5},{5,4},{6,7},{7,6},{8,9},{9,8},{10,11... | collective-permute-start | bytes 1769480 | tf_op jit(solution)/shard_map/ppermute | solution.py:434
  161.7 23.6 %collective-permute-start.10 = (bf16[4,48,3200]{2,1,0:T(8,128)(2,1)}, bf16[4,48,3200]{2,1,0:T(8,128)(2,1)}, u32[]{:S(2)}, u32[]{:S(2)}) collective-permute-start(bf16[4,48,3200]{2,1,0:T(8,128)(2,1)} %pad_maximum_fusion.1.refs_15_), channel_id=1, source_target_pairs={{0,4},{1,5},{2,6},{3,7},{4,0},{5,1},{6,2},{7,3},{8,12},{9,13},{10,... | collective-permute-start | bytes 3686408 | tf_op jit(solution)/shard_map/ppermute | solution.py:434
  163.2 23.4 %collective-permute-start.6 = (bf16[4,48,3200]{2,1,0:T(8,128)(2,1)}, bf16[4,48,3200]{2,1,0:T(8,128)(2,1)}, u32[]{:S(2)}, u32[]{:S(2)}) collective-permute-start(bf16[4,48,3200]{2,1,0:T(8,128)(2,1)} %collective-permute-done.4.refs_4_), channel_id=1, source_target_pairs={{0,16},{16,0},{1,17},{17,1},{2,18},{18,2},{3,19},{19,3},{4,20},{20... | collective-permute-start | bytes 3686408 | tf_op jit(solution)/shard_map/ppermute | solution.py:438
  169.6 26.3 %collective-permute-start.29 = (bf16[4,48,3072]{2,1,0:T(8,128)(2,1)}, bf16[4,48,3072]{2,1,0:T(8,128)(2,1)}, u32[]{:S(2)}, u32[]{:S(2)}) collective-permute-start(bf16[4,48,3072]{2,1,0:T(8,128)(2,1)} %pad_maximum_fusion.4.refs_19_), channel_id=1, source_target_pairs={{0,16},{16,0},{1,17},{17,1},{2,18},{18,2},{3,19},{19,3},{4,20},{20... | collective-permute-start | bytes 3538952 | tf_op jit(solution)/shard_map/ppermute | solution.py:438
  169.7 27.5 %collective-permute-start.34 = (bf16[4,48,3072]{2,1,0:T(8,128)(2,1)}, bf16[4,48,3072]{2,1,0:T(8,128)(2,1)}, u32[]{:S(2)}, u32[]{:S(2)}) collective-permute-start(bf16[4,48,3072]{2,1,0:T(8,128)(2,1)} %pad_maximum_fusion.5.refs_23_), channel_id=1, source_target_pairs={{0,2},{1,3},{2,0},{3,1},{4,6},{5,7},{6,4},{7,5},{8,10},{9,11},{10,... | collective-permute-start | bytes 3538952 | tf_op jit(solution)/shard_map/ppermute | solution.py:434
  185.3 37.2 %collective-permute-start.22 = (bf16[4,48,3072]{2,1,0:T(8,128)(2,1)}, bf16[4,48,3072]{2,1,0:T(8,128)(2,1)}, u32[]{:S(2)}, u32[]{:S(2)}) collective-permute-start(bf16[4,48,3072]{2,1,0:T(8,128)(2,1)} %pad_maximum_fusion.3.refs_11_), channel_id=1, source_target_pairs={{0,2},{1,3},{2,0},{3,1},{4,6},{5,7},{6,4},{7,5},{8,10},{9,11},{10,... | collective-permute-start | bytes 3538952 | tf_op jit(solution)/shard_map/ppermute | solution.py:434
  186.6 37.1 %collective-permute-start.12 = (bf16[4,48,3200]{2,1,0:T(8,128)(2,1)}, bf16[4,48,3200]{2,1,0:T(8,128)(2,1)}, u32[]{:S(2)}, u32[]{:S(2)}) collective-permute-start(bf16[4,48,3200]{2,1,0:T(8,128)(2,1)} %collective-permute-done.10.refs_16_), channel_id=1, source_target_pairs={{0,16},{16,0},{1,17},{17,1},{2,18},{18,2},{3,19},{19,3},{4,20},{20... | collective-permute-start | bytes 3686408 | tf_op jit(solution)/shard_map/ppermute | solution.py:438
  195.9 30.8 %collective-permute-start.23 = (bf16[4,48,3072]{2,1,0:T(8,128)(2,1)}, bf16[4,48,3072]{2,1,0:T(8,128)(2,1)}, u32[]{:S(2)}, u32[]{:S(2)}) collective-permute-start(bf16[4,48,3072]{2,1,0:T(8,128)(2,1)} %pad_maximum_fusion.3.refs_11_), channel_id=1, source_target_pairs={{0,16},{16,0},{1,17},{17,1},{2,18},{18,2},{3,19},{19,3},{4,20},{20... | collective-permute-start | bytes 3538952 | tf_op jit(solution)/shard_map/ppermute | solution.py:438
  197.2 29.4 %collective-permute-start.18 = (bf16[4,48,3072]{2,1,0:T(8,128)(2,1)}, bf16[4,48,3072]{2,1,0:T(8,128)(2,1)}, u32[]{:S(2)}, u32[]{:S(2)}) collective-permute-start(bf16[4,48,3072]{2,1,0:T(8,128)(2,1)} %collective-permute-done.16.refs_8_), channel_id=1, source_target_pairs={{0,16},{16,0},{1,17},{17,1},{2,18},{18,2},{3,19},{19,3},{4,20},{20... | collective-permute-start | bytes 3538952 | tf_op jit(solution)/shard_map/ppermute | solution.py:438
  199.2 27.4 %collective-permute-start.30 = (bf16[4,48,3072]{2,1,0:T(8,128)(2,1)}, bf16[4,48,3072]{2,1,0:T(8,128)(2,1)}, u32[]{:S(2)}, u32[]{:S(2)}) collective-permute-start(bf16[4,48,3072]{2,1,0:T(8,128)(2,1)} %collective-permute-done.28.refs_20_), channel_id=1, source_target_pairs={{0,16},{16,0},{1,17},{17,1},{2,18},{18,2},{3,19},{19,3},{4,20},{20... | collective-permute-start | bytes 3538952 | tf_op jit(solution)/shard_map/ppermute | solution.py:438
  241.7 46.0 %collective-permute-start.41 = (bf16[1,160,768]{2,1,0:T(8,128)(2,1)S(1)}, bf16[1,160,768]{2,1,0:T(8,128)(2,1)S(1)}, u32[]{:S(2)}, u32[]{:S(2)}) collective-permute-start(bf16[1,160,768]{2,1,0:T(8,128)(2,1)S(1)} %get-tuple-element.120), channel_id=1, source_target_pairs={{0,8},{1,9},{2,10},{3,11},{4,12},{5,13},{6,14},{7,15},{16,24},{17,... | collective-permute-start | bytes 737288 | tf_op jit(solution)/shard_map/ppermute | solution.py:444
  256.7 39.8 %collective-permute-start.40 = (bf16[1,160,768]{2,1,0:T(8,128)(2,1)S(1)}, bf16[1,160,768]{2,1,0:T(8,128)(2,1)S(1)}, u32[]{:S(2)}, u32[]{:S(2)}) collective-permute-start(bf16[1,160,768]{2,1,0:T(8,128)(2,1)S(1)} %get-tuple-element.119), channel_id=1, source_target_pairs={{0,8},{1,9},{2,10},{3,11},{4,12},{5,13},{6,14},{7,15},{16,24},{17,... | collective-permute-start | bytes 737288 | tf_op jit(solution)/shard_map/ppermute | solution.py:444
  271.5 27.8 %collective-permute-start.39 = (bf16[1,160,768]{2,1,0:T(8,128)(2,1)S(1)}, bf16[1,160,768]{2,1,0:T(8,128)(2,1)S(1)}, u32[]{:S(2)}, u32[]{:S(2)}) collective-permute-start(bf16[1,160,768]{2,1,0:T(8,128)(2,1)S(1)} %get-tuple-element.118), channel_id=1, source_target_pairs={{0,8},{1,9},{2,10},{3,11},{4,12},{5,13},{6,14},{7,15},{16,24},{17,... | collective-permute-start | bytes 737288 | tf_op jit(solution)/shard_map/ppermute | solution.py:444
  298.1 39.1 %collective-permute-start.44 = (bf16[1,160,768]{2,1,0:T(8,128)(2,1)S(1)}, bf16[1,160,768]{2,1,0:T(8,128)(2,1)S(1)}, u32[]{:S(2)}, u32[]{:S(2)}) collective-permute-start(bf16[1,160,768]{2,1,0:T(8,128)(2,1)S(1)} %get-tuple-element.154), channel_id=1, source_target_pairs={{8,0},{9,1},{10,2},{11,3},{12,4},{13,5},{14,6},{15,7},{24,16},{25,... | collective-permute-start | bytes 737288 | tf_op jit(solution)/shard_map/ppermute | solution.py:444
  306.8 56.8 %collective-permute-start.43 = (bf16[1,160,768]{2,1,0:T(8,128)(2,1)S(1)}, bf16[1,160,768]{2,1,0:T(8,128)(2,1)S(1)}, u32[]{:S(2)}, u32[]{:S(2)}) collective-permute-start(bf16[1,160,768]{2,1,0:T(8,128)(2,1)S(1)} %get-tuple-element.153), channel_id=1, source_target_pairs={{8,0},{9,1},{10,2},{11,3},{12,4},{13,5},{14,6},{15,7},{24,16},{25,... | collective-permute-start | bytes 737288 | tf_op jit(solution)/shard_map/ppermute | solution.py:444
  309.6 80.2 %collective-permute-start.42 = (bf16[1,160,768]{2,1,0:T(8,128)(2,1)S(1)}, bf16[1,160,768]{2,1,0:T(8,128)(2,1)S(1)}, u32[]{:S(2)}, u32[]{:S(2)}) collective-permute-start(bf16[1,160,768]{2,1,0:T(8,128)(2,1)S(1)} %get-tuple-element.152), channel_id=1, source_target_pairs={{8,0},{9,1},{10,2},{11,3},{12,4},{13,5},{14,6},{15,7},{24,16},{25,... | collective-permute-start | bytes 737288 | tf_op jit(solution)/shard_map/ppermute | solution.py:444
  434.6 56.5 %collective-permute-start.68 = (bf16[8,48,3072]{2,1,0:T(8,128)(2,1)}, bf16[8,48,3072]{2,1,0:T(8,128)(2,1)}, u32[]{:S(2)}, u32[]{:S(2)}) collective-permute-start(bf16[8,48,3072]{2,1,0:T(8,128)(2,1)} %get-tuple-element.213), channel_id=1, source_target_pairs={{0,16},{16,0},{1,17},{17,1},{2,18},{18,2},{3,19},{19,3},{4,20},{20... | collective-permute-start | bytes 7077896 | tf_op jit(solution)/shard_map/ppermute | solution.py:438
  434.6 60.7 %collective-permute-start.73 = (bf16[8,48,3072]{2,1,0:T(8,128)(2,1)}, bf16[8,48,3072]{2,1,0:T(8,128)(2,1)}, u32[]{:S(2)}, u32[]{:S(2)}) collective-permute-start(bf16[8,48,3072]{2,1,0:T(8,128)(2,1)} %get-tuple-element.215), channel_id=1, source_target_pairs={{0,16},{16,0},{1,17},{17,1},{2,18},{18,2},{3,19},{19,3},{4,20},{20... | collective-permute-start | bytes 7077896 | tf_op jit(solution)/shard_map/ppermute | solution.py:438
  450.0 59.8 %collective-permute-start.58 = (bf16[8,48,3072]{2,1,0:T(8,128)(2,1)}, bf16[8,48,3072]{2,1,0:T(8,128)(2,1)}, u32[]{:S(2)}, u32[]{:S(2)}) collective-permute-start(bf16[8,48,3072]{2,1,0:T(8,128)(2,1)} %get-tuple-element.208), channel_id=1, source_target_pairs={{0,16},{16,0},{1,17},{17,1},{2,18},{18,2},{3,19},{19,3},{4,20},{20... | collective-permute-start | bytes 7077896 | tf_op jit(solution)/shard_map/ppermute | solution.py:438
  451.8 29.9 %collective-permute-start.46 = (bf16[4,160,768]{2,1,0:T(8,128)(2,1)}, bf16[4,160,768]{2,1,0:T(8,128)(2,1)}, u32[]{:S(2)}, u32[]{:S(2)}) collective-permute-start(bf16[4,160,768]{2,1,0:T(8,128)(2,1)} %maximum_select_fusion), channel_id=1, source_target_pairs={{24,8},{8,16},{25,9},{9,17},{26,10},{10,18},{27,11},{11,19},{28,12... | collective-permute-start | bytes 2949128 | tf_op jit(solution)/shard_map/ppermute | solution.py:444
  481.6 30.9 %collective-permute-start.63 = (bf16[8,48,3072]{2,1,0:T(8,128)(2,1)}, bf16[8,48,3072]{2,1,0:T(8,128)(2,1)S(1)}, u32[]{:S(2)}, u32[]{:S(2)}) collective-permute-start(bf16[8,48,3072]{2,1,0:T(8,128)(2,1)} %get-tuple-element.210), channel_id=1, source_target_pairs={{0,16},{16,0},{1,17},{17,1},{2,18},{18,2},{3,19},{19,3},{4,20},{20... | collective-permute-start | bytes 7077896 | tf_op jit(solution)/shard_map/ppermute | solution.py:438
  489.6 25.2 %collective-permute-start.53 = (bf16[8,48,3072]{2,1,0:T(8,128)(2,1)}, bf16[8,48,3072]{2,1,0:T(8,128)(2,1)S(1)}, u32[]{:S(2)}, u32[]{:S(2)}) collective-permute-start(bf16[8,48,3072]{2,1,0:T(8,128)(2,1)} %get-tuple-element.204), channel_id=1, source_target_pairs={{0,16},{16,0},{1,17},{17,1},{2,18},{18,2},{3,19},{19,3},{4,20},{20... | collective-permute-start | bytes 7077896 | tf_op jit(solution)/shard_map/ppermute | solution.py:438
  491.9 24.5 %collective-permute-start.48 = (bf16[8,48,3072]{2,1,0:T(8,128)(2,1)S(1)}, bf16[8,48,3072]{2,1,0:T(8,128)(2,1)S(1)}, u32[]{:S(2)}, u32[]{:S(2)}) collective-permute-start(bf16[8,48,3072]{2,1,0:T(8,128)(2,1)S(1)} %copy-done.50), channel_id=1, source_target_pairs={{0,16},{16,0},{1,17},{17,1},{2,18},{18,2},{3,19},{19,3},{4,20},{20... | collective-permute-start | bytes 7077896 | tf_op jit(solution)/shard_map/ppermute | solution.py:438
  495.3 38.3 %collective-permute-start.69 = (bf16[4,48,3072]{2,1,0:T(8,128)(2,1)S(1)}, bf16[4,48,3072]{2,1,0:T(8,128)(2,1)S(1)}, u32[]{:S(2)}, u32[]{:S(2)}) collective-permute-start(bf16[4,48,3072]{2,1,0:T(8,128)(2,1)S(1)} %get-tuple-element.259), channel_id=1, source_target_pairs={{0,4},{1,5},{2,6},{3,7},{4,0},{5,1},{6,2},{7,3},{8,12},{9,13},{10,... | collective-permute-start | bytes 3538952 | tf_op jit(solution)/shard_map/ppermute | solution.py:434
  509.8 49.1 %collective-permute-start.74 = (bf16[4,48,3072]{2,1,0:T(8,128)(2,1)S(1)}, bf16[4,48,3072]{2,1,0:T(8,128)(2,1)S(1)}, u32[]{:S(2)}, u32[]{:S(2)}) collective-permute-start(bf16[4,48,3072]{2,1,0:T(8,128)(2,1)S(1)} %get-tuple-element.261), channel_id=1, source_target_pairs={{0,4},{1,5},{2,6},{3,7},{4,0},{5,1},{6,2},{7,3},{8,12},{9,13},{10,... | collective-permute-start | bytes 3538952 | tf_op jit(solution)/shard_map/ppermute | solution.py:434
  512.6 47.8 %collective-permute-start.59 = (bf16[4,48,3072]{2,1,0:T(8,128)(2,1)S(1)}, bf16[4,48,3072]{2,1,0:T(8,128)(2,1)S(1)}, u32[]{:S(2)}, u32[]{:S(2)}) collective-permute-start(bf16[4,48,3072]{2,1,0:T(8,128)(2,1)S(1)} %get-tuple-element.263), channel_id=1, source_target_pairs={{0,2},{1,3},{2,0},{3,1},{4,6},{5,7},{6,4},{7,5},{8,10},{9,11},{10,... | collective-permute-start | bytes 3538952 | tf_op jit(solution)/shard_map/ppermute | solution.py:434
  514.8 50.6 %collective-permute-start.64 = (bf16[4,48,3072]{2,1,0:T(8,128)(2,1)S(1)}, bf16[4,48,3072]{2,1,0:T(8,128)(2,1)S(1)}, u32[]{:S(2)}, u32[]{:S(2)}) collective-permute-start(bf16[4,48,3072]{2,1,0:T(8,128)(2,1)S(1)} %get-tuple-element.265), channel_id=1, source_target_pairs={{0,2},{1,3},{2,0},{3,1},{4,6},{5,7},{6,4},{7,5},{8,10},{9,11},{10,... | collective-permute-start | bytes 3538952 | tf_op jit(solution)/shard_map/ppermute | solution.py:434
  516.5 50.5 %collective-permute-start.54 = (bf16[4,48,3072]{2,1,0:T(8,128)(2,1)S(1)}, bf16[4,48,3072]{2,1,0:T(8,128)(2,1)S(1)}, u32[]{:S(2)}, u32[]{:S(2)}) collective-permute-start(bf16[4,48,3072]{2,1,0:T(8,128)(2,1)S(1)} %get-tuple-element.267), channel_id=1, source_target_pairs={{0,1},{1,0},{2,3},{3,2},{4,5},{5,4},{6,7},{7,6},{8,9},{9,8},{10,11... | collective-permute-start | bytes 3538952 | tf_op jit(solution)/shard_map/ppermute | solution.py:434
  533.6 35.4 %collective-permute-start.49 = (bf16[4,48,3072]{2,1,0:T(8,128)(2,1)S(1)}, bf16[4,48,3072]{2,1,0:T(8,128)(2,1)S(1)}, u32[]{:S(2)}, u32[]{:S(2)}) collective-permute-start(bf16[4,48,3072]{2,1,0:T(8,128)(2,1)S(1)} %get-tuple-element.269), channel_id=1, source_target_pairs={{0,1},{1,0},{2,3},{3,2},{4,5},{5,4},{6,7},{7,6},{8,9},{9,8},{10,11... | collective-permute-start | bytes 3538952 | tf_op jit(solution)/shard_map/ppermute | solution.py:434
  560.4 33.9 %collective-permute-start.75 = (bf16[2,48,3072]{2,1,0:T(8,128)(2,1)S(1)}, bf16[2,48,3072]{2,1,0:T(8,128)(2,1)S(1)}, u32[]{:S(2)}, u32[]{:S(2)}) collective-permute-start(bf16[2,48,3072]{2,1,0:T(8,128)(2,1)S(1)} %get-tuple-element.273), channel_id=1, source_target_pairs={{0,1},{1,0},{2,3},{3,2},{4,5},{5,4},{6,7},{7,6},{8,9},{9,8},{10,11... | collective-permute-start | bytes 1769480 | tf_op jit(solution)/shard_map/ppermute | solution.py:434
  565.4 29.4 %collective-permute-start.60 = (bf16[2,48,3072]{2,1,0:T(8,128)(2,1)S(1)}, bf16[2,48,3072]{2,1,0:T(8,128)(2,1)S(1)}, u32[]{:S(2)}, u32[]{:S(2)}) collective-permute-start(bf16[2,48,3072]{2,1,0:T(8,128)(2,1)S(1)} %get-tuple-element.275), channel_id=1, source_target_pairs={{0,4},{1,5},{2,6},{3,7},{4,0},{5,1},{6,2},{7,3},{8,12},{9,13},{10,... | collective-permute-start | bytes 1769480 | tf_op jit(solution)/shard_map/ppermute | solution.py:434
  567.0 29.0 %collective-permute-start.65 = (bf16[2,48,3072]{2,1,0:T(8,128)(2,1)S(1)}, bf16[2,48,3072]{2,1,0:T(8,128)(2,1)S(1)}, u32[]{:S(2)}, u32[]{:S(2)}) collective-permute-start(bf16[2,48,3072]{2,1,0:T(8,128)(2,1)S(1)} %get-tuple-element.277), channel_id=1, source_target_pairs={{0,4},{1,5},{2,6},{3,7},{4,0},{5,1},{6,2},{7,3},{8,12},{9,13},{10,... | collective-permute-start | bytes 1769480 | tf_op jit(solution)/shard_map/ppermute | solution.py:434
  569.0 27.5 %collective-permute-start.55 = (bf16[2,48,3072]{2,1,0:T(8,128)(2,1)S(1)}, bf16[2,48,3072]{2,1,0:T(8,128)(2,1)S(1)}, u32[]{:S(2)}, u32[]{:S(2)}) collective-permute-start(bf16[2,48,3072]{2,1,0:T(8,128)(2,1)S(1)} %get-tuple-element.279), channel_id=1, source_target_pairs={{0,2},{1,3},{2,0},{3,1},{4,6},{5,7},{6,4},{7,5},{8,10},{9,11},{10,... | collective-permute-start | bytes 1769480 | tf_op jit(solution)/shard_map/ppermute | solution.py:434
  607.9 25.8 %collective-permute-start.72 = (bf16[48,3072]{1,0:T(8,128)(2,1)S(1)}, bf16[48,3072]{1,0:T(8,128)(2,1)S(1)}, u32[]{:S(2)}, u32[]{:S(2)}) collective-permute-start(bf16[48,3072]{1,0:T(8,128)(2,1)S(1)} %bitcast_convert_fusion.1), channel_id=1, source_target_pairs={{16,8},{8,16},{17,9},{9,17},{18,10},{10,18},{19,11},{11,19},{20,12... | collective-permute-start | bytes 884744 | tf_op jit(solution)/shard_map/ppermute | solution.py:444
  613.7 39.9 %collective-permute-start.77 = (bf16[48,3072]{1,0:T(8,128)(2,1)S(1)}, bf16[48,3072]{1,0:T(8,128)(2,1)S(1)}, u32[]{:S(2)}, u32[]{:S(2)}) collective-permute-start(bf16[48,3072]{1,0:T(8,128)(2,1)S(1)} %bitcast_convert_fusion), channel_id=1, source_target_pairs={{16,8},{8,16},{17,9},{9,17},{18,10},{10,18},{19,11},{11,19},{20,12... | collective-permute-start | bytes 884744 | tf_op jit(solution)/shard_map/ppermute | solution.py:444
  615.8 39.0 %collective-permute-start.62 = (bf16[48,3072]{1,0:T(8,128)(2,1)S(1)}, bf16[48,3072]{1,0:T(8,128)(2,1)S(1)}, u32[]{:S(2)}, u32[]{:S(2)}) collective-permute-start(bf16[48,3072]{1,0:T(8,128)(2,1)S(1)} %bitcast_convert_fusion.3), channel_id=1, source_target_pairs={{16,8},{8,16},{17,9},{9,17},{18,10},{10,18},{19,11},{11,19},{20,12... | collective-permute-start | bytes 884744 | tf_op jit(solution)/shard_map/ppermute | solution.py:444
  620.5 35.5 %collective-permute-start.67 = (bf16[48,3072]{1,0:T(8,128)(2,1)S(1)}, bf16[48,3072]{1,0:T(8,128)(2,1)S(1)}, u32[]{:S(2)}, u32[]{:S(2)}) collective-permute-start(bf16[48,3072]{1,0:T(8,128)(2,1)S(1)} %bitcast_convert_fusion.2), channel_id=1, source_target_pairs={{16,8},{8,16},{17,9},{9,17},{18,10},{10,18},{19,11},{11,19},{20,12... | collective-permute-start | bytes 884744 | tf_op jit(solution)/shard_map/ppermute | solution.py:444
  622.5 27.1 %collective-permute-start.57 = (bf16[48,3072]{1,0:T(8,128)(2,1)S(1)}, bf16[48,3072]{1,0:T(8,128)(2,1)S(1)}, u32[]{:S(2)}, u32[]{:S(2)}) collective-permute-start(bf16[48,3072]{1,0:T(8,128)(2,1)S(1)} %bitcast_convert_fusion.4), channel_id=1, source_target_pairs={{16,8},{8,16},{17,9},{9,17},{18,10},{10,18},{19,11},{11,19},{20,12... | collective-permute-start | bytes 884744 | tf_op jit(solution)/shard_map/ppermute | solution.py:444
  (86 other events, 1344.5 us)

commit v2 on v1

v2 whole, which is shorter than its diff:
```python
import functools

import jax
import jax.numpy as jnp
from jax import lax
from jax.experimental import pallas as pl
from jax.experimental.pallas import tpu as pltpu
from jax.sharding import PartitionSpec as P

D = 768
HEADS = 12
HEAD_DIM = 64
FF = 3072
SEQ = 160
PAIRS = HEADS // 2
BLOCKS = 16
ROWS = D // BLOCKS
WIDE = 3072
EXTRA = 128
CHUNK = 768

EPS = 1e-05
NEG = -1e30
SQRT_HALF = 0.7071067811865476
INV_ROOT = 0.3989422804014327
SCALE = HEAD_DIM**-0.5

ROTATIONS = ((0, 1, 2), (1, 2, 0), (2, 0, 1))
F32 = jnp.float32
BF16 = jnp.bfloat16


def piece_masks(unit):
    one, two, three = (1 << bit for bit in ROTATIONS[unit])
    return [far | mask for far in (0, three) for mask in (0, one, two, two | one)]


def grad_masks(rotation):
    one, two, three = (1 << bit for bit in rotation)
    return [(one if p & 4 else 0) | (two if p & 2 else 0) | (three if p & 1 else 0) for p in range(8)]


def grad_place(mask, rotation):
    one, two, three = rotation
    return ((mask >> one) & 1) * 4 + ((mask >> two) & 1) * 2 + ((mask >> three) & 1)


def dot_nn(a, b):
    return jnp.dot(a, b, preferred_element_type=F32)


def dot_nt(a, b):
    return lax.dot_general(a, b, (((1,), (1,)), ((), ())), preferred_element_type=F32)


def dot_tn(a, b):
    return lax.dot_general(a, b, (((0,), (0,)), ((), ())), preferred_element_type=F32)


def row_mean(a):
    return jnp.sum(a, axis=-1, keepdims=True) * (1.0 / D)


def norm(summed):
    center = summed - row_mean(summed)
    inverse = lax.rsqrt(row_mean(center * center) + EPS)
    return center * inverse, inverse


def norm_back(grad, normed, inverse, gain):
    scaled = grad * gain
    return inverse * (scaled - row_mean(scaled) - normed * row_mean(scaled * normed))


def col_sum(a):
    return jnp.sum(a.astype(F32), axis=0, keepdims=True)


def lanes(start, width):
    return pl.ds(pl.multiple_of(start, 128), width)


def layer_kernel(back, slot, lead, count, *refs):
    refs = list(refs)
    take = lambda n: [refs.pop(0) for _ in range(n)]
    has_high, has_low = back and slot < count, not back or slot >= lead
    (meta,) = take(1)
    rows_ref, fbias_ref = take(2)
    own_pieces, twin_joined, twin_last = take(12), take(3), take(3)
    (chains_hbm,) = take(1)
    act_hbm, top_hbm = take(2) if has_high else (None, None)
    (grad_hbm,) = take(1) if back and has_low else (None,)
    n_out = 10 if back else 2
    n_scratch = 23 if back else 12
    take(len(refs) - n_out - n_scratch)
    outs = take(n_out)
    scr = take(n_scratch)
    win, wout, wfi, wfo, x_s, qkv, ctx, act, hl, y_s, acc, sems = scr[:12]
    if back:
        (gx16_o, y_o, gx_o, sum_o, fsum_o, sx_o, sctx_o, shid_o, sdf_o, sr_o) = outs
        gy_s, probs, slope, n1_s, n2_s, dr0, dpre, dfn, gx_s, sum_s, fsum_s = scr[12:]
    else:
        y1_o, y_o = outs
    high = meta[0] == 1
    low = meta[0] == 0
    active = (high | low) if has_high and has_low else (high if has_high else low)

    @pl.when(active)
    def _():
        shift = lead if back else 0
        index = jnp.where(high, slot, slot - shift)
        length = meta[1 + count + index]

        def fetch(src, dst, sem):
            pltpu.make_async_copy(src, dst, sem).start()

        if has_high:

            @pl.when(high)
            def _():
                fetch(act_hbm.at[0], x_s, sems.at[4, 0])
                fetch(top_hbm.at[slot], gy_s, sems.at[4, 1])

        if has_low:

            @pl.when(low)
            def _():
                fetch(chains_hbm.at[slot - shift], x_s, sems.at[4, 0])
                if back:
                    fetch(grad_hbm.at[0], gy_s, sems.at[4, 1])

        def load_from(side):
            def one(unit, col, width, dst, group):
                for q in range(4):
                    if side == 0:
                        src, first = own_pieces[unit * 4 + q], col
                    elif q < 3:
                        src, first = twin_joined[q], unit * WIDE + col
                    else:
                        src, first = twin_last[unit], col

                    def body(e, carry):
                        k = q * 4 + e
                        row = pl.multiple_of(meta[1 + 3 * count + unit * BLOCKS + k] * ROWS, 16)
                        fetch(src.at[e, :, first : first + width], dst.at[pl.ds(row, ROWS)], sems.at[group, k])
                        return carry

                    lax.fori_loop(0, 4, body, 0)

            one(0, 0, 3 * D, win, 0)
            one(0, 3 * D, D, wout, 1)
            one(1, 0, FF, wfi, 2)
            one(2, 0, FF, wfo, 3)

        side = meta[1 + 2 * count + index]
        pl.when(side == 0)(lambda: load_from(0))
        pl.when(side != 0)(lambda: load_from(1))

        def landed(dst, group):
            def body(k, carry):
                part = dst.at[pl.ds(0, ROWS)]
                pltpu.make_async_copy(part, part, sems.at[group, k]).wait()
                return carry

            lax.fori_loop(0, BLOCKS, body, 0)

        def small(row):
            return rows_ref[side, row : row + 1, :]

        pltpu.make_async_copy(x_s, x_s, sems.at[4, 0]).wait()
        landed(win, 0)
        x = x_s[...]
        zero_row = jnp.zeros((1, D), F32)
        for n, bias in enumerate((small(0), zero_row, small(1))):
            cols = slice(n * D, (n + 1) * D)
            qkv[:, cols] = (dot_nn(x, win[:, cols]) + bias).astype(BF16)

        low_half = lax.broadcasted_iota(jnp.int32, (1, 2 * HEAD_DIM), 1) < HEAD_DIM
        head_mask = (low_half.astype(F32).astype(BF16), (1 - low_half.astype(F32)).astype(BF16))
        live = lax.broadcasted_iota(jnp.int32, (SEQ, SEQ), 1) < length

        def heads_fwd(pair, carry):
            off = pair * 2 * HEAD_DIM
            q2 = qkv[:, lanes(off, 128)]
            k2 = qkv[:, lanes(D + off, 128)]
            v2 = qkv[:, lanes(2 * D + off, 128)]
            joined = None
            for side in range(2):
                raw = dot_nt(q2 * head_mask[side], k2)
                scores = jnp.where(live, raw * SCALE, NEG)
                expo = jnp.exp(scores - jnp.max(scores, axis=-1, keepdims=True))
                prob = expo * (1.0 / jnp.sum(expo, axis=-1, keepdims=True))
                if back:
                    probs[2 * pair + side] = prob
                part = dot_nn(prob.astype(BF16), v2 * head_mask[side])
                joined = part if joined is None else joined + part
            ctx[:, lanes(off, 128)] = joined.astype(BF16)
            return carry

        lax.fori_loop(0, PAIRS, heads_fwd, 0, unroll=True)

        landed(wout, 1)
        branch = dot_nn(ctx[...], wout[...]) + small(2)
        n1, i1 = norm(x.astype(F32) + branch)
        hidden = n1 * small(4) + small(6)
        if back:
            n1_s[...] = n1
        hl[...] = hidden.astype(BF16)
        acc[...] = hidden
        landed(wfi, 2)
        landed(wfo, 3)

        def ffn_fwd(n, carry):
            cols = lanes(n * CHUNK, CHUNK)
            pre = dot_nn(hl[...], wfi[:, cols]) + fbias_ref[side, :, cols]
            phi = 0.5 * (1.0 + lax.erf(pre * SQRT_HALF))
            act[:, cols] = (pre * phi).astype(BF16)
            if back:
                slope[:, cols] = phi + pre * jnp.exp(-0.5 * pre * pre) * INV_ROOT
            return carry

        lax.fori_loop(0, FF // CHUNK, ffn_fwd, 0, unroll=True)
        branch = dot_nt(act[...], wfo[...]) + small(3)
        n2, i2 = norm(acc[...] + branch)
        y_s[...] = (n2 * small(5) + small(7)).astype(BF16)
        copies = []

        def put(src, dst, sem):
            copy = pltpu.make_async_copy(src, dst, sem)
            copy.start()
            copies.append(copy)

        put(y_s, y_o.at[index], sems.at[5, 0])
        if not back:
            put(y_s, y1_o.at[0], sems.at[5, 1])
        else:
            put(x_s, sx_o.at[index], sems.at[5, 2])
            put(ctx, sctx_o.at[index], sems.at[5, 3])
            put(hl, shid_o.at[index], sems.at[5, 4])
            put(act, sr_o.at[2, index], sems.at[5, 5])
            pltpu.make_async_copy(gy_s, gy_s, sems.at[4, 1]).wait()
            alive = lax.broadcasted_iota(jnp.int32, (SEQ, D), 0) < jnp.where(high, length, SEQ)
            gy = jnp.where(alive, gy_s[...].astype(F32), 0.0)
            sum_s[5:6, :] = col_sum(gy * n2)
            sum_s[7:8, :] = col_sum(gy)
            gr2 = norm_back(gy, n2, i2, small(5))
            dfn[...] = gr2.astype(BF16)
            sum_s[3:4, :] = col_sum(dfn[...])
            put(dfn, sdf_o.at[index], sems.at[5, 6])
            n2_s[...] = gr2

            def ffn_back(n, carry):
                cols = lanes(n * CHUNK, CHUNK)
                d_act = dot_nn(dfn[...], wfo[:, cols])
                d_pre = (d_act * slope[:, cols]).astype(BF16)
                dpre[:, cols] = d_pre
                fsum_s[:, cols] = col_sum(d_pre)
                return carry

            lax.fori_loop(0, FF // CHUNK, ffn_back, 0, unroll=True)
            put(dpre, sr_o.at[1, index], sems.at[5, 7])
            gh = n2_s[...] + dot_nt(dpre[...], wfi[...]).astype(BF16).astype(F32)
            n1 = n1_s[...]
            sum_s[4:5, :] = col_sum(gh * n1)
            sum_s[6:7, :] = col_sum(gh)
            gr1 = norm_back(gh, n1, i1, small(4))
            acc[...] = gr1
            d_attn = gr1.astype(BF16)
            dr0[:, 3 * D :] = d_attn
            sum_s[2:3, :] = col_sum(d_attn)
            gx_s[...] = dot_nt(d_attn, wout[...]).astype(BF16)

            def heads_back(pair, carry):
                off = pair * 2 * HEAD_DIM
                q2 = qkv[:, lanes(off, 128)]
                k2 = qkv[:, lanes(D + off, 128)]
                v2 = qkv[:, lanes(2 * D + off, 128)]
                dc2 = gx_s[:, lanes(off, 128)]
                dq = dk = dv = None
                for side in range(2):
                    prob = probs[2 * pair + side]
                    dch = dc2 * head_mask[side]
                    d_prob = dot_nt(dch, v2)
                    inner = jnp.sum(prob * d_prob, axis=-1, keepdims=True)
                    d_raw = (prob * (d_prob - inner) * SCALE).astype(BF16)
                    a = dot_nn(d_raw, k2 * head_mask[side])
                    b = dot_tn(d_raw, q2 * head_mask[side])
                    c = dot_tn(prob.astype(BF16), dch)
                    dq, dk, dv = (a, b, c) if dq is None else (dq + a, dk + b, dv + c)
                dr0[:, lanes(off, 128)] = dq.astype(BF16)
                dr0[:, lanes(D + off, 128)] = dk.astype(BF16)
                dr0[:, lanes(2 * D + off, 128)] = dv.astype(BF16)
                return carry

            lax.fori_loop(0, PAIRS, heads_back, 0, unroll=True)
            put(dr0, sr_o.at[0, index], sems.at[5, 8])
            sum_s[0:1, :] = col_sum(dr0[:, :D])
            sum_s[1:2, :] = col_sum(dr0[:, 2 * D : 3 * D])
            grad_a = dot_nt(dr0[:, : 3 * D], win[...]) + acc[...]
            n1_s[...] = grad_a
            hl_out = grad_a.astype(BF16)
            gy_s[...] = hl_out
            put(sum_s, sum_o.at[index], sems.at[5, 11])
            put(fsum_s, fsum_o.at[index], sems.at[5, 12])
            put(n1_s, gx_o.at[index], sems.at[5, 9])
            put(gy_s, gx16_o.at[0], sems.at[5, 10])
        for copy in copies:
            copy.wait()


def grad_kernel(unit, at, meta, *refs):
    n_left = 2 if unit == 0 else 1
    left, (right,), outs, (turned,) = refs[:n_left], refs[n_left : n_left + 1], refs[n_left + 1 : n_left + 3], refs[-1:]
    count, half = right.shape[0], D // 2
    n = pl.program_id(0)

    @pl.when(n == 0)
    def _():
        for i in range(n_left):
            for side in range(2):
                chains = [jnp.where(meta[c] == side, left[i][c], jnp.zeros_like(left[i][c])) for c in range(count)]
                turned[i, side * half : (side + 1) * half, :] = jnp.concatenate(chains, 0).T

    pick = jnp.where(n == 3, 1, 0) if unit == 0 else 0
    total = dot_nn(turned[pick], right[...].reshape(count * SEQ, CHUNK)).astype(BF16)
    for side in range(2):
        for block in range(8):
            row = side * half + block * ROWS
            outs[side][meta[count + 2 + (unit * 2 + at) * 8 + block]] = total[row : row + ROWS]


ANY = pl.BlockSpec(memory_space=pl.ANY)
SMEM = pl.BlockSpec(memory_space=pltpu.SMEM)
VMEM = pl.BlockSpec(memory_space=pltpu.VMEM)


def shaped(shape, dtype):
    return jax.ShapeDtypeStruct(shape, dtype)


def saved_shapes(count):
    narrow = shaped((count, SEQ, D), BF16)
    return [
        narrow,
        shaped((count, SEQ, D), F32),
        shaped((count, 8, D), F32),
        shaped((count, 1, FF), F32),
        narrow,
        narrow,
        narrow,
        narrow,
        shaped((3, count, SEQ, WIDE), BF16),
    ]


def layer_call(back, slot, lead, count, meta, rows, fbias, pieces, sources, held):
    scratch = [
        pltpu.VMEM((D, 3 * D), BF16),
        pltpu.VMEM((D, D), BF16),
        pltpu.VMEM((D, FF), BF16),
        pltpu.VMEM((D, FF), BF16),
        pltpu.VMEM((SEQ, D), BF16),
        pltpu.VMEM((SEQ, 3 * D), BF16),
        pltpu.VMEM((SEQ, D), BF16),
        pltpu.VMEM((SEQ, FF), BF16),
        pltpu.VMEM((SEQ, D), BF16),
        pltpu.VMEM((SEQ, D), BF16),
        pltpu.VMEM((SEQ, D), F32),
        pltpu.SemaphoreType.DMA((6, BLOCKS)),
    ]
    if back:
        scratch += [
            pltpu.VMEM((SEQ, D), BF16),
            pltpu.VMEM((HEADS, SEQ, SEQ), F32),
            pltpu.VMEM((SEQ, FF), F32),
            pltpu.VMEM((SEQ, D), F32),
            pltpu.VMEM((SEQ, D), F32),
            pltpu.VMEM((SEQ, WIDE), BF16),
            pltpu.VMEM((SEQ, FF), BF16),
            pltpu.VMEM((SEQ, D), BF16),
            pltpu.VMEM((SEQ, D), BF16),
            pltpu.VMEM((8, D), F32),
            pltpu.VMEM((1, FF), F32),
        ]
    operands = [meta, rows, fbias, *pieces, *sources]
    specs = [SMEM, VMEM, VMEM] + [ANY] * (len(pieces) + len(sources))
    first = [shaped((1, SEQ, D), BF16)]
    kept = saved_shapes(count) if back else [shaped((count, SEQ, D), BF16)]
    aliases = {}
    for at, array in enumerate(held):
        if array is not None:
            aliases[len(operands)] = at + 1
            operands.append(array)
            specs.append(ANY)
    outs = pl.pallas_call(
        functools.partial(layer_kernel, back, slot, lead, count),
        out_shape=first + kept,
        in_specs=specs,
        out_specs=[ANY] * (1 + len(kept)),
        scratch_shapes=scratch,
        input_output_aliases=aliases,
        compiler_params=pltpu.CompilerParams(vmem_limit_bytes=50 * 1024 * 1024),
        cost_estimate=pl.CostEstimate(flops=1, bytes_accessed=1, transcendentals=0),
        name="layer_back" if back else "layer_fwd",
    )(*operands)
    return outs[0], list(outs[1:])


def grad_call(unit, at, meta, left, right):
    count = left[0].shape[0]
    right_spec = pl.BlockSpec((None, count, SEQ, CHUNK), lambda n, m: (unit, 0, 0, n))
    out = shaped((8, ROWS, WIDE), BF16)
    return pl.pallas_call(
        functools.partial(grad_kernel, unit, at),
        out_shape=[out] * 2,
        grid_spec=pltpu.PrefetchScalarGridSpec(
            num_scalar_prefetch=1,
            grid=(WIDE // CHUNK,),
            in_specs=[pl.BlockSpec((count, SEQ, D // 2), lambda n, m: (0, 0, m[count + at]))] * len(left)
            + [right_spec],
            out_specs=[pl.BlockSpec((8, ROWS, CHUNK), lambda n, m: (0, 0, n))] * 2,
            scratch_shapes=[
                pltpu.VMEM((len(left), D, count * SEQ), BF16),
            ],
        ),
        compiler_params=pltpu.CompilerParams(vmem_limit_bytes=50 * 1024 * 1024),
        cost_estimate=pl.CostEstimate(flops=1, bytes_accessed=1, transcendentals=0),
        name="layer_grad",
    )(meta, *left, right)


def swap_bit(array, bit):
    count = lax.axis_size("dp")
    return lax.ppermute(array, "dp", [(i, i ^ (1 << bit)) for i in range(count)])


def swap_section(array):
    return lax.ppermute(array, "section", [(0, 1), (1, 0)])


def along(array, pairs):
    count = lax.axis_size("dp")
    flat = [(s * count + i, t * count + k) for (s, i), (t, k) in pairs]
    return lax.ppermute(array, ("section", "dp"), flat)


def both(first, second):
    return (first.astype(F32) + second.astype(F32)).astype(BF16)


def after(array, *others):
    others = [other for other in others if other is not None]
    return lax.optimization_barrier((array, *others))[0] if others else array


class Waves:
    def __init__(self):
        self.before = ()

    def __call__(self, *sends):
        arrays = lax.optimization_barrier(tuple(array for array, _ in sends) + self.before)[: len(sends)]
        self.before = tuple(move(array) for array, (_, move) in zip(arrays, sends))
        return list(self.before)


def by_bit(bit):
    return lambda array: swap_bit(array, bit)


def by(pairs):
    return lambda array: along(array, pairs)


class Routes:
    def __init__(self, near):
        self.home_to_away = [((h, h * near + j), (1 - h, h * near + j)) for h in range(2) for j in range(near)]
        self.away_to_home = [(b, a) for a, b in self.home_to_away]
        self.straight = [((s, (1 - s) * near + j), (s, s * near + j)) for s in range(2) for j in range(near)]
        self.straight_back = [(b, a) for a, b in self.straight]
        self.crossed = [((s, (1 - s) * near + j), (1 - s, s * near + j)) for s in range(2) for j in range(near)]
        self.up = [((s, j), (s, near + j)) for s in range(2) for j in range(near)]
        self.down = [(b, a) for a, b in self.up]


def per_device(
    inputs,
    cotangent,
    chain_tags,
    chain_lengths,
    attn_in,
    attn_out,
    ffn_in,
    ffn_out,
    proj_bias,
    ffn_bias,
    norm_gain,
    norm_shift,
):
    n_dp = lax.axis_size("dp")
    near = n_dp // 2
    rows = attn_in.shape[2]
    count = inputs.shape[0]
    fast = near == 8 and rows == ROWS
    routes = Routes(near)
    section = lax.axis_index("section")
    place = lax.axis_index("dp")
    half = place // near
    spot = place % near
    at_home = section == half

    native = jnp.concatenate(
        [
            attn_in[0].astype(BF16),
            attn_out[0].astype(BF16),
            ffn_in[0].astype(BF16),
            jnp.swapaxes(ffn_out[0].astype(BF16), 1, 2),
        ],
        -1,
    )
    smalls = jnp.concatenate([proj_bias[0], norm_gain[0], norm_shift[0]], 1).astype(BF16)
    wides = ffn_bias[0].astype(BF16)
    numbers = jnp.concatenate([chain_tags, chain_lengths])
    crossing = routes.straight_back
    if fast:
        mine = jnp.where(section == 0, native[0], native[1])
        twin = jnp.where(section == 0, native[1], native[0])
        wave = Waves()
        cuts = (0, WIDE, 2 * WIDE, 3 * WIDE)

        def bits(held, step):
            return [(held[unit], by_bit(ROTATIONS[unit][step])) for unit in range(3)]

        def joined(held, got):
            return [jnp.concatenate([a, b], 0) for a, b in zip(held, got)]

        def own(blocks):
            return [blocks[None, :, cuts[unit] : cuts[unit + 1]] for unit in range(3)]

        def merged(held):
            return jnp.concatenate(held, -1)

        def one_bit(array, bit):
            return (array, by_bit(bit))

        small = jnp.pad(smalls, ((0, 0), (0, 0), (0, EXTRA - rows)))
        wide = jnp.pad(wides, ((0, 0), (0, 2 * EXTRA - 4 * rows))).reshape(2, 2, EXTRA)
        small = jnp.pad(jnp.concatenate([small, wide], 1), ((0, 0), (0, 6), (0, 0)))
        small_mine = jnp.where(section == 0, small[0], small[1])
        small_twin = jnp.where(section == 0, small[1], small[0])
        home, small_home = wave((twin, by(routes.home_to_away)), (small_twin, by(routes.home_to_away)))
        near_held = own(jnp.where(at_home, mine, home))
        *got, small_straight, cross_a = wave(
            *bits(near_held, 0), (small_mine, by(routes.straight)), (twin[:, : cuts[1]], by(routes.crossed))
        )
        near_held = joined(near_held, got)
        *got, small_crossed, cross_b = wave(
            *bits(near_held, 1), (small_twin, by(routes.crossed)), (twin[:, cuts[1] :], by(routes.crossed))
        )
        small_held = jnp.stack(
            [jnp.where(at_home, small_mine, small_home), jnp.where(at_home, small_straight, small_crossed)]
        )[None]
        near_held = joined(near_held, got)
        *near_far, small_got, straight = wave(
            *bits(near_held, 2), one_bit(small_held, 0), (mine, by(routes.straight))
        )
        small_held = jnp.concatenate([small_held, small_got], 0)
        away_held = own(jnp.where(at_home, straight, jnp.concatenate([cross_a, cross_b], -1)))
        *got, small_got, twin_near_held = wave(
            *bits(away_held, 0), one_bit(small_held, 1), (merged(near_held), swap_section)
        )
        small_held = jnp.concatenate([small_held, small_got], 0)
        away_held = joined(away_held, got)
        *got, small_got, twin_near_far = wave(
            *bits(away_held, 1), one_bit(small_held, 2), (merged(near_far), swap_section)
        )
        small_held = jnp.concatenate([small_held, small_got], 0)
        away_held = joined(away_held, got)
        *away_far, moved, twin_away_held = wave(
            *bits(away_held, 2),
            (jnp.where(half == 1, inputs, cotangent), by(crossing)),
            (merged(away_held), swap_section),
        )
        *twin_last, small_other, numbers_got = wave(
            *[(array, swap_section) for array in away_far], (small_held, swap_section), (numbers, by(crossing))
        )
        pieces = [array for group in zip(near_held, near_far, away_held, away_far) for array in group]
        pieces += [twin_near_held, twin_near_far, twin_away_held, *twin_last]

        def table(masks):
            near_ones = spot ^ jnp.asarray(masks, jnp.int32)
            return jnp.concatenate([near_ones + near * half, near_ones + near * (1 - half)])

        tables = [table(piece_masks(unit)) for unit in range(3)]
        places = [grad_place(spot ^ jnp.arange(8, dtype=jnp.int32), ROTATIONS[2 - unit]) for unit in range(3)]
        row_halves = [half, 1 - half]
        first_side = section
        small_order = (spot ^ jnp.arange(8, dtype=jnp.int32))
        small_order = jnp.stack([small_order + near * half, small_order + near * (1 - half)], 1).reshape(BLOCKS)
        pick = (small_order[None, :] == jnp.arange(BLOCKS, dtype=jnp.int32)[:, None]).astype(BF16)
        row_list, fbias_list = [], []
        for array in (small_held, small_other):
            laid = dot_nn(pick, array.reshape(BLOCKS, 16 * EXTRA)).reshape(BLOCKS, 16, EXTRA)
            row_list.append(jnp.swapaxes(laid[:, :8, :rows], 0, 1).reshape(8, D))
            fbias_list.append(laid[:, 8:10].reshape(BLOCKS, 2 * EXTRA)[:, : 4 * rows].reshape(1, FF))
        rows_all = jnp.stack(row_list)
        fbias_all = jnp.stack(fbias_list)
    else:
        tables = [jnp.arange(BLOCKS, dtype=jnp.int32)] * 3
        places = [jnp.arange(8, dtype=jnp.int32)] * 3
        row_halves = [jnp.int32(0), jnp.int32(1)]
        first_side = 0
        moved = along(jnp.where(half == 1, inputs, cotangent), crossing)
        numbers_got = along(numbers, crossing)

        def whole(array, dim):
            full = lax.all_gather(array, ("section", "dp"), axis=0).reshape((2, n_dp) + array.shape)
            full = lax.dynamic_index_in_dim(full, half, 0, keepdims=False)
            shape = array.shape[:dim] + (n_dp * array.shape[dim],) + array.shape[dim + 1 :]
            return jnp.moveaxis(full, 0, dim).reshape(shape)

        full = whole(native, 1).reshape(2, 4, 4, ROWS, 3 * WIDE)
        pieces = [full[0, q, :, :, unit * WIDE : (unit + 1) * WIDE] for unit in range(3) for q in range(4)]
        pieces += [full[1, q] for q in range(3)]
        pieces += [full[1, 3, :, :, unit * WIDE : (unit + 1) * WIDE] for unit in range(3)]
        rows_all = whole(smalls, 2).astype(F32)
        fbias_all = whole(wides, 1).astype(F32)[:, None, :]

    numbers = jnp.where(at_home, numbers, numbers_got)
    chains = jnp.where(at_home, inputs, moved)
    top_grad = jnp.where(at_home, cotangent, moved)
    sides = numbers[:count] ^ first_side
    meta = jnp.concatenate([half[None].astype(jnp.int32), numbers, sides.astype(jnp.int32)] + tables)
    grad_meta = jnp.concatenate(
        [sides.astype(jnp.int32)]
        + [value[None].astype(jnp.int32) for value in row_halves]
        + [place for unit in range(3) for place in (places[unit], places[unit])]
    )

    lead = 2
    call = functools.partial(layer_call, lead=lead, count=count, rows=rows_all, fbias=fbias_all, pieces=pieces)
    acts, grads, act_low, held = [None] * count, [None] * count, [None], [None] * 9
    token = None

    def forward(c):
        nonlocal token, act_low
        out, act_low = call(False, c, meta=after(meta, token), sources=[chains], held=act_low)
        acts[c], token = along(out, routes.up), out

    for c in range(count):
        forward(c)
    for slot in range(count + lead):
        sources = [chains]
        if slot < count:
            sources += [acts[slot], top_grad]
        if slot >= lead:
            sources.append(grads[slot - lead])
        out, held = call(True, slot, meta=after(meta, token), sources=sources, held=held)
        token = out
        if slot < count:
            grads[slot] = along(out, routes.down)
    act_high, grad_all, sums, fsums, s_x, s_ctx, s_hid, s_dffn, s_right = held
    act_all = jnp.where(half == 0, act_low[0], act_high)

    lefts = {2: [s_dffn], 1: [s_hid], 0: [s_x, s_ctx]}

    def gradient(unit, at, *others):
        return grad_call(unit, at, after(grad_meta, *others), lefts[unit], s_right)

    act_move = (
        jnp.where(section == 1, jnp.concatenate(acts, 0), act_all),
        by([pair for j in range(near) for pair in (((1, near + j), (0, near + j)), ((0, near + j), (1, j)))]),
    )
    grad_move = (
        jnp.where(section == 0, jnp.concatenate(grads, 0), grad_all.astype(BF16)),
        by([pair for j in range(near) for pair in (((0, j), (1, j)), ((1, j), (0, near + j)))]),
    )

    chosen = (sides[None, :] == jnp.arange(2, dtype=jnp.int32)[:, None]).astype(F32)
    row_sums = jnp.sum(chosen[:, :, None, None] * sums[None], axis=1)
    fbias_sums = jnp.sum(chosen[:, :, None] * fsums[None, :, 0], axis=1)
    small_grads = jnp.concatenate([jnp.swapaxes(row_sums, 1, 2), fbias_sums.reshape(2, D, 4)], -1)

    if fast:
        laid = jnp.concatenate([small_grads, jnp.zeros((2, D, EXTRA - 12), F32)], -1).astype(BF16)
        laid = jnp.swapaxes(laid.reshape(2, BLOCKS, ROWS, EXTRA), 0, 1)
        small_places = table(grad_masks(ROTATIONS[0]))
        pick = (small_places[:, None] == jnp.arange(BLOCKS, dtype=jnp.int32)[None, :]).astype(BF16)
        laid = dot_nn(pick, laid.reshape(BLOCKS, -1)).astype(BF16).reshape(2, 8, 2, ROWS, EXTRA)
        laid = jnp.transpose(laid, (2, 1, 0, 3, 4)).reshape(2, 8, 2 * ROWS, EXTRA)
        wave = Waves()

        def reduce_step(keep, got, step):
            width = 4 >> step
            send = [both(a[width:], b[width:]) for a, b in zip(keep, got)]
            return [both(a[:width], b[:width]) for a, b in zip(keep, got)], send

        def bits_out(send, step):
            return [(send[i], by_bit(ROTATIONS[i % 3][step])) for i in range(len(send))]

        units = (2, 1, 0)
        totals = {(unit, 1): gradient(unit, 1) for unit in units}
        keep = [totals[unit, 1][0] for unit in units] + [laid[0]]
        got = [swap_section(totals[unit, 1][1]) for unit in units] + [swap_section(laid[1])]
        near_got = []
        for step in range(3):
            if step == 0:
                totals[2, 0] = gradient(2, 0, totals[0, 1][0])
            keep, send = reduce_step(keep, got, step)
            if step == 0:
                totals[1, 0] = gradient(1, 0, *send)
                totals[0, 0] = gradient(0, 0, totals[1, 0][0])
            *got, other = wave(*bits_out(send, step), (totals[units[step], 0][1], swap_section))
            near_got.append(other)
        far_sum = [(a[0].astype(F32) + b[0].astype(F32)).astype(BF16) for a, b in zip(keep, got)]
        small_near = far_sum[3][:ROWS]
        far_sum = jnp.concatenate(far_sum[:3] + [far_sum[3][ROWS:]], -1)

        keep = [totals[unit, 0][0] for unit in units]
        keep, send = reduce_step(keep, near_got, 0)
        *got, straight, act_other = wave(*bits_out(send, 0), (far_sum, by(routes.straight_back)), act_move)
        keep, send = reduce_step(keep, got, 1)
        *got, cross_a, grad_other = wave(
            *bits_out(send, 1), (far_sum[:, : 2 * WIDE], by(routes.crossed)), grad_move
        )
        keep, send = reduce_step(keep, got, 2)
        *got, cross_b = wave(*bits_out(send, 2), (far_sum[:, 2 * WIDE :], by(routes.crossed)))
        near_sum = [a[0].astype(F32) + b[0].astype(F32) for a, b in zip(keep, got)] + [small_near.astype(F32)]
        (beside,) = wave((jnp.concatenate(near_sum, -1).astype(BF16), by(routes.away_to_home)))
        crossed = jnp.concatenate([cross_a, cross_b], -1)

        def settle(i, width):
            cols = slice(i * WIDE, i * WIDE + width)
            mine = jnp.where(at_home, near_sum[i], straight[:, cols].astype(F32))
            twin = jnp.where(at_home, beside[:, cols].astype(F32), crossed[:, cols].astype(F32))
            return jnp.stack([jnp.where(section == 0, mine, twin), jnp.where(section == 0, twin, mine)])

        unit_out = [None] * 3
        for i, unit in enumerate(units):
            unit_out[unit] = settle(i, WIDE)
        small_out = settle(3, EXTRA)
    else:

        def summed(array):
            layers = jnp.stack([jnp.where(half == layer, array, jnp.zeros_like(array)) for layer in range(2)])
            layers = jnp.swapaxes(layers, 1, 2).reshape(2 * n_dp, rows, 2, array.shape[-1])
            out = lax.psum_scatter(layers, ("section", "dp"), scatter_dimension=0, tiled=True)
            return jnp.swapaxes(out[0], 0, 1)

        unit_out = []
        totals = {(unit, at): gradient(unit, at) for unit in range(3) for at in range(2)}
        for unit in range(3):
            group = [
                jnp.concatenate([totals[unit, 0][side], totals[unit, 1][side]], 0).reshape(D, WIDE) for side in range(2)
            ]
            unit_out.append(summed(jnp.stack(group).astype(F32)))
        small_out = summed(small_grads)
        act_other, grad_other = act_move[1](act_move[0]), grad_move[1](grad_move[0])

    act_out = jnp.where(at_home, act_all, act_other)
    grad_out = jnp.where(at_home, grad_all, grad_other.astype(F32))

    turned = jnp.swapaxes(small_out[:, :, :8], 1, 2)
    return (
        act_out[None],
        grad_out[None],
        unit_out[0][None, :, :, : 3 * D],
        unit_out[0][None, :, :, 3 * D :],
        unit_out[1][None],
        jnp.swapaxes(unit_out[2], 1, 2)[None],
        turned[None, :, 0:4],
        small_out[:, :, 8:12].reshape(1, 2, 4 * rows),
        turned[None, :, 4:6],
        turned[None, :, 6:8],
    )


def solution(mesh):
    in_specs = (
        P("dp", None, None),
        P("dp", None, None),
        P("dp"),
        P("dp"),
        P("section", None, "dp", None),
        P("section", None, "dp", None),
        P("section", None, "dp", None),
        P("section", None, None, "dp"),
        P("section", None, None, "dp"),
        P("section", None, "dp"),
        P("section", None, None, "dp"),
        P("section", None, None, "dp"),
    )
    out_specs = (
        P("section", "dp", None, None),
        P("section", "dp", None, None),
        P("section", None, "dp", None),
        P("section", None, "dp", None),
        P("section", None, "dp", None),
        P("section", None, None, "dp"),
        P("section", None, None, "dp"),
        P("section", None, "dp"),
        P("section", None, None, "dp"),
        P("section", None, None, "dp"),
    )
    return jax.shard_map(
        per_device, mesh=mesh, in_specs=in_specs, out_specs=out_specs, check_vma=False
    )
```

time: 667 us -> 591 us (0.89)
  waiting for transfers between devices: 271 us -> 198 us
  Pallas kernels: 212 us -> 180 us
  other arithmetic: 39 us -> 57.7 us
  starting transfers between devices: 111 us -> 125 us
    ppermute x39 -> x42, waiting for transfers between devices: 188 us -> 124 us  [swap_bit(): return lax.ppermute(array, 'dp', [(i, i ^ 1 << bit) for i in range(count)])]
    pallas_call x15 -> x16, Pallas kernels: 212 us -> 180 us  [the longest x10 131 us: layer_call(): pl.pallas_call(functools.partial(layer_kernel, back, slot, lead, count),...]
    ppermute x19 -> x14, starting transfers between devices: 6.81 us -> 24.6 us  [swap_section(): return lax.ppermute(array, 'section', [(0, 1), (1, 0)])]
    ppermute x25 -> x23, waiting for transfers between devices: 79.8 us -> 66.9 us  [along(): return lax.ppermute(array, ('section', 'dp'), flat)]
    ppermute x25 -> x23, starting transfers between devices: 63.8 us -> 51.3 us  [along(): return lax.ppermute(array, ('section', 'dp'), flat)]
    ppermute x39 -> x42, starting transfers between devices: 40.1 us -> 49.3 us  [swap_bit(): return lax.ppermute(array, 'dp', [(i, i ^ 1 << bit) for i in range(count)])]
    slice x16 -> x4, local copies, waits for them, and re-layouts: 9.21 us -> 0.8 us  [the longest x1 0.73 us: per_device(): twin[:, :cuts[1]]]
    concatenate x14 -> x26, other arithmetic: 6.46 us -> 13.7 us  [the longest x12 7.69 us: joined(): return [jnp.concatenate([a, b], 0) for a, b in zip(held, got)]]
  transfers between devices with their start and end apart: 83 -> 79, of which waited for: 36 -> 34; matrix products, arithmetic and copies ran while one was open for 7% -> 8% of each run, Pallas kernels for 26% -> 24%
where the time goes in v2:
time: 591 us; the launch traced here: 581 us
  waiting for transfers between devices  198 us (34%)
  Pallas kernels  180 us (30%)
  starting transfers between devices  125 us (21%)
  other arithmetic  57.7 us (10%)
  local copies, waits for them, and re-layouts  17.5 us (3%)
    pallas_call x10, Pallas kernels, layer_call(): pl.pallas_call(functools.partial(layer_kernel, back, slot, lead, count),...  131 us
    ppermute x42, waiting for transfers between devices, swap_bit(): return lax.ppermute(array, 'dp', [(i, i ^ 1 << bit) for i in range(count)])  124 us
    ppermute x23, waiting for transfers between devices, along(): return lax.ppermute(array, ('section', 'dp'), flat)  66.9 us
    ppermute x23, starting transfers between devices, along(): return lax.ppermute(array, ('section', 'dp'), flat)  51.3 us
    ppermute x42, starting transfers between devices, swap_bit(): return lax.ppermute(array, 'dp', [(i, i ^ 1 << bit) for i in range(count)])  49.3 us
    pallas_call x6, Pallas kernels, grad_call(): pl.pallas_call(functools.partial(grad_kernel, unit, at), out_shape=[out]...  48.4 us
    ppermute x14, starting transfers between devices, swap_section(): return lax.ppermute(array, 'section', [(0, 1), (1, 0)])  24.6 us
    convert_element_type x21, other arithmetic, both(): return (first.astype(F32) + second.astype(F32)).astype(BF16)  20.6 us
  transfers between devices with their start and end apart: 79, of which 34 were waited for; matrix products, arithmetic and copies ran while one was open for 8% of the time, Pallas kernels for 24%

profile of v2, /device:TPU:1, one launch (start us, length us, event | category | flops | bytes accessed | tf_op | source)
XLA Modules:
  0.0 580.9 jit_solution(6332788023540144807)
XLA Ops:
  12.3 4.5 collective-permute-start.5
  19.4 2.8 collective-permute-start.6
  22.3 2.5 collective-permute-done.3
  25.0 6.5 %collective-permute-done.6 = bf16[48,3072]{1,0:T(8,128)(2,1)S(1)} collective-permute-done((bf16[48,3072]{1,0:T(8,128)(2,1)S(1)}, bf16[48,3072]{1,0:T(8,128)(2,1)S(1)}, u32[]{:S(2)}, u32[]{:S(2)}) %collective-permute-start.6) | collective-permute-done | bytes 294944 | tf_op jit(solution)/shard_map/ppermute | solution.py:444
  35.3 3.5 collective-permute-start.11
  40.4 13.2 %collective-permute-done.8 = bf16[2,48,3072]{2,1,0:T(8,128)(2,1)S(1)} collective-permute-done((bf16[2,48,3072]{2,1,0:T(8,128)(2,1)S(1)}, bf16[2,48,3072]{2,1,0:T(8,128)(2,1)S(1)}, u32[]{:S(2)}, u32[]{:S(2)}) %collective-permute-start.8) | collective-permute-done | bytes 589856 | tf_op jit(solution)/shard_map/ppermute | solution.py:434
  56.9 9.3 %collective-permute-start.14 = (bf16[4,48,3072]{2,1,0:T(8,128)(2,1)S(1)}, bf16[4,48,3072]{2,1,0:T(8,128)(2,1)S(1)}, u32[]{:S(2)}, u32[]{:S(2)}) collective-permute-start(bf16[4,48,3072]{2,1,0:T(8,128)(2,1)S(1)} %pad_maximum_fusion.2.refs_3_), channel_id=1, source_target_pairs={{0,4},{1,5},{2,6},{3,7},{4,0},{5,1},{6,2},{7,3},{8,12},{9,13},{10,... | collective-permute-start | bytes 3538952 | tf_op jit(solution)/shard_map/ppermute | solution.py:434
  66.3 2.4 collective-permute-start.16
  70.8 14.3 %collective-permute-done.14.refs_4_ = bf16[4,48,3072]{2,1,0:T(8,128)(2,1)S(1)} collective-permute-done((bf16[4,48,3072]{2,1,0:T(8,128)(2,1)S(1)}, bf16[4,48,3072]{2,1,0:T(8,128)(2,1)S(1)}, u32[]{:S(2)}, u32[]{:S(2)}) %collective-permute-start.14) | collective-permute-done | bytes 1179680 | tf_op jit(solution)/shard_map/ppermute | solution.py:434
  90.5 5.6 collective-permute-done.19
  105.3 10.7 %collective-permute-done.24 = bf16[2,48,3072]{2,1,0:T(8,128)(2,1)} collective-permute-done((bf16[2,48,3072]{2,1,0:T(8,128)(2,1)}, bf16[2,48,3072]{2,1,0:T(8,128)(2,1)}, u32[]{:S(2)}, u32[]{:S(2)}) %collective-permute-start.24) | collective-permute-done | bytes 589856 | tf_op jit(solution)/shard_map/ppermute | solution.py:434
  119.3 3.3 maximum_maximum_fusion.1
  128.7 25.6 %collective-permute-done.30 = bf16[4,160,768]{2,1,0:T(8,128)(2,1)} collective-permute-done((bf16[4,160,768]{2,1,0:T(8,128)(2,1)}, bf16[4,160,768]{2,1,0:T(8,128)(2,1)}, u32[]{:S(2)}, u32[]{:S(2)}) %collective-permute-start.30) | collective-permute-done | bytes 983072 | tf_op jit(solution)/shard_map/ppermute | solution.py:444
  156.6 2.4 collective-permute-done.27.refs_6_
  160.3 12.9 %collective-permute-start.33 = (bf16[8,2,16,128]{3,2,1,0:T(8,128)(2,1)S(1)}, bf16[8,2,16,128]{3,2,1,0:T(8,128)(2,1)S(1)}, u32[]{:S(2)}, u32[]{:S(2)}) collective-permute-start(bf16[8,2,16,128]{3,2,1,0:T(8,128)(2,1)S(1)} %pad_maximum_fusion.19), channel_id=1, source_target_pairs={{0,16},{16,0},{1,17},{17,1},{2,18},{18,2},{3,19},{19,3},{4,20},{20... | collective-permute-start | bytes 196616 | tf_op jit(solution)/shard_map/ppermute | solution.py:438
  179.8 10.5 %layer_fwd.4 = (bf16[1,160,768]{2,1,0:T(8,128)(2,1)S(1)}, bf16[4,160,768]{2,1,0:T(8,128)(2,1)S(1)}) custom-call(s32[61]{0:T(128)S(1)} %concatenate.138.refs_0_, f32[2,8,768]{2,1,0:T(8,128)S(1)} %constant_dynamic-update-slice_fusion.refs_1_, f32[2,1,3072]{2,1,0:T(1,128)S(1)} %constant_dynamic-update-slice_fusion.2.refs_2_, ...), custom_call_target="tpu_custom_call" | custom-call | flops 1 | bytes 1 | tf_op jit(solution)/shard_map/layer_fwd/pallas_call | solution.py:395
  191.6 10.8 %layer_fwd.5 = (bf16[1,160,768]{2,1,0:T(8,128)(2,1)S(1)}, bf16[4,160,768]{2,1,0:T(8,128)(2,1)S(1)}) custom-call(s32[61]{0:T(128)S(1)} %concatenate.138.refs_0_, f32[2,8,768]{2,1,0:T(8,128)S(1)} %constant_dynamic-update-slice_fusion.refs_1_, f32[2,1,3072]{2,1,0:T(1,128)S(1)} %constant_dynamic-update-slice_fusion.2.refs_2_, ...), custom_call_target="tpu_custom_call", output_to_operand_aliasing={{1}: (22, {})} | custom-call | flops 1 | bytes 1 | tf_op jit(solution)/shard_map/layer_fwd/pallas_call | solution.py:395
  203.7 10.5 %layer_fwd.6 = (bf16[1,160,768]{2,1,0:T(8,128)(2,1)S(1)}, bf16[4,160,768]{2,1,0:T(8,128)(2,1)S(1)}) custom-call(s32[61]{0:T(128)S(1)} %concatenate.138.refs_0_, f32[2,8,768]{2,1,0:T(8,128)S(1)} %constant_dynamic-update-slice_fusion.refs_1_, f32[2,1,3072]{2,1,0:T(1,128)S(1)} %constant_dynamic-update-slice_fusion.2.refs_2_, ...), custom_call_target="tpu_custom_call", output_to_operand_aliasing={{1}: (22, {})} | custom-call | flops 1 | bytes 1 | tf_op jit(solution)/shard_map/layer_fwd/pallas_call | solution.py:395
  215.5 10.5 %layer_fwd.7 = (bf16[1,160,768]{2,1,0:T(8,128)(2,1)S(1)}, bf16[4,160,768]{2,1,0:T(8,128)(2,1)S(1)}) custom-call(s32[61]{0:T(128)S(1)} %concatenate.138.refs_0_, f32[2,8,768]{2,1,0:T(8,128)S(1)} %constant_dynamic-update-slice_fusion.refs_1_, f32[2,1,3072]{2,1,0:T(1,128)S(1)} %constant_dynamic-update-slice_fusion.2.refs_2_, ...), custom_call_target="tpu_custom_call", output_to_operand_aliasing={{1}: (22, {})} | custom-call | flops 1 | bytes 1 | tf_op jit(solution)/shard_map/layer_fwd/pallas_call | solution.py:395
  227.0 9.8 %layer_back.6 = (bf16[1,160,768]{2,1,0:T(8,128)(2,1)S(1)}, bf16[4,160,768]{2,1,0:T(8,128)(2,1)S(1)}, f32[4,160,768]{2,1,0:T(8,128)}, f32[4,8,768]{2,1,0:T(8,128)...) custom-call(s32[61]{0:T(128)S(1)} %concatenate.138.refs_0_, ...), custom_call_target="tpu_custom_call" | custom-call | flops 1 | bytes 1 | tf_op jit(solution)/shard_map/layer_back/pallas_call | solution.py:395
  238.1 4.9 collective-permute-start.41
  245.9 6.6 %collective-permute-done.40.refs_24_ = bf16[1,160,768]{2,1,0:T(8,128)(2,1)S(1)} collective-permute-done((bf16[1,160,768]{2,1,0:T(8,128)(2,1)S(1)}, bf16[1,160,768]{2,1,0:T(8,128)(2,1)S(1)}, u32[]{:S(2)}, u32[]{:S(2)}) %collective-permute-start.40) | collective-permute-done | bytes 245792 | tf_op jit(solution)/shard_map/ppermute | solution.py:444
  252.4 19.7 %layer_back.8 = (bf16[1,160,768]{2,1,0:T(8,128)(2,1)}, bf16[4,160,768]{2,1,0:T(8,128)(2,1)S(1)}, f32[4,160,768]{2,1,0:T(8,128)}, f32[4,8,768]{2,1,0:T(8,128)S(1)...) custom-call(s32[61]{0:T(128)S(1)} %concatenate.138.refs_0_, ...), custom_call_target="tpu_custom_call", output_to_operand_aliasing={{1}: (25, {}), {2}: (26, {}), {3}: (27, {}), {4}: (28, {}),... | custom-call | flops 1 | bytes 1 | tf_op jit(solution)/shard_map/layer_back/pallas_call | solution.py:395
  274.6 19.3 %layer_back.9 = (bf16[1,160,768]{2,1,0:T(8,128)(2,1)}, bf16[4,160,768]{2,1,0:T(8,128)(2,1)S(1)}, f32[4,160,768]{2,1,0:T(8,128)}, f32[4,8,768]{2,1,0:T(8,128)S(1)...) custom-call(s32[61]{0:T(128)S(1)} %concatenate.138.refs_0_, ...), custom_call_target="tpu_custom_call", output_to_operand_aliasing={{1}: (25, {}), {2}: (26, {}), {3}: (27, {}), {4}: (28, {}),... | custom-call | flops 1 | bytes 1 | tf_op jit(solution)/shard_map/layer_back/pallas_call | solution.py:395
  296.1 19.3 %layer_back.10 = (bf16[1,160,768]{2,1,0:T(8,128)(2,1)}, bf16[4,160,768]{2,1,0:T(8,128)(2,1)S(1)}, f32[4,160,768]{2,1,0:T(8,128)}, f32[4,8,768]{2,1,0:T(8,128)S(1...) custom-call(s32[61]{0:T(128)S(1)} %concatenate.138.refs_0_, ...), custom_call_target="tpu_custom_call", output_to_operand_aliasing={{1}: (23, {}), {2}: (24, {}), {3}: (25, {}), {4}: (26, {}),... | custom-call | flops 1 | bytes 1 | tf_op jit(solution)/shard_map/layer_back/pallas_call | solution.py:395
  317.6 19.5 %layer_back.11 = (bf16[1,160,768]{2,1,0:T(8,128)(2,1)}, bf16[4,160,768]{2,1,0:T(8,128)(2,1)S(1)}, f32[4,160,768]{2,1,0:T(8,128)}, f32[4,8,768]{2,1,0:T(8,128)S(1...) custom-call(s32[61]{0:T(128)S(1)} %concatenate.138.refs_0_, ...), custom_call_target="tpu_custom_call", output_to_operand_aliasing={{1}: (23, {}), {2}: (24, {}), {3}: (25, {}), {4}: (26, {}),... | custom-call | flops 1 | bytes 1 | tf_op jit(solution)/shard_map/layer_back/pallas_call | solution.py:395
  339.7 8.4 %layer_grad.6 = (bf16[8,48,3072]{2,1,0:T(8,128)(2,1)}, bf16[8,48,3072]{2,1,0:T(8,128)(2,1)}) custom-call(s32[54]{0:T(128)S(1)} %concatenate.139.meta, bf16[4,160,768]{2,1,0:T(8,128)(2,1)S(1)} %get-tuple-element.269.refs_0_, bf16[4,160,768]{2,1,0:T(8,128)(2,1)S(1)} %copy-done.7, bf16[3,4,160,3072]{3,2,1,0:T(8,128)(2,1)} %get-tuple-element.271.refs_2_.refs_1_), custom_call_target="tpu_custom_call" | custom-call | flops 1 | bytes 1 | tf_op jit(solution)/shard_map/layer_grad/pallas_call | solution.py:413
  348.9 7.9 %layer_grad.8 = (bf16[8,48,3072]{2,1,0:T(8,128)(2,1)S(1)}, bf16[8,48,3072]{2,1,0:T(8,128)(2,1)}) custom-call(s32[54]{0:T(128)S(1)} %concatenate.139.meta, bf16[4,160,768]{2,1,0:T(8,128)(2,1)S(1)} %copy-done.3, bf16[3,4,160,3072]{3,2,1,0:T(8,128)(2,1)} %get-tuple-element.271.refs_2_.refs_1_), custom_call_target="tpu_custom_call" | custom-call | flops 1 | bytes 1 | tf_op jit(solution)/shard_map/layer_grad/pallas_call | solution.py:413
  358.4 7.8 %layer_grad.9 = (bf16[8,48,3072]{2,1,0:T(8,128)(2,1)S(1)}, bf16[8,48,3072]{2,1,0:T(8,128)(2,1)}) custom-call(s32[54]{0:T(128)S(1)} %concatenate.139.meta, bf16[4,160,768]{2,1,0:T(8,128)(2,1)S(1)} %copy-done.2, bf16[3,4,160,3072]{3,2,1,0:T(8,128)(2,1)} %get-tuple-element.271.refs_2_.refs_1_), custom_call_target="tpu_custom_call" | custom-call | flops 1 | bytes 1 | tf_op jit(solution)/shard_map/layer_grad/pallas_call | solution.py:413
  372.9 8.0 %layer_grad.7 = (bf16[8,48,3072]{2,1,0:T(8,128)(2,1)S(1)}, bf16[8,48,3072]{2,1,0:T(8,128)(2,1)}) custom-call(s32[54]{0:T(128)S(1)} %concatenate.139.meta, bf16[4,160,768]{2,1,0:T(8,128)(2,1)S(1)} %copy-done.3, bf16[3,4,160,3072]{3,2,1,0:T(8,128)(2,1)} %get-tuple-element.271.refs_2_.refs_1_), custom_call_target="tpu_custom_call" | custom-call | flops 1 | bytes 1 | tf_op jit(solution)/shard_map/layer_grad/pallas_call | solution.py:413
  381.0 4.7 add_convert_fusion.5
  385.8 4.1 add_convert_fusion.7
  395.0 2.4 maximum_select_fusion
  398.8 7.8 %layer_grad.10 = (bf16[8,48,3072]{2,1,0:T(8,128)(2,1)S(1)}, bf16[8,48,3072]{2,1,0:T(8,128)(2,1)}) custom-call(s32[54]{0:T(128)S(1)} %concatenate.139.meta, bf16[4,160,768]{2,1,0:T(8,128)(2,1)S(1)} %copy-done.2, bf16[3,4,160,3072]{3,2,1,0:T(8,128)(2,1)} %get-tuple-element.271.refs_2_.refs_1_), custom_call_target="tpu_custom_call" | custom-call | flops 1 | bytes 1 | tf_op jit(solution)/shard_map/layer_grad/pallas_call | solution.py:413
  406.7 8.5 %layer_grad.11 = (bf16[8,48,3072]{2,1,0:T(8,128)(2,1)}, bf16[8,48,3072]{2,1,0:T(8,128)(2,1)}) custom-call(s32[54]{0:T(128)S(1)} %concatenate.139.meta, bf16[4,160,768]{2,1,0:T(8,128)(2,1)S(1)} %copy-done.5, bf16[4,160,768]{2,1,0:T(8,128)(2,1)S(1)} %copy-done.8, bf16[3,4,160,3072]{3,2,1,0:T(8,128)(2,1)} %get-tuple-element.271.refs_2_.refs_1_), custom_call_target="tpu_custom_call" | custom-call | flops 1 | bytes 1 | tf_op jit(solution)/shard_map/layer_grad/pallas_call | solution.py:413
  415.2 6.5 %collective-permute-done.53 = bf16[4,96,128]{2,1,0:T(8,128)(2,1)S(1)} collective-permute-done((bf16[4,96,128]{2,1,0:T(8,128)(2,1)S(1)}, bf16[4,96,128]{2,1,0:T(8,128)(2,1)S(1)}, u32[]{:S(2)}, u32[]{:S(2)}) %collective-permute-start.53) | collective-permute-done | bytes 98336 | tf_op jit(solution)/shard_map/ppermute | solution.py:434
  432.6 11.3 %collective-permute-done.55 = bf16[2,48,3072]{2,1,0:T(8,128)(2,1)S(1)} collective-permute-done((bf16[2,48,3072]{2,1,0:T(8,128)(2,1)S(1)}, bf16[2,48,3072]{2,1,0:T(8,128)(2,1)S(1)}, u32[]{:S(2)}, u32[]{:S(2)}) %collective-permute-start.55) | collective-permute-done | bytes 589856 | tf_op jit(solution)/shard_map/ppermute | solution.py:434
  446.2 3.6 collective-permute-start.59
  461.7 17.7 %collective-permute-done.65 = bf16[4,48,3072]{2,1,0:T(8,128)(2,1)S(1)} collective-permute-done((bf16[4,48,3072]{2,1,0:T(8,128)(2,1)S(1)}, bf16[4,48,3072]{2,1,0:T(8,128)(2,1)S(1)}, u32[]{:S(2)}, u32[]{:S(2)}) %collective-permute-start.65) | collective-permute-done | bytes 1179680 | tf_op jit(solution)/shard_map/ppermute | solution.py:434
  479.9 2.6 collective-permute-done.66
  482.9 24.0 %collective-permute-done.67 = bf16[4,48,3072]{2,1,0:T(8,128)(2,1)S(1)} collective-permute-done((bf16[4,48,3072]{2,1,0:T(8,128)(2,1)S(1)}, bf16[4,48,3072]{2,1,0:T(8,128)(2,1)S(1)}, u32[]{:S(2)}, u32[]{:S(2)}) %collective-permute-start.67) | collective-permute-done | bytes 1179680 | tf_op jit(solution)/shard_map/ppermute | solution.py:434
  509.3 6.1 %collective-permute-start.73 = (bf16[48,6144]{1,0:T(8,128)(2,1)S(1)}, bf16[48,6144]{1,0:T(8,128)(2,1)S(1)}, u32[]{:S(2)}, u32[]{:S(2)}) collective-permute-start(bf16[48,6144]{1,0:T(8,128)(2,1)S(1)} %pad_maximum_fusion.16), channel_id=1, source_target_pairs={{8,16},{9,17},{10,18},{11,19},{12,20},{13,21},{14,22},{15,23},{16,... | collective-permute-start | bytes 1769480 | tf_op jit(solution)/shard_map/ppermute | solution.py:444
  517.4 2.4 collective-permute-done.70
  520.0 7.7 %collective-permute-done.72 = bf16[2,48,3072]{2,1,0:T(8,128)(2,1)S(1)} collective-permute-done((bf16[2,48,3072]{2,1,0:T(8,128)(2,1)S(1)}, bf16[2,48,3072]{2,1,0:T(8,128)(2,1)S(1)}, u32[]{:S(2)}, u32[]{:S(2)}) %collective-permute-start.72) | collective-permute-done | bytes 589856 | tf_op jit(solution)/shard_map/ppermute | solution.py:434
  528.9 13.7 %collective-permute-done.69 = bf16[4,160,768]{2,1,0:T(8,128)(2,1)S(1)} collective-permute-done((bf16[4,160,768]{2,1,0:T(8,128)(2,1)S(1)}, bf16[4,160,768]{2,1,0:T(8,128)(2,1)S(1)}, u32[]{:S(2)}, u32[]{:S(2)}) %collective-permute-start.69) | collective-permute-done | bytes 983072 | tf_op jit(solution)/shard_map/ppermute | solution.py:444
  542.7 8.8 %collective-permute-start.75 = (bf16[1,48,3072]{2,1,0:T(8,128)(2,1)S(1)}, bf16[1,48,3072]{2,1,0:T(8,128)(2,1)S(1)}, u32[]{:S(2)}, u32[]{:S(2)}) collective-permute-start(bf16[1,48,3072]{2,1,0:T(8,128)(2,1)S(1)} %add_convert_fusion.28), channel_id=1, source_target_pairs={{0,4},{1,5},{2,6},{3,7},{4,0},{5,1},{6,2},{7,3},{8,12},{9,13},{10,... | collective-permute-start | bytes 884744 | tf_op jit(solution)/shard_map/ppermute | solution.py:434
  552.2 6.1 %collective-permute-start.77 = (bf16[48,3200]{1,0:T(8,128)(2,1)S(1)}, bf16[48,3200]{1,0:T(8,128)(2,1)S(1)}, u32[]{:S(2)}, u32[]{:S(2)}) collective-permute-start(bf16[48,3200]{1,0:T(8,128)(2,1)S(1)} %pad_maximum_fusion.17), channel_id=1, source_target_pairs={{8,16},{9,17},{10,18},{11,19},{12,20},{13,21},{14,22},{15,23},{16,... | collective-permute-start | bytes 921608 | tf_op jit(solution)/shard_map/ppermute | solution.py:444
  560.0 6.0 %collective-permute-done.77 = bf16[48,3200]{1,0:T(8,128)(2,1)S(1)} collective-permute-done((bf16[48,3200]{1,0:T(8,128)(2,1)S(1)}, bf16[48,3200]{1,0:T(8,128)(2,1)S(1)}, u32[]{:S(2)}, u32[]{:S(2)}) %collective-permute-start.77) | collective-permute-done | bytes 307232 | tf_op jit(solution)/shard_map/ppermute | solution.py:444
  (397 shorter events, 141.4 us)
Async XLA Ops:
  33.7 20.0 %collective-permute-start.7 = (bf16[2,48,3072]{2,1,0:T(8,128)(2,1)S(1)}, bf16[2,48,3072]{2,1,0:T(8,128)(2,1)S(1)}, u32[]{:S(2)}, u32[]{:S(2)}) collective-permute-start(bf16[2,48,3072]{2,1,0:T(8,128)(2,1)S(1)} %pad_maximum_fusion.10), channel_id=1, source_target_pairs={{0,2},{1,3},{2,0},{3,1},{4,6},{5,7},{6,4},{7,5},{8,10},{9,11},{10,... | collective-permute-start | bytes 1769480 | tf_op jit(solution)/shard_map/ppermute | solution.py:434
  34.0 19.6 %collective-permute-start.8 = (bf16[2,48,3072]{2,1,0:T(8,128)(2,1)S(1)}, bf16[2,48,3072]{2,1,0:T(8,128)(2,1)S(1)}, u32[]{:S(2)}, u32[]{:S(2)}) collective-permute-start(bf16[2,48,3072]{2,1,0:T(8,128)(2,1)S(1)} %pad_maximum_fusion.11), channel_id=1, source_target_pairs={{0,4},{1,5},{2,6},{3,7},{4,0},{5,1},{6,2},{7,3},{8,12},{9,13},{10,... | collective-permute-start | bytes 1769480 | tf_op jit(solution)/shard_map/ppermute | solution.py:434
  35.3 19.4 %collective-permute-start.11 = (bf16[48,6144]{1,0:T(8,128)(2,1)S(1)}, bf16[48,6144]{1,0:T(8,128)(2,1)S(1)}, u32[]{:S(2)}, u32[]{:S(2)}) collective-permute-start(bf16[48,6144]{1,0:T(8,128)(2,1)S(1)} %slice.528), channel_id=1, source_target_pairs={{8,16},{9,17},{10,18},{11,19},{12,20},{13,21},{14,22},{15,23},{16,... | collective-permute-start | bytes 1769480 | tf_op jit(solution)/shard_map/ppermute | solution.py:444
  54.6 14.4 %collective-permute-start.13 = (bf16[1,2,16,128]{3,2,1,0:T(8,128)(2,1)S(1)}, bf16[1,2,16,128]{3,2,1,0:T(8,128)(2,1)S(1)}, u32[]{:S(2)}, u32[]{:S(2)}) collective-permute-start(bf16[1,2,16,128]{3,2,1,0:T(8,128)(2,1)S(1)} %maximum_bitcast_fusion.3), channel_id=1, source_target_pairs={{0,1},{1,0},{2,3},{3,2},{4,5},{5,4},{6,7},{7,6},{8,9},{9,8},{10,11... | collective-permute-start | bytes 24584 | tf_op jit(solution)/shard_map/ppermute | solution.py:434
  55.6 15.0 %collective-permute-start.12 = (bf16[48,9216]{1,0:T(8,128)(2,1)S(1)}, bf16[48,9216]{1,0:T(8,128)(2,1)S(1)}, u32[]{:S(2)}, u32[]{:S(2)}) collective-permute-start(bf16[48,9216]{1,0:T(8,128)(2,1)S(1)} %get-tuple-element.178), channel_id=1, source_target_pairs={{8,0},{9,1},{10,2},{11,3},{12,4},{13,5},{14,6},{15,7},{16,24},{17,... | collective-permute-start | bytes 2654216 | tf_op jit(solution)/shard_map/ppermute | solution.py:444
  56.9 28.2 %collective-permute-start.14 = (bf16[4,48,3072]{2,1,0:T(8,128)(2,1)S(1)}, bf16[4,48,3072]{2,1,0:T(8,128)(2,1)S(1)}, u32[]{:S(2)}, u32[]{:S(2)}) collective-permute-start(bf16[4,48,3072]{2,1,0:T(8,128)(2,1)S(1)} %pad_maximum_fusion.2.refs_3_), channel_id=1, source_target_pairs={{0,4},{1,5},{2,6},{3,7},{4,0},{5,1},{6,2},{7,3},{8,12},{9,13},{10,... | collective-permute-start | bytes 3538952 | tf_op jit(solution)/shard_map/ppermute | solution.py:434
  66.2 18.9 %collective-permute-start.15 = (bf16[4,48,3072]{2,1,0:T(8,128)(2,1)S(1)}, bf16[4,48,3072]{2,1,0:T(8,128)(2,1)S(1)}, u32[]{:S(2)}, u32[]{:S(2)}) collective-permute-start(bf16[4,48,3072]{2,1,0:T(8,128)(2,1)S(1)} %pad_maximum_fusion.3.refs_7_), channel_id=1, source_target_pairs={{0,1},{1,0},{2,3},{3,2},{4,5},{5,4},{6,7},{7,6},{8,9},{9,8},{10,11... | collective-permute-start | bytes 3538952 | tf_op jit(solution)/shard_map/ppermute | solution.py:434
  66.3 18.9 %collective-permute-start.16 = (bf16[4,48,3072]{2,1,0:T(8,128)(2,1)S(1)}, bf16[4,48,3072]{2,1,0:T(8,128)(2,1)S(1)}, u32[]{:S(2)}, u32[]{:S(2)}) collective-permute-start(bf16[4,48,3072]{2,1,0:T(8,128)(2,1)S(1)} %pad_maximum_fusion.4.refs_11_), channel_id=1, source_target_pairs={{0,2},{1,3},{2,0},{3,1},{4,6},{5,7},{6,4},{7,5},{8,10},{9,11},{10,... | collective-permute-start | bytes 3538952 | tf_op jit(solution)/shard_map/ppermute | solution.py:434
  98.8 24.9 %collective-permute-start.26 = (bf16[4,48,9216]{2,1,0:T(8,128)(2,1)}, bf16[4,48,9216]{2,1,0:T(8,128)(2,1)}, u32[]{:S(2)}, u32[]{:S(2)}) collective-permute-start(bf16[4,48,9216]{2,1,0:T(8,128)(2,1)} %pad_maximum_fusion), channel_id=1, source_target_pairs={{0,16},{16,0},{1,17},{17,1},{2,18},{18,2},{3,19},{19,3},{4,20},{20... | collective-permute-start | bytes 10616840 | tf_op jit(solution)/shard_map/ppermute | solution.py:438
  100.7 15.2 %collective-permute-start.24 = (bf16[2,48,3072]{2,1,0:T(8,128)(2,1)}, bf16[2,48,3072]{2,1,0:T(8,128)(2,1)}, u32[]{:S(2)}, u32[]{:S(2)}) collective-permute-start(bf16[2,48,3072]{2,1,0:T(8,128)(2,1)} %pad_maximum_fusion.15), channel_id=1, source_target_pairs={{0,1},{1,0},{2,3},{3,2},{4,5},{5,4},{6,7},{7,6},{8,9},{9,8},{10,11... | collective-permute-start | bytes 1769480 | tf_op jit(solution)/shard_map/ppermute | solution.py:434
  101.3 16.8 %collective-permute-start.23 = (bf16[2,48,3072]{2,1,0:T(8,128)(2,1)}, bf16[2,48,3072]{2,1,0:T(8,128)(2,1)S(1)}, u32[]{:S(2)}, u32[]{:S(2)}) collective-permute-start(bf16[2,48,3072]{2,1,0:T(8,128)(2,1)} %pad_maximum_fusion.14), channel_id=1, source_target_pairs={{0,4},{1,5},{2,6},{3,7},{4,0},{5,1},{6,2},{7,3},{8,12},{9,13},{10,... | collective-permute-start | bytes 1769480 | tf_op jit(solution)/shard_map/ppermute | solution.py:434
  102.4 21.4 %collective-permute-start.25 = (bf16[4,2,16,128]{3,2,1,0:T(8,128)(2,1)S(1)}, bf16[4,2,16,128]{3,2,1,0:T(8,128)(2,1)S(1)}, u32[]{:S(2)}, u32[]{:S(2)}) collective-permute-start(bf16[4,2,16,128]{3,2,1,0:T(8,128)(2,1)S(1)} %pad_maximum_fusion.21), channel_id=1, source_target_pairs={{0,4},{1,5},{2,6},{3,7},{4,0},{5,1},{6,2},{7,3},{8,12},{9,13},{10,... | collective-permute-start | bytes 98312 | tf_op jit(solution)/shard_map/ppermute | solution.py:434
  103.9 15.4 %collective-permute-start.22 = (bf16[2,48,3072]{2,1,0:T(8,128)(2,1)S(1)}, bf16[2,48,3072]{2,1,0:T(8,128)(2,1)S(1)}, u32[]{:S(2)}, u32[]{:S(2)}) collective-permute-start(bf16[2,48,3072]{2,1,0:T(8,128)(2,1)S(1)} %copy-done.53), channel_id=1, source_target_pairs={{0,2},{1,3},{2,0},{3,1},{4,6},{5,7},{6,4},{7,5},{8,10},{9,11},{10,... | collective-permute-start | bytes 1769480 | tf_op jit(solution)/shard_map/ppermute | solution.py:434
  123.8 35.2 %collective-permute-start.31 = (bf16[4,48,9216]{2,1,0:T(8,128)(2,1)}, bf16[4,48,9216]{2,1,0:T(8,128)(2,1)}, u32[]{:S(2)}, u32[]{:S(2)}) collective-permute-start(bf16[4,48,9216]{2,1,0:T(8,128)(2,1)} %maximum_maximum_fusion.1), channel_id=1, source_target_pairs={{0,16},{16,0},{1,17},{17,1},{2,18},{18,2},{3,19},{19,3},{4,20},{20... | collective-permute-start | bytes 10616840 | tf_op jit(solution)/shard_map/ppermute | solution.py:438
  124.9 29.4 %collective-permute-start.30 = (bf16[4,160,768]{2,1,0:T(8,128)(2,1)}, bf16[4,160,768]{2,1,0:T(8,128)(2,1)}, u32[]{:S(2)}, u32[]{:S(2)}) collective-permute-start(bf16[4,160,768]{2,1,0:T(8,128)(2,1)} %broadcast_select_fusion), channel_id=1, source_target_pairs={{0,8},{1,9},{2,10},{3,11},{4,12},{5,13},{6,14},{7,15},{24,16},{25,... | collective-permute-start | bytes 2949128 | tf_op jit(solution)/shard_map/ppermute | solution.py:444
  126.4 32.6 %collective-permute-start.27 = (bf16[4,48,3072]{2,1,0:T(8,128)(2,1)}, bf16[4,48,3072]{2,1,0:T(8,128)(2,1)}, u32[]{:S(2)}, u32[]{:S(2)}) collective-permute-start(bf16[4,48,3072]{2,1,0:T(8,128)(2,1)} %pad_maximum_fusion.5.refs_5_), channel_id=1, source_target_pairs={{0,4},{1,5},{2,6},{3,7},{4,0},{5,1},{6,2},{7,3},{8,12},{9,13},{10,... | collective-permute-start | bytes 3538952 | tf_op jit(solution)/shard_map/ppermute | solution.py:434
  126.5 32.5 %collective-permute-start.28 = (bf16[4,48,3072]{2,1,0:T(8,128)(2,1)}, bf16[4,48,3072]{2,1,0:T(8,128)(2,1)}, u32[]{:S(2)}, u32[]{:S(2)}) collective-permute-start(bf16[4,48,3072]{2,1,0:T(8,128)(2,1)} %pad_maximum_fusion.6.refs_9_), channel_id=1, source_target_pairs={{0,1},{1,0},{2,3},{3,2},{4,5},{5,4},{6,7},{7,6},{8,9},{9,8},{10,11... | collective-permute-start | bytes 3538952 | tf_op jit(solution)/shard_map/ppermute | solution.py:434
  127.1 31.9 %collective-permute-start.29 = (bf16[4,48,3072]{2,1,0:T(8,128)(2,1)}, bf16[4,48,3072]{2,1,0:T(8,128)(2,1)}, u32[]{:S(2)}, u32[]{:S(2)}) collective-permute-start(bf16[4,48,3072]{2,1,0:T(8,128)(2,1)} %pad_maximum_fusion.7.refs_13_), channel_id=1, source_target_pairs={{0,2},{1,3},{2,0},{3,1},{4,6},{5,7},{6,4},{7,5},{8,10},{9,11},{10,... | collective-permute-start | bytes 3538952 | tf_op jit(solution)/shard_map/ppermute | solution.py:434
  159.0 14.8 %collective-permute-start.32 = (s32[8]{0:T(128)S(1)}, s32[8]{0:T(128)S(1)}, u32[]{:S(2)}, u32[]{:S(2)}) collective-permute-start(s32[8]{0:T(128)S(1)} %pad_add_fusion.1), channel_id=1, source_target_pairs={{0,8},{1,9},{2,10},{3,11},{4,12},{5,13},{6,14},{7,15},{24,16},{25,... | collective-permute-start | bytes 104 | tf_op jit(solution)/shard_map/ppermute | solution.py:444
  190.3 36.7 %collective-permute-start.37 = (bf16[1,160,768]{2,1,0:T(8,128)(2,1)S(1)}, bf16[1,160,768]{2,1,0:T(8,128)(2,1)S(1)}, u32[]{:S(2)}, u32[]{:S(2)}) collective-permute-start(bf16[1,160,768]{2,1,0:T(8,128)(2,1)S(1)} %get-tuple-element.203), channel_id=1, source_target_pairs={{0,8},{1,9},{2,10},{3,11},{4,12},{5,13},{6,14},{7,15},{16,24},{17,... | collective-permute-start | bytes 737288 | tf_op jit(solution)/shard_map/ppermute | solution.py:444
  202.3 40.7 %collective-permute-start.38 = (bf16[1,160,768]{2,1,0:T(8,128)(2,1)S(1)}, bf16[1,160,768]{2,1,0:T(8,128)(2,1)S(1)}, u32[]{:S(2)}, u32[]{:S(2)}) collective-permute-start(bf16[1,160,768]{2,1,0:T(8,128)(2,1)S(1)} %get-tuple-element.206), channel_id=1, source_target_pairs={{0,8},{1,9},{2,10},{3,11},{4,12},{5,13},{6,14},{7,15},{16,24},{17,... | collective-permute-start | bytes 737288 | tf_op jit(solution)/shard_map/ppermute | solution.py:444
  214.2 31.7 %collective-permute-start.39 = (bf16[1,160,768]{2,1,0:T(8,128)(2,1)S(1)}, bf16[1,160,768]{2,1,0:T(8,128)(2,1)S(1)}, u32[]{:S(2)}, u32[]{:S(2)}) collective-permute-start(bf16[1,160,768]{2,1,0:T(8,128)(2,1)S(1)} %get-tuple-element.209), channel_id=1, source_target_pairs={{0,8},{1,9},{2,10},{3,11},{4,12},{5,13},{6,14},{7,15},{16,24},{17,... | collective-permute-start | bytes 737288 | tf_op jit(solution)/shard_map/ppermute | solution.py:444
  236.8 15.6 %collective-permute-start.40 = (bf16[1,160,768]{2,1,0:T(8,128)(2,1)S(1)}, bf16[1,160,768]{2,1,0:T(8,128)(2,1)S(1)}, u32[]{:S(2)}, u32[]{:S(2)}) collective-permute-start(bf16[1,160,768]{2,1,0:T(8,128)(2,1)S(1)} %get-tuple-element.215), channel_id=1, source_target_pairs={{8,0},{9,1},{10,2},{11,3},{12,4},{13,5},{14,6},{15,7},{24,16},{25,... | collective-permute-start | bytes 737288 | tf_op jit(solution)/shard_map/ppermute | solution.py:444
  238.1 35.3 %collective-permute-start.41 = (bf16[1,160,768]{2,1,0:T(8,128)(2,1)S(1)}, bf16[1,160,768]{2,1,0:T(8,128)(2,1)S(1)}, u32[]{:S(2)}, u32[]{:S(2)}) collective-permute-start(bf16[1,160,768]{2,1,0:T(8,128)(2,1)S(1)} %get-tuple-element.213), channel_id=1, source_target_pairs={{0,8},{1,9},{2,10},{3,11},{4,12},{5,13},{6,14},{7,15},{16,24},{17,... | collective-permute-start | bytes 737288 | tf_op jit(solution)/shard_map/ppermute | solution.py:444
  244.5 30.1 %collective-permute-start.42 = (bf16[1,160,768]{2,1,0:T(8,128)(2,1)S(1)}, bf16[1,160,768]{2,1,0:T(8,128)(2,1)S(1)}, u32[]{:S(2)}, u32[]{:S(2)}) collective-permute-start(bf16[1,160,768]{2,1,0:T(8,128)(2,1)S(1)} %get-tuple-element.226), channel_id=1, source_target_pairs={{8,0},{9,1},{10,2},{11,3},{12,4},{13,5},{14,6},{15,7},{24,16},{25,... | collective-permute-start | bytes 737288 | tf_op jit(solution)/shard_map/ppermute | solution.py:444
  272.1 24.0 %collective-permute-start.44 = (bf16[1,160,768]{2,1,0:T(8,128)(2,1)}, bf16[1,160,768]{2,1,0:T(8,128)(2,1)}, u32[]{:S(2)}, u32[]{:S(2)}) collective-permute-start(bf16[1,160,768]{2,1,0:T(8,128)(2,1)} %get-tuple-element.237), channel_id=1, source_target_pairs={{8,0},{9,1},{10,2},{11,3},{12,4},{13,5},{14,6},{15,7},{24,16},{25,... | collective-permute-start | bytes 737288 | tf_op jit(solution)/shard_map/ppermute | solution.py:444
  294.0 23.6 %collective-permute-start.43 = (bf16[1,160,768]{2,1,0:T(8,128)(2,1)}, bf16[1,160,768]{2,1,0:T(8,128)(2,1)}, u32[]{:S(2)}, u32[]{:S(2)}) collective-permute-start(bf16[1,160,768]{2,1,0:T(8,128)(2,1)} %get-tuple-element.248), channel_id=1, source_target_pairs={{8,0},{9,1},{10,2},{11,3},{12,4},{13,5},{14,6},{15,7},{24,16},{25,... | collective-permute-start | bytes 737288 | tf_op jit(solution)/shard_map/ppermute | solution.py:444
  348.0 33.0 %collective-permute-start.47 = (bf16[8,48,3072]{2,1,0:T(8,128)(2,1)}, bf16[8,48,3072]{2,1,0:T(8,128)(2,1)}, u32[]{:S(2)}, u32[]{:S(2)}) collective-permute-start(bf16[8,48,3072]{2,1,0:T(8,128)(2,1)} %get-tuple-element.281), channel_id=1, source_target_pairs={{0,16},{16,0},{1,17},{17,1},{2,18},{18,2},{3,19},{19,3},{4,20},{20... | collective-permute-start | bytes 7077896 | tf_op jit(solution)/shard_map/ppermute | solution.py:438
  358.2 27.5 %collective-permute-start.45 = (bf16[8,48,3072]{2,1,0:T(8,128)(2,1)}, bf16[8,48,3072]{2,1,0:T(8,128)(2,1)}, u32[]{:S(2)}, u32[]{:S(2)}) collective-permute-start(bf16[8,48,3072]{2,1,0:T(8,128)(2,1)} %get-tuple-element.277), channel_id=1, source_target_pairs={{0,16},{16,0},{1,17},{17,1},{2,18},{18,2},{3,19},{19,3},{4,20},{20... | collective-permute-start | bytes 7077896 | tf_op jit(solution)/shard_map/ppermute | solution.py:438
  370.6 19.3 %collective-permute-start.46 = (bf16[8,48,3072]{2,1,0:T(8,128)(2,1)}, bf16[8,48,3072]{2,1,0:T(8,128)(2,1)S(1)}, u32[]{:S(2)}, u32[]{:S(2)}) collective-permute-start(bf16[8,48,3072]{2,1,0:T(8,128)(2,1)} %get-tuple-element.280), channel_id=1, source_target_pairs={{0,16},{16,0},{1,17},{17,1},{2,18},{18,2},{3,19},{19,3},{4,20},{20... | collective-permute-start | bytes 7077896 | tf_op jit(solution)/shard_map/ppermute | solution.py:438
  392.2 29.5 %collective-permute-start.50 = (bf16[4,48,3072]{2,1,0:T(8,128)(2,1)}, bf16[4,48,3072]{2,1,0:T(8,128)(2,1)}, u32[]{:S(2)}, u32[]{:S(2)}) collective-permute-start(bf16[4,48,3072]{2,1,0:T(8,128)(2,1)} %get-tuple-element.288), channel_id=1, source_target_pairs={{0,1},{1,0},{2,3},{3,2},{4,5},{5,4},{6,7},{7,6},{8,9},{9,8},{10,11... | collective-permute-start | bytes 3538952 | tf_op jit(solution)/shard_map/ppermute | solution.py:434
  392.2 29.5 %collective-permute-start.53 = (bf16[4,96,128]{2,1,0:T(8,128)(2,1)S(1)}, bf16[4,96,128]{2,1,0:T(8,128)(2,1)S(1)}, u32[]{:S(2)}, u32[]{:S(2)}) collective-permute-start(bf16[4,96,128]{2,1,0:T(8,128)(2,1)S(1)} %get-tuple-element.291), channel_id=1, source_target_pairs={{0,1},{1,0},{2,3},{3,2},{4,5},{5,4},{6,7},{7,6},{8,9},{9,8},{10,11... | collective-permute-start | bytes 294920 | tf_op jit(solution)/shard_map/ppermute | solution.py:434
  393.6 29.8 %collective-permute-start.51 = (bf16[4,48,3072]{2,1,0:T(8,128)(2,1)}, bf16[4,48,3072]{2,1,0:T(8,128)(2,1)S(1)}, u32[]{:S(2)}, u32[]{:S(2)}) collective-permute-start(bf16[4,48,3072]{2,1,0:T(8,128)(2,1)} %get-tuple-element.289), channel_id=1, source_target_pairs={{0,2},{1,3},{2,0},{3,1},{4,6},{5,7},{6,4},{7,5},{8,10},{9,11},{10,... | collective-permute-start | bytes 3538952 | tf_op jit(solution)/shard_map/ppermute | solution.py:434
  397.4 28.8 %collective-permute-start.52 = (bf16[4,48,3072]{2,1,0:T(8,128)(2,1)}, bf16[4,48,3072]{2,1,0:T(8,128)(2,1)}, u32[]{:S(2)}, u32[]{:S(2)}) collective-permute-start(bf16[4,48,3072]{2,1,0:T(8,128)(2,1)} %get-tuple-element.290), channel_id=1, source_target_pairs={{0,4},{1,5},{2,6},{3,7},{4,0},{5,1},{6,2},{7,3},{8,12},{9,13},{10,... | collective-permute-start | bytes 3538952 | tf_op jit(solution)/shard_map/ppermute | solution.py:434
  397.4 30.7 %collective-permute-start.49 = (bf16[8,48,3072]{2,1,0:T(8,128)(2,1)}, bf16[8,48,3072]{2,1,0:T(8,128)(2,1)S(1)}, u32[]{:S(2)}, u32[]{:S(2)}) collective-permute-start(bf16[8,48,3072]{2,1,0:T(8,128)(2,1)} %get-tuple-element.285), channel_id=1, source_target_pairs={{0,16},{16,0},{1,17},{17,1},{2,18},{18,2},{3,19},{19,3},{4,20},{20... | collective-permute-start | bytes 7077896 | tf_op jit(solution)/shard_map/ppermute | solution.py:438
  429.5 14.4 %collective-permute-start.55 = (bf16[2,48,3072]{2,1,0:T(8,128)(2,1)S(1)}, bf16[2,48,3072]{2,1,0:T(8,128)(2,1)S(1)}, u32[]{:S(2)}, u32[]{:S(2)}) collective-permute-start(bf16[2,48,3072]{2,1,0:T(8,128)(2,1)S(1)} %get-tuple-element.296), channel_id=1, source_target_pairs={{0,2},{1,3},{2,0},{3,1},{4,6},{5,7},{6,4},{7,5},{8,10},{9,11},{10,... | collective-permute-start | bytes 1769480 | tf_op jit(solution)/shard_map/ppermute | solution.py:434
  429.7 14.4 %collective-permute-start.57 = (bf16[2,48,3072]{2,1,0:T(8,128)(2,1)S(1)}, bf16[2,48,3072]{2,1,0:T(8,128)(2,1)S(1)}, u32[]{:S(2)}, u32[]{:S(2)}) collective-permute-start(bf16[2,48,3072]{2,1,0:T(8,128)(2,1)S(1)} %get-tuple-element.298), channel_id=1, source_target_pairs={{0,1},{1,0},{2,3},{3,2},{4,5},{5,4},{6,7},{7,6},{8,9},{9,8},{10,11... | collective-permute-start | bytes 1769480 | tf_op jit(solution)/shard_map/ppermute | solution.py:434
  429.8 14.3 %collective-permute-start.54 = (bf16[8,48,3072]{2,1,0:T(8,128)(2,1)S(1)}, bf16[8,48,3072]{2,1,0:T(8,128)(2,1)S(1)}, u32[]{:S(2)}, u32[]{:S(2)}) collective-permute-start(bf16[8,48,3072]{2,1,0:T(8,128)(2,1)S(1)} %copy-done.65), channel_id=1, source_target_pairs={{0,16},{16,0},{1,17},{17,1},{2,18},{18,2},{3,19},{19,3},{4,20},{20... | collective-permute-start | bytes 7077896 | tf_op jit(solution)/shard_map/ppermute | solution.py:438
  454.8 24.7 %collective-permute-start.65 = (bf16[4,48,3072]{2,1,0:T(8,128)(2,1)S(1)}, bf16[4,48,3072]{2,1,0:T(8,128)(2,1)S(1)}, u32[]{:S(2)}, u32[]{:S(2)}) collective-permute-start(bf16[4,48,3072]{2,1,0:T(8,128)(2,1)S(1)} %get-tuple-element.308), channel_id=1, source_target_pairs={{0,1},{1,0},{2,3},{3,2},{4,5},{5,4},{6,7},{7,6},{8,9},{9,8},{10,11... | collective-permute-start | bytes 3538952 | tf_op jit(solution)/shard_map/ppermute | solution.py:434
  457.5 25.0 %collective-permute-start.66 = (bf16[4,48,3072]{2,1,0:T(8,128)(2,1)S(1)}, bf16[4,48,3072]{2,1,0:T(8,128)(2,1)S(1)}, u32[]{:S(2)}, u32[]{:S(2)}) collective-permute-start(bf16[4,48,3072]{2,1,0:T(8,128)(2,1)S(1)} %get-tuple-element.309), channel_id=1, source_target_pairs={{0,2},{1,3},{2,0},{3,1},{4,6},{5,7},{6,4},{7,5},{8,10},{9,11},{10,... | collective-permute-start | bytes 3538952 | tf_op jit(solution)/shard_map/ppermute | solution.py:434
  458.2 49.1 %collective-permute-start.68 = (bf16[48,9344]{1,0:T(8,128)(2,1)S(1)}, bf16[48,9344]{1,0:T(8,128)(2,1)S(1)}, u32[]{:S(2)}, u32[]{:S(2)}) collective-permute-start(bf16[48,9344]{1,0:T(8,128)(2,1)S(1)} %pad_maximum_fusion.8), channel_id=1, source_target_pairs={{0,8},{1,9},{2,10},{3,11},{4,12},{5,13},{6,14},{7,15},{24,16},{25,... | collective-permute-start | bytes 2691080 | tf_op jit(solution)/shard_map/ppermute | solution.py:444
  459.5 47.8 %collective-permute-start.64 = (bf16[4,160,768]{2,1,0:T(8,128)(2,1)S(1)}, bf16[4,160,768]{2,1,0:T(8,128)(2,1)S(1)}, u32[]{:S(2)}, u32[]{:S(2)}) collective-permute-start(bf16[4,160,768]{2,1,0:T(8,128)(2,1)S(1)} %copy-done.50), channel_id=1, source_target_pairs={{24,8},{8,16},{25,9},{9,17},{26,10},{10,18},{27,11},{11,19},{28,12... | collective-permute-start | bytes 2949128 | tf_op jit(solution)/shard_map/ppermute | solution.py:444
  460.8 46.1 %collective-permute-start.67 = (bf16[4,48,3072]{2,1,0:T(8,128)(2,1)S(1)}, bf16[4,48,3072]{2,1,0:T(8,128)(2,1)S(1)}, u32[]{:S(2)}, u32[]{:S(2)}) collective-permute-start(bf16[4,48,3072]{2,1,0:T(8,128)(2,1)S(1)} %get-tuple-element.310), channel_id=1, source_target_pairs={{0,4},{1,5},{2,6},{3,7},{4,0},{5,1},{6,2},{7,3},{8,12},{9,13},{10,... | collective-permute-start | bytes 3538952 | tf_op jit(solution)/shard_map/ppermute | solution.py:434
  509.3 18.4 %collective-permute-start.72 = (bf16[2,48,3072]{2,1,0:T(8,128)(2,1)S(1)}, bf16[2,48,3072]{2,1,0:T(8,128)(2,1)S(1)}, u32[]{:S(2)}, u32[]{:S(2)}) collective-permute-start(bf16[2,48,3072]{2,1,0:T(8,128)(2,1)S(1)} %get-tuple-element.315), channel_id=1, source_target_pairs={{0,4},{1,5},{2,6},{3,7},{4,0},{5,1},{6,2},{7,3},{8,12},{9,13},{10,... | collective-permute-start | bytes 1769480 | tf_op jit(solution)/shard_map/ppermute | solution.py:434
  509.3 19.5 %collective-permute-start.73 = (bf16[48,6144]{1,0:T(8,128)(2,1)S(1)}, bf16[48,6144]{1,0:T(8,128)(2,1)S(1)}, u32[]{:S(2)}, u32[]{:S(2)}) collective-permute-start(bf16[48,6144]{1,0:T(8,128)(2,1)S(1)} %pad_maximum_fusion.16), channel_id=1, source_target_pairs={{8,16},{9,17},{10,18},{11,19},{12,20},{13,21},{14,22},{15,23},{16,... | collective-permute-start | bytes 1769480 | tf_op jit(solution)/shard_map/ppermute | solution.py:444
  515.5 27.1 %collective-permute-start.69 = (bf16[4,160,768]{2,1,0:T(8,128)(2,1)S(1)}, bf16[4,160,768]{2,1,0:T(8,128)(2,1)S(1)}, u32[]{:S(2)}, u32[]{:S(2)}) collective-permute-start(bf16[4,160,768]{2,1,0:T(8,128)(2,1)S(1)} %maximum_select_fusion.1), channel_id=1, source_target_pairs={{0,16},{16,8},{1,17},{17,9},{2,18},{18,10},{3,19},{19,11},{4,20},{... | collective-permute-start | bytes 2949128 | tf_op jit(solution)/shard_map/ppermute | solution.py:444
  542.6 15.8 %collective-permute-start.74 = (bf16[1,48,3072]{2,1,0:T(8,128)(2,1)S(1)}, bf16[1,48,3072]{2,1,0:T(8,128)(2,1)S(1)}, u32[]{:S(2)}, u32[]{:S(2)}) collective-permute-start(bf16[1,48,3072]{2,1,0:T(8,128)(2,1)S(1)} %add_convert_fusion.26), channel_id=1, source_target_pairs={{0,2},{1,3},{2,0},{3,1},{4,6},{5,7},{6,4},{7,5},{8,10},{9,11},{10,... | collective-permute-start | bytes 884744 | tf_op jit(solution)/shard_map/ppermute | solution.py:434
  542.7 15.8 %collective-permute-start.75 = (bf16[1,48,3072]{2,1,0:T(8,128)(2,1)S(1)}, bf16[1,48,3072]{2,1,0:T(8,128)(2,1)S(1)}, u32[]{:S(2)}, u32[]{:S(2)}) collective-permute-start(bf16[1,48,3072]{2,1,0:T(8,128)(2,1)S(1)} %add_convert_fusion.28), channel_id=1, source_target_pairs={{0,4},{1,5},{2,6},{3,7},{4,0},{5,1},{6,2},{7,3},{8,12},{9,13},{10,... | collective-permute-start | bytes 884744 | tf_op jit(solution)/shard_map/ppermute | solution.py:434
  (97 other events, 1010.2 us)

commit v3 on v2

--- a/solution.py
+++ b/solution.py
@@ -311,22 +311,35 @@
 def grad_kernel(unit, at, meta, *refs):
     n_left = 2 if unit == 0 else 1
     left, (right,), outs, (turned,) = refs[:n_left], refs[n_left : n_left + 1], refs[n_left + 1 : n_left + 3], refs[-1:]
-    count, half = right.shape[0], D // 2
+    count = right.shape[0]
     n = pl.program_id(0)
+    chain_of = [[meta[c] for c in range(count)], [meta[count - 1 - c] for c in range(count)]]
 
     @pl.when(n == 0)
     def _():
         for i in range(n_left):
             for side in range(2):
-                chains = [jnp.where(meta[c] == side, left[i][c], jnp.zeros_like(left[i][c])) for c in range(count)]
-                turned[i, side * half : (side + 1) * half, :] = jnp.concatenate(chains, 0).T
+                turned[i, side] = jnp.concatenate([left[i][c] for c in chain_of[side]], 0).T
 
     pick = jnp.where(n == 3, 1, 0) if unit == 0 else 0
-    total = dot_nn(turned[pick], right[...].reshape(count * SEQ, CHUNK)).astype(BF16)
-    for side in range(2):
+
+    def put(side, total):
         for block in range(8):
-            row = side * half + block * ROWS
-            outs[side][meta[count + 2 + (unit * 2 + at) * 8 + block]] = total[row : row + ROWS]
+            place = meta[count + 3 + (unit * 2 + at) * 8 + block]
+            outs[side][place] = total[block * ROWS : (block + 1) * ROWS]
+
+    def with_first(first):
+        @pl.when(meta[count] == first)
+        def _():
+            for side, many in ((0, first), (1, count - first)):
+                if many:
+                    rows = jnp.concatenate([right[c] for c in chain_of[side][:many]], 0)
+                    put(side, dot_nn(turned[pick, side, :, : many * SEQ], rows).astype(BF16))
+                else:
+                    put(side, jnp.zeros((D // 2, CHUNK), BF16))
+
+    for first in range(count + 1):
+        with_first(first)
 
 
 ANY = pl.BlockSpec(memory_space=pl.ANY)
@@ -416,11 +429,11 @@
         grid_spec=pltpu.PrefetchScalarGridSpec(
             num_scalar_prefetch=1,
             grid=(WIDE // CHUNK,),
-            in_specs=[pl.BlockSpec((count, SEQ, D // 2), lambda n, m: (0, 0, m[count + at]))] * len(left)
+            in_specs=[pl.BlockSpec((count, SEQ, D // 2), lambda n, m: (0, 0, m[count + 1 + at]))] * len(left)
             + [right_spec],
             out_specs=[pl.BlockSpec((8, ROWS, CHUNK), lambda n, m: (0, 0, n))] * 2,
             scratch_shapes=[
-                pltpu.VMEM((len(left), D, count * SEQ), BF16),
+                pltpu.VMEM((len(left), 2, D // 2, count * SEQ), BF16),
             ],
         ),
         compiler_params=pltpu.CompilerParams(vmem_limit_bytes=50 * 1024 * 1024),
@@ -545,6 +558,7 @@
         small = jnp.pad(smalls, ((0, 0), (0, 0), (0, EXTRA - rows)))
         wide = jnp.pad(wides, ((0, 0), (0, 2 * EXTRA - 4 * rows))).reshape(2, 2, EXTRA)
         small = jnp.pad(jnp.concatenate([small, wide], 1), ((0, 0), (0, 6), (0, 0)))
+        small = small.at[:, 10, : 2 * count].set(numbers.astype(BF16)[None])
         small_mine = jnp.where(section == 0, small[0], small[1])
         small_twin = jnp.where(section == 0, small[1], small[0])
         home, small_home = wave((twin, by(routes.home_to_away)), (small_twin, by(routes.home_to_away)))
@@ -580,9 +594,8 @@
             (jnp.where(half == 1, inputs, cotangent), by(crossing)),
             (merged(away_held), swap_section),
         )
-        *twin_last, small_other, numbers_got = wave(
-            *[(array, swap_section) for array in away_far], (small_held, swap_section), (numbers, by(crossing))
-        )
+        *twin_last, small_other = wave(*[(array, swap_section) for array in away_far], (small_held, swap_section))
+        numbers_got = small_crossed[10, : 2 * count].astype(F32).astype(jnp.int32)
         pieces = [array for group in zip(near_held, near_far, away_held, away_far) for array in group]
         pieces += [twin_near_held, twin_near_far, twin_away_held, *twin_last]
 
@@ -630,8 +643,13 @@
     top_grad = jnp.where(at_home, cotangent, moved)
     sides = numbers[:count] ^ first_side
     meta = jnp.concatenate([half[None].astype(jnp.int32), numbers, sides.astype(jnp.int32)] + tables)
+    later = jnp.arange(count)[:, None] < jnp.arange(count)[None, :]
+    rank = jnp.sum((sides[:, None] > sides[None, :]) | ((sides[:, None] == sides[None, :]) & later.T), axis=1)
+    sorted_chains = jnp.sum(
+        jnp.where(rank[None, :] == jnp.arange(count)[:, None], jnp.arange(count)[None, :], 0), axis=1
+    )
     grad_meta = jnp.concatenate(
-        [sides.astype(jnp.int32)]
+        [sorted_chains.astype(jnp.int32), jnp.sum(1 - sides)[None].astype(jnp.int32)]
         + [value[None].astype(jnp.int32) for value in row_halves]
         + [place for unit in range(3) for place in (places[unit], places[unit])]
     )
@@ -699,9 +717,12 @@
 
         units = (2, 1, 0)
         totals = {(unit, 1): gradient(unit, 1) for unit in units}
-        keep = [totals[unit, 1][0] for unit in units] + [laid[0]]
-        got = [swap_section(totals[unit, 1][1]) for unit in units] + [swap_section(laid[1])]
+        keep = [totals[unit, 1][0] for unit in units]
+        got = [swap_section(totals[unit, 1][1]) for unit in units]
+        act_other, grad_other = act_move[1](act_move[0]), grad_move[1](grad_move[0])
+        wave.before = (act_other, grad_other)
         near_got = []
+        small_keep, small_extra = [laid[0]], (laid[1], swap_section)
         for step in range(3):
             if step == 0:
                 totals[2, 0] = gradient(2, 0, totals[0, 1][0])
@@ -709,24 +730,33 @@
             if step == 0:
                 totals[1, 0] = gradient(1, 0, *send)
                 totals[0, 0] = gradient(0, 0, totals[1, 0][0])
-            *got, other = wave(*bits_out(send, step), (totals[units[step], 0][1], swap_section))
+            small_got, *got, other = wave(
+                small_extra, *bits_out(send, step), (totals[units[step], 0][1], swap_section)
+            )
             near_got.append(other)
-        far_sum = [(a[0].astype(F32) + b[0].astype(F32)).astype(BF16) for a, b in zip(keep, got)]
-        small_near = far_sum[3][:ROWS]
-        far_sum = jnp.concatenate(far_sum[:3] + [far_sum[3][ROWS:]], -1)
+            small_keep, (small_send,) = reduce_step(small_keep, [small_got], step)
+            small_extra = (small_send, by_bit(ROTATIONS[0][step]))
+        far_sum = jnp.concatenate([(a[0].astype(F32) + b[0].astype(F32)).astype(BF16) for a, b in zip(keep, got)], -1)
 
         keep = [totals[unit, 0][0] for unit in units]
         keep, send = reduce_step(keep, near_got, 0)
-        *got, straight, act_other = wave(*bits_out(send, 0), (far_sum, by(routes.straight_back)), act_move)
+        small_got, *got, straight = wave(small_extra, *bits_out(send, 0), (far_sum, by(routes.straight_back)))
+        small_end = (small_keep[0][0].astype(F32) + small_got[0].astype(F32)).astype(BF16)
         keep, send = reduce_step(keep, got, 1)
-        *got, cross_a, grad_other = wave(
-            *bits_out(send, 1), (far_sum[:, : 2 * WIDE], by(routes.crossed)), grad_move
+        small_straight, *got, cross_a = wave(
+            (small_end[ROWS:], by(routes.straight_back)),
+            *bits_out(send, 1),
+            (far_sum[:, : 2 * WIDE], by(routes.crossed)),
         )
         keep, send = reduce_step(keep, got, 2)
-        *got, cross_b = wave(*bits_out(send, 2), (far_sum[:, 2 * WIDE :], by(routes.crossed)))
-        near_sum = [a[0].astype(F32) + b[0].astype(F32) for a, b in zip(keep, got)] + [small_near.astype(F32)]
+        *got, cross_b = wave(
+            *bits_out(send, 2),
+            (jnp.concatenate([far_sum[:, 2 * WIDE :], small_end[ROWS:]], -1), by(routes.crossed)),
+        )
+        near_sum = [a[0].astype(F32) + b[0].astype(F32) for a, b in zip(keep, got)] + [small_end[:ROWS].astype(F32)]
         (beside,) = wave((jnp.concatenate(near_sum, -1).astype(BF16), by(routes.away_to_home)))
         crossed = jnp.concatenate([cross_a, cross_b], -1)
+        straight = jnp.concatenate([straight, small_straight], -1)
 
         def settle(i, width):
             cols = slice(i * WIDE, i * WIDE + width)

time: 591 us -> 569 us (0.963)
  starting transfers between devices: 125 us -> 114 us
  Pallas kernels: 180 us -> 172 us
    ppermute x23, waiting for transfers between devices: 66.9 us -> 47 us  [along(): return lax.ppermute(array, ('section', 'dp'), flat)]
    ppermute x42, waiting for transfers between devices: 124 us -> 141 us  [swap_bit(): return lax.ppermute(array, 'dp', [(i, i ^ 1 << bit) for i in range(count)])]
    ppermute x14, starting transfers between devices: 24.6 us -> 12.8 us  [swap_section(): return lax.ppermute(array, 'section', [(0, 1), (1, 0)])]
    pallas_call x6, Pallas kernels: 48.4 us -> 40.7 us  [grad_call(): pl.pallas_call(functools.partial(grad_kernel, unit, at), out_shape=[out]...]
    unnamed x138 -> x132, local copies, waits for them, and re-layouts: 12.2 us -> 10.7 us
  transfers between devices with their start and end apart: 79 -> 79, of which waited for: 34 -> 33; matrix products, arithmetic and copies ran while one was open for 8% -> 9% of each run, Pallas kernels for 24% -> 24%
where the time goes in v3:
time: 569 us; the launch traced here: 560 us
  waiting for transfers between devices  194 us (34%)
  Pallas kernels  172 us (30%)
  starting transfers between devices  114 us (20%)
  other arithmetic  58.6 us (10%)
  local copies, waits for them, and re-layouts  17.5 us (3%)
    ppermute x42, waiting for transfers between devices, swap_bit(): return lax.ppermute(array, 'dp', [(i, i ^ 1 << bit) for i in range(count)])  141 us
    pallas_call x10, Pallas kernels, layer_call(): pl.pallas_call(functools.partial(layer_kernel, back, slot, lead, count),...  131 us
    ppermute x42, starting transfers between devices, swap_bit(): return lax.ppermute(array, 'dp', [(i, i ^ 1 << bit) for i in range(count)])  52.1 us
    ppermute x23, starting transfers between devices, along(): return lax.ppermute(array, ('section', 'dp'), flat)  49.1 us
    ppermute x23, waiting for transfers between devices, along(): return lax.ppermute(array, ('section', 'dp'), flat)  47 us
    pallas_call x6, Pallas kernels, grad_call(): pl.pallas_call(functools.partial(grad_kernel, unit, at), out_shape=[out]...  40.7 us
    convert_element_type x21, other arithmetic, both(): return (first.astype(F32) + second.astype(F32)).astype(BF16)  20.2 us
    ppermute x14, starting transfers between devices, swap_section(): return lax.ppermute(array, 'section', [(0, 1), (1, 0)])  12.8 us
  transfers between devices with their start and end apart: 79, of which 33 were waited for; matrix products, arithmetic and copies ran while one was open for 9% of the time, Pallas kernels for 24%

profile of v3, /device:TPU:1, one launch (start us, length us, event | category | flops | bytes accessed | tf_op | source)
XLA Modules:
  0.0 559.6 jit_solution(11553428198586201869)
XLA Ops:
  12.6 4.5 collective-permute-start.5
  19.7 2.8 collective-permute-start.6
  22.5 2.5 collective-permute-done.3
  25.2 6.5 %collective-permute-done.6 = bf16[48,3072]{1,0:T(8,128)(2,1)S(1)} collective-permute-done((bf16[48,3072]{1,0:T(8,128)(2,1)S(1)}, bf16[48,3072]{1,0:T(8,128)(2,1)S(1)}, u32[]{:S(2)}, u32[]{:S(2)}) %collective-permute-start.6) | collective-permute-done | bytes 294944 | tf_op jit(solution)/shard_map/ppermute | solution.py:457
  35.5 3.5 collective-permute-start.11
  40.6 13.2 %collective-permute-done.9 = bf16[2,48,3072]{2,1,0:T(8,128)(2,1)S(1)} collective-permute-done((bf16[2,48,3072]{2,1,0:T(8,128)(2,1)S(1)}, bf16[2,48,3072]{2,1,0:T(8,128)(2,1)S(1)}, u32[]{:S(2)}, u32[]{:S(2)}) %collective-permute-start.9) | collective-permute-done | bytes 589856 | tf_op jit(solution)/shard_map/ppermute | solution.py:447
  57.2 9.3 %collective-permute-start.14 = (bf16[4,48,3072]{2,1,0:T(8,128)(2,1)S(1)}, bf16[4,48,3072]{2,1,0:T(8,128)(2,1)S(1)}, u32[]{:S(2)}, u32[]{:S(2)}) collective-permute-start(bf16[4,48,3072]{2,1,0:T(8,128)(2,1)S(1)} %pad_maximum_fusion.2.refs_3_), channel_id=1, source_target_pairs={{0,4},{1,5},{2,6},{3,7},{4,0},{5,1},{6,2},{7,3},{8,12},{9,13},{10,... | collective-permute-start | bytes 3538952 | tf_op jit(solution)/shard_map/ppermute | solution.py:447
  71.1 14.3 %collective-permute-done.14.refs_4_ = bf16[4,48,3072]{2,1,0:T(8,128)(2,1)S(1)} collective-permute-done((bf16[4,48,3072]{2,1,0:T(8,128)(2,1)S(1)}, bf16[4,48,3072]{2,1,0:T(8,128)(2,1)S(1)}, u32[]{:S(2)}, u32[]{:S(2)}) %collective-permute-start.14) | collective-permute-done | bytes 1179680 | tf_op jit(solution)/shard_map/ppermute | solution.py:447
  90.8 5.6 collective-permute-done.20
  105.6 10.7 %collective-permute-done.25 = bf16[2,48,3072]{2,1,0:T(8,128)(2,1)} collective-permute-done((bf16[2,48,3072]{2,1,0:T(8,128)(2,1)}, bf16[2,48,3072]{2,1,0:T(8,128)(2,1)}, u32[]{:S(2)}, u32[]{:S(2)}) %collective-permute-start.25) | collective-permute-done | bytes 589856 | tf_op jit(solution)/shard_map/ppermute | solution.py:447
  118.6 3.3 maximum_maximum_fusion.1
  130.8 17.4 %collective-permute-done.30 = bf16[4,160,768]{2,1,0:T(8,128)(2,1)S(1)} collective-permute-done((bf16[4,160,768]{2,1,0:T(8,128)(2,1)}, bf16[4,160,768]{2,1,0:T(8,128)(2,1)S(1)}, u32[]{:S(2)}, u32[]{:S(2)}) %collective-permute-start.30) | collective-permute-done | bytes 983072 | tf_op jit(solution)/shard_map/ppermute | solution.py:457
  148.2 15.6 %collective-permute-done.27.refs_6_ = bf16[4,48,3072]{2,1,0:T(8,128)(2,1)} collective-permute-done((bf16[4,48,3072]{2,1,0:T(8,128)(2,1)}, bf16[4,48,3072]{2,1,0:T(8,128)(2,1)}, u32[]{:S(2)}, u32[]{:S(2)}) %collective-permute-start.27) | collective-permute-done | bytes 1179680 | tf_op jit(solution)/shard_map/ppermute | solution.py:447
  171.3 10.5 %layer_fwd.4 = (bf16[1,160,768]{2,1,0:T(8,128)(2,1)S(1)}, bf16[4,160,768]{2,1,0:T(8,128)(2,1)S(1)}) custom-call(s32[61]{0:T(128)S(1)} %concatenate.129.refs_0_, f32[2,8,768]{2,1,0:T(8,128)S(1)} %constant_dynamic-update-slice_fusion.refs_1_, f32[2,1,3072]{2,1,0:T(1,128)S(1)} %constant_dynamic-update-slice_fusion.2.refs_2_, ...), custom_call_target="tpu_custom_call" | custom-call | flops 1 | bytes 1 | tf_op jit(solution)/shard_map/layer_fwd/pallas_call | solution.py:408
  183.1 11.1 %layer_fwd.5 = (bf16[1,160,768]{2,1,0:T(8,128)(2,1)S(1)}, bf16[4,160,768]{2,1,0:T(8,128)(2,1)S(1)}) custom-call(s32[61]{0:T(128)S(1)} %concatenate.129.refs_0_, f32[2,8,768]{2,1,0:T(8,128)S(1)} %constant_dynamic-update-slice_fusion.refs_1_, f32[2,1,3072]{2,1,0:T(1,128)S(1)} %constant_dynamic-update-slice_fusion.2.refs_2_, ...), custom_call_target="tpu_custom_call", output_to_operand_aliasing={{1}: (22, {})} | custom-call | flops 1 | bytes 1 | tf_op jit(solution)/shard_map/layer_fwd/pallas_call | solution.py:408
  195.6 10.5 %layer_fwd.6 = (bf16[1,160,768]{2,1,0:T(8,128)(2,1)S(1)}, bf16[4,160,768]{2,1,0:T(8,128)(2,1)S(1)}) custom-call(s32[61]{0:T(128)S(1)} %concatenate.129.refs_0_, f32[2,8,768]{2,1,0:T(8,128)S(1)} %constant_dynamic-update-slice_fusion.refs_1_, f32[2,1,3072]{2,1,0:T(1,128)S(1)} %constant_dynamic-update-slice_fusion.2.refs_2_, ...), custom_call_target="tpu_custom_call", output_to_operand_aliasing={{1}: (22, {})} | custom-call | flops 1 | bytes 1 | tf_op jit(solution)/shard_map/layer_fwd/pallas_call | solution.py:408
  207.4 10.4 %layer_fwd.7 = (bf16[1,160,768]{2,1,0:T(8,128)(2,1)S(1)}, bf16[4,160,768]{2,1,0:T(8,128)(2,1)S(1)}) custom-call(s32[61]{0:T(128)S(1)} %concatenate.129.refs_0_, f32[2,8,768]{2,1,0:T(8,128)S(1)} %constant_dynamic-update-slice_fusion.refs_1_, f32[2,1,3072]{2,1,0:T(1,128)S(1)} %constant_dynamic-update-slice_fusion.2.refs_2_, ...), custom_call_target="tpu_custom_call", output_to_operand_aliasing={{1}: (22, {})} | custom-call | flops 1 | bytes 1 | tf_op jit(solution)/shard_map/layer_fwd/pallas_call | solution.py:408
  218.8 9.8 %layer_back.6 = (bf16[1,160,768]{2,1,0:T(8,128)(2,1)S(1)}, bf16[4,160,768]{2,1,0:T(8,128)(2,1)S(1)}, f32[4,160,768]{2,1,0:T(8,128)}, f32[4,8,768]{2,1,0:T(8,128)...) custom-call(s32[61]{0:T(128)S(1)} %concatenate.129.refs_0_, ...), custom_call_target="tpu_custom_call" | custom-call | flops 1 | bytes 1 | tf_op jit(solution)/shard_map/layer_back/pallas_call | solution.py:408
  229.9 4.9 collective-permute-start.40
  239.1 19.5 %layer_back.8 = (bf16[1,160,768]{2,1,0:T(8,128)(2,1)}, bf16[4,160,768]{2,1,0:T(8,128)(2,1)S(1)}, f32[4,160,768]{2,1,0:T(8,128)}, f32[4,8,768]{2,1,0:T(8,128)S(1)...) custom-call(s32[61]{0:T(128)S(1)} %concatenate.129.refs_0_, ...), custom_call_target="tpu_custom_call", output_to_operand_aliasing={{1}: (25, {}), {2}: (26, {}), {3}: (27, {}), {4}: (28, {}),... | custom-call | flops 1 | bytes 1 | tf_op jit(solution)/shard_map/layer_back/pallas_call | solution.py:408
  261.3 19.3 %layer_back.9 = (bf16[1,160,768]{2,1,0:T(8,128)(2,1)}, bf16[4,160,768]{2,1,0:T(8,128)(2,1)S(1)}, f32[4,160,768]{2,1,0:T(8,128)}, f32[4,8,768]{2,1,0:T(8,128)S(1)...) custom-call(s32[61]{0:T(128)S(1)} %concatenate.129.refs_0_, ...), custom_call_target="tpu_custom_call", output_to_operand_aliasing={{1}: (25, {}), {2}: (26, {}), {3}: (27, {}), {4}: (28, {}),... | custom-call | flops 1 | bytes 1 | tf_op jit(solution)/shard_map/layer_back/pallas_call | solution.py:408
  282.9 19.4 %layer_back.10 = (bf16[1,160,768]{2,1,0:T(8,128)(2,1)}, bf16[4,160,768]{2,1,0:T(8,128)(2,1)S(1)}, f32[4,160,768]{2,1,0:T(8,128)}, f32[4,8,768]{2,1,0:T(8,128)S(1...) custom-call(s32[61]{0:T(128)S(1)} %concatenate.129.refs_0_, ...), custom_call_target="tpu_custom_call", output_to_operand_aliasing={{1}: (23, {}), {2}: (24, {}), {3}: (25, {}), {4}: (26, {}),... | custom-call | flops 1 | bytes 1 | tf_op jit(solution)/shard_map/layer_back/pallas_call | solution.py:408
  304.1 19.3 %layer_back.11 = (bf16[1,160,768]{2,1,0:T(8,128)(2,1)}, bf16[4,160,768]{2,1,0:T(8,128)(2,1)S(1)}, f32[4,160,768]{2,1,0:T(8,128)}, f32[4,8,768]{2,1,0:T(8,128)S(1...) custom-call(s32[61]{0:T(128)S(1)} %concatenate.129.refs_0_, ...), custom_call_target="tpu_custom_call", output_to_operand_aliasing={{1}: (23, {}), {2}: (24, {}), {3}: (25, {}), {4}: (26, {}),... | custom-call | flops 1 | bytes 1 | tf_op jit(solution)/shard_map/layer_back/pallas_call | solution.py:408
  326.0 7.2 %layer_grad.8 = (bf16[8,48,3072]{2,1,0:T(8,128)(2,1)}, bf16[8,48,3072]{2,1,0:T(8,128)(2,1)}) custom-call(s32[55]{0:T(128)S(1)} %concatenate.148.meta, bf16[4,160,768]{2,1,0:T(8,128)(2,1)S(1)} %get-tuple-element.287.refs_0_, bf16[4,160,768]{2,1,0:T(8,128)(2,1)S(1)} %copy-done.7, bf16[3,4,160,3072]{3,2,1,0:T(8,128)(2,1)} %get-tuple-element.281.refs_1_.refs_2_), custom_call_target="tpu_custom_call" | custom-call | flops 1 | bytes 1 | tf_op jit(solution)/shard_map/layer_grad/pallas_call | solution.py:426
  333.8 6.5 %layer_grad.6 = (bf16[8,48,3072]{2,1,0:T(8,128)(2,1)S(1)}, bf16[8,48,3072]{2,1,0:T(8,128)(2,1)}) custom-call(s32[55]{0:T(128)S(1)} %concatenate.148.meta, bf16[4,160,768]{2,1,0:T(8,128)(2,1)S(1)} %copy-done.3, bf16[3,4,160,3072]{3,2,1,0:T(8,128)(2,1)} %get-tuple-element.281.refs_1_.refs_2_), custom_call_target="tpu_custom_call" | custom-call | flops 1 | bytes 1 | tf_op jit(solution)/shard_map/layer_grad/pallas_call | solution.py:426
  342.0 6.5 %layer_grad.7 = (bf16[8,48,3072]{2,1,0:T(8,128)(2,1)S(1)}, bf16[8,48,3072]{2,1,0:T(8,128)(2,1)}) custom-call(s32[55]{0:T(128)S(1)} %concatenate.148.meta, bf16[4,160,768]{2,1,0:T(8,128)(2,1)S(1)} %copy-done.2, bf16[3,4,160,3072]{3,2,1,0:T(8,128)(2,1)} %get-tuple-element.281.refs_1_.refs_2_), custom_call_target="tpu_custom_call" | custom-call | flops 1 | bytes 1 | tf_op jit(solution)/shard_map/layer_grad/pallas_call | solution.py:426
  362.7 6.5 %layer_grad.11 = (bf16[8,48,3072]{2,1,0:T(8,128)(2,1)S(1)}, bf16[8,48,3072]{2,1,0:T(8,128)(2,1)}) custom-call(s32[55]{0:T(128)S(1)} %concatenate.148.meta, bf16[4,160,768]{2,1,0:T(8,128)(2,1)S(1)} %copy-done.3, bf16[3,4,160,3072]{3,2,1,0:T(8,128)(2,1)} %get-tuple-element.281.refs_1_.refs_2_), custom_call_target="tpu_custom_call" | custom-call | flops 1 | bytes 1 | tf_op jit(solution)/shard_map/layer_grad/pallas_call | solution.py:426
  369.2 4.4 add_convert_fusion.6
  373.6 3.7 add_convert_fusion.8
  377.4 3.9 add_convert_fusion.7
  381.3 6.8 %collective-permute-done.44 = bf16[4,160,768]{2,1,0:T(8,128)(2,1)} collective-permute-done((bf16[4,160,768]{2,1,0:T(8,128)(2,1)}, bf16[4,160,768]{2,1,0:T(8,128)(2,1)}, u32[]{:S(2)}, u32[]{:S(2)}) %collective-permute-start.44) | collective-permute-done | bytes 983072 | tf_op jit(solution)/shard_map/ppermute | solution.py:457
  388.1 6.2 %collective-permute-start.50 = (bf16[4,48,3072]{2,1,0:T(8,128)(2,1)}, bf16[4,48,3072]{2,1,0:T(8,128)(2,1)}, u32[]{:S(2)}, u32[]{:S(2)}) collective-permute-start(bf16[4,48,3072]{2,1,0:T(8,128)(2,1)} %get-tuple-element.300), channel_id=1, source_target_pairs={{0,1},{1,0},{2,3},{3,2},{4,5},{5,4},{6,7},{7,6},{8,9},{9,8},{10,11... | collective-permute-start | bytes 3538952 | tf_op jit(solution)/shard_map/ppermute | solution.py:447
  395.8 6.6 %layer_grad.9 = (bf16[8,48,3072]{2,1,0:T(8,128)(2,1)S(1)}, bf16[8,48,3072]{2,1,0:T(8,128)(2,1)}) custom-call(s32[55]{0:T(128)S(1)} %concatenate.148.meta, bf16[4,160,768]{2,1,0:T(8,128)(2,1)S(1)} %copy-done.2, bf16[3,4,160,3072]{3,2,1,0:T(8,128)(2,1)} %get-tuple-element.281.refs_1_.refs_2_), custom_call_target="tpu_custom_call" | custom-call | flops 1 | bytes 1 | tf_op jit(solution)/shard_map/layer_grad/pallas_call | solution.py:426
  402.4 7.4 %layer_grad.10 = (bf16[8,48,3072]{2,1,0:T(8,128)(2,1)}, bf16[8,48,3072]{2,1,0:T(8,128)(2,1)}) custom-call(s32[55]{0:T(128)S(1)} %concatenate.148.meta, bf16[4,160,768]{2,1,0:T(8,128)(2,1)S(1)} %copy-done.5, bf16[4,160,768]{2,1,0:T(8,128)(2,1)S(1)} %copy-done.8, bf16[3,4,160,3072]{3,2,1,0:T(8,128)(2,1)} %get-tuple-element.281.refs_1_.refs_2_), custom_call_target="tpu_custom_call" | custom-call | flops 1 | bytes 1 | tf_op jit(solution)/shard_map/layer_grad/pallas_call | solution.py:426
  410.8 7.2 %collective-permute-done.50 = bf16[4,48,3072]{2,1,0:T(8,128)(2,1)} collective-permute-done((bf16[4,48,3072]{2,1,0:T(8,128)(2,1)}, bf16[4,48,3072]{2,1,0:T(8,128)(2,1)}, u32[]{:S(2)}, u32[]{:S(2)}) %collective-permute-start.50) | collective-permute-done | bytes 1179680 | tf_op jit(solution)/shard_map/ppermute | solution.py:447
  423.4 13.4 %collective-permute-done.52 = bf16[4,48,3072]{2,1,0:T(8,128)(2,1)S(1)} collective-permute-done((bf16[4,48,3072]{2,1,0:T(8,128)(2,1)}, bf16[4,48,3072]{2,1,0:T(8,128)(2,1)S(1)}, u32[]{:S(2)}, u32[]{:S(2)}) %collective-permute-start.52) | collective-permute-done | bytes 1179680 | tf_op jit(solution)/shard_map/ppermute | solution.py:447
  442.6 8.4 %collective-permute-done.55 = bf16[2,48,3072]{2,1,0:T(8,128)(2,1)S(1)} collective-permute-done((bf16[2,48,3072]{2,1,0:T(8,128)(2,1)S(1)}, bf16[2,48,3072]{2,1,0:T(8,128)(2,1)S(1)}, u32[]{:S(2)}, u32[]{:S(2)}) %collective-permute-start.55) | collective-permute-done | bytes 589856 | tf_op jit(solution)/shard_map/ppermute | solution.py:447
  456.3 3.5 collective-permute-start.59
  469.0 31.4 %collective-permute-done.65 = bf16[1,96,128]{2,1,0:T(8,128)(2,1)S(1)} collective-permute-done((bf16[1,96,128]{2,1,0:T(8,128)(2,1)S(1)}, bf16[1,96,128]{2,1,0:T(8,128)(2,1)S(1)}, u32[]{:S(2)}, u32[]{:S(2)}) %collective-permute-start.65) | collective-permute-done | bytes 24608 | tf_op jit(solution)/shard_map/ppermute | solution.py:447
  505.7 5.2 collective-permute-start.73
  511.0 2.5 collective-permute-done.69
  514.3 6.4 %collective-permute-done.71 = bf16[2,48,3072]{2,1,0:T(8,128)(2,1)S(1)} collective-permute-done((bf16[2,48,3072]{2,1,0:T(8,128)(2,1)S(1)}, bf16[2,48,3072]{2,1,0:T(8,128)(2,1)S(1)}, u32[]{:S(2)}, u32[]{:S(2)}) %collective-permute-start.71) | collective-permute-done | bytes 589856 | tf_op jit(solution)/shard_map/ppermute | solution.py:447
  520.8 4.5 collective-permute-done.73
  525.9 3.6 collective-permute-start.75
  530.4 4.4 collective-permute-start.77
  535.0 3.2 collective-permute-done.75
  539.1 3.7 collective-permute-done.77
  546.4 2.7 select_bitcast_fusion
  (395 shorter events, 147.1 us)
Async XLA Ops:
  33.9 20.0 %collective-permute-start.8 = (bf16[2,48,3072]{2,1,0:T(8,128)(2,1)S(1)}, bf16[2,48,3072]{2,1,0:T(8,128)(2,1)S(1)}, u32[]{:S(2)}, u32[]{:S(2)}) collective-permute-start(bf16[2,48,3072]{2,1,0:T(8,128)(2,1)S(1)} %pad_maximum_fusion.10), channel_id=1, source_target_pairs={{0,2},{1,3},{2,0},{3,1},{4,6},{5,7},{6,4},{7,5},{8,10},{9,11},{10,... | collective-permute-start | bytes 1769480 | tf_op jit(solution)/shard_map/ppermute | solution.py:447
  34.2 19.6 %collective-permute-start.9 = (bf16[2,48,3072]{2,1,0:T(8,128)(2,1)S(1)}, bf16[2,48,3072]{2,1,0:T(8,128)(2,1)S(1)}, u32[]{:S(2)}, u32[]{:S(2)}) collective-permute-start(bf16[2,48,3072]{2,1,0:T(8,128)(2,1)S(1)} %pad_maximum_fusion.11), channel_id=1, source_target_pairs={{0,4},{1,5},{2,6},{3,7},{4,0},{5,1},{6,2},{7,3},{8,12},{9,13},{10,... | collective-permute-start | bytes 1769480 | tf_op jit(solution)/shard_map/ppermute | solution.py:447
  35.5 19.4 %collective-permute-start.11 = (bf16[48,6144]{1,0:T(8,128)(2,1)S(1)}, bf16[48,6144]{1,0:T(8,128)(2,1)S(1)}, u32[]{:S(2)}, u32[]{:S(2)}) collective-permute-start(bf16[48,6144]{1,0:T(8,128)(2,1)S(1)} %slice.553), channel_id=1, source_target_pairs={{8,16},{9,17},{10,18},{11,19},{12,20},{13,21},{14,22},{15,23},{16,... | collective-permute-start | bytes 1769480 | tf_op jit(solution)/shard_map/ppermute | solution.py:457
  54.9 14.4 %collective-permute-start.12 = (bf16[1,2,16,128]{3,2,1,0:T(8,128)(2,1)S(1)}, bf16[1,2,16,128]{3,2,1,0:T(8,128)(2,1)S(1)}, u32[]{:S(2)}, u32[]{:S(2)}) collective-permute-start(bf16[1,2,16,128]{3,2,1,0:T(8,128)(2,1)S(1)} %maximum_bitcast_fusion.3), channel_id=1, source_target_pairs={{0,1},{1,0},{2,3},{3,2},{4,5},{5,4},{6,7},{7,6},{8,9},{9,8},{10,11... | collective-permute-start | bytes 24584 | tf_op jit(solution)/shard_map/ppermute | solution.py:447
  55.9 15.0 %collective-permute-start.13 = (bf16[48,9216]{1,0:T(8,128)(2,1)S(1)}, bf16[48,9216]{1,0:T(8,128)(2,1)S(1)}, u32[]{:S(2)}, u32[]{:S(2)}) collective-permute-start(bf16[48,9216]{1,0:T(8,128)(2,1)S(1)} %get-tuple-element.190), channel_id=1, source_target_pairs={{8,0},{9,1},{10,2},{11,3},{12,4},{13,5},{14,6},{15,7},{16,24},{17,... | collective-permute-start | bytes 2654216 | tf_op jit(solution)/shard_map/ppermute | solution.py:457
  57.2 28.2 %collective-permute-start.14 = (bf16[4,48,3072]{2,1,0:T(8,128)(2,1)S(1)}, bf16[4,48,3072]{2,1,0:T(8,128)(2,1)S(1)}, u32[]{:S(2)}, u32[]{:S(2)}) collective-permute-start(bf16[4,48,3072]{2,1,0:T(8,128)(2,1)S(1)} %pad_maximum_fusion.2.refs_3_), channel_id=1, source_target_pairs={{0,4},{1,5},{2,6},{3,7},{4,0},{5,1},{6,2},{7,3},{8,12},{9,13},{10,... | collective-permute-start | bytes 3538952 | tf_op jit(solution)/shard_map/ppermute | solution.py:447
  66.5 18.9 %collective-permute-start.15 = (bf16[4,48,3072]{2,1,0:T(8,128)(2,1)S(1)}, bf16[4,48,3072]{2,1,0:T(8,128)(2,1)S(1)}, u32[]{:S(2)}, u32[]{:S(2)}) collective-permute-start(bf16[4,48,3072]{2,1,0:T(8,128)(2,1)S(1)} %pad_maximum_fusion.3.refs_7_), channel_id=1, source_target_pairs={{0,1},{1,0},{2,3},{3,2},{4,5},{5,4},{6,7},{7,6},{8,9},{9,8},{10,11... | collective-permute-start | bytes 3538952 | tf_op jit(solution)/shard_map/ppermute | solution.py:447
  66.5 18.9 %collective-permute-start.16 = (bf16[4,48,3072]{2,1,0:T(8,128)(2,1)S(1)}, bf16[4,48,3072]{2,1,0:T(8,128)(2,1)S(1)}, u32[]{:S(2)}, u32[]{:S(2)}) collective-permute-start(bf16[4,48,3072]{2,1,0:T(8,128)(2,1)S(1)} %pad_maximum_fusion.4.refs_11_), channel_id=1, source_target_pairs={{0,2},{1,3},{2,0},{3,1},{4,6},{5,7},{6,4},{7,5},{8,10},{9,11},{10,... | collective-permute-start | bytes 3538952 | tf_op jit(solution)/shard_map/ppermute | solution.py:447
  85.4 13.7 %collective-permute-start.21 = (bf16[4,48,9216]{2,1,0:T(8,128)(2,1)S(1)}, bf16[4,48,9216]{2,1,0:T(8,128)(2,1)}, u32[]{:S(2)}, u32[]{:S(2)}) collective-permute-start(bf16[4,48,9216]{2,1,0:T(8,128)(2,1)S(1)} %maximum_maximum_fusion), channel_id=1, source_target_pairs={{0,16},{16,0},{1,17},{17,1},{2,18},{18,2},{3,19},{19,3},{4,20},{20... | collective-permute-start | bytes 10616840 | tf_op jit(solution)/shard_map/ppermute | solution.py:451
  99.1 24.0 %collective-permute-start.26 = (bf16[4,48,9216]{2,1,0:T(8,128)(2,1)}, bf16[4,48,9216]{2,1,0:T(8,128)(2,1)}, u32[]{:S(2)}, u32[]{:S(2)}) collective-permute-start(bf16[4,48,9216]{2,1,0:T(8,128)(2,1)} %pad_maximum_fusion), channel_id=1, source_target_pairs={{0,16},{16,0},{1,17},{17,1},{2,18},{18,2},{3,19},{19,3},{4,20},{20... | collective-permute-start | bytes 10616840 | tf_op jit(solution)/shard_map/ppermute | solution.py:451
  101.0 15.2 %collective-permute-start.25 = (bf16[2,48,3072]{2,1,0:T(8,128)(2,1)}, bf16[2,48,3072]{2,1,0:T(8,128)(2,1)}, u32[]{:S(2)}, u32[]{:S(2)}) collective-permute-start(bf16[2,48,3072]{2,1,0:T(8,128)(2,1)} %pad_maximum_fusion.15), channel_id=1, source_target_pairs={{0,1},{1,0},{2,3},{3,2},{4,5},{5,4},{6,7},{7,6},{8,9},{9,8},{10,11... | collective-permute-start | bytes 1769480 | tf_op jit(solution)/shard_map/ppermute | solution.py:447
  101.6 15.8 %collective-permute-start.24 = (bf16[2,48,3072]{2,1,0:T(8,128)(2,1)}, bf16[2,48,3072]{2,1,0:T(8,128)(2,1)S(1)}, u32[]{:S(2)}, u32[]{:S(2)}) collective-permute-start(bf16[2,48,3072]{2,1,0:T(8,128)(2,1)} %pad_maximum_fusion.14), channel_id=1, source_target_pairs={{0,4},{1,5},{2,6},{3,7},{4,0},{5,1},{6,2},{7,3},{8,12},{9,13},{10,... | collective-permute-start | bytes 1769480 | tf_op jit(solution)/shard_map/ppermute | solution.py:447
  102.7 20.4 %collective-permute-start.22 = (bf16[4,2,16,128]{3,2,1,0:T(8,128)(2,1)S(1)}, bf16[4,2,16,128]{3,2,1,0:T(8,128)(2,1)S(1)}, u32[]{:S(2)}, u32[]{:S(2)}) collective-permute-start(bf16[4,2,16,128]{3,2,1,0:T(8,128)(2,1)S(1)} %pad_maximum_fusion.21), channel_id=1, source_target_pairs={{0,4},{1,5},{2,6},{3,7},{4,0},{5,1},{6,2},{7,3},{8,12},{9,13},{10,... | collective-permute-start | bytes 98312 | tf_op jit(solution)/shard_map/ppermute | solution.py:447
  104.2 14.4 %collective-permute-start.23 = (bf16[2,48,3072]{2,1,0:T(8,128)(2,1)S(1)}, bf16[2,48,3072]{2,1,0:T(8,128)(2,1)S(1)}, u32[]{:S(2)}, u32[]{:S(2)}) collective-permute-start(bf16[2,48,3072]{2,1,0:T(8,128)(2,1)S(1)} %copy-done.49), channel_id=1, source_target_pairs={{0,2},{1,3},{2,0},{3,1},{4,6},{5,7},{6,4},{7,5},{8,10},{9,11},{10,... | collective-permute-start | bytes 1769480 | tf_op jit(solution)/shard_map/ppermute | solution.py:447
  123.1 40.8 %collective-permute-start.31 = (bf16[4,48,9216]{2,1,0:T(8,128)(2,1)}, bf16[4,48,9216]{2,1,0:T(8,128)(2,1)}, u32[]{:S(2)}, u32[]{:S(2)}) collective-permute-start(bf16[4,48,9216]{2,1,0:T(8,128)(2,1)} %maximum_maximum_fusion.1), channel_id=1, source_target_pairs={{0,16},{16,0},{1,17},{17,1},{2,18},{18,2},{3,19},{19,3},{4,20},{20... | collective-permute-start | bytes 10616840 | tf_op jit(solution)/shard_map/ppermute | solution.py:451
  125.4 38.4 %collective-permute-start.27 = (bf16[4,48,3072]{2,1,0:T(8,128)(2,1)}, bf16[4,48,3072]{2,1,0:T(8,128)(2,1)}, u32[]{:S(2)}, u32[]{:S(2)}) collective-permute-start(bf16[4,48,3072]{2,1,0:T(8,128)(2,1)} %pad_maximum_fusion.5.refs_5_), channel_id=1, source_target_pairs={{0,4},{1,5},{2,6},{3,7},{4,0},{5,1},{6,2},{7,3},{8,12},{9,13},{10,... | collective-permute-start | bytes 3538952 | tf_op jit(solution)/shard_map/ppermute | solution.py:447
  125.5 38.3 %collective-permute-start.28 = (bf16[4,48,3072]{2,1,0:T(8,128)(2,1)}, bf16[4,48,3072]{2,1,0:T(8,128)(2,1)}, u32[]{:S(2)}, u32[]{:S(2)}) collective-permute-start(bf16[4,48,3072]{2,1,0:T(8,128)(2,1)} %pad_maximum_fusion.6.refs_9_), channel_id=1, source_target_pairs={{0,1},{1,0},{2,3},{3,2},{4,5},{5,4},{6,7},{7,6},{8,9},{9,8},{10,11... | collective-permute-start | bytes 3538952 | tf_op jit(solution)/shard_map/ppermute | solution.py:447
  126.4 37.5 %collective-permute-start.29 = (bf16[4,48,3072]{2,1,0:T(8,128)(2,1)S(1)}, bf16[4,48,3072]{2,1,0:T(8,128)(2,1)}, u32[]{:S(2)}, u32[]{:S(2)}) collective-permute-start(bf16[4,48,3072]{2,1,0:T(8,128)(2,1)S(1)} %pad_maximum_fusion.7.refs_13_), channel_id=1, source_target_pairs={{0,2},{1,3},{2,0},{3,1},{4,6},{5,7},{6,4},{7,5},{8,10},{9,11},{10,... | collective-permute-start | bytes 3538952 | tf_op jit(solution)/shard_map/ppermute | solution.py:447
  127.8 20.5 %collective-permute-start.30 = (bf16[4,160,768]{2,1,0:T(8,128)(2,1)}, bf16[4,160,768]{2,1,0:T(8,128)(2,1)S(1)}, u32[]{:S(2)}, u32[]{:S(2)}) collective-permute-start(bf16[4,160,768]{2,1,0:T(8,128)(2,1)} %broadcast_select_fusion), channel_id=1, source_target_pairs={{0,8},{1,9},{2,10},{3,11},{4,12},{5,13},{6,14},{7,15},{24,16},{25,... | collective-permute-start | bytes 2949128 | tf_op jit(solution)/shard_map/ppermute | solution.py:457
  181.8 37.0 %collective-permute-start.36 = (bf16[1,160,768]{2,1,0:T(8,128)(2,1)S(1)}, bf16[1,160,768]{2,1,0:T(8,128)(2,1)S(1)}, u32[]{:S(2)}, u32[]{:S(2)}) collective-permute-start(bf16[1,160,768]{2,1,0:T(8,128)(2,1)S(1)} %get-tuple-element.213), channel_id=1, source_target_pairs={{0,8},{1,9},{2,10},{3,11},{4,12},{5,13},{6,14},{7,15},{16,24},{17,... | collective-permute-start | bytes 737288 | tf_op jit(solution)/shard_map/ppermute | solution.py:457
  194.3 40.6 %collective-permute-start.37 = (bf16[1,160,768]{2,1,0:T(8,128)(2,1)S(1)}, bf16[1,160,768]{2,1,0:T(8,128)(2,1)S(1)}, u32[]{:S(2)}, u32[]{:S(2)}) collective-permute-start(bf16[1,160,768]{2,1,0:T(8,128)(2,1)S(1)} %get-tuple-element.216), channel_id=1, source_target_pairs={{0,8},{1,9},{2,10},{3,11},{4,12},{5,13},{6,14},{7,15},{16,24},{17,... | collective-permute-start | bytes 737288 | tf_op jit(solution)/shard_map/ppermute | solution.py:457
  206.1 31.6 %collective-permute-start.38 = (bf16[1,160,768]{2,1,0:T(8,128)(2,1)S(1)}, bf16[1,160,768]{2,1,0:T(8,128)(2,1)S(1)}, u32[]{:S(2)}, u32[]{:S(2)}) collective-permute-start(bf16[1,160,768]{2,1,0:T(8,128)(2,1)S(1)} %get-tuple-element.219), channel_id=1, source_target_pairs={{0,8},{1,9},{2,10},{3,11},{4,12},{5,13},{6,14},{7,15},{16,24},{17,... | collective-permute-start | bytes 737288 | tf_op jit(solution)/shard_map/ppermute | solution.py:457
  229.9 30.0 %collective-permute-start.40 = (bf16[1,160,768]{2,1,0:T(8,128)(2,1)S(1)}, bf16[1,160,768]{2,1,0:T(8,128)(2,1)S(1)}, u32[]{:S(2)}, u32[]{:S(2)}) collective-permute-start(bf16[1,160,768]{2,1,0:T(8,128)(2,1)S(1)} %get-tuple-element.223), channel_id=1, source_target_pairs={{0,8},{1,9},{2,10},{3,11},{4,12},{5,13},{6,14},{7,15},{16,24},{17,... | collective-permute-start | bytes 737288 | tf_op jit(solution)/shard_map/ppermute | solution.py:457
  236.3 25.0 %collective-permute-start.41 = (bf16[1,160,768]{2,1,0:T(8,128)(2,1)S(1)}, bf16[1,160,768]{2,1,0:T(8,128)(2,1)S(1)}, u32[]{:S(2)}, u32[]{:S(2)}) collective-permute-start(bf16[1,160,768]{2,1,0:T(8,128)(2,1)S(1)} %get-tuple-element.236), channel_id=1, source_target_pairs={{8,0},{9,1},{10,2},{11,3},{12,4},{13,5},{14,6},{15,7},{24,16},{25,... | collective-permute-start | bytes 737288 | tf_op jit(solution)/shard_map/ppermute | solution.py:457
  258.6 24.4 %collective-permute-start.43 = (bf16[1,160,768]{2,1,0:T(8,128)(2,1)}, bf16[1,160,768]{2,1,0:T(8,128)(2,1)}, u32[]{:S(2)}, u32[]{:S(2)}) collective-permute-start(bf16[1,160,768]{2,1,0:T(8,128)(2,1)} %get-tuple-element.247), channel_id=1, source_target_pairs={{8,0},{9,1},{10,2},{11,3},{12,4},{13,5},{14,6},{15,7},{24,16},{25,... | collective-permute-start | bytes 737288 | tf_op jit(solution)/shard_map/ppermute | solution.py:457
  280.6 23.5 %collective-permute-start.42 = (bf16[1,160,768]{2,1,0:T(8,128)(2,1)}, bf16[1,160,768]{2,1,0:T(8,128)(2,1)}, u32[]{:S(2)}, u32[]{:S(2)}) collective-permute-start(bf16[1,160,768]{2,1,0:T(8,128)(2,1)} %get-tuple-element.258), channel_id=1, source_target_pairs={{8,0},{9,1},{10,2},{11,3},{12,4},{13,5},{14,6},{15,7},{24,16},{25,... | collective-permute-start | bytes 737288 | tf_op jit(solution)/shard_map/ppermute | solution.py:457
  333.2 36.0 %collective-permute-start.48 = (bf16[8,48,3072]{2,1,0:T(8,128)(2,1)}, bf16[8,48,3072]{2,1,0:T(8,128)(2,1)}, u32[]{:S(2)}, u32[]{:S(2)}) collective-permute-start(bf16[8,48,3072]{2,1,0:T(8,128)(2,1)} %get-tuple-element.290), channel_id=1, source_target_pairs={{0,16},{16,0},{1,17},{17,1},{2,18},{18,2},{3,19},{19,3},{4,20},{20... | collective-permute-start | bytes 7077896 | tf_op jit(solution)/shard_map/ppermute | solution.py:451
  341.8 31.8 %collective-permute-start.46 = (bf16[8,48,3072]{2,1,0:T(8,128)(2,1)}, bf16[8,48,3072]{2,1,0:T(8,128)(2,1)}, u32[]{:S(2)}, u32[]{:S(2)}) collective-permute-start(bf16[8,48,3072]{2,1,0:T(8,128)(2,1)} %get-tuple-element.283), channel_id=1, source_target_pairs={{0,16},{16,0},{1,17},{17,1},{2,18},{18,2},{3,19},{19,3},{4,20},{20... | collective-permute-start | bytes 7077896 | tf_op jit(solution)/shard_map/ppermute | solution.py:451
  352.9 24.5 %collective-permute-start.47 = (bf16[8,48,3072]{2,1,0:T(8,128)(2,1)}, bf16[8,48,3072]{2,1,0:T(8,128)(2,1)}, u32[]{:S(2)}, u32[]{:S(2)}) collective-permute-start(bf16[8,48,3072]{2,1,0:T(8,128)(2,1)} %get-tuple-element.286), channel_id=1, source_target_pairs={{0,16},{16,0},{1,17},{17,1},{2,18},{18,2},{3,19},{19,3},{4,20},{20... | collective-permute-start | bytes 7077896 | tf_op jit(solution)/shard_map/ppermute | solution.py:451
  357.9 23.4 %collective-permute-start.45 = (bf16[4,160,768]{2,1,0:T(8,128)(2,1)}, bf16[4,160,768]{2,1,0:T(8,128)(2,1)}, u32[]{:S(2)}, u32[]{:S(2)}) collective-permute-start(bf16[4,160,768]{2,1,0:T(8,128)(2,1)} %maximum_select_fusion.1), channel_id=1, source_target_pairs={{0,16},{16,8},{1,17},{17,9},{2,18},{18,10},{3,19},{19,11},{4,20},{... | collective-permute-start | bytes 2949128 | tf_op jit(solution)/shard_map/ppermute | solution.py:457
  361.0 27.2 %collective-permute-start.44 = (bf16[4,160,768]{2,1,0:T(8,128)(2,1)}, bf16[4,160,768]{2,1,0:T(8,128)(2,1)}, u32[]{:S(2)}, u32[]{:S(2)}) collective-permute-start(bf16[4,160,768]{2,1,0:T(8,128)(2,1)} %maximum_select_fusion), channel_id=1, source_target_pairs={{24,8},{8,16},{25,9},{9,17},{26,10},{10,18},{27,11},{11,19},{28,12... | collective-permute-start | bytes 2949128 | tf_op jit(solution)/shard_map/ppermute | solution.py:457
  388.1 29.8 %collective-permute-start.50 = (bf16[4,48,3072]{2,1,0:T(8,128)(2,1)}, bf16[4,48,3072]{2,1,0:T(8,128)(2,1)}, u32[]{:S(2)}, u32[]{:S(2)}) collective-permute-start(bf16[4,48,3072]{2,1,0:T(8,128)(2,1)} %get-tuple-element.300), channel_id=1, source_target_pairs={{0,1},{1,0},{2,3},{3,2},{4,5},{5,4},{6,7},{7,6},{8,9},{9,8},{10,11... | collective-permute-start | bytes 3538952 | tf_op jit(solution)/shard_map/ppermute | solution.py:447
  394.4 16.4 %collective-permute-start.49 = (bf16[8,96,128]{2,1,0:T(8,128)(2,1)S(1)}, bf16[8,96,128]{2,1,0:T(8,128)(2,1)S(1)}, u32[]{:S(2)}, u32[]{:S(2)}) collective-permute-start(bf16[8,96,128]{2,1,0:T(8,128)(2,1)S(1)} %bitcast.204), channel_id=1, source_target_pairs={{0,16},{16,0},{1,17},{17,1},{2,18},{18,2},{3,19},{19,3},{4,20},{20... | collective-permute-start | bytes 589832 | tf_op jit(solution)/shard_map/ppermute | solution.py:451
  394.4 27.3 %collective-permute-start.51 = (bf16[4,48,3072]{2,1,0:T(8,128)(2,1)}, bf16[4,48,3072]{2,1,0:T(8,128)(2,1)}, u32[]{:S(2)}, u32[]{:S(2)}) collective-permute-start(bf16[4,48,3072]{2,1,0:T(8,128)(2,1)} %get-tuple-element.301), channel_id=1, source_target_pairs={{0,2},{1,3},{2,0},{3,1},{4,6},{5,7},{6,4},{7,5},{8,10},{9,11},{10,... | collective-permute-start | bytes 3538952 | tf_op jit(solution)/shard_map/ppermute | solution.py:447
  409.8 26.9 %collective-permute-start.52 = (bf16[4,48,3072]{2,1,0:T(8,128)(2,1)}, bf16[4,48,3072]{2,1,0:T(8,128)(2,1)S(1)}, u32[]{:S(2)}, u32[]{:S(2)}) collective-permute-start(bf16[4,48,3072]{2,1,0:T(8,128)(2,1)} %get-tuple-element.302), channel_id=1, source_target_pairs={{0,4},{1,5},{2,6},{3,7},{4,0},{5,1},{6,2},{7,3},{8,12},{9,13},{10,... | collective-permute-start | bytes 3538952 | tf_op jit(solution)/shard_map/ppermute | solution.py:447
  409.9 27.3 %collective-permute-start.53 = (bf16[8,48,3072]{2,1,0:T(8,128)(2,1)}, bf16[8,48,3072]{2,1,0:T(8,128)(2,1)S(1)}, u32[]{:S(2)}, u32[]{:S(2)}) collective-permute-start(bf16[8,48,3072]{2,1,0:T(8,128)(2,1)} %get-tuple-element.304), channel_id=1, source_target_pairs={{0,16},{16,0},{1,17},{17,1},{2,18},{18,2},{3,19},{19,3},{4,20},{20... | collective-permute-start | bytes 7077896 | tf_op jit(solution)/shard_map/ppermute | solution.py:451
  438.1 12.9 %collective-permute-start.55 = (bf16[2,48,3072]{2,1,0:T(8,128)(2,1)S(1)}, bf16[2,48,3072]{2,1,0:T(8,128)(2,1)S(1)}, u32[]{:S(2)}, u32[]{:S(2)}) collective-permute-start(bf16[2,48,3072]{2,1,0:T(8,128)(2,1)S(1)} %get-tuple-element.306), channel_id=1, source_target_pairs={{0,2},{1,3},{2,0},{3,1},{4,6},{5,7},{6,4},{7,5},{8,10},{9,11},{10,... | collective-permute-start | bytes 1769480 | tf_op jit(solution)/shard_map/ppermute | solution.py:447
  438.1 12.9 %collective-permute-start.56 = (bf16[2,48,3072]{2,1,0:T(8,128)(2,1)S(1)}, bf16[2,48,3072]{2,1,0:T(8,128)(2,1)S(1)}, u32[]{:S(2)}, u32[]{:S(2)}) collective-permute-start(bf16[2,48,3072]{2,1,0:T(8,128)(2,1)S(1)} %get-tuple-element.307), channel_id=1, source_target_pairs={{0,4},{1,5},{2,6},{3,7},{4,0},{5,1},{6,2},{7,3},{8,12},{9,13},{10,... | collective-permute-start | bytes 1769480 | tf_op jit(solution)/shard_map/ppermute | solution.py:447
  438.4 14.4 %collective-permute-start.57 = (bf16[2,48,3072]{2,1,0:T(8,128)(2,1)S(1)}, bf16[2,48,3072]{2,1,0:T(8,128)(2,1)S(1)}, u32[]{:S(2)}, u32[]{:S(2)}) collective-permute-start(bf16[2,48,3072]{2,1,0:T(8,128)(2,1)S(1)} %get-tuple-element.308), channel_id=1, source_target_pairs={{0,1},{1,0},{2,3},{3,2},{4,5},{5,4},{6,7},{7,6},{8,9},{9,8},{10,11... | collective-permute-start | bytes 1769480 | tf_op jit(solution)/shard_map/ppermute | solution.py:447
  439.1 13.8 %collective-permute-start.58 = (bf16[8,48,3072]{2,1,0:T(8,128)(2,1)S(1)}, bf16[8,48,3072]{2,1,0:T(8,128)(2,1)S(1)}, u32[]{:S(2)}, u32[]{:S(2)}) collective-permute-start(bf16[8,48,3072]{2,1,0:T(8,128)(2,1)S(1)} %copy-done.62), channel_id=1, source_target_pairs={{0,16},{16,0},{1,17},{17,1},{2,18},{18,2},{3,19},{19,3},{4,20},{20... | collective-permute-start | bytes 7077896 | tf_op jit(solution)/shard_map/ppermute | solution.py:451
  464.9 35.5 %collective-permute-start.64 = (bf16[4,48,3072]{2,1,0:T(8,128)(2,1)S(1)}, bf16[4,48,3072]{2,1,0:T(8,128)(2,1)S(1)}, u32[]{:S(2)}, u32[]{:S(2)}) collective-permute-start(bf16[4,48,3072]{2,1,0:T(8,128)(2,1)S(1)} %get-tuple-element.317), channel_id=1, source_target_pairs={{0,4},{1,5},{2,6},{3,7},{4,0},{5,1},{6,2},{7,3},{8,12},{9,13},{10,... | collective-permute-start | bytes 3538952 | tf_op jit(solution)/shard_map/ppermute | solution.py:447
  465.3 35.1 %collective-permute-start.65 = (bf16[1,96,128]{2,1,0:T(8,128)(2,1)S(1)}, bf16[1,96,128]{2,1,0:T(8,128)(2,1)S(1)}, u32[]{:S(2)}, u32[]{:S(2)}) collective-permute-start(bf16[1,96,128]{2,1,0:T(8,128)(2,1)S(1)} %add_convert_fusion.43), channel_id=1, source_target_pairs={{0,4},{1,5},{2,6},{3,7},{4,0},{5,1},{6,2},{7,3},{8,12},{9,13},{10,... | collective-permute-start | bytes 73736 | tf_op jit(solution)/shard_map/ppermute | solution.py:447
  466.4 35.1 %collective-permute-start.68 = (bf16[48,9216]{1,0:T(8,128)(2,1)S(1)}, bf16[48,9216]{1,0:T(8,128)(2,1)S(1)}, u32[]{:S(2)}, u32[]{:S(2)}) collective-permute-start(bf16[48,9216]{1,0:T(8,128)(2,1)S(1)} %pad_maximum_fusion.9), channel_id=1, source_target_pairs={{0,8},{1,9},{2,10},{3,11},{4,12},{5,13},{6,14},{7,15},{24,16},{25,... | collective-permute-start | bytes 2654216 | tf_op jit(solution)/shard_map/ppermute | solution.py:457
  467.7 33.0 %collective-permute-start.66 = (bf16[4,48,3072]{2,1,0:T(8,128)(2,1)S(1)}, bf16[4,48,3072]{2,1,0:T(8,128)(2,1)S(1)}, u32[]{:S(2)}, u32[]{:S(2)}) collective-permute-start(bf16[4,48,3072]{2,1,0:T(8,128)(2,1)S(1)} %get-tuple-element.319), channel_id=1, source_target_pairs={{0,1},{1,0},{2,3},{3,2},{4,5},{5,4},{6,7},{7,6},{8,9},{9,8},{10,11... | collective-permute-start | bytes 3538952 | tf_op jit(solution)/shard_map/ppermute | solution.py:447
  468.4 32.8 %collective-permute-start.67 = (bf16[4,48,3072]{2,1,0:T(8,128)(2,1)S(1)}, bf16[4,48,3072]{2,1,0:T(8,128)(2,1)S(1)}, u32[]{:S(2)}, u32[]{:S(2)}) collective-permute-start(bf16[4,48,3072]{2,1,0:T(8,128)(2,1)S(1)} %get-tuple-element.320), channel_id=1, source_target_pairs={{0,2},{1,3},{2,0},{3,1},{4,6},{5,7},{6,4},{7,5},{8,10},{9,11},{10,... | collective-permute-start | bytes 3538952 | tf_op jit(solution)/shard_map/ppermute | solution.py:447
  502.3 18.5 %collective-permute-start.72 = (bf16[48,128]{1,0:T(8,128)(2,1)S(1)}, bf16[48,128]{1,0:T(8,128)(2,1)S(1)}, u32[]{:S(2)}, u32[]{:S(2)}) collective-permute-start(bf16[48,128]{1,0:T(8,128)(2,1)S(1)} %get-tuple-element.325), channel_id=1, source_target_pairs={{0,8},{1,9},{2,10},{3,11},{4,12},{5,13},{6,14},{7,15},{24,16},{25,... | collective-permute-start | bytes 36872 | tf_op jit(solution)/shard_map/ppermute | solution.py:457
  503.7 17.1 %collective-permute-start.71 = (bf16[2,48,3072]{2,1,0:T(8,128)(2,1)S(1)}, bf16[2,48,3072]{2,1,0:T(8,128)(2,1)S(1)}, u32[]{:S(2)}, u32[]{:S(2)}) collective-permute-start(bf16[2,48,3072]{2,1,0:T(8,128)(2,1)S(1)} %get-tuple-element.324), channel_id=1, source_target_pairs={{0,4},{1,5},{2,6},{3,7},{4,0},{5,1},{6,2},{7,3},{8,12},{9,13},{10,... | collective-permute-start | bytes 1769480 | tf_op jit(solution)/shard_map/ppermute | solution.py:447
  505.7 19.6 %collective-permute-start.73 = (bf16[48,6144]{1,0:T(8,128)(2,1)S(1)}, bf16[48,6144]{1,0:T(8,128)(2,1)}, u32[]{:S(2)}, u32[]{:S(2)}) collective-permute-start(bf16[48,6144]{1,0:T(8,128)(2,1)S(1)} %pad_maximum_fusion.16), channel_id=1, source_target_pairs={{8,16},{9,17},{10,18},{11,19},{12,20},{13,21},{14,22},{15,23},{16,... | collective-permute-start | bytes 1769480 | tf_op jit(solution)/shard_map/ppermute | solution.py:457
  (94 other events, 841.0 us)

commit v4 on v3

--- a/solution.py
+++ b/solution.py
@@ -90,17 +90,17 @@
     (chains_hbm,) = take(1)
     act_hbm, top_hbm = take(2) if has_high else (None, None)
     (grad_hbm,) = take(1) if back and has_low else (None,)
-    n_out = 10 if back else 2
-    n_scratch = 23 if back else 12
+    n_out = 8 if back else 1
+    n_scratch = 24 if back else 12
     take(len(refs) - n_out - n_scratch)
     outs = take(n_out)
     scr = take(n_scratch)
     win, wout, wfi, wfo, x_s, qkv, ctx, act, hl, y_s, acc, sems = scr[:12]
     if back:
-        (gx16_o, y_o, gx_o, sum_o, fsum_o, sx_o, sctx_o, shid_o, sdf_o, sr_o) = outs
-        gy_s, probs, slope, n1_s, n2_s, dr0, dpre, dfn, gx_s, sum_s, fsum_s = scr[12:]
+        (gx16_o, y_o, gx_o, sum_o, fsum_o, sl_o, sr_o, give_o) = outs
+        gy_s, probs, slope, n1_s, n2_s, dr0, dpre, dfn, gx_s, sum_s, fsum_s, low_s = scr[12:]
     else:
-        y1_o, y_o = outs
+        (y1_o,) = outs
     high = meta[0] == 1
     low = meta[0] == 0
     active = (high | low) if has_high and has_low else (high if has_high else low)
@@ -230,13 +230,13 @@
             copy.start()
             copies.append(copy)
 
-        put(y_s, y_o.at[index], sems.at[5, 0])
         if not back:
             put(y_s, y1_o.at[0], sems.at[5, 1])
         else:
-            put(x_s, sx_o.at[index], sems.at[5, 2])
-            put(ctx, sctx_o.at[index], sems.at[5, 3])
-            put(hl, shid_o.at[index], sems.at[5, 4])
+            put(y_s, y_o.at[index], sems.at[5, 0])
+            put(x_s, sl_o.at[2, index], sems.at[5, 2])
+            put(ctx, sl_o.at[3, index], sems.at[5, 3])
+            put(hl, sl_o.at[1, index], sems.at[5, 4])
             put(act, sr_o.at[2, index], sems.at[5, 5])
             pltpu.make_async_copy(gy_s, gy_s, sems.at[4, 1]).wait()
             alive = lax.broadcasted_iota(jnp.int32, (SEQ, D), 0) < jnp.where(high, length, SEQ)
@@ -246,7 +246,7 @@
             gr2 = norm_back(gy, n2, i2, small(5))
             dfn[...] = gr2.astype(BF16)
             sum_s[3:4, :] = col_sum(dfn[...])
-            put(dfn, sdf_o.at[index], sems.at[5, 6])
+            put(dfn, sl_o.at[0, index], sems.at[5, 6])
             n2_s[...] = gr2
 
             def ffn_back(n, carry):
@@ -298,12 +298,15 @@
             sum_s[1:2, :] = col_sum(dr0[:, 2 * D : 3 * D])
             grad_a = dot_nt(dr0[:, : 3 * D], win[...]) + acc[...]
             n1_s[...] = grad_a
-            hl_out = grad_a.astype(BF16)
-            gy_s[...] = hl_out
+            low_s[...] = grad_a.astype(BF16)
             put(sum_s, sum_o.at[index], sems.at[5, 11])
             put(fsum_s, fsum_o.at[index], sems.at[5, 12])
             put(n1_s, gx_o.at[index], sems.at[5, 9])
-            put(gy_s, gx16_o.at[0], sems.at[5, 10])
+            put(low_s, gx16_o.at[0], sems.at[5, 10])
+            section = meta[1 + 3 * count + 3 * BLOCKS]
+            for here, core, source in ((high, 1, x_s), (high, 0, y_s), (low, 0, gy_s), (low, 1, low_s)):
+                pl.when(here & (section == core))(functools.partial(fetch, source, give_o.at[index], sems.at[5, 13]))
+            pltpu.make_async_copy(low_s, low_s, sems.at[5, 13]).wait()
         for copy in copies:
             copy.wait()
 
@@ -325,7 +328,7 @@
 
     def put(side, total):
         for block in range(8):
-            place = meta[count + 3 + (unit * 2 + at) * 8 + block]
+            place = meta[count + 1 + (2 - unit) * 8 + block]
             outs[side][place] = total[block * ROWS : (block + 1) * ROWS]
 
     def with_first(first):
@@ -358,11 +361,9 @@
         shaped((count, SEQ, D), F32),
         shaped((count, 8, D), F32),
         shaped((count, 1, FF), F32),
+        shaped((4, count, SEQ, D), BF16),
+        shaped((3, count, SEQ, WIDE), BF16),
         narrow,
-        narrow,
-        narrow,
-        narrow,
-        shaped((3, count, SEQ, WIDE), BF16),
     ]
 
 
@@ -394,11 +395,12 @@
             pltpu.VMEM((SEQ, D), BF16),
             pltpu.VMEM((8, D), F32),
             pltpu.VMEM((1, FF), F32),
+            pltpu.VMEM((SEQ, D), BF16),
         ]
     operands = [meta, rows, fbias, *pieces, *sources]
     specs = [SMEM, VMEM, VMEM] + [ANY] * (len(pieces) + len(sources))
     first = [shaped((1, SEQ, D), BF16)]
-    kept = saved_shapes(count) if back else [shaped((count, SEQ, D), BF16)]
+    kept = saved_shapes(count) if back else []
     aliases = {}
     for at, array in enumerate(held):
         if array is not None:
@@ -420,26 +422,27 @@
 
 
 def grad_call(unit, at, meta, left, right):
-    count = left[0].shape[0]
-    right_spec = pl.BlockSpec((None, count, SEQ, CHUNK), lambda n, m: (unit, 0, 0, n))
-    out = shaped((8, ROWS, WIDE), BF16)
+    count = left.shape[1]
+    which = {2: [0], 1: [1], 0: [2, 3]}[unit]
+
+    def left_of(which):
+        return pl.BlockSpec((None, count, SEQ, D // 2), lambda n, m: (which, 0, 0, m[count + 1 + 24 + at]))
+
     return pl.pallas_call(
         functools.partial(grad_kernel, unit, at),
-        out_shape=[out] * 2,
+        out_shape=[shaped((8, ROWS, WIDE), BF16)] * 2,
         grid_spec=pltpu.PrefetchScalarGridSpec(
             num_scalar_prefetch=1,
             grid=(WIDE // CHUNK,),
-            in_specs=[pl.BlockSpec((count, SEQ, D // 2), lambda n, m: (0, 0, m[count + 1 + at]))] * len(left)
-            + [right_spec],
+            in_specs=[left_of(i) for i in which]
+            + [pl.BlockSpec((None, count, SEQ, CHUNK), lambda n, m: (unit, 0, 0, n))],
             out_specs=[pl.BlockSpec((8, ROWS, CHUNK), lambda n, m: (0, 0, n))] * 2,
-            scratch_shapes=[
-                pltpu.VMEM((len(left), 2, D // 2, count * SEQ), BF16),
-            ],
+            scratch_shapes=[pltpu.VMEM((len(which), 2, D // 2, count * SEQ), BF16)],
         ),
         compiler_params=pltpu.CompilerParams(vmem_limit_bytes=50 * 1024 * 1024),
         cost_estimate=pl.CostEstimate(flops=1, bytes_accessed=1, transcendentals=0),
         name="layer_grad",
-    )(meta, *left, right)
+    )(meta, *[left] * len(which), right)
 
 
 def swap_bit(array, bit):
@@ -642,7 +645,8 @@
     chains = jnp.where(at_home, inputs, moved)
     top_grad = jnp.where(at_home, cotangent, moved)
     sides = numbers[:count] ^ first_side
-    meta = jnp.concatenate([half[None].astype(jnp.int32), numbers, sides.astype(jnp.int32)] + tables)
+    meta = [half[None].astype(jnp.int32), numbers, sides.astype(jnp.int32)] + tables
+    meta = jnp.concatenate(meta + [section[None].astype(jnp.int32)])
     later = jnp.arange(count)[:, None] < jnp.arange(count)[None, :]
     rank = jnp.sum((sides[:, None] > sides[None, :]) | ((sides[:, None] == sides[None, :]) & later.T), axis=1)
     sorted_chains = jnp.sum(
@@ -650,18 +654,18 @@
     )
     grad_meta = jnp.concatenate(
         [sorted_chains.astype(jnp.int32), jnp.sum(1 - sides)[None].astype(jnp.int32)]
+        + [places[unit] for unit in (2, 1, 0)]
         + [value[None].astype(jnp.int32) for value in row_halves]
-        + [place for unit in range(3) for place in (places[unit], places[unit])]
     )
 
     lead = 2
     call = functools.partial(layer_call, lead=lead, count=count, rows=rows_all, fbias=fbias_all, pieces=pieces)
-    acts, grads, act_low, held = [None] * count, [None] * count, [None], [None] * 9
+    acts, grads, held = [None] * count, [None] * count, [None] * 7
     token = None
 
     def forward(c):
-        nonlocal token, act_low
-        out, act_low = call(False, c, meta=after(meta, token), sources=[chains], held=act_low)
+        nonlocal token
+        out, _ = call(False, c, meta=after(meta, token), sources=[chains], held=[])
         acts[c], token = along(out, routes.up), out
 
     for c in range(count):
@@ -676,22 +680,15 @@
         token = out
         if slot < count:
             grads[slot] = along(out, routes.down)
-    act_high, grad_all, sums, fsums, s_x, s_ctx, s_hid, s_dffn, s_right = held
-    act_all = jnp.where(half == 0, act_low[0], act_high)
-
-    lefts = {2: [s_dffn], 1: [s_hid], 0: [s_x, s_ctx]}
+    act_all, grad_all, sums, fsums, s_left, s_right, give = held
+
 
     def gradient(unit, at, *others):
-        return grad_call(unit, at, after(grad_meta, *others), lefts[unit], s_right)
-
-    act_move = (
-        jnp.where(section == 1, jnp.concatenate(acts, 0), act_all),
-        by([pair for j in range(near) for pair in (((1, near + j), (0, near + j)), ((0, near + j), (1, j)))]),
-    )
-    grad_move = (
-        jnp.where(section == 0, jnp.concatenate(grads, 0), grad_all.astype(BF16)),
-        by([pair for j in range(near) for pair in (((0, j), (1, j)), ((1, j), (0, near + j)))]),
-    )
+        return grad_call(unit, at, after(grad_meta, *others), s_left, s_right)
+
+    act_move = by([pair for j in range(near) for pair in (((1, near + j), (0, near + j)), ((0, near + j), (1, j)))])
+    grad_move = by([pair for j in range(near) for pair in (((0, j), (1, j)), ((1, j), (0, near + j)))])
+    act_other, grad_other = act_move(give), grad_move(give)
 
     chosen = (sides[None, :] == jnp.arange(2, dtype=jnp.int32)[:, None]).astype(F32)
     row_sums = jnp.sum(chosen[:, :, None, None] * sums[None], axis=1)
@@ -716,31 +713,34 @@
             return [(send[i], by_bit(ROTATIONS[i % 3][step])) for i in range(len(send))]
 
         units = (2, 1, 0)
-        totals = {(unit, 1): gradient(unit, 1) for unit in units}
-        keep = [totals[unit, 1][0] for unit in units]
-        got = [swap_section(totals[unit, 1][1]) for unit in units]
-        act_other, grad_other = act_move[1](act_move[0]), grad_move[1](grad_move[0])
+        terms = [gradient(unit, 1) for unit in units]
+        keep = [own for own, _ in terms]
+        got = [swap_section(other) for _, other in terms]
         wave.before = (act_other, grad_other)
-        near_got = []
-        small_keep, small_extra = [laid[0]], (laid[1], swap_section)
-        for step in range(3):
-            if step == 0:
-                totals[2, 0] = gradient(2, 0, totals[0, 1][0])
+        near_terms = [gradient(2, 0, keep[2])]
+        send = [both(a[4:], b[4:]) for a, b in zip(keep, got)]
+        near_terms += [gradient(1, 0, *send)]
+        near_terms += [gradient(0, 0, near_terms[1][0])]
+        near_keep = [own for own, _ in near_terms]
+        small_got, *far_got, other = wave((laid[1], swap_section), *bits_out(send, 0), (near_terms[0][1], swap_section))
+        near_got = [other]
+        keep = [both(after(a, *send)[:4], b[:4]) for a, b in zip(keep, got)]
+        got = far_got
+        small_keep = [laid[0]]
+        for step in (1, 2):
+            small_keep, small_send = reduce_step(small_keep, [small_got], step - 1)
             keep, send = reduce_step(keep, got, step)
-            if step == 0:
-                totals[1, 0] = gradient(1, 0, *send)
-                totals[0, 0] = gradient(0, 0, totals[1, 0][0])
             small_got, *got, other = wave(
-                small_extra, *bits_out(send, step), (totals[units[step], 0][1], swap_section)
+                one_bit(small_send[0], step - 1), *bits_out(send, step), (near_terms[step][1], swap_section)
             )
             near_got.append(other)
-            small_keep, (small_send,) = reduce_step(small_keep, [small_got], step)
-            small_extra = (small_send, by_bit(ROTATIONS[0][step]))
         far_sum = jnp.concatenate([(a[0].astype(F32) + b[0].astype(F32)).astype(BF16) for a, b in zip(keep, got)], -1)
 
-        keep = [totals[unit, 0][0] for unit in units]
-        keep, send = reduce_step(keep, near_got, 0)
-        small_got, *got, straight = wave(small_extra, *bits_out(send, 0), (far_sum, by(routes.straight_back)))
+        keep, send = reduce_step(near_keep, near_got, 0)
+        small_keep, small_send = reduce_step(small_keep, [small_got], 2)
+        small_got, *got, straight = wave(
+            one_bit(small_send[0], 2), *bits_out(send, 0), (far_sum, by(routes.straight_back))
+        )
         small_end = (small_keep[0][0].astype(F32) + small_got[0].astype(F32)).astype(BF16)
         keep, send = reduce_step(keep, got, 1)
         small_straight, *got, cross_a = wave(
@@ -777,14 +777,11 @@
             return jnp.swapaxes(out[0], 0, 1)
 
         unit_out = []
-        totals = {(unit, at): gradient(unit, at) for unit in range(3) for at in range(2)}
         for unit in range(3):
-            group = [
-                jnp.concatenate([totals[unit, 0][side], totals[unit, 1][side]], 0).reshape(D, WIDE) for side in range(2)
-            ]
+            terms = [gradient(unit, at) for at in range(2)]
+            group = [jnp.concatenate([part[side] for part in terms], 0).reshape(D, WIDE) for side in range(2)]
             unit_out.append(summed(jnp.stack(group).astype(F32)))
         small_out = summed(small_grads)
-        act_other, grad_other = act_move[1](act_move[0]), grad_move[1](grad_move[0])
 
     act_out = jnp.where(at_home, act_all, act_other)
     grad_out = jnp.where(at_home, grad_all, grad_other.astype(F32))

time: 569 us -> 539 us (0.947)
  waiting for transfers between devices: 194 us -> 148 us
  starting transfers between devices: 114 us -> 123 us
  local copies, waits for them, and re-layouts: 17.5 us -> 24.6 us
    ppermute x42, waiting for transfers between devices: 141 us -> 118 us  [swap_bit(): return lax.ppermute(array, 'dp', [(i, i ^ 1 << bit) for i in range(count)])]
    ppermute x23, waiting for transfers between devices: 47 us -> 28.4 us  [along(): return lax.ppermute(array, ('section', 'dp'), flat)]
    ppermute x42, starting transfers between devices: 52.1 us -> 58.2 us  [swap_bit(): return lax.ppermute(array, 'dp', [(i, i ^ 1 << bit) for i in range(count)])]
    ppermute x14, waiting for transfers between devices: 6.97 us -> 1.26 us  [swap_section(): return lax.ppermute(array, 'section', [(0, 1), (1, 0)])]
    unnamed x132 -> x112, local copies, waits for them, and re-layouts: 10.7 us -> 12.5 us
    convert_element_type x21 -> x24, other arithmetic: 20.2 us -> 21.6 us  [both(): return (first.astype(F32) + second.astype(F32)).astype(BF16)]
  transfers between devices with their start and end apart: 79 -> 79, of which waited for: 33 -> 26; matrix products, arithmetic and copies ran while one was open for 9% -> 12% of each run, Pallas kernels for 24% -> 25%
where the time goes in v4:
time: 539 us; the launch traced here: 528 us
  Pallas kernels  169 us (31%)
  waiting for transfers between devices  148 us (27%)
  starting transfers between devices  123 us (23%)
  other arithmetic  60.4 us (11%)
  local copies, waits for them, and re-layouts  24.6 us (5%)
    pallas_call x10, Pallas kernels, layer_call(): pl.pallas_call(functools.partial(layer_kernel, back, slot, lead, count),...  128 us
    ppermute x42, waiting for transfers between devices, swap_bit(): return lax.ppermute(array, 'dp', [(i, i ^ 1 << bit) for i in range(count)])  118 us
    ppermute x42, starting transfers between devices, swap_bit(): return lax.ppermute(array, 'dp', [(i, i ^ 1 << bit) for i in range(count)])  58.2 us
    ppermute x23, starting transfers between devices, along(): return lax.ppermute(array, ('section', 'dp'), flat)  49.6 us
    pallas_call x6, Pallas kernels, grad_call(): pl.pallas_call(functools.partial(grad_kernel, unit, at), out_shape=[shape...  41.1 us
    ppermute x23, waiting for transfers between devices, along(): return lax.ppermute(array, ('section', 'dp'), flat)  28.4 us
    convert_element_type x24, other arithmetic, both(): return (first.astype(F32) + second.astype(F32)).astype(BF16)  21.6 us
    ppermute x14, starting transfers between devices, swap_section(): return lax.ppermute(array, 'section', [(0, 1), (1, 0)])  15 us
  transfers between devices with their start and end apart: 79, of which 26 were waited for; matrix products, arithmetic and copies ran while one was open for 12% of the time, Pallas kernels for 25%

profile of v4, /device:TPU:1, one launch (start us, length us, event | category | flops | bytes accessed | tf_op | source)
XLA Modules:
  0.0 528.4 jit_solution(5087874650686028566)
XLA Ops:
  12.6 4.5 collective-permute-start.5
  19.7 2.8 collective-permute-start.6
  22.5 2.5 collective-permute-done.3
  25.2 6.5 %collective-permute-done.6 = bf16[48,3072]{1,0:T(8,128)(2,1)S(1)} collective-permute-done((bf16[48,3072]{1,0:T(8,128)(2,1)S(1)}, bf16[48,3072]{1,0:T(8,128)(2,1)S(1)}, u32[]{:S(2)}, u32[]{:S(2)}) %collective-permute-start.6) | collective-permute-done | bytes 294944 | tf_op jit(solution)/shard_map/ppermute | solution.py:460
  35.5 3.5 collective-permute-start.11
  40.6 13.2 %collective-permute-done.9 = bf16[2,48,3072]{2,1,0:T(8,128)(2,1)S(1)} collective-permute-done((bf16[2,48,3072]{2,1,0:T(8,128)(2,1)S(1)}, bf16[2,48,3072]{2,1,0:T(8,128)(2,1)S(1)}, u32[]{:S(2)}, u32[]{:S(2)}) %collective-permute-start.9) | collective-permute-done | bytes 589856 | tf_op jit(solution)/shard_map/ppermute | solution.py:450
  57.2 9.3 %collective-permute-start.14 = (bf16[4,48,3072]{2,1,0:T(8,128)(2,1)S(1)}, bf16[4,48,3072]{2,1,0:T(8,128)(2,1)S(1)}, u32[]{:S(2)}, u32[]{:S(2)}) collective-permute-start(bf16[4,48,3072]{2,1,0:T(8,128)(2,1)S(1)} %pad_maximum_fusion.2.refs_3_), channel_id=1, source_target_pairs={{0,4},{1,5},{2,6},{3,7},{4,0},{5,1},{6,2},{7,3},{8,12},{9,13},{10,... | collective-permute-start | bytes 3538952 | tf_op jit(solution)/shard_map/ppermute | solution.py:450
  66.5 2.4 collective-permute-start.16
  71.1 14.3 %collective-permute-done.14.refs_4_ = bf16[4,48,3072]{2,1,0:T(8,128)(2,1)S(1)} collective-permute-done((bf16[4,48,3072]{2,1,0:T(8,128)(2,1)S(1)}, bf16[4,48,3072]{2,1,0:T(8,128)(2,1)S(1)}, u32[]{:S(2)}, u32[]{:S(2)}) %collective-permute-start.14) | collective-permute-done | bytes 1179680 | tf_op jit(solution)/shard_map/ppermute | solution.py:450
  91.3 5.0 collective-permute-done.20
  101.6 2.3 broadcast_select_fusion
  106.7 9.5 %collective-permute-done.25 = bf16[2,48,3072]{2,1,0:T(8,128)(2,1)} collective-permute-done((bf16[2,48,3072]{2,1,0:T(8,128)(2,1)}, bf16[2,48,3072]{2,1,0:T(8,128)(2,1)}, u32[]{:S(2)}, u32[]{:S(2)}) %collective-permute-start.25) | collective-permute-done | bytes 589856 | tf_op jit(solution)/shard_map/ppermute | solution.py:450
  119.6 3.3 maximum_maximum_fusion.1
  136.8 13.4 %collective-permute-done.30 = bf16[4,160,768]{2,1,0:T(8,128)(2,1)S(1)} collective-permute-done((bf16[4,160,768]{2,1,0:T(8,128)(2,1)}, bf16[4,160,768]{2,1,0:T(8,128)(2,1)S(1)}, u32[]{:S(2)}, u32[]{:S(2)}) %collective-permute-start.30) | collective-permute-done | bytes 983072 | tf_op jit(solution)/shard_map/ppermute | solution.py:460
  150.3 16.1 %collective-permute-done.27.refs_6_ = bf16[4,48,3072]{2,1,0:T(8,128)(2,1)} collective-permute-done((bf16[4,48,3072]{2,1,0:T(8,128)(2,1)}, bf16[4,48,3072]{2,1,0:T(8,128)(2,1)}, u32[]{:S(2)}, u32[]{:S(2)}) %collective-permute-start.27) | collective-permute-done | bytes 1179680 | tf_op jit(solution)/shard_map/ppermute | solution.py:450
  167.8 2.3 broadcast_select_fusion.1
  174.6 9.9 %layer_fwd.4 = bf16[1,160,768]{2,1,0:T(8,128)(2,1)S(1)} custom-call(s32[62]{0:T(128)S(1)} %concatenate.123.refs_0_, f32[2,8,768]{2,1,0:T(8,128)S(1)} %constant_dynamic-update-slice_fusion.refs_1_, f32[2,1,3072]{2,1,0:T(1,128)S(1)} %constant_dynamic-update-slice_fusion.2.refs_2_, bf16[4,48,3072]{2,1,0:T(8,128)(2,1)S(1)} %pad_maximum_fusion.2.refs_3_, ...), custom_call_target="tpu_custom_call" | custom-call | flops 1 | bytes 1 | tf_op jit(solution)/shard_map/layer_fwd/pallas_call | solution.py:410
  186.2 10.1 %layer_fwd.5 = bf16[1,160,768]{2,1,0:T(8,128)(2,1)S(1)} custom-call(s32[62]{0:T(128)S(1)} %concatenate.123.refs_0_, f32[2,8,768]{2,1,0:T(8,128)S(1)} %constant_dynamic-update-slice_fusion.refs_1_, f32[2,1,3072]{2,1,0:T(1,128)S(1)} %constant_dynamic-update-slice_fusion.2.refs_2_, bf16[4,48,3072]{2,1,0:T(8,128)(2,1)S(1)} %pad_maximum_fusion.2.refs_3_, ...), custom_call_target="tpu_custom_call" | custom-call | flops 1 | bytes 1 | tf_op jit(solution)/shard_map/layer_fwd/pallas_call | solution.py:410
  197.7 10.1 %layer_fwd.6 = bf16[1,160,768]{2,1,0:T(8,128)(2,1)S(1)} custom-call(s32[62]{0:T(128)S(1)} %concatenate.123.refs_0_, f32[2,8,768]{2,1,0:T(8,128)S(1)} %constant_dynamic-update-slice_fusion.refs_1_, f32[2,1,3072]{2,1,0:T(1,128)S(1)} %constant_dynamic-update-slice_fusion.2.refs_2_, bf16[4,48,3072]{2,1,0:T(8,128)(2,1)S(1)} %pad_maximum_fusion.2.refs_3_, ...), custom_call_target="tpu_custom_call" | custom-call | flops 1 | bytes 1 | tf_op jit(solution)/shard_map/layer_fwd/pallas_call | solution.py:410
  209.1 10.3 %layer_fwd.7 = bf16[1,160,768]{2,1,0:T(8,128)(2,1)S(1)} custom-call(s32[62]{0:T(128)S(1)} %concatenate.123.refs_0_, f32[2,8,768]{2,1,0:T(8,128)S(1)} %constant_dynamic-update-slice_fusion.refs_1_, f32[2,1,3072]{2,1,0:T(1,128)S(1)} %constant_dynamic-update-slice_fusion.2.refs_2_, bf16[4,48,3072]{2,1,0:T(8,128)(2,1)S(1)} %pad_maximum_fusion.2.refs_3_, ...), custom_call_target="tpu_custom_call" | custom-call | flops 1 | bytes 1 | tf_op jit(solution)/shard_map/layer_fwd/pallas_call | solution.py:410
  222.2 4.9 collective-permute-start.40
  227.1 9.8 %layer_back.7 = (bf16[1,160,768]{2,1,0:T(8,128)(2,1)S(1)}, bf16[4,160,768]{2,1,0:T(8,128)(2,1)S(1)}, f32[4,160,768]{2,1,0:T(8,128)}, f32[4,8,768]{2,1,0:T(8,128)...) custom-call(s32[62]{0:T(128)S(1)} %concatenate.123.refs_0_, ...), custom_call_target="tpu_custom_call", output_to_operand_aliasing={{1}: (24, {}), {2}: (25, {}), {3}: (26, {}), {4}: (27, {}),... | custom-call | flops 1 | bytes 1 | tf_op jit(solution)/shard_map/layer_back/pallas_call | solution.py:410
  238.3 19.1 %layer_back.8 = (bf16[1,160,768]{2,1,0:T(8,128)(2,1)}, bf16[4,160,768]{2,1,0:T(8,128)(2,1)S(1)}, f32[4,160,768]{2,1,0:T(8,128)}, f32[4,8,768]{2,1,0:T(8,128)S(1)...) custom-call(s32[62]{0:T(128)S(1)} %concatenate.123.refs_0_, ...), custom_call_target="tpu_custom_call", output_to_operand_aliasing={{1}: (25, {}), {2}: (26, {}), {3}: (27, {}), {4}: (28, {}),... | custom-call | flops 1 | bytes 1 | tf_op jit(solution)/shard_map/layer_back/pallas_call | solution.py:410
  258.7 19.3 %layer_back.9 = (bf16[1,160,768]{2,1,0:T(8,128)(2,1)}, bf16[4,160,768]{2,1,0:T(8,128)(2,1)S(1)}, f32[4,160,768]{2,1,0:T(8,128)}, f32[4,8,768]{2,1,0:T(8,128)S(1)...) custom-call(s32[62]{0:T(128)S(1)} %concatenate.123.refs_0_, ...), custom_call_target="tpu_custom_call", output_to_operand_aliasing={{1}: (25, {}), {2}: (26, {}), {3}: (27, {}), {4}: (28, {}),... | custom-call | flops 1 | bytes 1 | tf_op jit(solution)/shard_map/layer_back/pallas_call | solution.py:410
  280.3 18.8 %layer_back.10 = (bf16[1,160,768]{2,1,0:T(8,128)(2,1)}, bf16[4,160,768]{2,1,0:T(8,128)(2,1)S(1)}, f32[4,160,768]{2,1,0:T(8,128)}, f32[4,8,768]{2,1,0:T(8,128)S(1...) custom-call(s32[62]{0:T(128)S(1)} %concatenate.123.refs_0_, ...), custom_call_target="tpu_custom_call", output_to_operand_aliasing={{1}: (23, {}), {2}: (24, {}), {3}: (25, {}), {4}: (26, {}),... | custom-call | flops 1 | bytes 1 | tf_op jit(solution)/shard_map/layer_back/pallas_call | solution.py:410
  299.1 19.2 %layer_back.11 = (bf16[1,160,768]{2,1,0:T(8,128)(2,1)}, bf16[4,160,768]{2,1,0:T(8,128)(2,1)S(1)}, f32[4,160,768]{2,1,0:T(8,128)}, f32[4,8,768]{2,1,0:T(8,128)S(1...) custom-call(s32[62]{0:T(128)S(1)} %concatenate.123.refs_0_, ...), custom_call_target="tpu_custom_call", output_to_operand_aliasing={{1}: (23, {}), {2}: (24, {}), {3}: (25, {}), {4}: (26, {}),... | custom-call | flops 1 | bytes 1 | tf_op jit(solution)/shard_map/layer_back/pallas_call | solution.py:410
  318.4 7.1 %layer_grad.8 = (bf16[8,48,3072]{2,1,0:T(8,128)(2,1)S(1)}, bf16[8,48,3072]{2,1,0:T(8,128)(2,1)}) custom-call(s32[31]{0:T(128)S(1)} %concatenate.140.meta, bf16[4,4,160,768]{3,2,1,0:T(8,128)(2,1)} %get-tuple-element.246.refs_0_.refs_1_, bf16[4,4,160,768]{3,2,1,0:T(8,128)(2,1)} %get-tuple-element.246.refs_0_.refs_1_, ...), custom_call_target="tpu_custom_call" | custom-call | flops 1 | bytes 1 | tf_op jit(solution)/shard_map/layer_grad/pallas_call | solution.py:431
  328.2 6.7 %layer_grad.7 = (bf16[8,48,3072]{2,1,0:T(8,128)(2,1)S(1)}, bf16[8,48,3072]{2,1,0:T(8,128)(2,1)}) custom-call(s32[31]{0:T(128)S(1)} %concatenate.140.meta, bf16[4,4,160,768]{3,2,1,0:T(8,128)(2,1)} %get-tuple-element.246.refs_0_.refs_1_, bf16[3,4,160,3072]{3,2,1,0:T(8,128)(2,1)} %get-tuple-element.247.refs_1_.refs_2_), custom_call_target="tpu_custom_call" | custom-call | flops 1 | bytes 1 | tf_op jit(solution)/shard_map/layer_grad/pallas_call | solution.py:431
  339.9 6.7 %layer_grad.6 = (bf16[8,48,3072]{2,1,0:T(8,128)(2,1)S(1)}, bf16[8,48,3072]{2,1,0:T(8,128)(2,1)}) custom-call(s32[31]{0:T(128)S(1)} %concatenate.140.meta, bf16[4,4,160,768]{3,2,1,0:T(8,128)(2,1)} %get-tuple-element.246.refs_0_.refs_1_, bf16[3,4,160,3072]{3,2,1,0:T(8,128)(2,1)} %get-tuple-element.247.refs_1_.refs_2_), custom_call_target="tpu_custom_call" | custom-call | flops 1 | bytes 1 | tf_op jit(solution)/shard_map/layer_grad/pallas_call | solution.py:431
  348.0 6.7 %layer_grad.11 = (bf16[8,48,3072]{2,1,0:T(8,128)(2,1)S(1)}, bf16[8,48,3072]{2,1,0:T(8,128)(2,1)}) custom-call(s32[31]{0:T(128)S(1)} %concatenate.140.meta, bf16[4,4,160,768]{3,2,1,0:T(8,128)(2,1)} %get-tuple-element.246.refs_0_.refs_1_, bf16[3,4,160,3072]{3,2,1,0:T(8,128)(2,1)} %get-tuple-element.247.refs_1_.refs_2_), custom_call_target="tpu_custom_call" | custom-call | flops 1 | bytes 1 | tf_op jit(solution)/shard_map/layer_grad/pallas_call | solution.py:431
  364.8 2.7 add_convert_fusion.11
  369.9 4.7 collective-permute-start.52
  380.9 6.9 %layer_grad.9 = (bf16[8,48,3072]{2,1,0:T(8,128)(2,1)S(1)}, bf16[8,48,3072]{2,1,0:T(8,128)(2,1)}) custom-call(s32[31]{0:T(128)S(1)} %concatenate.140.meta, bf16[4,4,160,768]{3,2,1,0:T(8,128)(2,1)} %get-tuple-element.246.refs_0_.refs_1_, bf16[3,4,160,3072]{3,2,1,0:T(8,128)(2,1)} %get-tuple-element.247.refs_1_.refs_2_), custom_call_target="tpu_custom_call" | custom-call | flops 1 | bytes 1 | tf_op jit(solution)/shard_map/layer_grad/pallas_call | solution.py:431
  387.8 7.1 %layer_grad.10 = (bf16[8,48,3072]{2,1,0:T(8,128)(2,1)S(1)}, bf16[8,48,3072]{2,1,0:T(8,128)(2,1)}) custom-call(s32[31]{0:T(128)S(1)} %concatenate.140.meta, bf16[4,4,160,768]{3,2,1,0:T(8,128)(2,1)} %get-tuple-element.246.refs_0_.refs_1_, bf16[4,4,160,768]{3,2,1,0:T(8,128)(2,1)} %get-tuple-element.246.refs_0_.refs_1_, ...), custom_call_target="tpu_custom_call" | custom-call | flops 1 | bytes 1 | tf_op jit(solution)/shard_map/layer_grad/pallas_call | solution.py:431
  402.9 4.4 collective-permute-start.56
  408.4 2.4 collective-permute-start.58
  411.7 4.4 collective-permute-done.55
  416.1 3.0 collective-permute-done.56
  423.7 3.2 collective-permute-start.59
  437.2 30.1 %collective-permute-done.65 = bf16[1,96,128]{2,1,0:T(8,128)(2,1)S(1)} collective-permute-done((bf16[1,96,128]{2,1,0:T(8,128)(2,1)S(1)}, bf16[1,96,128]{2,1,0:T(8,128)(2,1)S(1)}, u32[]{:S(2)}, u32[]{:S(2)}) %collective-permute-start.65) | collective-permute-done | bytes 24608 | tf_op jit(solution)/shard_map/ppermute | solution.py:450
  472.4 2.4 collective-permute-start.71
  474.7 4.6 collective-permute-start.73
  482.1 9.2 %collective-permute-done.71 = bf16[2,48,3072]{2,1,0:T(8,128)(2,1)S(1)} collective-permute-done((bf16[2,48,3072]{2,1,0:T(8,128)(2,1)S(1)}, bf16[2,48,3072]{2,1,0:T(8,128)(2,1)S(1)}, u32[]{:S(2)}, u32[]{:S(2)}) %collective-permute-start.71) | collective-permute-done | bytes 589856 | tf_op jit(solution)/shard_map/ppermute | solution.py:450
  491.3 3.0 collective-permute-done.73
  495.0 3.3 collective-permute-start.75
  498.5 5.1 collective-permute-start.77
  503.8 4.1 collective-permute-done.75
  515.1 2.7 select_bitcast_fusion
  (376 shorter events, 152.8 us)
Async XLA Ops:
  33.9 20.0 %collective-permute-start.8 = (bf16[2,48,3072]{2,1,0:T(8,128)(2,1)S(1)}, bf16[2,48,3072]{2,1,0:T(8,128)(2,1)S(1)}, u32[]{:S(2)}, u32[]{:S(2)}) collective-permute-start(bf16[2,48,3072]{2,1,0:T(8,128)(2,1)S(1)} %pad_maximum_fusion.10), channel_id=1, source_target_pairs={{0,2},{1,3},{2,0},{3,1},{4,6},{5,7},{6,4},{7,5},{8,10},{9,11},{10,... | collective-permute-start | bytes 1769480 | tf_op jit(solution)/shard_map/ppermute | solution.py:450
  34.2 19.6 %collective-permute-start.9 = (bf16[2,48,3072]{2,1,0:T(8,128)(2,1)S(1)}, bf16[2,48,3072]{2,1,0:T(8,128)(2,1)S(1)}, u32[]{:S(2)}, u32[]{:S(2)}) collective-permute-start(bf16[2,48,3072]{2,1,0:T(8,128)(2,1)S(1)} %pad_maximum_fusion.11), channel_id=1, source_target_pairs={{0,4},{1,5},{2,6},{3,7},{4,0},{5,1},{6,2},{7,3},{8,12},{9,13},{10,... | collective-permute-start | bytes 1769480 | tf_op jit(solution)/shard_map/ppermute | solution.py:450
  35.5 19.3 %collective-permute-start.11 = (bf16[48,6144]{1,0:T(8,128)(2,1)S(1)}, bf16[48,6144]{1,0:T(8,128)(2,1)S(1)}, u32[]{:S(2)}, u32[]{:S(2)}) collective-permute-start(bf16[48,6144]{1,0:T(8,128)(2,1)S(1)} %slice.553), channel_id=1, source_target_pairs={{8,16},{9,17},{10,18},{11,19},{12,20},{13,21},{14,22},{15,23},{16,... | collective-permute-start | bytes 1769480 | tf_op jit(solution)/shard_map/ppermute | solution.py:460
  54.8 14.4 %collective-permute-start.12 = (bf16[1,2,16,128]{3,2,1,0:T(8,128)(2,1)S(1)}, bf16[1,2,16,128]{3,2,1,0:T(8,128)(2,1)S(1)}, u32[]{:S(2)}, u32[]{:S(2)}) collective-permute-start(bf16[1,2,16,128]{3,2,1,0:T(8,128)(2,1)S(1)} %maximum_bitcast_fusion.3), channel_id=1, source_target_pairs={{0,1},{1,0},{2,3},{3,2},{4,5},{5,4},{6,7},{7,6},{8,9},{9,8},{10,11... | collective-permute-start | bytes 24584 | tf_op jit(solution)/shard_map/ppermute | solution.py:450
  55.8 15.0 %collective-permute-start.13 = (bf16[48,9216]{1,0:T(8,128)(2,1)S(1)}, bf16[48,9216]{1,0:T(8,128)(2,1)S(1)}, u32[]{:S(2)}, u32[]{:S(2)}) collective-permute-start(bf16[48,9216]{1,0:T(8,128)(2,1)S(1)} %get-tuple-element.173), channel_id=1, source_target_pairs={{8,0},{9,1},{10,2},{11,3},{12,4},{13,5},{14,6},{15,7},{16,24},{17,... | collective-permute-start | bytes 2654216 | tf_op jit(solution)/shard_map/ppermute | solution.py:460
  57.2 28.2 %collective-permute-start.14 = (bf16[4,48,3072]{2,1,0:T(8,128)(2,1)S(1)}, bf16[4,48,3072]{2,1,0:T(8,128)(2,1)S(1)}, u32[]{:S(2)}, u32[]{:S(2)}) collective-permute-start(bf16[4,48,3072]{2,1,0:T(8,128)(2,1)S(1)} %pad_maximum_fusion.2.refs_3_), channel_id=1, source_target_pairs={{0,4},{1,5},{2,6},{3,7},{4,0},{5,1},{6,2},{7,3},{8,12},{9,13},{10,... | collective-permute-start | bytes 3538952 | tf_op jit(solution)/shard_map/ppermute | solution.py:450
  66.5 18.9 %collective-permute-start.15 = (bf16[4,48,3072]{2,1,0:T(8,128)(2,1)S(1)}, bf16[4,48,3072]{2,1,0:T(8,128)(2,1)S(1)}, u32[]{:S(2)}, u32[]{:S(2)}) collective-permute-start(bf16[4,48,3072]{2,1,0:T(8,128)(2,1)S(1)} %pad_maximum_fusion.3.refs_7_), channel_id=1, source_target_pairs={{0,1},{1,0},{2,3},{3,2},{4,5},{5,4},{6,7},{7,6},{8,9},{9,8},{10,11... | collective-permute-start | bytes 3538952 | tf_op jit(solution)/shard_map/ppermute | solution.py:450
  66.5 18.9 %collective-permute-start.16 = (bf16[4,48,3072]{2,1,0:T(8,128)(2,1)S(1)}, bf16[4,48,3072]{2,1,0:T(8,128)(2,1)S(1)}, u32[]{:S(2)}, u32[]{:S(2)}) collective-permute-start(bf16[4,48,3072]{2,1,0:T(8,128)(2,1)S(1)} %pad_maximum_fusion.4.refs_11_), channel_id=1, source_target_pairs={{0,2},{1,3},{2,0},{3,1},{4,6},{5,7},{6,4},{7,5},{8,10},{9,11},{10,... | collective-permute-start | bytes 3538952 | tf_op jit(solution)/shard_map/ppermute | solution.py:450
  85.4 13.7 %collective-permute-start.21 = (bf16[4,48,9216]{2,1,0:T(8,128)(2,1)S(1)}, bf16[4,48,9216]{2,1,0:T(8,128)(2,1)}, u32[]{:S(2)}, u32[]{:S(2)}) collective-permute-start(bf16[4,48,9216]{2,1,0:T(8,128)(2,1)S(1)} %maximum_maximum_fusion), channel_id=1, source_target_pairs={{0,16},{16,0},{1,17},{17,1},{2,18},{18,2},{3,19},{19,3},{4,20},{20... | collective-permute-start | bytes 10616840 | tf_op jit(solution)/shard_map/ppermute | solution.py:454
  99.1 25.5 %collective-permute-start.26 = (bf16[4,48,9216]{2,1,0:T(8,128)(2,1)}, bf16[4,48,9216]{2,1,0:T(8,128)(2,1)}, u32[]{:S(2)}, u32[]{:S(2)}) collective-permute-start(bf16[4,48,9216]{2,1,0:T(8,128)(2,1)} %pad_maximum_fusion), channel_id=1, source_target_pairs={{0,16},{16,0},{1,17},{17,1},{2,18},{18,2},{3,19},{19,3},{4,20},{20... | collective-permute-start | bytes 10616840 | tf_op jit(solution)/shard_map/ppermute | solution.py:454
  101.0 15.2 %collective-permute-start.25 = (bf16[2,48,3072]{2,1,0:T(8,128)(2,1)}, bf16[2,48,3072]{2,1,0:T(8,128)(2,1)}, u32[]{:S(2)}, u32[]{:S(2)}) collective-permute-start(bf16[2,48,3072]{2,1,0:T(8,128)(2,1)} %pad_maximum_fusion.15), channel_id=1, source_target_pairs={{0,1},{1,0},{2,3},{3,2},{4,5},{5,4},{6,7},{7,6},{8,9},{9,8},{10,11... | collective-permute-start | bytes 1769480 | tf_op jit(solution)/shard_map/ppermute | solution.py:450
  101.6 16.8 %collective-permute-start.24 = (bf16[2,48,3072]{2,1,0:T(8,128)(2,1)}, bf16[2,48,3072]{2,1,0:T(8,128)(2,1)S(1)}, u32[]{:S(2)}, u32[]{:S(2)}) collective-permute-start(bf16[2,48,3072]{2,1,0:T(8,128)(2,1)} %pad_maximum_fusion.14), channel_id=1, source_target_pairs={{0,4},{1,5},{2,6},{3,7},{4,0},{5,1},{6,2},{7,3},{8,12},{9,13},{10,... | collective-permute-start | bytes 1769480 | tf_op jit(solution)/shard_map/ppermute | solution.py:450
  104.0 20.0 %collective-permute-start.22 = (bf16[4,2,16,128]{3,2,1,0:T(8,128)(2,1)S(1)}, bf16[4,2,16,128]{3,2,1,0:T(8,128)(2,1)S(1)}, u32[]{:S(2)}, u32[]{:S(2)}) collective-permute-start(bf16[4,2,16,128]{3,2,1,0:T(8,128)(2,1)S(1)} %copy-done.35), channel_id=1, source_target_pairs={{0,4},{1,5},{2,6},{3,7},{4,0},{5,1},{6,2},{7,3},{8,12},{9,13},{10,... | collective-permute-start | bytes 98312 | tf_op jit(solution)/shard_map/ppermute | solution.py:450
  105.3 14.2 %collective-permute-start.23 = (bf16[2,48,3072]{2,1,0:T(8,128)(2,1)S(1)}, bf16[2,48,3072]{2,1,0:T(8,128)(2,1)S(1)}, u32[]{:S(2)}, u32[]{:S(2)}) collective-permute-start(bf16[2,48,3072]{2,1,0:T(8,128)(2,1)S(1)} %copy-done.28), channel_id=1, source_target_pairs={{0,2},{1,3},{2,0},{3,1},{4,6},{5,7},{6,4},{7,5},{8,10},{9,11},{10,... | collective-permute-start | bytes 1769480 | tf_op jit(solution)/shard_map/ppermute | solution.py:450
  124.6 41.7 %collective-permute-start.31 = (bf16[4,48,9216]{2,1,0:T(8,128)(2,1)}, bf16[4,48,9216]{2,1,0:T(8,128)(2,1)}, u32[]{:S(2)}, u32[]{:S(2)}) collective-permute-start(bf16[4,48,9216]{2,1,0:T(8,128)(2,1)} %maximum_maximum_fusion.1), channel_id=1, source_target_pairs={{0,16},{16,0},{1,17},{17,1},{2,18},{18,2},{3,19},{19,3},{4,20},{20... | collective-permute-start | bytes 10616840 | tf_op jit(solution)/shard_map/ppermute | solution.py:454
  127.9 38.5 %collective-permute-start.27 = (bf16[4,48,3072]{2,1,0:T(8,128)(2,1)}, bf16[4,48,3072]{2,1,0:T(8,128)(2,1)}, u32[]{:S(2)}, u32[]{:S(2)}) collective-permute-start(bf16[4,48,3072]{2,1,0:T(8,128)(2,1)} %pad_maximum_fusion.5.refs_5_), channel_id=1, source_target_pairs={{0,4},{1,5},{2,6},{3,7},{4,0},{5,1},{6,2},{7,3},{8,12},{9,13},{10,... | collective-permute-start | bytes 3538952 | tf_op jit(solution)/shard_map/ppermute | solution.py:450
  128.0 38.4 %collective-permute-start.28 = (bf16[4,48,3072]{2,1,0:T(8,128)(2,1)}, bf16[4,48,3072]{2,1,0:T(8,128)(2,1)}, u32[]{:S(2)}, u32[]{:S(2)}) collective-permute-start(bf16[4,48,3072]{2,1,0:T(8,128)(2,1)} %pad_maximum_fusion.6.refs_9_), channel_id=1, source_target_pairs={{0,1},{1,0},{2,3},{3,2},{4,5},{5,4},{6,7},{7,6},{8,9},{9,8},{10,11... | collective-permute-start | bytes 3538952 | tf_op jit(solution)/shard_map/ppermute | solution.py:450
  128.9 37.5 %collective-permute-start.29 = (bf16[4,48,3072]{2,1,0:T(8,128)(2,1)}, bf16[4,48,3072]{2,1,0:T(8,128)(2,1)}, u32[]{:S(2)}, u32[]{:S(2)}) collective-permute-start(bf16[4,48,3072]{2,1,0:T(8,128)(2,1)} %pad_maximum_fusion.7.refs_13_), channel_id=1, source_target_pairs={{0,2},{1,3},{2,0},{3,1},{4,6},{5,7},{6,4},{7,5},{8,10},{9,11},{10,... | collective-permute-start | bytes 3538952 | tf_op jit(solution)/shard_map/ppermute | solution.py:450
  131.0 19.2 %collective-permute-start.30 = (bf16[4,160,768]{2,1,0:T(8,128)(2,1)}, bf16[4,160,768]{2,1,0:T(8,128)(2,1)S(1)}, u32[]{:S(2)}, u32[]{:S(2)}) collective-permute-start(bf16[4,160,768]{2,1,0:T(8,128)(2,1)} %broadcast_select_fusion), channel_id=1, source_target_pairs={{0,8},{1,9},{2,10},{3,11},{4,12},{5,13},{6,14},{7,15},{24,16},{25,... | collective-permute-start | bytes 2949128 | tf_op jit(solution)/shard_map/ppermute | solution.py:460
  184.6 34.9 %collective-permute-start.36 = (bf16[1,160,768]{2,1,0:T(8,128)(2,1)S(1)}, bf16[1,160,768]{2,1,0:T(8,128)(2,1)S(1)}, u32[]{:S(2)}, u32[]{:S(2)}) collective-permute-start(bf16[1,160,768]{2,1,0:T(8,128)(2,1)S(1)} %layer_fwd.4), channel_id=1, source_target_pairs={{0,8},{1,9},{2,10},{3,11},{4,12},{5,13},{6,14},{7,15},{16,24},{17,... | collective-permute-start | bytes 737288 | tf_op jit(solution)/shard_map/ppermute | solution.py:460
  196.3 30.8 %collective-permute-start.37 = (bf16[1,160,768]{2,1,0:T(8,128)(2,1)S(1)}, bf16[1,160,768]{2,1,0:T(8,128)(2,1)S(1)}, u32[]{:S(2)}, u32[]{:S(2)}) collective-permute-start(bf16[1,160,768]{2,1,0:T(8,128)(2,1)S(1)} %layer_fwd.5), channel_id=1, source_target_pairs={{0,8},{1,9},{2,10},{3,11},{4,12},{5,13},{6,14},{7,15},{16,24},{17,... | collective-permute-start | bytes 737288 | tf_op jit(solution)/shard_map/ppermute | solution.py:460
  207.8 30.5 %collective-permute-start.38 = (bf16[1,160,768]{2,1,0:T(8,128)(2,1)S(1)}, bf16[1,160,768]{2,1,0:T(8,128)(2,1)S(1)}, u32[]{:S(2)}, u32[]{:S(2)}) collective-permute-start(bf16[1,160,768]{2,1,0:T(8,128)(2,1)S(1)} %layer_fwd.6), channel_id=1, source_target_pairs={{0,8},{1,9},{2,10},{3,11},{4,12},{5,13},{6,14},{7,15},{16,24},{17,... | collective-permute-start | bytes 737288 | tf_op jit(solution)/shard_map/ppermute | solution.py:460
  220.9 17.4 %collective-permute-start.39 = (bf16[1,160,768]{2,1,0:T(8,128)(2,1)S(1)}, bf16[1,160,768]{2,1,0:T(8,128)(2,1)S(1)}, u32[]{:S(2)}, u32[]{:S(2)}) collective-permute-start(bf16[1,160,768]{2,1,0:T(8,128)(2,1)S(1)} %get-tuple-element.200), channel_id=1, source_target_pairs={{8,0},{9,1},{10,2},{11,3},{12,4},{13,5},{14,6},{15,7},{24,16},{25,... | collective-permute-start | bytes 737288 | tf_op jit(solution)/shard_map/ppermute | solution.py:460
  222.2 36.5 %collective-permute-start.40 = (bf16[1,160,768]{2,1,0:T(8,128)(2,1)S(1)}, bf16[1,160,768]{2,1,0:T(8,128)(2,1)S(1)}, u32[]{:S(2)}, u32[]{:S(2)}) collective-permute-start(bf16[1,160,768]{2,1,0:T(8,128)(2,1)S(1)} %layer_fwd.7), channel_id=1, source_target_pairs={{0,8},{1,9},{2,10},{3,11},{4,12},{5,13},{6,14},{7,15},{16,24},{17,... | collective-permute-start | bytes 737288 | tf_op jit(solution)/shard_map/ppermute | solution.py:460
  237.0 21.7 %collective-permute-start.41 = (bf16[1,160,768]{2,1,0:T(8,128)(2,1)S(1)}, bf16[1,160,768]{2,1,0:T(8,128)(2,1)S(1)}, u32[]{:S(2)}, u32[]{:S(2)}) collective-permute-start(bf16[1,160,768]{2,1,0:T(8,128)(2,1)S(1)} %get-tuple-element.209), channel_id=1, source_target_pairs={{8,0},{9,1},{10,2},{11,3},{12,4},{13,5},{14,6},{15,7},{24,16},{25,... | collective-permute-start | bytes 737288 | tf_op jit(solution)/shard_map/ppermute | solution.py:460
  257.4 22.9 %collective-permute-start.43 = (bf16[1,160,768]{2,1,0:T(8,128)(2,1)}, bf16[1,160,768]{2,1,0:T(8,128)(2,1)}, u32[]{:S(2)}, u32[]{:S(2)}) collective-permute-start(bf16[1,160,768]{2,1,0:T(8,128)(2,1)} %get-tuple-element.218), channel_id=1, source_target_pairs={{8,0},{9,1},{10,2},{11,3},{12,4},{13,5},{14,6},{15,7},{24,16},{25,... | collective-permute-start | bytes 737288 | tf_op jit(solution)/shard_map/ppermute | solution.py:460
  278.0 21.2 %collective-permute-start.42 = (bf16[1,160,768]{2,1,0:T(8,128)(2,1)}, bf16[1,160,768]{2,1,0:T(8,128)(2,1)S(1)}, u32[]{:S(2)}, u32[]{:S(2)}) collective-permute-start(bf16[1,160,768]{2,1,0:T(8,128)(2,1)} %get-tuple-element.227), channel_id=1, source_target_pairs={{8,0},{9,1},{10,2},{11,3},{12,4},{13,5},{14,6},{15,7},{24,16},{25,... | collective-permute-start | bytes 737288 | tf_op jit(solution)/shard_map/ppermute | solution.py:460
  326.8 33.3 %collective-permute-start.48 = (bf16[8,48,3072]{2,1,0:T(8,128)(2,1)}, bf16[8,48,3072]{2,1,0:T(8,128)(2,1)}, u32[]{:S(2)}, u32[]{:S(2)}) collective-permute-start(bf16[8,48,3072]{2,1,0:T(8,128)(2,1)} %get-tuple-element.253), channel_id=1, source_target_pairs={{0,16},{16,0},{1,17},{17,1},{2,18},{18,2},{3,19},{19,3},{4,20},{20... | collective-permute-start | bytes 7077896 | tf_op jit(solution)/shard_map/ppermute | solution.py:454
  336.3 26.5 %collective-permute-start.47 = (bf16[8,48,3072]{2,1,0:T(8,128)(2,1)}, bf16[8,48,3072]{2,1,0:T(8,128)(2,1)}, u32[]{:S(2)}, u32[]{:S(2)}) collective-permute-start(bf16[8,48,3072]{2,1,0:T(8,128)(2,1)} %get-tuple-element.251), channel_id=1, source_target_pairs={{0,16},{16,0},{1,17},{17,1},{2,18},{18,2},{3,19},{19,3},{4,20},{20... | collective-permute-start | bytes 7077896 | tf_op jit(solution)/shard_map/ppermute | solution.py:454
  336.5 31.0 %collective-permute-start.45 = (bf16[4,160,768]{2,1,0:T(8,128)(2,1)S(1)}, bf16[4,160,768]{2,1,0:T(8,128)(2,1)}, u32[]{:S(2)}, u32[]{:S(2)}) collective-permute-start(bf16[4,160,768]{2,1,0:T(8,128)(2,1)S(1)} %get-tuple-element.244), channel_id=1, source_target_pairs={{0,16},{16,8},{1,17},{17,9},{2,18},{18,10},{3,19},{19,11},{4,20},{... | collective-permute-start | bytes 2949128 | tf_op jit(solution)/shard_map/ppermute | solution.py:460
  338.4 29.1 %collective-permute-start.44 = (bf16[4,160,768]{2,1,0:T(8,128)(2,1)S(1)}, bf16[4,160,768]{2,1,0:T(8,128)(2,1)}, u32[]{:S(2)}, u32[]{:S(2)}) collective-permute-start(bf16[4,160,768]{2,1,0:T(8,128)(2,1)S(1)} %get-tuple-element.244), channel_id=1, source_target_pairs={{24,8},{8,16},{25,9},{9,17},{26,10},{10,18},{27,11},{11,19},{28,12... | collective-permute-start | bytes 2949128 | tf_op jit(solution)/shard_map/ppermute | solution.py:460
  367.5 27.4 %collective-permute-start.49 = (bf16[8,96,128]{2,1,0:T(8,128)(2,1)S(1)}, bf16[8,96,128]{2,1,0:T(8,128)(2,1)}, u32[]{:S(2)}, u32[]{:S(2)}) collective-permute-start(bf16[8,96,128]{2,1,0:T(8,128)(2,1)S(1)} %bitcast.205), channel_id=1, source_target_pairs={{0,16},{16,0},{1,17},{17,1},{2,18},{18,2},{3,19},{19,3},{4,20},{20... | collective-permute-start | bytes 589832 | tf_op jit(solution)/shard_map/ppermute | solution.py:454
  367.5 28.4 %collective-permute-start.50 = (bf16[4,48,3072]{2,1,0:T(8,128)(2,1)}, bf16[4,48,3072]{2,1,0:T(8,128)(2,1)}, u32[]{:S(2)}, u32[]{:S(2)}) collective-permute-start(bf16[4,48,3072]{2,1,0:T(8,128)(2,1)} %add_convert_fusion.11), channel_id=1, source_target_pairs={{0,1},{1,0},{2,3},{3,2},{4,5},{5,4},{6,7},{7,6},{8,9},{9,8},{10,11... | collective-permute-start | bytes 3538952 | tf_op jit(solution)/shard_map/ppermute | solution.py:450
  368.3 29.3 %collective-permute-start.51 = (bf16[4,48,3072]{2,1,0:T(8,128)(2,1)S(1)}, bf16[4,48,3072]{2,1,0:T(8,128)(2,1)}, u32[]{:S(2)}, u32[]{:S(2)}) collective-permute-start(bf16[4,48,3072]{2,1,0:T(8,128)(2,1)S(1)} %add_convert_fusion.10), channel_id=1, source_target_pairs={{0,2},{1,3},{2,0},{3,1},{4,6},{5,7},{6,4},{7,5},{8,10},{9,11},{10,... | collective-permute-start | bytes 3538952 | tf_op jit(solution)/shard_map/ppermute | solution.py:450
  369.9 30.1 %collective-permute-start.52 = (bf16[4,48,3072]{2,1,0:T(8,128)(2,1)S(1)}, bf16[4,48,3072]{2,1,0:T(8,128)(2,1)}, u32[]{:S(2)}, u32[]{:S(2)}) collective-permute-start(bf16[4,48,3072]{2,1,0:T(8,128)(2,1)S(1)} %add_convert_fusion.9), channel_id=1, source_target_pairs={{0,4},{1,5},{2,6},{3,7},{4,0},{5,1},{6,2},{7,3},{8,12},{9,13},{10,... | collective-permute-start | bytes 3538952 | tf_op jit(solution)/shard_map/ppermute | solution.py:450
  374.6 27.2 %collective-permute-start.53 = (bf16[8,48,3072]{2,1,0:T(8,128)(2,1)}, bf16[8,48,3072]{2,1,0:T(8,128)(2,1)S(1)}, u32[]{:S(2)}, u32[]{:S(2)}) collective-permute-start(bf16[8,48,3072]{2,1,0:T(8,128)(2,1)} %get-tuple-element.270), channel_id=1, source_target_pairs={{0,16},{16,0},{1,17},{17,1},{2,18},{18,2},{3,19},{19,3},{4,20},{20... | collective-permute-start | bytes 7077896 | tf_op jit(solution)/shard_map/ppermute | solution.py:454
  402.9 13.1 %collective-permute-start.55 = (bf16[2,48,3072]{2,1,0:T(8,128)(2,1)S(1)}, bf16[2,48,3072]{2,1,0:T(8,128)(2,1)S(1)}, u32[]{:S(2)}, u32[]{:S(2)}) collective-permute-start(bf16[2,48,3072]{2,1,0:T(8,128)(2,1)S(1)} %get-tuple-element.272), channel_id=1, source_target_pairs={{0,2},{1,3},{2,0},{3,1},{4,6},{5,7},{6,4},{7,5},{8,10},{9,11},{10,... | collective-permute-start | bytes 1769480 | tf_op jit(solution)/shard_map/ppermute | solution.py:450
  402.9 16.2 %collective-permute-start.56 = (bf16[2,48,3072]{2,1,0:T(8,128)(2,1)S(1)}, bf16[2,48,3072]{2,1,0:T(8,128)(2,1)S(1)}, u32[]{:S(2)}, u32[]{:S(2)}) collective-permute-start(bf16[2,48,3072]{2,1,0:T(8,128)(2,1)S(1)} %get-tuple-element.273), channel_id=1, source_target_pairs={{0,4},{1,5},{2,6},{3,7},{4,0},{5,1},{6,2},{7,3},{8,12},{9,13},{10,... | collective-permute-start | bytes 1769480 | tf_op jit(solution)/shard_map/ppermute | solution.py:450
  431.9 35.3 %collective-permute-start.64 = (bf16[4,48,3072]{2,1,0:T(8,128)(2,1)S(1)}, bf16[4,48,3072]{2,1,0:T(8,128)(2,1)S(1)}, u32[]{:S(2)}, u32[]{:S(2)}) collective-permute-start(bf16[4,48,3072]{2,1,0:T(8,128)(2,1)S(1)} %get-tuple-element.283), channel_id=1, source_target_pairs={{0,4},{1,5},{2,6},{3,7},{4,0},{5,1},{6,2},{7,3},{8,12},{9,13},{10,... | collective-permute-start | bytes 3538952 | tf_op jit(solution)/shard_map/ppermute | solution.py:450
  433.4 33.9 %collective-permute-start.65 = (bf16[1,96,128]{2,1,0:T(8,128)(2,1)S(1)}, bf16[1,96,128]{2,1,0:T(8,128)(2,1)S(1)}, u32[]{:S(2)}, u32[]{:S(2)}) collective-permute-start(bf16[1,96,128]{2,1,0:T(8,128)(2,1)S(1)} %add_convert_fusion.43), channel_id=1, source_target_pairs={{0,4},{1,5},{2,6},{3,7},{4,0},{5,1},{6,2},{7,3},{8,12},{9,13},{10,... | collective-permute-start | bytes 73736 | tf_op jit(solution)/shard_map/ppermute | solution.py:450
  433.5 35.0 %collective-permute-start.68 = (bf16[48,9216]{1,0:T(8,128)(2,1)S(1)}, bf16[48,9216]{1,0:T(8,128)(2,1)S(1)}, u32[]{:S(2)}, u32[]{:S(2)}) collective-permute-start(bf16[48,9216]{1,0:T(8,128)(2,1)S(1)} %pad_maximum_fusion.9), channel_id=1, source_target_pairs={{0,8},{1,9},{2,10},{3,11},{4,12},{5,13},{6,14},{7,15},{24,16},{25,... | collective-permute-start | bytes 2654216 | tf_op jit(solution)/shard_map/ppermute | solution.py:460
  435.1 32.6 %collective-permute-start.66 = (bf16[4,48,3072]{2,1,0:T(8,128)(2,1)S(1)}, bf16[4,48,3072]{2,1,0:T(8,128)(2,1)S(1)}, u32[]{:S(2)}, u32[]{:S(2)}) collective-permute-start(bf16[4,48,3072]{2,1,0:T(8,128)(2,1)S(1)} %get-tuple-element.285), channel_id=1, source_target_pairs={{0,1},{1,0},{2,3},{3,2},{4,5},{5,4},{6,7},{7,6},{8,9},{9,8},{10,11... | collective-permute-start | bytes 3538952 | tf_op jit(solution)/shard_map/ppermute | solution.py:450
  436.4 31.7 %collective-permute-start.67 = (bf16[4,48,3072]{2,1,0:T(8,128)(2,1)S(1)}, bf16[4,48,3072]{2,1,0:T(8,128)(2,1)S(1)}, u32[]{:S(2)}, u32[]{:S(2)}) collective-permute-start(bf16[4,48,3072]{2,1,0:T(8,128)(2,1)S(1)} %get-tuple-element.286), channel_id=1, source_target_pairs={{0,2},{1,3},{2,0},{3,1},{4,6},{5,7},{6,4},{7,5},{8,10},{9,11},{10,... | collective-permute-start | bytes 3538952 | tf_op jit(solution)/shard_map/ppermute | solution.py:450
  470.0 21.3 %collective-permute-start.72 = (bf16[48,128]{1,0:T(8,128)(2,1)S(1)}, bf16[48,128]{1,0:T(8,128)(2,1)S(1)}, u32[]{:S(2)}, u32[]{:S(2)}) collective-permute-start(bf16[48,128]{1,0:T(8,128)(2,1)S(1)} %get-tuple-element.291), channel_id=1, source_target_pairs={{0,8},{1,9},{2,10},{3,11},{4,12},{5,13},{6,14},{7,15},{24,16},{25,... | collective-permute-start | bytes 36872 | tf_op jit(solution)/shard_map/ppermute | solution.py:460
  472.4 18.9 %collective-permute-start.71 = (bf16[2,48,3072]{2,1,0:T(8,128)(2,1)S(1)}, bf16[2,48,3072]{2,1,0:T(8,128)(2,1)S(1)}, u32[]{:S(2)}, u32[]{:S(2)}) collective-permute-start(bf16[2,48,3072]{2,1,0:T(8,128)(2,1)S(1)} %get-tuple-element.290), channel_id=1, source_target_pairs={{0,4},{1,5},{2,6},{3,7},{4,0},{5,1},{6,2},{7,3},{8,12},{9,13},{10,... | collective-permute-start | bytes 1769480 | tf_op jit(solution)/shard_map/ppermute | solution.py:450
  474.7 19.6 %collective-permute-start.73 = (bf16[48,6144]{1,0:T(8,128)(2,1)S(1)}, bf16[48,6144]{1,0:T(8,128)(2,1)S(1)}, u32[]{:S(2)}, u32[]{:S(2)}) collective-permute-start(bf16[48,6144]{1,0:T(8,128)(2,1)S(1)} %pad_maximum_fusion.16), channel_id=1, source_target_pairs={{8,16},{9,17},{10,18},{11,19},{12,20},{13,21},{14,22},{15,23},{16,... | collective-permute-start | bytes 1769480 | tf_op jit(solution)/shard_map/ppermute | solution.py:460
  495.0 12.8 %collective-permute-start.75 = (bf16[1,48,3072]{2,1,0:T(8,128)(2,1)S(1)}, bf16[1,48,3072]{2,1,0:T(8,128)(2,1)S(1)}, u32[]{:S(2)}, u32[]{:S(2)}) collective-permute-start(bf16[1,48,3072]{2,1,0:T(8,128)(2,1)S(1)} %add_convert_fusion.28), channel_id=1, source_target_pairs={{0,4},{1,5},{2,6},{3,7},{4,0},{5,1},{6,2},{7,3},{8,12},{9,13},{10,... | collective-permute-start | bytes 884744 | tf_op jit(solution)/shard_map/ppermute | solution.py:450
  498.5 12.9 %collective-permute-start.77 = (bf16[48,3200]{1,0:T(8,128)(2,1)S(1)}, bf16[48,3200]{1,0:T(8,128)(2,1)S(1)}, u32[]{:S(2)}, u32[]{:S(2)}) collective-permute-start(bf16[48,3200]{1,0:T(8,128)(2,1)S(1)} %pad_maximum_fusion.17), channel_id=1, source_target_pairs={{8,16},{9,17},{10,18},{11,19},{12,20},{13,21},{14,22},{15,23},{16,... | collective-permute-start | bytes 921608 | tf_op jit(solution)/shard_map/ppermute | solution.py:460
  (84 other events, 919.5 us)

commit v5 on v4

--- a/solution.py
+++ b/solution.py
@@ -562,19 +562,17 @@
         wide = jnp.pad(wides, ((0, 0), (0, 2 * EXTRA - 4 * rows))).reshape(2, 2, EXTRA)
         small = jnp.pad(jnp.concatenate([small, wide], 1), ((0, 0), (0, 6), (0, 0)))
         small = small.at[:, 10, : 2 * count].set(numbers.astype(BF16)[None])
-        small_mine = jnp.where(section == 0, small[0], small[1])
-        small_twin = jnp.where(section == 0, small[1], small[0])
-        home, small_home = wave((twin, by(routes.home_to_away)), (small_twin, by(routes.home_to_away)))
+        home, small_home = wave((twin, by(routes.home_to_away)), (small, by(routes.home_to_away)))
         near_held = own(jnp.where(at_home, mine, home))
         *got, small_straight, cross_a = wave(
-            *bits(near_held, 0), (small_mine, by(routes.straight)), (twin[:, : cuts[1]], by(routes.crossed))
+            *bits(near_held, 0), (small, by(routes.straight)), (twin[:, : cuts[1]], by(routes.crossed))
         )
         near_held = joined(near_held, got)
         *got, small_crossed, cross_b = wave(
-            *bits(near_held, 1), (small_twin, by(routes.crossed)), (twin[:, cuts[1] :], by(routes.crossed))
+            *bits(near_held, 1), (small, by(routes.crossed)), (twin[:, cuts[1] :], by(routes.crossed))
         )
         small_held = jnp.stack(
-            [jnp.where(at_home, small_mine, small_home), jnp.where(at_home, small_straight, small_crossed)]
+            [jnp.where(at_home, small, small_home), jnp.where(at_home, small_straight, small_crossed)]
         )[None]
         near_held = joined(near_held, got)
         *near_far, small_got, straight = wave(
@@ -587,18 +585,18 @@
         )
         small_held = jnp.concatenate([small_held, small_got], 0)
         away_held = joined(away_held, got)
-        *got, small_got, twin_near_far = wave(
-            *bits(away_held, 1), one_bit(small_held, 2), (merged(near_far), swap_section)
+        *got, moved, twin_near_far = wave(
+            *bits(away_held, 1),
+            (jnp.where(half == 1, inputs, cotangent), by(crossing)),
+            (merged(near_far), swap_section),
+        )
+        away_held = joined(away_held, got)
+        *away_far, small_got, twin_away_held = wave(
+            *bits(away_held, 2), one_bit(small_held, 2), (merged(away_held), swap_section)
         )
         small_held = jnp.concatenate([small_held, small_got], 0)
-        away_held = joined(away_held, got)
-        *away_far, moved, twin_away_held = wave(
-            *bits(away_held, 2),
-            (jnp.where(half == 1, inputs, cotangent), by(crossing)),
-            (merged(away_held), swap_section),
-        )
-        *twin_last, small_other = wave(*[(array, swap_section) for array in away_far], (small_held, swap_section))
-        numbers_got = small_crossed[10, : 2 * count].astype(F32).astype(jnp.int32)
+        twin_last = wave(*[(array, swap_section) for array in away_far])
+        numbers_got = small_crossed[0, 10, : 2 * count].astype(F32).astype(jnp.int32)
         pieces = [array for group in zip(near_held, near_far, away_held, away_far) for array in group]
         pieces += [twin_near_held, twin_near_far, twin_away_held, *twin_last]
 
@@ -614,10 +612,11 @@
         small_order = jnp.stack([small_order + near * half, small_order + near * (1 - half)], 1).reshape(BLOCKS)
         pick = (small_order[None, :] == jnp.arange(BLOCKS, dtype=jnp.int32)[:, None]).astype(BF16)
         row_list, fbias_list = [], []
-        for array in (small_held, small_other):
-            laid = dot_nn(pick, array.reshape(BLOCKS, 16 * EXTRA)).reshape(BLOCKS, 16, EXTRA)
-            row_list.append(jnp.swapaxes(laid[:, :8, :rows], 0, 1).reshape(8, D))
-            fbias_list.append(laid[:, 8:10].reshape(BLOCKS, 2 * EXTRA)[:, : 4 * rows].reshape(1, FF))
+        laid = dot_nn(pick, small_held.reshape(BLOCKS, 2 * 16 * EXTRA)).reshape(BLOCKS, 2, 16, EXTRA)
+        laid = jnp.where(section == 0, laid, laid[:, ::-1])
+        for side in range(2):
+            row_list.append(jnp.swapaxes(laid[:, side, :8, :rows], 0, 1).reshape(8, D))
+            fbias_list.append(laid[:, side, 8:10].reshape(BLOCKS, 2 * EXTRA)[:, : 4 * rows].reshape(1, FF))
         rows_all = jnp.stack(row_list)
         fbias_all = jnp.stack(fbias_list)
     else:

time: 539 us -> 532 us (0.987)
  waiting for transfers between devices: 148 us -> 162 us
  starting transfers between devices: 123 us -> 113 us
  local copies, waits for them, and re-layouts: 24.6 us -> 19 us
    ppermute x42, waiting for transfers between devices: 118 us -> 135 us  [swap_bit(): return lax.ppermute(array, 'dp', [(i, i ^ 1 << bit) for i in range(count)])]
    ppermute x42, starting transfers between devices: 58.2 us -> 49.5 us  [swap_bit(): return lax.ppermute(array, 'dp', [(i, i ^ 1 << bit) for i in range(count)])]
    ppermute x23, waiting for transfers between devices: 28.4 us -> 19.7 us  [along(): return lax.ppermute(array, ('section', 'dp'), flat)]
    ppermute x14 -> x13, waiting for transfers between devices: 1.26 us -> 6.74 us  [swap_section(): return lax.ppermute(array, 'section', [(0, 1), (1, 0)])]
    ppermute x14 -> x13, starting transfers between devices: 15 us -> 12.4 us  [swap_section(): return lax.ppermute(array, 'section', [(0, 1), (1, 0)])]
    unnamed x112 -> x107, local copies, waits for them, and re-layouts: 12.5 us -> 12.1 us
  transfers between devices with their start and end apart: 79 -> 78, of which waited for: 26 -> 29; matrix products, arithmetic and copies ran while one was open for 12% -> 10% of each run, Pallas kernels for 25% -> 25%
where the time goes in v5:
time: 532 us; the launch traced here: 522 us
  Pallas kernels  169 us (32%)
  waiting for transfers between devices  162 us (30%)
  starting transfers between devices  113 us (21%)
  other arithmetic  56.3 us (11%)
  local copies, waits for them, and re-layouts  19 us (4%)
    ppermute x42, waiting for transfers between devices, swap_bit(): return lax.ppermute(array, 'dp', [(i, i ^ 1 << bit) for i in range(count)])  135 us
    pallas_call x10, Pallas kernels, layer_call(): pl.pallas_call(functools.partial(layer_kernel, back, slot, lead, count),...  128 us
    ppermute x23, starting transfers between devices, along(): return lax.ppermute(array, ('section', 'dp'), flat)  51 us
    ppermute x42, starting transfers between devices, swap_bit(): return lax.ppermute(array, 'dp', [(i, i ^ 1 << bit) for i in range(count)])  49.5 us
    pallas_call x6, Pallas kernels, grad_call(): pl.pallas_call(functools.partial(grad_kernel, unit, at), out_shape=[shape...  41.1 us
    convert_element_type x24, other arithmetic, both(): return (first.astype(F32) + second.astype(F32)).astype(BF16)  21.6 us
    ppermute x23, waiting for transfers between devices, along(): return lax.ppermute(array, ('section', 'dp'), flat)  19.7 us
    ppermute x13, starting transfers between devices, swap_section(): return lax.ppermute(array, 'section', [(0, 1), (1, 0)])  12.4 us
  transfers between devices with their start and end apart: 78, of which 29 were waited for; matrix products, arithmetic and copies ran while one was open for 10% of the time, Pallas kernels for 25%

profile of v5, /device:TPU:1, one launch (start us, length us, event | category | flops | bytes accessed | tf_op | source)
XLA Modules:
  0.0 522.2 jit_solution(9265949050960599591)
XLA Ops:
  12.5 4.6 collective-permute-start.5
  19.6 2.8 collective-permute-start.6
  22.5 2.5 collective-permute-done.3
  25.2 6.5 %collective-permute-done.6 = bf16[48,3072]{1,0:T(8,128)(2,1)S(1)} collective-permute-done((bf16[48,3072]{1,0:T(8,128)(2,1)S(1)}, bf16[48,3072]{1,0:T(8,128)(2,1)S(1)}, u32[]{:S(2)}, u32[]{:S(2)}) %collective-permute-start.6) | collective-permute-done | bytes 294944 | tf_op jit(solution)/shard_map/ppermute | solution.py:460
  35.4 3.5 collective-permute-start.11
  40.5 13.4 %collective-permute-done.9 = bf16[2,48,3072]{2,1,0:T(8,128)(2,1)S(1)} collective-permute-done((bf16[2,48,3072]{2,1,0:T(8,128)(2,1)S(1)}, bf16[2,48,3072]{2,1,0:T(8,128)(2,1)S(1)}, u32[]{:S(2)}, u32[]{:S(2)}) %collective-permute-start.9) | collective-permute-done | bytes 589856 | tf_op jit(solution)/shard_map/ppermute | solution.py:450
  57.1 9.3 %collective-permute-start.14 = (bf16[4,48,3072]{2,1,0:T(8,128)(2,1)S(1)}, bf16[4,48,3072]{2,1,0:T(8,128)(2,1)S(1)}, u32[]{:S(2)}, u32[]{:S(2)}) collective-permute-start(bf16[4,48,3072]{2,1,0:T(8,128)(2,1)S(1)} %pad_maximum_fusion.2.refs_3_), channel_id=1, source_target_pairs={{0,4},{1,5},{2,6},{3,7},{4,0},{5,1},{6,2},{7,3},{8,12},{9,13},{10,... | collective-permute-start | bytes 3538952 | tf_op jit(solution)/shard_map/ppermute | solution.py:450
  66.5 2.4 collective-permute-start.16
  68.8 2.3 maximum_maximum_fusion
  72.9 12.5 %collective-permute-done.14.refs_4_ = bf16[4,48,3072]{2,1,0:T(8,128)(2,1)S(1)} collective-permute-done((bf16[4,48,3072]{2,1,0:T(8,128)(2,1)S(1)}, bf16[4,48,3072]{2,1,0:T(8,128)(2,1)S(1)}, u32[]{:S(2)}, u32[]{:S(2)}) %collective-permute-start.14) | collective-permute-done | bytes 1179680 | tf_op jit(solution)/shard_map/ppermute | solution.py:450
  87.6 2.3 collective-permute-start.17
  92.3 6.9 %collective-permute-done.20 = bf16[1,48,3072]{2,1,0:T(8,128)(2,1)S(1)} collective-permute-done((bf16[1,48,3072]{2,1,0:T(8,128)(2,1)S(1)}, bf16[1,48,3072]{2,1,0:T(8,128)(2,1)S(1)}, u32[]{:S(2)}, u32[]{:S(2)}) %collective-permute-start.20) | collective-permute-done | bytes 294944 | tf_op jit(solution)/shard_map/ppermute | solution.py:450
  104.0 11.5 %collective-permute-done.24 = bf16[2,48,3072]{2,1,0:T(8,128)(2,1)S(1)} collective-permute-done((bf16[2,48,3072]{2,1,0:T(8,128)(2,1)S(1)}, bf16[2,48,3072]{2,1,0:T(8,128)(2,1)S(1)}, u32[]{:S(2)}, u32[]{:S(2)}) %collective-permute-start.24) | collective-permute-done | bytes 589856 | tf_op jit(solution)/shard_map/ppermute | solution.py:450
  116.6 8.8 %collective-permute-done.23 = bf16[2,48,3072]{2,1,0:T(8,128)(2,1)S(1)} collective-permute-done((bf16[2,48,3072]{2,1,0:T(8,128)(2,1)S(1)}, bf16[2,48,3072]{2,1,0:T(8,128)(2,1)S(1)}, u32[]{:S(2)}, u32[]{:S(2)}) %collective-permute-start.23) | collective-permute-done | bytes 589856 | tf_op jit(solution)/shard_map/ppermute | solution.py:450
  127.8 2.3 maximum_maximum_fusion.1
  137.7 2.3 broadcast_select_fusion.1
  140.0 22.0 %collective-permute-done.27 = bf16[4,2,2,16,128]{4,3,2,1,0:T(8,128)(2,1)S(1)} collective-permute-done((bf16[4,2,2,16,128]{4,3,2,1,0:T(8,128)(2,1)S(1)}, bf16[4,2,2,16,128]{4,3,2,1,0:T(8,128)(2,1)S(1)}, u32[]{:S(2)}, u32[]{:S(2)}) %collective-permute-start.27) | collective-permute-done | bytes 65568 | tf_op jit(solution)/shard_map/ppermute | solution.py:450
  171.0 10.1 %layer_fwd.4 = bf16[1,160,768]{2,1,0:T(8,128)(2,1)S(1)} custom-call(s32[62]{0:T(128)S(1)} %concatenate.123.refs_0_, f32[2,8,768]{2,1,0:T(8,128)S(1)} %constant_dynamic-update-slice_fusion.refs_1_, f32[2,1,3072]{2,1,0:T(1,128)S(1)} %constant_dynamic-update-slice_fusion.2.refs_2_, bf16[4,48,3072]{2,1,0:T(8,128)(2,1)S(1)} %pad_maximum_fusion.2.refs_3_, ...), custom_call_target="tpu_custom_call" | custom-call | flops 1 | bytes 1 | tf_op jit(solution)/shard_map/layer_fwd/pallas_call | solution.py:410
  182.8 10.1 %layer_fwd.5 = bf16[1,160,768]{2,1,0:T(8,128)(2,1)S(1)} custom-call(s32[62]{0:T(128)S(1)} %concatenate.123.refs_0_, f32[2,8,768]{2,1,0:T(8,128)S(1)} %constant_dynamic-update-slice_fusion.refs_1_, f32[2,1,3072]{2,1,0:T(1,128)S(1)} %constant_dynamic-update-slice_fusion.2.refs_2_, bf16[4,48,3072]{2,1,0:T(8,128)(2,1)S(1)} %pad_maximum_fusion.2.refs_3_, ...), custom_call_target="tpu_custom_call" | custom-call | flops 1 | bytes 1 | tf_op jit(solution)/shard_map/layer_fwd/pallas_call | solution.py:410
  194.3 9.9 %layer_fwd.6 = bf16[1,160,768]{2,1,0:T(8,128)(2,1)S(1)} custom-call(s32[62]{0:T(128)S(1)} %concatenate.123.refs_0_, f32[2,8,768]{2,1,0:T(8,128)S(1)} %constant_dynamic-update-slice_fusion.refs_1_, f32[2,1,3072]{2,1,0:T(1,128)S(1)} %constant_dynamic-update-slice_fusion.2.refs_2_, bf16[4,48,3072]{2,1,0:T(8,128)(2,1)S(1)} %pad_maximum_fusion.2.refs_3_, ...), custom_call_target="tpu_custom_call" | custom-call | flops 1 | bytes 1 | tf_op jit(solution)/shard_map/layer_fwd/pallas_call | solution.py:410
  205.5 10.3 %layer_fwd.7 = bf16[1,160,768]{2,1,0:T(8,128)(2,1)S(1)} custom-call(s32[62]{0:T(128)S(1)} %concatenate.123.refs_0_, f32[2,8,768]{2,1,0:T(8,128)S(1)} %constant_dynamic-update-slice_fusion.refs_1_, f32[2,1,3072]{2,1,0:T(1,128)S(1)} %constant_dynamic-update-slice_fusion.2.refs_2_, bf16[4,48,3072]{2,1,0:T(8,128)(2,1)S(1)} %pad_maximum_fusion.2.refs_3_, ...), custom_call_target="tpu_custom_call" | custom-call | flops 1 | bytes 1 | tf_op jit(solution)/shard_map/layer_fwd/pallas_call | solution.py:410
  218.6 4.9 collective-permute-start.39
  223.5 9.8 %layer_back.7 = (bf16[1,160,768]{2,1,0:T(8,128)(2,1)S(1)}, bf16[4,160,768]{2,1,0:T(8,128)(2,1)S(1)}, f32[4,160,768]{2,1,0:T(8,128)}, f32[4,8,768]{2,1,0:T(8,128)...) custom-call(s32[62]{0:T(128)S(1)} %concatenate.123.refs_0_, ...), custom_call_target="tpu_custom_call", output_to_operand_aliasing={{1}: (24, {}), {2}: (25, {}), {3}: (26, {}), {4}: (27, {}),... | custom-call | flops 1 | bytes 1 | tf_op jit(solution)/shard_map/layer_back/pallas_call | solution.py:410
  234.7 19.1 %layer_back.8 = (bf16[1,160,768]{2,1,0:T(8,128)(2,1)}, bf16[4,160,768]{2,1,0:T(8,128)(2,1)S(1)}, f32[4,160,768]{2,1,0:T(8,128)}, f32[4,8,768]{2,1,0:T(8,128)S(1)...) custom-call(s32[62]{0:T(128)S(1)} %concatenate.123.refs_0_, ...), custom_call_target="tpu_custom_call", output_to_operand_aliasing={{1}: (25, {}), {2}: (26, {}), {3}: (27, {}), {4}: (28, {}),... | custom-call | flops 1 | bytes 1 | tf_op jit(solution)/shard_map/layer_back/pallas_call | solution.py:410
  255.1 19.3 %layer_back.9 = (bf16[1,160,768]{2,1,0:T(8,128)(2,1)}, bf16[4,160,768]{2,1,0:T(8,128)(2,1)S(1)}, f32[4,160,768]{2,1,0:T(8,128)}, f32[4,8,768]{2,1,0:T(8,128)S(1)...) custom-call(s32[62]{0:T(128)S(1)} %concatenate.123.refs_0_, ...), custom_call_target="tpu_custom_call", output_to_operand_aliasing={{1}: (25, {}), {2}: (26, {}), {3}: (27, {}), {4}: (28, {}),... | custom-call | flops 1 | bytes 1 | tf_op jit(solution)/shard_map/layer_back/pallas_call | solution.py:410
  276.7 18.8 %layer_back.10 = (bf16[1,160,768]{2,1,0:T(8,128)(2,1)}, bf16[4,160,768]{2,1,0:T(8,128)(2,1)S(1)}, f32[4,160,768]{2,1,0:T(8,128)}, f32[4,8,768]{2,1,0:T(8,128)S(1...) custom-call(s32[62]{0:T(128)S(1)} %concatenate.123.refs_0_, ...), custom_call_target="tpu_custom_call", output_to_operand_aliasing={{1}: (23, {}), {2}: (24, {}), {3}: (25, {}), {4}: (26, {}),... | custom-call | flops 1 | bytes 1 | tf_op jit(solution)/shard_map/layer_back/pallas_call | solution.py:410
  296.3 19.2 %layer_back.11 = (bf16[1,160,768]{2,1,0:T(8,128)(2,1)}, bf16[4,160,768]{2,1,0:T(8,128)(2,1)S(1)}, f32[4,160,768]{2,1,0:T(8,128)}, f32[4,8,768]{2,1,0:T(8,128)S(1...) custom-call(s32[62]{0:T(128)S(1)} %concatenate.123.refs_0_, ...), custom_call_target="tpu_custom_call", output_to_operand_aliasing={{1}: (23, {}), {2}: (24, {}), {3}: (25, {}), {4}: (26, {}),... | custom-call | flops 1 | bytes 1 | tf_op jit(solution)/shard_map/layer_back/pallas_call | solution.py:410
  315.5 7.1 %layer_grad.8 = (bf16[8,48,3072]{2,1,0:T(8,128)(2,1)S(1)}, bf16[8,48,3072]{2,1,0:T(8,128)(2,1)}) custom-call(s32[31]{0:T(128)S(1)} %concatenate.140.meta, bf16[4,4,160,768]{3,2,1,0:T(8,128)(2,1)} %get-tuple-element.244.refs_0_.refs_1_, bf16[4,4,160,768]{3,2,1,0:T(8,128)(2,1)} %get-tuple-element.244.refs_0_.refs_1_, ...), custom_call_target="tpu_custom_call" | custom-call | flops 1 | bytes 1 | tf_op jit(solution)/shard_map/layer_grad/pallas_call | solution.py:431
  324.6 6.6 %layer_grad.7 = (bf16[8,48,3072]{2,1,0:T(8,128)(2,1)S(1)}, bf16[8,48,3072]{2,1,0:T(8,128)(2,1)}) custom-call(s32[31]{0:T(128)S(1)} %concatenate.140.meta, bf16[4,4,160,768]{3,2,1,0:T(8,128)(2,1)} %get-tuple-element.244.refs_0_.refs_1_, bf16[3,4,160,3072]{3,2,1,0:T(8,128)(2,1)} %get-tuple-element.245.refs_1_.refs_2_), custom_call_target="tpu_custom_call" | custom-call | flops 1 | bytes 1 | tf_op jit(solution)/shard_map/layer_grad/pallas_call | solution.py:431
  336.2 6.6 %layer_grad.6 = (bf16[8,48,3072]{2,1,0:T(8,128)(2,1)S(1)}, bf16[8,48,3072]{2,1,0:T(8,128)(2,1)}) custom-call(s32[31]{0:T(128)S(1)} %concatenate.140.meta, bf16[4,4,160,768]{3,2,1,0:T(8,128)(2,1)} %get-tuple-element.244.refs_0_.refs_1_, bf16[3,4,160,3072]{3,2,1,0:T(8,128)(2,1)} %get-tuple-element.245.refs_1_.refs_2_), custom_call_target="tpu_custom_call" | custom-call | flops 1 | bytes 1 | tf_op jit(solution)/shard_map/layer_grad/pallas_call | solution.py:431
  344.3 6.7 %layer_grad.11 = (bf16[8,48,3072]{2,1,0:T(8,128)(2,1)S(1)}, bf16[8,48,3072]{2,1,0:T(8,128)(2,1)}) custom-call(s32[31]{0:T(128)S(1)} %concatenate.140.meta, bf16[4,4,160,768]{3,2,1,0:T(8,128)(2,1)} %get-tuple-element.244.refs_0_.refs_1_, bf16[3,4,160,3072]{3,2,1,0:T(8,128)(2,1)} %get-tuple-element.245.refs_1_.refs_2_), custom_call_target="tpu_custom_call" | custom-call | flops 1 | bytes 1 | tf_op jit(solution)/shard_map/layer_grad/pallas_call | solution.py:431
  361.1 2.7 add_convert_fusion.11
  364.3 3.0 collective-permute-start.50
  373.4 6.9 %layer_grad.9 = (bf16[8,48,3072]{2,1,0:T(8,128)(2,1)S(1)}, bf16[8,48,3072]{2,1,0:T(8,128)(2,1)}) custom-call(s32[31]{0:T(128)S(1)} %concatenate.140.meta, bf16[4,4,160,768]{3,2,1,0:T(8,128)(2,1)} %get-tuple-element.244.refs_0_.refs_1_, bf16[3,4,160,3072]{3,2,1,0:T(8,128)(2,1)} %get-tuple-element.245.refs_1_.refs_2_), custom_call_target="tpu_custom_call" | custom-call | flops 1 | bytes 1 | tf_op jit(solution)/shard_map/layer_grad/pallas_call | solution.py:431
  380.3 7.0 %layer_grad.10 = (bf16[8,48,3072]{2,1,0:T(8,128)(2,1)S(1)}, bf16[8,48,3072]{2,1,0:T(8,128)(2,1)}) custom-call(s32[31]{0:T(128)S(1)} %concatenate.140.meta, bf16[4,4,160,768]{3,2,1,0:T(8,128)(2,1)} %get-tuple-element.244.refs_0_.refs_1_, bf16[4,4,160,768]{3,2,1,0:T(8,128)(2,1)} %get-tuple-element.244.refs_0_.refs_1_, ...), custom_call_target="tpu_custom_call" | custom-call | flops 1 | bytes 1 | tf_op jit(solution)/shard_map/layer_grad/pallas_call | solution.py:431
  388.4 3.0 collective-permute-done.49
  397.4 2.7 collective-permute-start.54
  403.8 8.4 %collective-permute-done.54 = bf16[2,48,3072]{2,1,0:T(8,128)(2,1)S(1)} collective-permute-done((bf16[2,48,3072]{2,1,0:T(8,128)(2,1)S(1)}, bf16[2,48,3072]{2,1,0:T(8,128)(2,1)S(1)}, u32[]{:S(2)}, u32[]{:S(2)}) %collective-permute-start.54) | collective-permute-done | bytes 589856 | tf_op jit(solution)/shard_map/ppermute | solution.py:450
  416.5 4.2 collective-permute-start.58
  429.7 32.3 %collective-permute-done.64 = bf16[1,96,128]{2,1,0:T(8,128)(2,1)S(1)} collective-permute-done((bf16[1,96,128]{2,1,0:T(8,128)(2,1)S(1)}, bf16[1,96,128]{2,1,0:T(8,128)(2,1)S(1)}, u32[]{:S(2)}, u32[]{:S(2)}) %collective-permute-start.64) | collective-permute-done | bytes 24608 | tf_op jit(solution)/shard_map/ppermute | solution.py:450
  467.4 5.8 %collective-permute-start.72 = (bf16[48,6144]{1,0:T(8,128)(2,1)S(1)}, bf16[48,6144]{1,0:T(8,128)(2,1)S(1)}, u32[]{:S(2)}, u32[]{:S(2)}) collective-permute-start(bf16[48,6144]{1,0:T(8,128)(2,1)S(1)} %pad_maximum_fusion.16), channel_id=1, source_target_pairs={{8,16},{9,17},{10,18},{11,19},{12,20},{13,21},{14,22},{15,23},{16,... | collective-permute-start | bytes 1769480 | tf_op jit(solution)/shard_map/ppermute | solution.py:460
  473.2 2.8 collective-permute-done.68
  477.8 5.2 collective-permute-done.70
  483.1 3.9 collective-permute-done.72
  488.4 3.1 collective-permute-start.74
  492.1 5.2 %collective-permute-start.76 = (bf16[48,3200]{1,0:T(8,128)(2,1)S(1)}, bf16[48,3200]{1,0:T(8,128)(2,1)S(1)}, u32[]{:S(2)}, u32[]{:S(2)}) collective-permute-start(bf16[48,3200]{1,0:T(8,128)(2,1)S(1)} %pad_maximum_fusion.17), channel_id=1, source_target_pairs={{8,16},{9,17},{10,18},{11,19},{12,20},{13,21},{14,22},{15,23},{16,... | collective-permute-start | bytes 921608 | tf_op jit(solution)/shard_map/ppermute | solution.py:460
  500.4 4.8 collective-permute-done.76
  508.8 2.7 select_bitcast_fusion
  (369 shorter events, 141.2 us)
Async XLA Ops:
  33.9 20.2 %collective-permute-start.8 = (bf16[2,48,3072]{2,1,0:T(8,128)(2,1)S(1)}, bf16[2,48,3072]{2,1,0:T(8,128)(2,1)S(1)}, u32[]{:S(2)}, u32[]{:S(2)}) collective-permute-start(bf16[2,48,3072]{2,1,0:T(8,128)(2,1)S(1)} %pad_maximum_fusion.10), channel_id=1, source_target_pairs={{0,2},{1,3},{2,0},{3,1},{4,6},{5,7},{6,4},{7,5},{8,10},{9,11},{10,... | collective-permute-start | bytes 1769480 | tf_op jit(solution)/shard_map/ppermute | solution.py:450
  34.2 19.8 %collective-permute-start.9 = (bf16[2,48,3072]{2,1,0:T(8,128)(2,1)S(1)}, bf16[2,48,3072]{2,1,0:T(8,128)(2,1)S(1)}, u32[]{:S(2)}, u32[]{:S(2)}) collective-permute-start(bf16[2,48,3072]{2,1,0:T(8,128)(2,1)S(1)} %pad_maximum_fusion.11), channel_id=1, source_target_pairs={{0,4},{1,5},{2,6},{3,7},{4,0},{5,1},{6,2},{7,3},{8,12},{9,13},{10,... | collective-permute-start | bytes 1769480 | tf_op jit(solution)/shard_map/ppermute | solution.py:450
  35.4 19.3 %collective-permute-start.11 = (bf16[48,6144]{1,0:T(8,128)(2,1)S(1)}, bf16[48,6144]{1,0:T(8,128)(2,1)S(1)}, u32[]{:S(2)}, u32[]{:S(2)}) collective-permute-start(bf16[48,6144]{1,0:T(8,128)(2,1)S(1)} %slice.541), channel_id=1, source_target_pairs={{8,16},{9,17},{10,18},{11,19},{12,20},{13,21},{14,22},{15,23},{16,... | collective-permute-start | bytes 1769480 | tf_op jit(solution)/shard_map/ppermute | solution.py:460
  54.8 16.4 %collective-permute-start.12 = (bf16[1,2,2,16,128]{4,3,2,1,0:T(8,128)(2,1)S(1)}, bf16[1,2,2,16,128]{4,3,2,1,0:T(8,128)(2,1)S(1)}, u32[]{:S(2)}, u32[]{:S(2)}) collective-permute-start(bf16[1,2,2,16,128]{4,3,2,1,0:T(8,128)(2,1)S(1)} %maximum_bitcast_fusion.3), channel_id=1, source_target_pairs={{0,1},{1,0},{2,3},{3,2},{4,5},{5,4},{6,7},{7,6},{8,9},{9,8},{10,11... | collective-permute-start | bytes 49160 | tf_op jit(solution)/shard_map/ppermute | solution.py:450
  55.8 16.0 %collective-permute-start.13 = (bf16[48,9216]{1,0:T(8,128)(2,1)S(1)}, bf16[48,9216]{1,0:T(8,128)(2,1)S(1)}, u32[]{:S(2)}, u32[]{:S(2)}) collective-permute-start(bf16[48,9216]{1,0:T(8,128)(2,1)S(1)} %get-tuple-element.172), channel_id=1, source_target_pairs={{8,0},{9,1},{10,2},{11,3},{12,4},{13,5},{14,6},{15,7},{16,24},{17,... | collective-permute-start | bytes 2654216 | tf_op jit(solution)/shard_map/ppermute | solution.py:460
  57.1 28.3 %collective-permute-start.14 = (bf16[4,48,3072]{2,1,0:T(8,128)(2,1)S(1)}, bf16[4,48,3072]{2,1,0:T(8,128)(2,1)S(1)}, u32[]{:S(2)}, u32[]{:S(2)}) collective-permute-start(bf16[4,48,3072]{2,1,0:T(8,128)(2,1)S(1)} %pad_maximum_fusion.2.refs_3_), channel_id=1, source_target_pairs={{0,4},{1,5},{2,6},{3,7},{4,0},{5,1},{6,2},{7,3},{8,12},{9,13},{10,... | collective-permute-start | bytes 3538952 | tf_op jit(solution)/shard_map/ppermute | solution.py:450
  66.4 19.0 %collective-permute-start.15 = (bf16[4,48,3072]{2,1,0:T(8,128)(2,1)S(1)}, bf16[4,48,3072]{2,1,0:T(8,128)(2,1)S(1)}, u32[]{:S(2)}, u32[]{:S(2)}) collective-permute-start(bf16[4,48,3072]{2,1,0:T(8,128)(2,1)S(1)} %pad_maximum_fusion.3.refs_7_), channel_id=1, source_target_pairs={{0,1},{1,0},{2,3},{3,2},{4,5},{5,4},{6,7},{7,6},{8,9},{9,8},{10,11... | collective-permute-start | bytes 3538952 | tf_op jit(solution)/shard_map/ppermute | solution.py:450
  66.5 18.9 %collective-permute-start.16 = (bf16[4,48,3072]{2,1,0:T(8,128)(2,1)S(1)}, bf16[4,48,3072]{2,1,0:T(8,128)(2,1)}, u32[]{:S(2)}, u32[]{:S(2)}) collective-permute-start(bf16[4,48,3072]{2,1,0:T(8,128)(2,1)S(1)} %pad_maximum_fusion.4.refs_11_), channel_id=1, source_target_pairs={{0,2},{1,3},{2,0},{3,1},{4,6},{5,7},{6,4},{7,5},{8,10},{9,11},{10,... | collective-permute-start | bytes 3538952 | tf_op jit(solution)/shard_map/ppermute | solution.py:450
  85.4 14.0 %collective-permute-start.21 = (bf16[4,48,9216]{2,1,0:T(8,128)(2,1)}, bf16[4,48,9216]{2,1,0:T(8,128)(2,1)}, u32[]{:S(2)}, u32[]{:S(2)}) collective-permute-start(bf16[4,48,9216]{2,1,0:T(8,128)(2,1)} %maximum_maximum_fusion), channel_id=1, source_target_pairs={{0,16},{16,0},{1,17},{17,1},{2,18},{18,2},{3,19},{19,3},{4,20},{20... | collective-permute-start | bytes 10616840 | tf_op jit(solution)/shard_map/ppermute | solution.py:454
  99.4 32.8 %collective-permute-start.26 = (bf16[4,48,9216]{2,1,0:T(8,128)(2,1)S(1)}, bf16[4,48,9216]{2,1,0:T(8,128)(2,1)}, u32[]{:S(2)}, u32[]{:S(2)}) collective-permute-start(bf16[4,48,9216]{2,1,0:T(8,128)(2,1)S(1)} %pad_maximum_fusion), channel_id=1, source_target_pairs={{0,16},{16,0},{1,17},{17,1},{2,18},{18,2},{3,19},{19,3},{4,20},{20... | collective-permute-start | bytes 10616840 | tf_op jit(solution)/shard_map/ppermute | solution.py:454
  100.6 14.9 %collective-permute-start.24 = (bf16[2,48,3072]{2,1,0:T(8,128)(2,1)S(1)}, bf16[2,48,3072]{2,1,0:T(8,128)(2,1)S(1)}, u32[]{:S(2)}, u32[]{:S(2)}) collective-permute-start(bf16[2,48,3072]{2,1,0:T(8,128)(2,1)S(1)} %pad_maximum_fusion.15), channel_id=1, source_target_pairs={{0,1},{1,0},{2,3},{3,2},{4,5},{5,4},{6,7},{7,6},{8,9},{9,8},{10,11... | collective-permute-start | bytes 1769480 | tf_op jit(solution)/shard_map/ppermute | solution.py:450
  101.2 24.2 %collective-permute-start.23 = (bf16[2,48,3072]{2,1,0:T(8,128)(2,1)S(1)}, bf16[2,48,3072]{2,1,0:T(8,128)(2,1)S(1)}, u32[]{:S(2)}, u32[]{:S(2)}) collective-permute-start(bf16[2,48,3072]{2,1,0:T(8,128)(2,1)S(1)} %pad_maximum_fusion.14), channel_id=1, source_target_pairs={{0,4},{1,5},{2,6},{3,7},{4,0},{5,1},{6,2},{7,3},{8,12},{9,13},{10,... | collective-permute-start | bytes 1769480 | tf_op jit(solution)/shard_map/ppermute | solution.py:450
  101.3 25.4 %collective-permute-start.22 = (bf16[2,48,3072]{2,1,0:T(8,128)(2,1)S(1)}, bf16[2,48,3072]{2,1,0:T(8,128)(2,1)S(1)}, u32[]{:S(2)}, u32[]{:S(2)}) collective-permute-start(bf16[2,48,3072]{2,1,0:T(8,128)(2,1)S(1)} %pad_maximum_fusion.13), channel_id=1, source_target_pairs={{0,2},{1,3},{2,0},{3,1},{4,6},{5,7},{6,4},{7,5},{8,10},{9,11},{10,... | collective-permute-start | bytes 1769480 | tf_op jit(solution)/shard_map/ppermute | solution.py:450
  102.7 29.5 %collective-permute-start.25 = (bf16[4,160,768]{2,1,0:T(8,128)(2,1)S(1)}, bf16[4,160,768]{2,1,0:T(8,128)(2,1)}, u32[]{:S(2)}, u32[]{:S(2)}) collective-permute-start(bf16[4,160,768]{2,1,0:T(8,128)(2,1)S(1)} %broadcast_select_fusion), channel_id=1, source_target_pairs={{0,8},{1,9},{2,10},{3,11},{4,12},{5,13},{6,14},{7,15},{24,16},{25,... | collective-permute-start | bytes 2949128 | tf_op jit(solution)/shard_map/ppermute | solution.py:460
  132.2 31.8 %collective-permute-start.31 = (bf16[4,48,9216]{2,1,0:T(8,128)(2,1)}, bf16[4,48,9216]{2,1,0:T(8,128)(2,1)}, u32[]{:S(2)}, u32[]{:S(2)}) collective-permute-start(bf16[4,48,9216]{2,1,0:T(8,128)(2,1)} %maximum_maximum_fusion.1), channel_id=1, source_target_pairs={{0,16},{16,0},{1,17},{17,1},{2,18},{18,2},{3,19},{19,3},{4,20},{20... | collective-permute-start | bytes 10616840 | tf_op jit(solution)/shard_map/ppermute | solution.py:454
  132.4 31.5 %collective-permute-start.28 = (bf16[4,48,3072]{2,1,0:T(8,128)(2,1)}, bf16[4,48,3072]{2,1,0:T(8,128)(2,1)}, u32[]{:S(2)}, u32[]{:S(2)}) collective-permute-start(bf16[4,48,3072]{2,1,0:T(8,128)(2,1)} %pad_maximum_fusion.5.refs_5_), channel_id=1, source_target_pairs={{0,4},{1,5},{2,6},{3,7},{4,0},{5,1},{6,2},{7,3},{8,12},{9,13},{10,... | collective-permute-start | bytes 3538952 | tf_op jit(solution)/shard_map/ppermute | solution.py:450
  134.3 29.6 %collective-permute-start.29 = (bf16[4,48,3072]{2,1,0:T(8,128)(2,1)}, bf16[4,48,3072]{2,1,0:T(8,128)(2,1)}, u32[]{:S(2)}, u32[]{:S(2)}) collective-permute-start(bf16[4,48,3072]{2,1,0:T(8,128)(2,1)} %pad_maximum_fusion.6.refs_9_), channel_id=1, source_target_pairs={{0,1},{1,0},{2,3},{3,2},{4,5},{5,4},{6,7},{7,6},{8,9},{9,8},{10,11... | collective-permute-start | bytes 3538952 | tf_op jit(solution)/shard_map/ppermute | solution.py:450
  134.7 29.3 %collective-permute-start.30 = (bf16[4,48,3072]{2,1,0:T(8,128)(2,1)}, bf16[4,48,3072]{2,1,0:T(8,128)(2,1)}, u32[]{:S(2)}, u32[]{:S(2)}) collective-permute-start(bf16[4,48,3072]{2,1,0:T(8,128)(2,1)} %pad_maximum_fusion.7.refs_13_), channel_id=1, source_target_pairs={{0,2},{1,3},{2,0},{3,1},{4,6},{5,7},{6,4},{7,5},{8,10},{9,11},{10,... | collective-permute-start | bytes 3538952 | tf_op jit(solution)/shard_map/ppermute | solution.py:450
  136.2 25.8 %collective-permute-start.27 = (bf16[4,2,2,16,128]{4,3,2,1,0:T(8,128)(2,1)S(1)}, bf16[4,2,2,16,128]{4,3,2,1,0:T(8,128)(2,1)S(1)}, u32[]{:S(2)}, u32[]{:S(2)}) collective-permute-start(bf16[4,2,2,16,128]{4,3,2,1,0:T(8,128)(2,1)S(1)} %pad_maximum_fusion.20), channel_id=1, source_target_pairs={{0,4},{1,5},{2,6},{3,7},{4,0},{5,1},{6,2},{7,3},{8,12},{9,13},{10,... | collective-permute-start | bytes 196616 | tf_op jit(solution)/shard_map/ppermute | solution.py:450
  181.2 34.7 %collective-permute-start.35 = (bf16[1,160,768]{2,1,0:T(8,128)(2,1)S(1)}, bf16[1,160,768]{2,1,0:T(8,128)(2,1)S(1)}, u32[]{:S(2)}, u32[]{:S(2)}) collective-permute-start(bf16[1,160,768]{2,1,0:T(8,128)(2,1)S(1)} %layer_fwd.4), channel_id=1, source_target_pairs={{0,8},{1,9},{2,10},{3,11},{4,12},{5,13},{6,14},{7,15},{16,24},{17,... | collective-permute-start | bytes 737288 | tf_op jit(solution)/shard_map/ppermute | solution.py:460
  192.9 30.6 %collective-permute-start.36 = (bf16[1,160,768]{2,1,0:T(8,128)(2,1)S(1)}, bf16[1,160,768]{2,1,0:T(8,128)(2,1)S(1)}, u32[]{:S(2)}, u32[]{:S(2)}) collective-permute-start(bf16[1,160,768]{2,1,0:T(8,128)(2,1)S(1)} %layer_fwd.5), channel_id=1, source_target_pairs={{0,8},{1,9},{2,10},{3,11},{4,12},{5,13},{6,14},{7,15},{16,24},{17,... | collective-permute-start | bytes 737288 | tf_op jit(solution)/shard_map/ppermute | solution.py:460
  204.2 30.5 %collective-permute-start.37 = (bf16[1,160,768]{2,1,0:T(8,128)(2,1)S(1)}, bf16[1,160,768]{2,1,0:T(8,128)(2,1)S(1)}, u32[]{:S(2)}, u32[]{:S(2)}) collective-permute-start(bf16[1,160,768]{2,1,0:T(8,128)(2,1)S(1)} %layer_fwd.6), channel_id=1, source_target_pairs={{0,8},{1,9},{2,10},{3,11},{4,12},{5,13},{6,14},{7,15},{16,24},{17,... | collective-permute-start | bytes 737288 | tf_op jit(solution)/shard_map/ppermute | solution.py:460
  217.3 17.4 %collective-permute-start.38 = (bf16[1,160,768]{2,1,0:T(8,128)(2,1)S(1)}, bf16[1,160,768]{2,1,0:T(8,128)(2,1)S(1)}, u32[]{:S(2)}, u32[]{:S(2)}) collective-permute-start(bf16[1,160,768]{2,1,0:T(8,128)(2,1)S(1)} %get-tuple-element.198), channel_id=1, source_target_pairs={{8,0},{9,1},{10,2},{11,3},{12,4},{13,5},{14,6},{15,7},{24,16},{25,... | collective-permute-start | bytes 737288 | tf_op jit(solution)/shard_map/ppermute | solution.py:460
  218.6 36.5 %collective-permute-start.39 = (bf16[1,160,768]{2,1,0:T(8,128)(2,1)S(1)}, bf16[1,160,768]{2,1,0:T(8,128)(2,1)S(1)}, u32[]{:S(2)}, u32[]{:S(2)}) collective-permute-start(bf16[1,160,768]{2,1,0:T(8,128)(2,1)S(1)} %layer_fwd.7), channel_id=1, source_target_pairs={{0,8},{1,9},{2,10},{3,11},{4,12},{5,13},{6,14},{7,15},{16,24},{17,... | collective-permute-start | bytes 737288 | tf_op jit(solution)/shard_map/ppermute | solution.py:460
  233.4 21.7 %collective-permute-start.40 = (bf16[1,160,768]{2,1,0:T(8,128)(2,1)S(1)}, bf16[1,160,768]{2,1,0:T(8,128)(2,1)S(1)}, u32[]{:S(2)}, u32[]{:S(2)}) collective-permute-start(bf16[1,160,768]{2,1,0:T(8,128)(2,1)S(1)} %get-tuple-element.207), channel_id=1, source_target_pairs={{8,0},{9,1},{10,2},{11,3},{12,4},{13,5},{14,6},{15,7},{24,16},{25,... | collective-permute-start | bytes 737288 | tf_op jit(solution)/shard_map/ppermute | solution.py:460
  253.8 22.9 %collective-permute-start.42 = (bf16[1,160,768]{2,1,0:T(8,128)(2,1)}, bf16[1,160,768]{2,1,0:T(8,128)(2,1)}, u32[]{:S(2)}, u32[]{:S(2)}) collective-permute-start(bf16[1,160,768]{2,1,0:T(8,128)(2,1)} %get-tuple-element.216), channel_id=1, source_target_pairs={{8,0},{9,1},{10,2},{11,3},{12,4},{13,5},{14,6},{15,7},{24,16},{25,... | collective-permute-start | bytes 737288 | tf_op jit(solution)/shard_map/ppermute | solution.py:460
  274.4 21.9 %collective-permute-start.41 = (bf16[1,160,768]{2,1,0:T(8,128)(2,1)}, bf16[1,160,768]{2,1,0:T(8,128)(2,1)S(1)}, u32[]{:S(2)}, u32[]{:S(2)}) collective-permute-start(bf16[1,160,768]{2,1,0:T(8,128)(2,1)} %get-tuple-element.225), channel_id=1, source_target_pairs={{8,0},{9,1},{10,2},{11,3},{12,4},{13,5},{14,6},{15,7},{24,16},{25,... | collective-permute-start | bytes 737288 | tf_op jit(solution)/shard_map/ppermute | solution.py:460
  324.0 32.5 %collective-permute-start.47 = (bf16[8,48,3072]{2,1,0:T(8,128)(2,1)}, bf16[8,48,3072]{2,1,0:T(8,128)(2,1)}, u32[]{:S(2)}, u32[]{:S(2)}) collective-permute-start(bf16[8,48,3072]{2,1,0:T(8,128)(2,1)} %get-tuple-element.251), channel_id=1, source_target_pairs={{0,16},{16,0},{1,17},{17,1},{2,18},{18,2},{3,19},{19,3},{4,20},{20... | collective-permute-start | bytes 7077896 | tf_op jit(solution)/shard_map/ppermute | solution.py:454
  332.6 26.5 %collective-permute-start.46 = (bf16[8,48,3072]{2,1,0:T(8,128)(2,1)}, bf16[8,48,3072]{2,1,0:T(8,128)(2,1)}, u32[]{:S(2)}, u32[]{:S(2)}) collective-permute-start(bf16[8,48,3072]{2,1,0:T(8,128)(2,1)} %get-tuple-element.249), channel_id=1, source_target_pairs={{0,16},{16,0},{1,17},{17,1},{2,18},{18,2},{3,19},{19,3},{4,20},{20... | collective-permute-start | bytes 7077896 | tf_op jit(solution)/shard_map/ppermute | solution.py:454
  332.8 31.1 %collective-permute-start.44 = (bf16[4,160,768]{2,1,0:T(8,128)(2,1)S(1)}, bf16[4,160,768]{2,1,0:T(8,128)(2,1)}, u32[]{:S(2)}, u32[]{:S(2)}) collective-permute-start(bf16[4,160,768]{2,1,0:T(8,128)(2,1)S(1)} %get-tuple-element.242), channel_id=1, source_target_pairs={{0,16},{16,8},{1,17},{17,9},{2,18},{18,10},{3,19},{19,11},{4,20},{... | collective-permute-start | bytes 2949128 | tf_op jit(solution)/shard_map/ppermute | solution.py:460
  334.7 29.2 %collective-permute-start.43 = (bf16[4,160,768]{2,1,0:T(8,128)(2,1)S(1)}, bf16[4,160,768]{2,1,0:T(8,128)(2,1)}, u32[]{:S(2)}, u32[]{:S(2)}) collective-permute-start(bf16[4,160,768]{2,1,0:T(8,128)(2,1)S(1)} %get-tuple-element.242), channel_id=1, source_target_pairs={{24,8},{8,16},{25,9},{9,17},{26,10},{10,18},{27,11},{11,19},{28,12... | collective-permute-start | bytes 2949128 | tf_op jit(solution)/shard_map/ppermute | solution.py:460
  363.8 23.5 %collective-permute-start.48 = (bf16[8,96,128]{2,1,0:T(8,128)(2,1)S(1)}, bf16[8,96,128]{2,1,0:T(8,128)(2,1)}, u32[]{:S(2)}, u32[]{:S(2)}) collective-permute-start(bf16[8,96,128]{2,1,0:T(8,128)(2,1)S(1)} %bitcast.188), channel_id=1, source_target_pairs={{0,16},{16,0},{1,17},{17,1},{2,18},{18,2},{3,19},{19,3},{4,20},{20... | collective-permute-start | bytes 589832 | tf_op jit(solution)/shard_map/ppermute | solution.py:454
  363.9 27.5 %collective-permute-start.49 = (bf16[4,48,3072]{2,1,0:T(8,128)(2,1)}, bf16[4,48,3072]{2,1,0:T(8,128)(2,1)}, u32[]{:S(2)}, u32[]{:S(2)}) collective-permute-start(bf16[4,48,3072]{2,1,0:T(8,128)(2,1)} %add_convert_fusion.11), channel_id=1, source_target_pairs={{0,1},{1,0},{2,3},{3,2},{4,5},{5,4},{6,7},{7,6},{8,9},{9,8},{10,11... | collective-permute-start | bytes 3538952 | tf_op jit(solution)/shard_map/ppermute | solution.py:450
  364.3 28.7 %collective-permute-start.50 = (bf16[4,48,3072]{2,1,0:T(8,128)(2,1)S(1)}, bf16[4,48,3072]{2,1,0:T(8,128)(2,1)}, u32[]{:S(2)}, u32[]{:S(2)}) collective-permute-start(bf16[4,48,3072]{2,1,0:T(8,128)(2,1)S(1)} %add_convert_fusion.10), channel_id=1, source_target_pairs={{0,2},{1,3},{2,0},{3,1},{4,6},{5,7},{6,4},{7,5},{8,10},{9,11},{10,... | collective-permute-start | bytes 3538952 | tf_op jit(solution)/shard_map/ppermute | solution.py:450
  367.3 27.6 %collective-permute-start.51 = (bf16[4,48,3072]{2,1,0:T(8,128)(2,1)S(1)}, bf16[4,48,3072]{2,1,0:T(8,128)(2,1)}, u32[]{:S(2)}, u32[]{:S(2)}) collective-permute-start(bf16[4,48,3072]{2,1,0:T(8,128)(2,1)S(1)} %add_convert_fusion.9), channel_id=1, source_target_pairs={{0,4},{1,5},{2,6},{3,7},{4,0},{5,1},{6,2},{7,3},{8,12},{9,13},{10,... | collective-permute-start | bytes 3538952 | tf_op jit(solution)/shard_map/ppermute | solution.py:450
  367.3 29.4 %collective-permute-start.52 = (bf16[8,48,3072]{2,1,0:T(8,128)(2,1)}, bf16[8,48,3072]{2,1,0:T(8,128)(2,1)S(1)}, u32[]{:S(2)}, u32[]{:S(2)}) collective-permute-start(bf16[8,48,3072]{2,1,0:T(8,128)(2,1)} %get-tuple-element.268), channel_id=1, source_target_pairs={{0,16},{16,0},{1,17},{17,1},{2,18},{18,2},{3,19},{19,3},{4,20},{20... | collective-permute-start | bytes 7077896 | tf_op jit(solution)/shard_map/ppermute | solution.py:454
  397.4 14.8 %collective-permute-start.54 = (bf16[2,48,3072]{2,1,0:T(8,128)(2,1)S(1)}, bf16[2,48,3072]{2,1,0:T(8,128)(2,1)S(1)}, u32[]{:S(2)}, u32[]{:S(2)}) collective-permute-start(bf16[2,48,3072]{2,1,0:T(8,128)(2,1)S(1)} %get-tuple-element.270), channel_id=1, source_target_pairs={{0,2},{1,3},{2,0},{3,1},{4,6},{5,7},{6,4},{7,5},{8,10},{9,11},{10,... | collective-permute-start | bytes 1769480 | tf_op jit(solution)/shard_map/ppermute | solution.py:450
  400.1 13.0 %collective-permute-start.55 = (bf16[2,48,3072]{2,1,0:T(8,128)(2,1)S(1)}, bf16[2,48,3072]{2,1,0:T(8,128)(2,1)S(1)}, u32[]{:S(2)}, u32[]{:S(2)}) collective-permute-start(bf16[2,48,3072]{2,1,0:T(8,128)(2,1)S(1)} %get-tuple-element.271), channel_id=1, source_target_pairs={{0,4},{1,5},{2,6},{3,7},{4,0},{5,1},{6,2},{7,3},{8,12},{9,13},{10,... | collective-permute-start | bytes 1769480 | tf_op jit(solution)/shard_map/ppermute | solution.py:450
  400.1 13.1 %collective-permute-start.56 = (bf16[2,48,3072]{2,1,0:T(8,128)(2,1)S(1)}, bf16[2,48,3072]{2,1,0:T(8,128)(2,1)S(1)}, u32[]{:S(2)}, u32[]{:S(2)}) collective-permute-start(bf16[2,48,3072]{2,1,0:T(8,128)(2,1)S(1)} %get-tuple-element.272), channel_id=1, source_target_pairs={{0,1},{1,0},{2,3},{3,2},{4,5},{5,4},{6,7},{7,6},{8,9},{9,8},{10,11... | collective-permute-start | bytes 1769480 | tf_op jit(solution)/shard_map/ppermute | solution.py:450
  425.7 36.4 %collective-permute-start.63 = (bf16[4,48,3072]{2,1,0:T(8,128)(2,1)S(1)}, bf16[4,48,3072]{2,1,0:T(8,128)(2,1)S(1)}, u32[]{:S(2)}, u32[]{:S(2)}) collective-permute-start(bf16[4,48,3072]{2,1,0:T(8,128)(2,1)S(1)} %get-tuple-element.281), channel_id=1, source_target_pairs={{0,4},{1,5},{2,6},{3,7},{4,0},{5,1},{6,2},{7,3},{8,12},{9,13},{10,... | collective-permute-start | bytes 3538952 | tf_op jit(solution)/shard_map/ppermute | solution.py:450
  425.8 36.2 %collective-permute-start.64 = (bf16[1,96,128]{2,1,0:T(8,128)(2,1)S(1)}, bf16[1,96,128]{2,1,0:T(8,128)(2,1)S(1)}, u32[]{:S(2)}, u32[]{:S(2)}) collective-permute-start(bf16[1,96,128]{2,1,0:T(8,128)(2,1)S(1)} %add_convert_fusion.43), channel_id=1, source_target_pairs={{0,4},{1,5},{2,6},{3,7},{4,0},{5,1},{6,2},{7,3},{8,12},{9,13},{10,... | collective-permute-start | bytes 73736 | tf_op jit(solution)/shard_map/ppermute | solution.py:450
  427.2 36.0 %collective-permute-start.67 = (bf16[48,9216]{1,0:T(8,128)(2,1)S(1)}, bf16[48,9216]{1,0:T(8,128)(2,1)S(1)}, u32[]{:S(2)}, u32[]{:S(2)}) collective-permute-start(bf16[48,9216]{1,0:T(8,128)(2,1)S(1)} %pad_maximum_fusion.9), channel_id=1, source_target_pairs={{0,8},{1,9},{2,10},{3,11},{4,12},{5,13},{6,14},{7,15},{24,16},{25,... | collective-permute-start | bytes 2654216 | tf_op jit(solution)/shard_map/ppermute | solution.py:460
  428.8 33.6 %collective-permute-start.65 = (bf16[4,48,3072]{2,1,0:T(8,128)(2,1)S(1)}, bf16[4,48,3072]{2,1,0:T(8,128)(2,1)S(1)}, u32[]{:S(2)}, u32[]{:S(2)}) collective-permute-start(bf16[4,48,3072]{2,1,0:T(8,128)(2,1)S(1)} %get-tuple-element.283), channel_id=1, source_target_pairs={{0,1},{1,0},{2,3},{3,2},{4,5},{5,4},{6,7},{7,6},{8,9},{9,8},{10,11... | collective-permute-start | bytes 3538952 | tf_op jit(solution)/shard_map/ppermute | solution.py:450
  429.7 33.1 %collective-permute-start.66 = (bf16[4,48,3072]{2,1,0:T(8,128)(2,1)S(1)}, bf16[4,48,3072]{2,1,0:T(8,128)(2,1)S(1)}, u32[]{:S(2)}, u32[]{:S(2)}) collective-permute-start(bf16[4,48,3072]{2,1,0:T(8,128)(2,1)S(1)} %get-tuple-element.284), channel_id=1, source_target_pairs={{0,2},{1,3},{2,0},{3,1},{4,6},{5,7},{6,4},{7,5},{8,10},{9,11},{10,... | collective-permute-start | bytes 3538952 | tf_op jit(solution)/shard_map/ppermute | solution.py:450
  464.3 18.7 %collective-permute-start.71 = (bf16[48,128]{1,0:T(8,128)(2,1)S(1)}, bf16[48,128]{1,0:T(8,128)(2,1)S(1)}, u32[]{:S(2)}, u32[]{:S(2)}) collective-permute-start(bf16[48,128]{1,0:T(8,128)(2,1)S(1)} %get-tuple-element.289), channel_id=1, source_target_pairs={{0,8},{1,9},{2,10},{3,11},{4,12},{5,13},{6,14},{7,15},{24,16},{25,... | collective-permute-start | bytes 36872 | tf_op jit(solution)/shard_map/ppermute | solution.py:460
  465.7 17.3 %collective-permute-start.70 = (bf16[2,48,3072]{2,1,0:T(8,128)(2,1)S(1)}, bf16[2,48,3072]{2,1,0:T(8,128)(2,1)S(1)}, u32[]{:S(2)}, u32[]{:S(2)}) collective-permute-start(bf16[2,48,3072]{2,1,0:T(8,128)(2,1)S(1)} %get-tuple-element.288), channel_id=1, source_target_pairs={{0,4},{1,5},{2,6},{3,7},{4,0},{5,1},{6,2},{7,3},{8,12},{9,13},{10,... | collective-permute-start | bytes 1769480 | tf_op jit(solution)/shard_map/ppermute | solution.py:450
  467.4 19.6 %collective-permute-start.72 = (bf16[48,6144]{1,0:T(8,128)(2,1)S(1)}, bf16[48,6144]{1,0:T(8,128)(2,1)S(1)}, u32[]{:S(2)}, u32[]{:S(2)}) collective-permute-start(bf16[48,6144]{1,0:T(8,128)(2,1)S(1)} %pad_maximum_fusion.16), channel_id=1, source_target_pairs={{8,16},{9,17},{10,18},{11,19},{12,20},{13,21},{14,22},{15,23},{16,... | collective-permute-start | bytes 1769480 | tf_op jit(solution)/shard_map/ppermute | solution.py:460
  492.1 13.1 %collective-permute-start.76 = (bf16[48,3200]{1,0:T(8,128)(2,1)S(1)}, bf16[48,3200]{1,0:T(8,128)(2,1)S(1)}, u32[]{:S(2)}, u32[]{:S(2)}) collective-permute-start(bf16[48,3200]{1,0:T(8,128)(2,1)S(1)} %pad_maximum_fusion.17), channel_id=1, source_target_pairs={{8,16},{9,17},{10,18},{11,19},{12,20},{13,21},{14,22},{15,23},{16,... | collective-permute-start | bytes 921608 | tf_op jit(solution)/shard_map/ppermute | solution.py:460
  (79 other events, 931.8 us)

commit v6 on v5

--- a/solution.py
+++ b/solution.py
@@ -737,20 +737,18 @@
 
         keep, send = reduce_step(near_keep, near_got, 0)
         small_keep, small_send = reduce_step(small_keep, [small_got], 2)
-        small_got, *got, straight = wave(
-            one_bit(small_send[0], 2), *bits_out(send, 0), (far_sum, by(routes.straight_back))
+        small_got, *got, cross_a = wave(
+            one_bit(small_send[0], 2), *bits_out(send, 0), (far_sum[:, :WIDE], by(routes.crossed))
         )
         small_end = (small_keep[0][0].astype(F32) + small_got[0].astype(F32)).astype(BF16)
         keep, send = reduce_step(keep, got, 1)
-        small_straight, *got, cross_a = wave(
-            (small_end[ROWS:], by(routes.straight_back)),
-            *bits_out(send, 1),
-            (far_sum[:, : 2 * WIDE], by(routes.crossed)),
+        small_straight, *got, straight = wave(
+            (small_end[ROWS:], by(routes.straight_back)), *bits_out(send, 1), (far_sum, by(routes.straight_back))
         )
         keep, send = reduce_step(keep, got, 2)
         *got, cross_b = wave(
             *bits_out(send, 2),
-            (jnp.concatenate([far_sum[:, 2 * WIDE :], small_end[ROWS:]], -1), by(routes.crossed)),
+            (jnp.concatenate([far_sum[:, WIDE:], small_end[ROWS:]], -1), by(routes.crossed)),
         )
         near_sum = [a[0].astype(F32) + b[0].astype(F32) for a, b in zip(keep, got)] + [small_end[:ROWS].astype(F32)]
         (beside,) = wave((jnp.concatenate(near_sum, -1).astype(BF16), by(routes.away_to_home)))

time: 532 us -> 536 us (level)
  waiting for transfers between devices: 162 us -> 173 us
  starting transfers between devices: 113 us -> 104 us
    ppermute x42, starting transfers between devices: 49.5 us -> 40 us  [swap_bit(): return lax.ppermute(array, 'dp', [(i, i ^ 1 << bit) for i in range(count)])]
    ppermute x42, waiting for transfers between devices: 135 us -> 144 us  [swap_bit(): return lax.ppermute(array, 'dp', [(i, i ^ 1 << bit) for i in range(count)])]
    unnamed x107 -> x109, local copies, waits for them, and re-layouts: 12.1 us -> 12.1 us
  transfers between devices with their start and end apart: 78 -> 78, of which waited for: 29 -> 30; matrix products, arithmetic and copies ran while one was open for 10% -> 10% of each run, Pallas kernels for 25% -> 25%
where the time goes in v6:
time: 536 us; the launch traced here: 525 us
  waiting for transfers between devices  173 us (32%)
  Pallas kernels  169 us (32%)
  starting transfers between devices  104 us (19%)
  other arithmetic  56.5 us (11%)
  local copies, waits for them, and re-layouts  19.1 us (4%)
    ppermute x42, waiting for transfers between devices, swap_bit(): return lax.ppermute(array, 'dp', [(i, i ^ 1 << bit) for i in range(count)])  144 us
    pallas_call x10, Pallas kernels, layer_call(): pl.pallas_call(functools.partial(layer_kernel, back, slot, lead, count),...  128 us
    ppermute x23, starting transfers between devices, along(): return lax.ppermute(array, ('section', 'dp'), flat)  50.3 us
    pallas_call x6, Pallas kernels, grad_call(): pl.pallas_call(functools.partial(grad_kernel, unit, at), out_shape=[shape...  41.4 us
    ppermute x42, starting transfers between devices, swap_bit(): return lax.ppermute(array, 'dp', [(i, i ^ 1 << bit) for i in range(count)])  40 us
    ppermute x23, waiting for transfers between devices, along(): return lax.ppermute(array, ('section', 'dp'), flat)  22.3 us
    convert_element_type x24, other arithmetic, both(): return (first.astype(F32) + second.astype(F32)).astype(BF16)  21.7 us
    ppermute x13, starting transfers between devices, swap_section(): return lax.ppermute(array, 'section', [(0, 1), (1, 0)])  13.8 us
  transfers between devices with their start and end apart: 78, of which 30 were waited for; matrix products, arithmetic and copies ran while one was open for 10% of the time, Pallas kernels for 25%

profile of v6, /device:TPU:1, one launch (start us, length us, event | category | flops | bytes accessed | tf_op | source)
XLA Modules:
  0.0 524.9 jit_solution(17427183251606869148)
XLA Ops:
  12.5 4.6 collective-permute-start.5
  19.6 2.8 collective-permute-start.6
  22.5 2.5 collective-permute-done.3
  25.2 6.5 %collective-permute-done.6 = bf16[48,3072]{1,0:T(8,128)(2,1)S(1)} collective-permute-done((bf16[48,3072]{1,0:T(8,128)(2,1)S(1)}, bf16[48,3072]{1,0:T(8,128)(2,1)S(1)}, u32[]{:S(2)}, u32[]{:S(2)}) %collective-permute-start.6) | collective-permute-done | bytes 294944 | tf_op jit(solution)/shard_map/ppermute | solution.py:460
  35.4 3.5 collective-permute-start.11
  40.5 13.4 %collective-permute-done.9 = bf16[2,48,3072]{2,1,0:T(8,128)(2,1)S(1)} collective-permute-done((bf16[2,48,3072]{2,1,0:T(8,128)(2,1)S(1)}, bf16[2,48,3072]{2,1,0:T(8,128)(2,1)S(1)}, u32[]{:S(2)}, u32[]{:S(2)}) %collective-permute-start.9) | collective-permute-done | bytes 589856 | tf_op jit(solution)/shard_map/ppermute | solution.py:450
  57.1 9.3 %collective-permute-start.14 = (bf16[4,48,3072]{2,1,0:T(8,128)(2,1)S(1)}, bf16[4,48,3072]{2,1,0:T(8,128)(2,1)S(1)}, u32[]{:S(2)}, u32[]{:S(2)}) collective-permute-start(bf16[4,48,3072]{2,1,0:T(8,128)(2,1)S(1)} %pad_maximum_fusion.2.refs_3_), channel_id=1, source_target_pairs={{0,4},{1,5},{2,6},{3,7},{4,0},{5,1},{6,2},{7,3},{8,12},{9,13},{10,... | collective-permute-start | bytes 3538952 | tf_op jit(solution)/shard_map/ppermute | solution.py:450
  66.5 2.4 collective-permute-start.16
  68.8 2.3 maximum_maximum_fusion
  72.9 12.5 %collective-permute-done.14.refs_4_ = bf16[4,48,3072]{2,1,0:T(8,128)(2,1)S(1)} collective-permute-done((bf16[4,48,3072]{2,1,0:T(8,128)(2,1)S(1)}, bf16[4,48,3072]{2,1,0:T(8,128)(2,1)S(1)}, u32[]{:S(2)}, u32[]{:S(2)}) %collective-permute-start.14) | collective-permute-done | bytes 1179680 | tf_op jit(solution)/shard_map/ppermute | solution.py:450
  87.6 2.3 collective-permute-start.17
  92.3 6.9 %collective-permute-done.20 = bf16[1,48,3072]{2,1,0:T(8,128)(2,1)S(1)} collective-permute-done((bf16[1,48,3072]{2,1,0:T(8,128)(2,1)S(1)}, bf16[1,48,3072]{2,1,0:T(8,128)(2,1)S(1)}, u32[]{:S(2)}, u32[]{:S(2)}) %collective-permute-start.20) | collective-permute-done | bytes 294944 | tf_op jit(solution)/shard_map/ppermute | solution.py:450
  104.0 11.5 %collective-permute-done.24 = bf16[2,48,3072]{2,1,0:T(8,128)(2,1)S(1)} collective-permute-done((bf16[2,48,3072]{2,1,0:T(8,128)(2,1)S(1)}, bf16[2,48,3072]{2,1,0:T(8,128)(2,1)S(1)}, u32[]{:S(2)}, u32[]{:S(2)}) %collective-permute-start.24) | collective-permute-done | bytes 589856 | tf_op jit(solution)/shard_map/ppermute | solution.py:450
  116.6 8.8 %collective-permute-done.23 = bf16[2,48,3072]{2,1,0:T(8,128)(2,1)S(1)} collective-permute-done((bf16[2,48,3072]{2,1,0:T(8,128)(2,1)S(1)}, bf16[2,48,3072]{2,1,0:T(8,128)(2,1)S(1)}, u32[]{:S(2)}, u32[]{:S(2)}) %collective-permute-start.23) | collective-permute-done | bytes 589856 | tf_op jit(solution)/shard_map/ppermute | solution.py:450
  127.8 2.3 maximum_maximum_fusion.1
  137.7 2.3 broadcast_select_fusion.1
  140.0 22.0 %collective-permute-done.27 = bf16[4,2,2,16,128]{4,3,2,1,0:T(8,128)(2,1)S(1)} collective-permute-done((bf16[4,2,2,16,128]{4,3,2,1,0:T(8,128)(2,1)S(1)}, bf16[4,2,2,16,128]{4,3,2,1,0:T(8,128)(2,1)S(1)}, u32[]{:S(2)}, u32[]{:S(2)}) %collective-permute-start.27) | collective-permute-done | bytes 65568 | tf_op jit(solution)/shard_map/ppermute | solution.py:450
  171.0 9.9 %layer_fwd.4 = bf16[1,160,768]{2,1,0:T(8,128)(2,1)S(1)} custom-call(s32[62]{0:T(128)S(1)} %concatenate.122.refs_0_, f32[2,8,768]{2,1,0:T(8,128)S(1)} %constant_dynamic-update-slice_fusion.refs_1_, f32[2,1,3072]{2,1,0:T(1,128)S(1)} %constant_dynamic-update-slice_fusion.2.refs_2_, bf16[4,48,3072]{2,1,0:T(8,128)(2,1)S(1)} %pad_maximum_fusion.2.refs_3_, ...), custom_call_target="tpu_custom_call" | custom-call | flops 1 | bytes 1 | tf_op jit(solution)/shard_map/layer_fwd/pallas_call | solution.py:410
  182.6 10.1 %layer_fwd.5 = bf16[1,160,768]{2,1,0:T(8,128)(2,1)S(1)} custom-call(s32[62]{0:T(128)S(1)} %concatenate.122.refs_0_, f32[2,8,768]{2,1,0:T(8,128)S(1)} %constant_dynamic-update-slice_fusion.refs_1_, f32[2,1,3072]{2,1,0:T(1,128)S(1)} %constant_dynamic-update-slice_fusion.2.refs_2_, bf16[4,48,3072]{2,1,0:T(8,128)(2,1)S(1)} %pad_maximum_fusion.2.refs_3_, ...), custom_call_target="tpu_custom_call" | custom-call | flops 1 | bytes 1 | tf_op jit(solution)/shard_map/layer_fwd/pallas_call | solution.py:410
  194.1 9.9 %layer_fwd.6 = bf16[1,160,768]{2,1,0:T(8,128)(2,1)S(1)} custom-call(s32[62]{0:T(128)S(1)} %concatenate.122.refs_0_, f32[2,8,768]{2,1,0:T(8,128)S(1)} %constant_dynamic-update-slice_fusion.refs_1_, f32[2,1,3072]{2,1,0:T(1,128)S(1)} %constant_dynamic-update-slice_fusion.2.refs_2_, bf16[4,48,3072]{2,1,0:T(8,128)(2,1)S(1)} %pad_maximum_fusion.2.refs_3_, ...), custom_call_target="tpu_custom_call" | custom-call | flops 1 | bytes 1 | tf_op jit(solution)/shard_map/layer_fwd/pallas_call | solution.py:410
  205.3 10.1 %layer_fwd.7 = bf16[1,160,768]{2,1,0:T(8,128)(2,1)S(1)} custom-call(s32[62]{0:T(128)S(1)} %concatenate.122.refs_0_, f32[2,8,768]{2,1,0:T(8,128)S(1)} %constant_dynamic-update-slice_fusion.refs_1_, f32[2,1,3072]{2,1,0:T(1,128)S(1)} %constant_dynamic-update-slice_fusion.2.refs_2_, bf16[4,48,3072]{2,1,0:T(8,128)(2,1)S(1)} %pad_maximum_fusion.2.refs_3_, ...), custom_call_target="tpu_custom_call" | custom-call | flops 1 | bytes 1 | tf_op jit(solution)/shard_map/layer_fwd/pallas_call | solution.py:410
  218.2 4.9 collective-permute-start.39
  223.1 9.8 %layer_back.7 = (bf16[1,160,768]{2,1,0:T(8,128)(2,1)S(1)}, bf16[4,160,768]{2,1,0:T(8,128)(2,1)S(1)}, f32[4,160,768]{2,1,0:T(8,128)}, f32[4,8,768]{2,1,0:T(8,128)...) custom-call(s32[62]{0:T(128)S(1)} %concatenate.122.refs_0_, ...), custom_call_target="tpu_custom_call", output_to_operand_aliasing={{1}: (24, {}), {2}: (25, {}), {3}: (26, {}), {4}: (27, {}),... | custom-call | flops 1 | bytes 1 | tf_op jit(solution)/shard_map/layer_back/pallas_call | solution.py:410
  234.3 19.1 %layer_back.8 = (bf16[1,160,768]{2,1,0:T(8,128)(2,1)}, bf16[4,160,768]{2,1,0:T(8,128)(2,1)S(1)}, f32[4,160,768]{2,1,0:T(8,128)}, f32[4,8,768]{2,1,0:T(8,128)S(1)...) custom-call(s32[62]{0:T(128)S(1)} %concatenate.122.refs_0_, ...), custom_call_target="tpu_custom_call", output_to_operand_aliasing={{1}: (25, {}), {2}: (26, {}), {3}: (27, {}), {4}: (28, {}),... | custom-call | flops 1 | bytes 1 | tf_op jit(solution)/shard_map/layer_back/pallas_call | solution.py:410
  254.7 19.3 %layer_back.9 = (bf16[1,160,768]{2,1,0:T(8,128)(2,1)}, bf16[4,160,768]{2,1,0:T(8,128)(2,1)S(1)}, f32[4,160,768]{2,1,0:T(8,128)}, f32[4,8,768]{2,1,0:T(8,128)S(1)...) custom-call(s32[62]{0:T(128)S(1)} %concatenate.122.refs_0_, ...), custom_call_target="tpu_custom_call", output_to_operand_aliasing={{1}: (25, {}), {2}: (26, {}), {3}: (27, {}), {4}: (28, {}),... | custom-call | flops 1 | bytes 1 | tf_op jit(solution)/shard_map/layer_back/pallas_call | solution.py:410
  276.3 18.8 %layer_back.10 = (bf16[1,160,768]{2,1,0:T(8,128)(2,1)}, bf16[4,160,768]{2,1,0:T(8,128)(2,1)S(1)}, f32[4,160,768]{2,1,0:T(8,128)}, f32[4,8,768]{2,1,0:T(8,128)S(1...) custom-call(s32[62]{0:T(128)S(1)} %concatenate.122.refs_0_, ...), custom_call_target="tpu_custom_call", output_to_operand_aliasing={{1}: (23, {}), {2}: (24, {}), {3}: (25, {}), {4}: (26, {}),... | custom-call | flops 1 | bytes 1 | tf_op jit(solution)/shard_map/layer_back/pallas_call | solution.py:410
  295.1 19.2 %layer_back.11 = (bf16[1,160,768]{2,1,0:T(8,128)(2,1)}, bf16[4,160,768]{2,1,0:T(8,128)(2,1)S(1)}, f32[4,160,768]{2,1,0:T(8,128)}, f32[4,8,768]{2,1,0:T(8,128)S(1...) custom-call(s32[62]{0:T(128)S(1)} %concatenate.122.refs_0_, ...), custom_call_target="tpu_custom_call", output_to_operand_aliasing={{1}: (23, {}), {2}: (24, {}), {3}: (25, {}), {4}: (26, {}),... | custom-call | flops 1 | bytes 1 | tf_op jit(solution)/shard_map/layer_back/pallas_call | solution.py:410
  314.3 7.1 %layer_grad.8 = (bf16[8,48,3072]{2,1,0:T(8,128)(2,1)S(1)}, bf16[8,48,3072]{2,1,0:T(8,128)(2,1)}) custom-call(s32[31]{0:T(128)S(1)} %concatenate.139.meta, bf16[4,4,160,768]{3,2,1,0:T(8,128)(2,1)} %get-tuple-element.244.refs_0_.refs_1_, bf16[4,4,160,768]{3,2,1,0:T(8,128)(2,1)} %get-tuple-element.244.refs_0_.refs_1_, ...), custom_call_target="tpu_custom_call" | custom-call | flops 1 | bytes 1 | tf_op jit(solution)/shard_map/layer_grad/pallas_call | solution.py:431
  324.6 6.7 %layer_grad.7 = (bf16[8,48,3072]{2,1,0:T(8,128)(2,1)S(1)}, bf16[8,48,3072]{2,1,0:T(8,128)(2,1)}) custom-call(s32[31]{0:T(128)S(1)} %concatenate.139.meta, bf16[4,4,160,768]{3,2,1,0:T(8,128)(2,1)} %get-tuple-element.244.refs_0_.refs_1_, bf16[3,4,160,3072]{3,2,1,0:T(8,128)(2,1)} %get-tuple-element.245.refs_1_.refs_2_), custom_call_target="tpu_custom_call" | custom-call | flops 1 | bytes 1 | tf_op jit(solution)/shard_map/layer_grad/pallas_call | solution.py:431
  336.7 6.7 %layer_grad.6 = (bf16[8,48,3072]{2,1,0:T(8,128)(2,1)S(1)}, bf16[8,48,3072]{2,1,0:T(8,128)(2,1)}) custom-call(s32[31]{0:T(128)S(1)} %concatenate.139.meta, bf16[4,4,160,768]{3,2,1,0:T(8,128)(2,1)} %get-tuple-element.244.refs_0_.refs_1_, bf16[3,4,160,3072]{3,2,1,0:T(8,128)(2,1)} %get-tuple-element.245.refs_1_.refs_2_), custom_call_target="tpu_custom_call" | custom-call | flops 1 | bytes 1 | tf_op jit(solution)/shard_map/layer_grad/pallas_call | solution.py:431
  344.9 6.7 %layer_grad.11 = (bf16[8,48,3072]{2,1,0:T(8,128)(2,1)S(1)}, bf16[8,48,3072]{2,1,0:T(8,128)(2,1)}) custom-call(s32[31]{0:T(128)S(1)} %concatenate.139.meta, bf16[4,4,160,768]{3,2,1,0:T(8,128)(2,1)} %get-tuple-element.244.refs_0_.refs_1_, bf16[3,4,160,3072]{3,2,1,0:T(8,128)(2,1)} %get-tuple-element.245.refs_1_.refs_2_), custom_call_target="tpu_custom_call" | custom-call | flops 1 | bytes 1 | tf_op jit(solution)/shard_map/layer_grad/pallas_call | solution.py:431
  353.5 2.6 collective-permute-start.45
  362.5 2.7 add_convert_fusion.11
  372.0 7.0 %layer_grad.9 = (bf16[8,48,3072]{2,1,0:T(8,128)(2,1)S(1)}, bf16[8,48,3072]{2,1,0:T(8,128)(2,1)}) custom-call(s32[31]{0:T(128)S(1)} %concatenate.139.meta, bf16[4,4,160,768]{3,2,1,0:T(8,128)(2,1)} %get-tuple-element.244.refs_0_.refs_1_, bf16[3,4,160,3072]{3,2,1,0:T(8,128)(2,1)} %get-tuple-element.245.refs_1_.refs_2_), custom_call_target="tpu_custom_call" | custom-call | flops 1 | bytes 1 | tf_op jit(solution)/shard_map/layer_grad/pallas_call | solution.py:431
  378.9 7.1 %layer_grad.10 = (bf16[8,48,3072]{2,1,0:T(8,128)(2,1)S(1)}, bf16[8,48,3072]{2,1,0:T(8,128)(2,1)}) custom-call(s32[31]{0:T(128)S(1)} %concatenate.139.meta, bf16[4,4,160,768]{3,2,1,0:T(8,128)(2,1)} %get-tuple-element.244.refs_0_.refs_1_, bf16[4,4,160,768]{3,2,1,0:T(8,128)(2,1)} %get-tuple-element.244.refs_0_.refs_1_, ...), custom_call_target="tpu_custom_call" | custom-call | flops 1 | bytes 1 | tf_op jit(solution)/shard_map/layer_grad/pallas_call | solution.py:431
  387.1 5.6 %collective-permute-done.49 = bf16[4,48,3072]{2,1,0:T(8,128)(2,1)} collective-permute-done((bf16[4,48,3072]{2,1,0:T(8,128)(2,1)}, bf16[4,48,3072]{2,1,0:T(8,128)(2,1)}, u32[]{:S(2)}, u32[]{:S(2)}) %collective-permute-start.49) | collective-permute-done | bytes 1179680 | tf_op jit(solution)/shard_map/ppermute | solution.py:450
  402.5 9.5 %collective-permute-done.54 = bf16[2,48,3072]{2,1,0:T(8,128)(2,1)S(1)} collective-permute-done((bf16[2,48,3072]{2,1,0:T(8,128)(2,1)S(1)}, bf16[2,48,3072]{2,1,0:T(8,128)(2,1)S(1)}, u32[]{:S(2)}, u32[]{:S(2)}) %collective-permute-start.54) | collective-permute-done | bytes 589856 | tf_op jit(solution)/shard_map/ppermute | solution.py:450
  416.2 3.2 collective-permute-start.58
  426.1 6.7 %collective-permute-start.67 = (bf16[48,3072]{1,0:T(8,128)(2,1)S(1)}, bf16[48,3072]{1,0:T(8,128)(2,1)S(1)}, u32[]{:S(2)}, u32[]{:S(2)}) collective-permute-start(bf16[48,3072]{1,0:T(8,128)(2,1)S(1)} %fusion.4), channel_id=1, source_target_pairs={{8,16},{9,17},{10,18},{11,19},{12,20},{13,21},{14,22},{15,23},{16,... | collective-permute-start | bytes 884744 | tf_op jit(solution)/shard_map/ppermute | solution.py:460
  434.1 20.5 %collective-permute-done.63 = bf16[4,48,3072]{2,1,0:T(8,128)(2,1)S(1)} collective-permute-done((bf16[4,48,3072]{2,1,0:T(8,128)(2,1)S(1)}, bf16[4,48,3072]{2,1,0:T(8,128)(2,1)S(1)}, u32[]{:S(2)}, u32[]{:S(2)}) %collective-permute-start.63) | collective-permute-done | bytes 1179680 | tf_op jit(solution)/shard_map/ppermute | solution.py:450
  455.0 3.3 collective-permute-done.65
  464.9 9.6 %collective-permute-done.68 = bf16[2,48,3072]{2,1,0:T(8,128)(2,1)S(1)} collective-permute-done((bf16[2,48,3072]{2,1,0:T(8,128)(2,1)S(1)}, bf16[2,48,3072]{2,1,0:T(8,128)(2,1)S(1)}, u32[]{:S(2)}, u32[]{:S(2)}) %collective-permute-start.68) | collective-permute-done | bytes 589856 | tf_op jit(solution)/shard_map/ppermute | solution.py:450
  476.3 8.8 %collective-permute-done.70 = bf16[2,48,3072]{2,1,0:T(8,128)(2,1)S(1)} collective-permute-done((bf16[2,48,3072]{2,1,0:T(8,128)(2,1)S(1)}, bf16[2,48,3072]{2,1,0:T(8,128)(2,1)S(1)}, u32[]{:S(2)}, u32[]{:S(2)}) %collective-permute-start.70) | collective-permute-done | bytes 589856 | tf_op jit(solution)/shard_map/ppermute | solution.py:450
  485.2 2.6 collective-permute-done.72
  489.1 4.0 collective-permute-start.76
  493.1 3.5 collective-permute-done.73
  498.3 9.5 %collective-permute-done.76 = bf16[48,6272]{1,0:T(8,128)(2,1)S(1)} collective-permute-done((bf16[48,6272]{1,0:T(8,128)(2,1)S(1)}, bf16[48,6272]{1,0:T(8,128)(2,1)S(1)}, u32[]{:S(2)}, u32[]{:S(2)}) %collective-permute-start.76) | collective-permute-done | bytes 602144 | tf_op jit(solution)/shard_map/ppermute | solution.py:460
  511.4 2.7 select_bitcast_fusion
  (370 shorter events, 138.9 us)
Async XLA Ops:
  33.9 20.2 %collective-permute-start.8 = (bf16[2,48,3072]{2,1,0:T(8,128)(2,1)S(1)}, bf16[2,48,3072]{2,1,0:T(8,128)(2,1)S(1)}, u32[]{:S(2)}, u32[]{:S(2)}) collective-permute-start(bf16[2,48,3072]{2,1,0:T(8,128)(2,1)S(1)} %pad_maximum_fusion.11), channel_id=1, source_target_pairs={{0,2},{1,3},{2,0},{3,1},{4,6},{5,7},{6,4},{7,5},{8,10},{9,11},{10,... | collective-permute-start | bytes 1769480 | tf_op jit(solution)/shard_map/ppermute | solution.py:450
  34.2 19.8 %collective-permute-start.9 = (bf16[2,48,3072]{2,1,0:T(8,128)(2,1)S(1)}, bf16[2,48,3072]{2,1,0:T(8,128)(2,1)S(1)}, u32[]{:S(2)}, u32[]{:S(2)}) collective-permute-start(bf16[2,48,3072]{2,1,0:T(8,128)(2,1)S(1)} %pad_maximum_fusion.12), channel_id=1, source_target_pairs={{0,4},{1,5},{2,6},{3,7},{4,0},{5,1},{6,2},{7,3},{8,12},{9,13},{10,... | collective-permute-start | bytes 1769480 | tf_op jit(solution)/shard_map/ppermute | solution.py:450
  35.4 19.3 %collective-permute-start.11 = (bf16[48,6144]{1,0:T(8,128)(2,1)S(1)}, bf16[48,6144]{1,0:T(8,128)(2,1)S(1)}, u32[]{:S(2)}, u32[]{:S(2)}) collective-permute-start(bf16[48,6144]{1,0:T(8,128)(2,1)S(1)} %slice.537), channel_id=1, source_target_pairs={{8,16},{9,17},{10,18},{11,19},{12,20},{13,21},{14,22},{15,23},{16,... | collective-permute-start | bytes 1769480 | tf_op jit(solution)/shard_map/ppermute | solution.py:460
  54.8 16.3 %collective-permute-start.12 = (bf16[1,2,2,16,128]{4,3,2,1,0:T(8,128)(2,1)S(1)}, bf16[1,2,2,16,128]{4,3,2,1,0:T(8,128)(2,1)S(1)}, u32[]{:S(2)}, u32[]{:S(2)}) collective-permute-start(bf16[1,2,2,16,128]{4,3,2,1,0:T(8,128)(2,1)S(1)} %maximum_bitcast_fusion.3), channel_id=1, source_target_pairs={{0,1},{1,0},{2,3},{3,2},{4,5},{5,4},{6,7},{7,6},{8,9},{9,8},{10,11... | collective-permute-start | bytes 49160 | tf_op jit(solution)/shard_map/ppermute | solution.py:450
  55.8 16.0 %collective-permute-start.13 = (bf16[48,9216]{1,0:T(8,128)(2,1)S(1)}, bf16[48,9216]{1,0:T(8,128)(2,1)S(1)}, u32[]{:S(2)}, u32[]{:S(2)}) collective-permute-start(bf16[48,9216]{1,0:T(8,128)(2,1)S(1)} %get-tuple-element.172), channel_id=1, source_target_pairs={{8,0},{9,1},{10,2},{11,3},{12,4},{13,5},{14,6},{15,7},{16,24},{17,... | collective-permute-start | bytes 2654216 | tf_op jit(solution)/shard_map/ppermute | solution.py:460
  57.1 28.3 %collective-permute-start.14 = (bf16[4,48,3072]{2,1,0:T(8,128)(2,1)S(1)}, bf16[4,48,3072]{2,1,0:T(8,128)(2,1)S(1)}, u32[]{:S(2)}, u32[]{:S(2)}) collective-permute-start(bf16[4,48,3072]{2,1,0:T(8,128)(2,1)S(1)} %pad_maximum_fusion.2.refs_3_), channel_id=1, source_target_pairs={{0,4},{1,5},{2,6},{3,7},{4,0},{5,1},{6,2},{7,3},{8,12},{9,13},{10,... | collective-permute-start | bytes 3538952 | tf_op jit(solution)/shard_map/ppermute | solution.py:450
  66.4 19.0 %collective-permute-start.15 = (bf16[4,48,3072]{2,1,0:T(8,128)(2,1)S(1)}, bf16[4,48,3072]{2,1,0:T(8,128)(2,1)S(1)}, u32[]{:S(2)}, u32[]{:S(2)}) collective-permute-start(bf16[4,48,3072]{2,1,0:T(8,128)(2,1)S(1)} %pad_maximum_fusion.3.refs_7_), channel_id=1, source_target_pairs={{0,1},{1,0},{2,3},{3,2},{4,5},{5,4},{6,7},{7,6},{8,9},{9,8},{10,11... | collective-permute-start | bytes 3538952 | tf_op jit(solution)/shard_map/ppermute | solution.py:450
  66.5 18.9 %collective-permute-start.16 = (bf16[4,48,3072]{2,1,0:T(8,128)(2,1)S(1)}, bf16[4,48,3072]{2,1,0:T(8,128)(2,1)}, u32[]{:S(2)}, u32[]{:S(2)}) collective-permute-start(bf16[4,48,3072]{2,1,0:T(8,128)(2,1)S(1)} %pad_maximum_fusion.4.refs_11_), channel_id=1, source_target_pairs={{0,2},{1,3},{2,0},{3,1},{4,6},{5,7},{6,4},{7,5},{8,10},{9,11},{10,... | collective-permute-start | bytes 3538952 | tf_op jit(solution)/shard_map/ppermute | solution.py:450
  85.4 14.0 %collective-permute-start.21 = (bf16[4,48,9216]{2,1,0:T(8,128)(2,1)}, bf16[4,48,9216]{2,1,0:T(8,128)(2,1)}, u32[]{:S(2)}, u32[]{:S(2)}) collective-permute-start(bf16[4,48,9216]{2,1,0:T(8,128)(2,1)} %maximum_maximum_fusion), channel_id=1, source_target_pairs={{0,16},{16,0},{1,17},{17,1},{2,18},{18,2},{3,19},{19,3},{4,20},{20... | collective-permute-start | bytes 10616840 | tf_op jit(solution)/shard_map/ppermute | solution.py:454
  99.4 32.8 %collective-permute-start.26 = (bf16[4,48,9216]{2,1,0:T(8,128)(2,1)S(1)}, bf16[4,48,9216]{2,1,0:T(8,128)(2,1)}, u32[]{:S(2)}, u32[]{:S(2)}) collective-permute-start(bf16[4,48,9216]{2,1,0:T(8,128)(2,1)S(1)} %pad_maximum_fusion), channel_id=1, source_target_pairs={{0,16},{16,0},{1,17},{17,1},{2,18},{18,2},{3,19},{19,3},{4,20},{20... | collective-permute-start | bytes 10616840 | tf_op jit(solution)/shard_map/ppermute | solution.py:454
  100.6 14.9 %collective-permute-start.24 = (bf16[2,48,3072]{2,1,0:T(8,128)(2,1)S(1)}, bf16[2,48,3072]{2,1,0:T(8,128)(2,1)S(1)}, u32[]{:S(2)}, u32[]{:S(2)}) collective-permute-start(bf16[2,48,3072]{2,1,0:T(8,128)(2,1)S(1)} %pad_maximum_fusion.16), channel_id=1, source_target_pairs={{0,1},{1,0},{2,3},{3,2},{4,5},{5,4},{6,7},{7,6},{8,9},{9,8},{10,11... | collective-permute-start | bytes 1769480 | tf_op jit(solution)/shard_map/ppermute | solution.py:450
  101.2 24.2 %collective-permute-start.23 = (bf16[2,48,3072]{2,1,0:T(8,128)(2,1)S(1)}, bf16[2,48,3072]{2,1,0:T(8,128)(2,1)S(1)}, u32[]{:S(2)}, u32[]{:S(2)}) collective-permute-start(bf16[2,48,3072]{2,1,0:T(8,128)(2,1)S(1)} %pad_maximum_fusion.15), channel_id=1, source_target_pairs={{0,4},{1,5},{2,6},{3,7},{4,0},{5,1},{6,2},{7,3},{8,12},{9,13},{10,... | collective-permute-start | bytes 1769480 | tf_op jit(solution)/shard_map/ppermute | solution.py:450
  101.3 25.4 %collective-permute-start.22 = (bf16[2,48,3072]{2,1,0:T(8,128)(2,1)S(1)}, bf16[2,48,3072]{2,1,0:T(8,128)(2,1)S(1)}, u32[]{:S(2)}, u32[]{:S(2)}) collective-permute-start(bf16[2,48,3072]{2,1,0:T(8,128)(2,1)S(1)} %pad_maximum_fusion.14), channel_id=1, source_target_pairs={{0,2},{1,3},{2,0},{3,1},{4,6},{5,7},{6,4},{7,5},{8,10},{9,11},{10,... | collective-permute-start | bytes 1769480 | tf_op jit(solution)/shard_map/ppermute | solution.py:450
  102.7 29.5 %collective-permute-start.25 = (bf16[4,160,768]{2,1,0:T(8,128)(2,1)S(1)}, bf16[4,160,768]{2,1,0:T(8,128)(2,1)}, u32[]{:S(2)}, u32[]{:S(2)}) collective-permute-start(bf16[4,160,768]{2,1,0:T(8,128)(2,1)S(1)} %broadcast_select_fusion), channel_id=1, source_target_pairs={{0,8},{1,9},{2,10},{3,11},{4,12},{5,13},{6,14},{7,15},{24,16},{25,... | collective-permute-start | bytes 2949128 | tf_op jit(solution)/shard_map/ppermute | solution.py:460
  132.2 31.8 %collective-permute-start.31 = (bf16[4,48,9216]{2,1,0:T(8,128)(2,1)}, bf16[4,48,9216]{2,1,0:T(8,128)(2,1)}, u32[]{:S(2)}, u32[]{:S(2)}) collective-permute-start(bf16[4,48,9216]{2,1,0:T(8,128)(2,1)} %maximum_maximum_fusion.1), channel_id=1, source_target_pairs={{0,16},{16,0},{1,17},{17,1},{2,18},{18,2},{3,19},{19,3},{4,20},{20... | collective-permute-start | bytes 10616840 | tf_op jit(solution)/shard_map/ppermute | solution.py:454
  132.4 31.5 %collective-permute-start.28 = (bf16[4,48,3072]{2,1,0:T(8,128)(2,1)}, bf16[4,48,3072]{2,1,0:T(8,128)(2,1)}, u32[]{:S(2)}, u32[]{:S(2)}) collective-permute-start(bf16[4,48,3072]{2,1,0:T(8,128)(2,1)} %pad_maximum_fusion.5.refs_5_), channel_id=1, source_target_pairs={{0,4},{1,5},{2,6},{3,7},{4,0},{5,1},{6,2},{7,3},{8,12},{9,13},{10,... | collective-permute-start | bytes 3538952 | tf_op jit(solution)/shard_map/ppermute | solution.py:450
  134.3 29.6 %collective-permute-start.29 = (bf16[4,48,3072]{2,1,0:T(8,128)(2,1)}, bf16[4,48,3072]{2,1,0:T(8,128)(2,1)}, u32[]{:S(2)}, u32[]{:S(2)}) collective-permute-start(bf16[4,48,3072]{2,1,0:T(8,128)(2,1)} %pad_maximum_fusion.6.refs_9_), channel_id=1, source_target_pairs={{0,1},{1,0},{2,3},{3,2},{4,5},{5,4},{6,7},{7,6},{8,9},{9,8},{10,11... | collective-permute-start | bytes 3538952 | tf_op jit(solution)/shard_map/ppermute | solution.py:450
  134.7 29.3 %collective-permute-start.30 = (bf16[4,48,3072]{2,1,0:T(8,128)(2,1)}, bf16[4,48,3072]{2,1,0:T(8,128)(2,1)}, u32[]{:S(2)}, u32[]{:S(2)}) collective-permute-start(bf16[4,48,3072]{2,1,0:T(8,128)(2,1)} %pad_maximum_fusion.7.refs_13_), channel_id=1, source_target_pairs={{0,2},{1,3},{2,0},{3,1},{4,6},{5,7},{6,4},{7,5},{8,10},{9,11},{10,... | collective-permute-start | bytes 3538952 | tf_op jit(solution)/shard_map/ppermute | solution.py:450
  136.2 25.8 %collective-permute-start.27 = (bf16[4,2,2,16,128]{4,3,2,1,0:T(8,128)(2,1)S(1)}, bf16[4,2,2,16,128]{4,3,2,1,0:T(8,128)(2,1)S(1)}, u32[]{:S(2)}, u32[]{:S(2)}) collective-permute-start(bf16[4,2,2,16,128]{4,3,2,1,0:T(8,128)(2,1)S(1)} %pad_maximum_fusion.19), channel_id=1, source_target_pairs={{0,4},{1,5},{2,6},{3,7},{4,0},{5,1},{6,2},{7,3},{8,12},{9,13},{10,... | collective-permute-start | bytes 196616 | tf_op jit(solution)/shard_map/ppermute | solution.py:450
  181.0 34.5 %collective-permute-start.35 = (bf16[1,160,768]{2,1,0:T(8,128)(2,1)S(1)}, bf16[1,160,768]{2,1,0:T(8,128)(2,1)S(1)}, u32[]{:S(2)}, u32[]{:S(2)}) collective-permute-start(bf16[1,160,768]{2,1,0:T(8,128)(2,1)S(1)} %layer_fwd.4), channel_id=1, source_target_pairs={{0,8},{1,9},{2,10},{3,11},{4,12},{5,13},{6,14},{7,15},{16,24},{17,... | collective-permute-start | bytes 737288 | tf_op jit(solution)/shard_map/ppermute | solution.py:460
  192.7 30.4 %collective-permute-start.36 = (bf16[1,160,768]{2,1,0:T(8,128)(2,1)S(1)}, bf16[1,160,768]{2,1,0:T(8,128)(2,1)S(1)}, u32[]{:S(2)}, u32[]{:S(2)}) collective-permute-start(bf16[1,160,768]{2,1,0:T(8,128)(2,1)S(1)} %layer_fwd.5), channel_id=1, source_target_pairs={{0,8},{1,9},{2,10},{3,11},{4,12},{5,13},{6,14},{7,15},{16,24},{17,... | collective-permute-start | bytes 737288 | tf_op jit(solution)/shard_map/ppermute | solution.py:460
  204.0 30.3 %collective-permute-start.37 = (bf16[1,160,768]{2,1,0:T(8,128)(2,1)S(1)}, bf16[1,160,768]{2,1,0:T(8,128)(2,1)S(1)}, u32[]{:S(2)}, u32[]{:S(2)}) collective-permute-start(bf16[1,160,768]{2,1,0:T(8,128)(2,1)S(1)} %layer_fwd.6), channel_id=1, source_target_pairs={{0,8},{1,9},{2,10},{3,11},{4,12},{5,13},{6,14},{7,15},{16,24},{17,... | collective-permute-start | bytes 737288 | tf_op jit(solution)/shard_map/ppermute | solution.py:460
  216.9 17.4 %collective-permute-start.38 = (bf16[1,160,768]{2,1,0:T(8,128)(2,1)S(1)}, bf16[1,160,768]{2,1,0:T(8,128)(2,1)S(1)}, u32[]{:S(2)}, u32[]{:S(2)}) collective-permute-start(bf16[1,160,768]{2,1,0:T(8,128)(2,1)S(1)} %get-tuple-element.198), channel_id=1, source_target_pairs={{8,0},{9,1},{10,2},{11,3},{12,4},{13,5},{14,6},{15,7},{24,16},{25,... | collective-permute-start | bytes 737288 | tf_op jit(solution)/shard_map/ppermute | solution.py:460
  218.2 36.5 %collective-permute-start.39 = (bf16[1,160,768]{2,1,0:T(8,128)(2,1)S(1)}, bf16[1,160,768]{2,1,0:T(8,128)(2,1)S(1)}, u32[]{:S(2)}, u32[]{:S(2)}) collective-permute-start(bf16[1,160,768]{2,1,0:T(8,128)(2,1)S(1)} %layer_fwd.7), channel_id=1, source_target_pairs={{0,8},{1,9},{2,10},{3,11},{4,12},{5,13},{6,14},{7,15},{16,24},{17,... | collective-permute-start | bytes 737288 | tf_op jit(solution)/shard_map/ppermute | solution.py:460
  233.0 21.7 %collective-permute-start.40 = (bf16[1,160,768]{2,1,0:T(8,128)(2,1)S(1)}, bf16[1,160,768]{2,1,0:T(8,128)(2,1)S(1)}, u32[]{:S(2)}, u32[]{:S(2)}) collective-permute-start(bf16[1,160,768]{2,1,0:T(8,128)(2,1)S(1)} %get-tuple-element.207), channel_id=1, source_target_pairs={{8,0},{9,1},{10,2},{11,3},{12,4},{13,5},{14,6},{15,7},{24,16},{25,... | collective-permute-start | bytes 737288 | tf_op jit(solution)/shard_map/ppermute | solution.py:460
  253.4 22.9 %collective-permute-start.42 = (bf16[1,160,768]{2,1,0:T(8,128)(2,1)}, bf16[1,160,768]{2,1,0:T(8,128)(2,1)}, u32[]{:S(2)}, u32[]{:S(2)}) collective-permute-start(bf16[1,160,768]{2,1,0:T(8,128)(2,1)} %get-tuple-element.216), channel_id=1, source_target_pairs={{8,0},{9,1},{10,2},{11,3},{12,4},{13,5},{14,6},{15,7},{24,16},{25,... | collective-permute-start | bytes 737288 | tf_op jit(solution)/shard_map/ppermute | solution.py:460
  274.0 21.1 %collective-permute-start.41 = (bf16[1,160,768]{2,1,0:T(8,128)(2,1)}, bf16[1,160,768]{2,1,0:T(8,128)(2,1)S(1)}, u32[]{:S(2)}, u32[]{:S(2)}) collective-permute-start(bf16[1,160,768]{2,1,0:T(8,128)(2,1)} %get-tuple-element.225), channel_id=1, source_target_pairs={{8,0},{9,1},{10,2},{11,3},{12,4},{13,5},{14,6},{15,7},{24,16},{25,... | collective-permute-start | bytes 737288 | tf_op jit(solution)/shard_map/ppermute | solution.py:460
  322.8 35.0 %collective-permute-start.47 = (bf16[8,48,3072]{2,1,0:T(8,128)(2,1)}, bf16[8,48,3072]{2,1,0:T(8,128)(2,1)}, u32[]{:S(2)}, u32[]{:S(2)}) collective-permute-start(bf16[8,48,3072]{2,1,0:T(8,128)(2,1)} %get-tuple-element.251), channel_id=1, source_target_pairs={{0,16},{16,0},{1,17},{17,1},{2,18},{18,2},{3,19},{19,3},{4,20},{20... | collective-permute-start | bytes 7077896 | tf_op jit(solution)/shard_map/ppermute | solution.py:454
  332.7 27.8 %collective-permute-start.46 = (bf16[8,48,3072]{2,1,0:T(8,128)(2,1)}, bf16[8,48,3072]{2,1,0:T(8,128)(2,1)}, u32[]{:S(2)}, u32[]{:S(2)}) collective-permute-start(bf16[8,48,3072]{2,1,0:T(8,128)(2,1)} %get-tuple-element.249), channel_id=1, source_target_pairs={{0,16},{16,0},{1,17},{17,1},{2,18},{18,2},{3,19},{19,3},{4,20},{20... | collective-permute-start | bytes 7077896 | tf_op jit(solution)/shard_map/ppermute | solution.py:454
  333.3 31.9 %collective-permute-start.44 = (bf16[4,160,768]{2,1,0:T(8,128)(2,1)S(1)}, bf16[4,160,768]{2,1,0:T(8,128)(2,1)}, u32[]{:S(2)}, u32[]{:S(2)}) collective-permute-start(bf16[4,160,768]{2,1,0:T(8,128)(2,1)S(1)} %get-tuple-element.242), channel_id=1, source_target_pairs={{0,16},{16,8},{1,17},{17,9},{2,18},{18,10},{3,19},{19,11},{4,20},{... | collective-permute-start | bytes 2949128 | tf_op jit(solution)/shard_map/ppermute | solution.py:460
  335.2 30.0 %collective-permute-start.43 = (bf16[4,160,768]{2,1,0:T(8,128)(2,1)S(1)}, bf16[4,160,768]{2,1,0:T(8,128)(2,1)}, u32[]{:S(2)}, u32[]{:S(2)}) collective-permute-start(bf16[4,160,768]{2,1,0:T(8,128)(2,1)S(1)} %get-tuple-element.242), channel_id=1, source_target_pairs={{24,8},{8,16},{25,9},{9,17},{26,10},{10,18},{27,11},{11,19},{28,12... | collective-permute-start | bytes 2949128 | tf_op jit(solution)/shard_map/ppermute | solution.py:460
  365.2 20.9 %collective-permute-start.48 = (bf16[8,96,128]{2,1,0:T(8,128)(2,1)S(1)}, bf16[8,96,128]{2,1,0:T(8,128)(2,1)}, u32[]{:S(2)}, u32[]{:S(2)}) collective-permute-start(bf16[8,96,128]{2,1,0:T(8,128)(2,1)S(1)} %bitcast.188), channel_id=1, source_target_pairs={{0,16},{16,0},{1,17},{17,1},{2,18},{18,2},{3,19},{19,3},{4,20},{20... | collective-permute-start | bytes 589832 | tf_op jit(solution)/shard_map/ppermute | solution.py:454
  365.2 27.5 %collective-permute-start.49 = (bf16[4,48,3072]{2,1,0:T(8,128)(2,1)}, bf16[4,48,3072]{2,1,0:T(8,128)(2,1)}, u32[]{:S(2)}, u32[]{:S(2)}) collective-permute-start(bf16[4,48,3072]{2,1,0:T(8,128)(2,1)} %add_convert_fusion.11), channel_id=1, source_target_pairs={{0,1},{1,0},{2,3},{3,2},{4,5},{5,4},{6,7},{7,6},{8,9},{9,8},{10,11... | collective-permute-start | bytes 3538952 | tf_op jit(solution)/shard_map/ppermute | solution.py:450
  365.3 29.1 %collective-permute-start.50 = (bf16[4,48,3072]{2,1,0:T(8,128)(2,1)S(1)}, bf16[4,48,3072]{2,1,0:T(8,128)(2,1)}, u32[]{:S(2)}, u32[]{:S(2)}) collective-permute-start(bf16[4,48,3072]{2,1,0:T(8,128)(2,1)S(1)} %add_convert_fusion.10), channel_id=1, source_target_pairs={{0,2},{1,3},{2,0},{3,1},{4,6},{5,7},{6,4},{7,5},{8,10},{9,11},{10,... | collective-permute-start | bytes 3538952 | tf_op jit(solution)/shard_map/ppermute | solution.py:450
  365.9 30.3 %collective-permute-start.51 = (bf16[4,48,3072]{2,1,0:T(8,128)(2,1)S(1)}, bf16[4,48,3072]{2,1,0:T(8,128)(2,1)}, u32[]{:S(2)}, u32[]{:S(2)}) collective-permute-start(bf16[4,48,3072]{2,1,0:T(8,128)(2,1)S(1)} %add_convert_fusion.9), channel_id=1, source_target_pairs={{0,4},{1,5},{2,6},{3,7},{4,0},{5,1},{6,2},{7,3},{8,12},{9,13},{10,... | collective-permute-start | bytes 3538952 | tf_op jit(solution)/shard_map/ppermute | solution.py:450
  365.9 32.1 %collective-permute-start.52 = (bf16[8,48,3072]{2,1,0:T(8,128)(2,1)}, bf16[8,48,3072]{2,1,0:T(8,128)(2,1)S(1)}, u32[]{:S(2)}, u32[]{:S(2)}) collective-permute-start(bf16[8,48,3072]{2,1,0:T(8,128)(2,1)} %get-tuple-element.268), channel_id=1, source_target_pairs={{0,16},{16,0},{1,17},{17,1},{2,18},{18,2},{3,19},{19,3},{4,20},{20... | collective-permute-start | bytes 7077896 | tf_op jit(solution)/shard_map/ppermute | solution.py:454
  398.7 15.0 %collective-permute-start.56 = (bf16[2,48,3072]{2,1,0:T(8,128)(2,1)S(1)}, bf16[2,48,3072]{2,1,0:T(8,128)(2,1)S(1)}, u32[]{:S(2)}, u32[]{:S(2)}) collective-permute-start(bf16[2,48,3072]{2,1,0:T(8,128)(2,1)S(1)} %get-tuple-element.272), channel_id=1, source_target_pairs={{0,1},{1,0},{2,3},{3,2},{4,5},{5,4},{6,7},{7,6},{8,9},{9,8},{10,11... | collective-permute-start | bytes 1769480 | tf_op jit(solution)/shard_map/ppermute | solution.py:450
  399.5 14.3 %collective-permute-start.57 = (bf16[8,48,3072]{2,1,0:T(8,128)(2,1)S(1)}, bf16[8,48,3072]{2,1,0:T(8,128)(2,1)S(1)}, u32[]{:S(2)}, u32[]{:S(2)}) collective-permute-start(bf16[8,48,3072]{2,1,0:T(8,128)(2,1)S(1)} %copy-done.49), channel_id=1, source_target_pairs={{0,16},{16,0},{1,17},{17,1},{2,18},{18,2},{3,19},{19,3},{4,20},{20... | collective-permute-start | bytes 7077896 | tf_op jit(solution)/shard_map/ppermute | solution.py:454
  425.7 28.9 %collective-permute-start.63 = (bf16[4,48,3072]{2,1,0:T(8,128)(2,1)S(1)}, bf16[4,48,3072]{2,1,0:T(8,128)(2,1)S(1)}, u32[]{:S(2)}, u32[]{:S(2)}) collective-permute-start(bf16[4,48,3072]{2,1,0:T(8,128)(2,1)S(1)} %get-tuple-element.281), channel_id=1, source_target_pairs={{0,4},{1,5},{2,6},{3,7},{4,0},{5,1},{6,2},{7,3},{8,12},{9,13},{10,... | collective-permute-start | bytes 3538952 | tf_op jit(solution)/shard_map/ppermute | solution.py:450
  426.1 33.1 %collective-permute-start.67 = (bf16[48,3072]{1,0:T(8,128)(2,1)S(1)}, bf16[48,3072]{1,0:T(8,128)(2,1)S(1)}, u32[]{:S(2)}, u32[]{:S(2)}) collective-permute-start(bf16[48,3072]{1,0:T(8,128)(2,1)S(1)} %fusion.4), channel_id=1, source_target_pairs={{8,16},{9,17},{10,18},{11,19},{12,20},{13,21},{14,22},{15,23},{16,... | collective-permute-start | bytes 884744 | tf_op jit(solution)/shard_map/ppermute | solution.py:460
  432.9 25.4 %collective-permute-start.65 = (bf16[4,48,3072]{2,1,0:T(8,128)(2,1)S(1)}, bf16[4,48,3072]{2,1,0:T(8,128)(2,1)S(1)}, u32[]{:S(2)}, u32[]{:S(2)}) collective-permute-start(bf16[4,48,3072]{2,1,0:T(8,128)(2,1)S(1)} %get-tuple-element.283), channel_id=1, source_target_pairs={{0,1},{1,0},{2,3},{3,2},{4,5},{5,4},{6,7},{7,6},{8,9},{9,8},{10,11... | collective-permute-start | bytes 3538952 | tf_op jit(solution)/shard_map/ppermute | solution.py:450
  433.3 25.7 %collective-permute-start.66 = (bf16[4,48,3072]{2,1,0:T(8,128)(2,1)S(1)}, bf16[4,48,3072]{2,1,0:T(8,128)(2,1)S(1)}, u32[]{:S(2)}, u32[]{:S(2)}) collective-permute-start(bf16[4,48,3072]{2,1,0:T(8,128)(2,1)S(1)} %get-tuple-element.284), channel_id=1, source_target_pairs={{0,2},{1,3},{2,0},{3,1},{4,6},{5,7},{6,4},{7,5},{8,10},{9,11},{10,... | collective-permute-start | bytes 3538952 | tf_op jit(solution)/shard_map/ppermute | solution.py:450
  459.3 15.2 %collective-permute-start.68 = (bf16[2,48,3072]{2,1,0:T(8,128)(2,1)S(1)}, bf16[2,48,3072]{2,1,0:T(8,128)(2,1)S(1)}, u32[]{:S(2)}, u32[]{:S(2)}) collective-permute-start(bf16[2,48,3072]{2,1,0:T(8,128)(2,1)S(1)} %get-tuple-element.286), channel_id=1, source_target_pairs={{0,1},{1,0},{2,3},{3,2},{4,5},{5,4},{6,7},{7,6},{8,9},{9,8},{10,11... | collective-permute-start | bytes 1769480 | tf_op jit(solution)/shard_map/ppermute | solution.py:450
  460.5 24.7 %collective-permute-start.71 = (bf16[48,128]{1,0:T(8,128)(2,1)S(1)}, bf16[48,128]{1,0:T(8,128)(2,1)S(1)}, u32[]{:S(2)}, u32[]{:S(2)}) collective-permute-start(bf16[48,128]{1,0:T(8,128)(2,1)S(1)} %get-tuple-element.289), channel_id=1, source_target_pairs={{0,8},{1,9},{2,10},{3,11},{4,12},{5,13},{6,14},{7,15},{24,16},{25,... | collective-permute-start | bytes 36872 | tf_op jit(solution)/shard_map/ppermute | solution.py:460
  461.8 14.4 %collective-permute-start.69 = (bf16[2,48,3072]{2,1,0:T(8,128)(2,1)S(1)}, bf16[2,48,3072]{2,1,0:T(8,128)(2,1)S(1)}, u32[]{:S(2)}, u32[]{:S(2)}) collective-permute-start(bf16[2,48,3072]{2,1,0:T(8,128)(2,1)S(1)} %get-tuple-element.287), channel_id=1, source_target_pairs={{0,2},{1,3},{2,0},{3,1},{4,6},{5,7},{6,4},{7,5},{8,10},{9,11},{10,... | collective-permute-start | bytes 1769480 | tf_op jit(solution)/shard_map/ppermute | solution.py:450
  462.2 23.0 %collective-permute-start.70 = (bf16[2,48,3072]{2,1,0:T(8,128)(2,1)S(1)}, bf16[2,48,3072]{2,1,0:T(8,128)(2,1)S(1)}, u32[]{:S(2)}, u32[]{:S(2)}) collective-permute-start(bf16[2,48,3072]{2,1,0:T(8,128)(2,1)S(1)} %get-tuple-element.288), channel_id=1, source_target_pairs={{0,4},{1,5},{2,6},{3,7},{4,0},{5,1},{6,2},{7,3},{8,12},{9,13},{10,... | collective-permute-start | bytes 1769480 | tf_op jit(solution)/shard_map/ppermute | solution.py:450
  463.6 24.2 %collective-permute-start.72 = (bf16[48,9216]{1,0:T(8,128)(2,1)S(1)}, bf16[48,9216]{1,0:T(8,128)(2,1)S(1)}, u32[]{:S(2)}, u32[]{:S(2)}) collective-permute-start(bf16[48,9216]{1,0:T(8,128)(2,1)S(1)} %pad_maximum_fusion.9), channel_id=1, source_target_pairs={{0,8},{1,9},{2,10},{3,11},{4,12},{5,13},{6,14},{7,15},{24,16},{25,... | collective-permute-start | bytes 2654216 | tf_op jit(solution)/shard_map/ppermute | solution.py:460
  489.1 18.7 %collective-permute-start.76 = (bf16[48,6272]{1,0:T(8,128)(2,1)S(1)}, bf16[48,6272]{1,0:T(8,128)(2,1)S(1)}, u32[]{:S(2)}, u32[]{:S(2)}) collective-permute-start(bf16[48,6272]{1,0:T(8,128)(2,1)S(1)} %pad_maximum_fusion.10), channel_id=1, source_target_pairs={{8,16},{9,17},{10,18},{11,19},{12,20},{13,21},{14,22},{15,23},{16,... | collective-permute-start | bytes 1806344 | tf_op jit(solution)/shard_map/ppermute | solution.py:460
  (80 other events, 908.0 us)

commit v7 on v6

--- a/solution.py
+++ b/solution.py
@@ -738,7 +738,7 @@
         keep, send = reduce_step(near_keep, near_got, 0)
         small_keep, small_send = reduce_step(small_keep, [small_got], 2)
         small_got, *got, cross_a = wave(
-            one_bit(small_send[0], 2), *bits_out(send, 0), (far_sum[:, :WIDE], by(routes.crossed))
+            one_bit(small_send[0], 2), *bits_out(send, 0), (far_sum[:, : 2 * WIDE], by(routes.crossed))
         )
         small_end = (small_keep[0][0].astype(F32) + small_got[0].astype(F32)).astype(BF16)
         keep, send = reduce_step(keep, got, 1)
@@ -748,7 +748,7 @@
         keep, send = reduce_step(keep, got, 2)
         *got, cross_b = wave(
             *bits_out(send, 2),
-            (jnp.concatenate([far_sum[:, WIDE:], small_end[ROWS:]], -1), by(routes.crossed)),
+            (jnp.concatenate([far_sum[:, 2 * WIDE :], small_end[ROWS:]], -1), by(routes.crossed)),
         )
         near_sum = [a[0].astype(F32) + b[0].astype(F32) for a, b in zip(keep, got)] + [small_end[:ROWS].astype(F32)]
         (beside,) = wave((jnp.concatenate(near_sum, -1).astype(BF16), by(routes.away_to_home)))

time: 536 us -> 533 us (level)
  waiting for transfers between devices: 173 us -> 158 us
  starting transfers between devices: 104 us -> 117 us
    ppermute x42, starting transfers between devices: 40 us -> 52.7 us  [swap_bit(): return lax.ppermute(array, 'dp', [(i, i ^ 1 << bit) for i in range(count)])]
    ppermute x42, waiting for transfers between devices: 144 us -> 136 us  [swap_bit(): return lax.ppermute(array, 'dp', [(i, i ^ 1 << bit) for i in range(count)])]
    ppermute x23, waiting for transfers between devices: 22.3 us -> 15.8 us  [along(): return lax.ppermute(array, ('section', 'dp'), flat)]
    unnamed x109 -> x107, local copies, waits for them, and re-layouts: 12.1 us -> 12.1 us
where the time goes in v7:
time: 533 us; the launch traced here: 523 us
  Pallas kernels  169 us (32%)
  waiting for transfers between devices  158 us (30%)
  starting transfers between devices  117 us (22%)
  other arithmetic  56.4 us (11%)
  local copies, waits for them, and re-layouts  19 us (4%)
    ppermute x42, waiting for transfers between devices, swap_bit(): return lax.ppermute(array, 'dp', [(i, i ^ 1 << bit) for i in range(count)])  136 us
    pallas_call x10, Pallas kernels, layer_call(): pl.pallas_call(functools.partial(layer_kernel, back, slot, lead, count),...  128 us
    ppermute x42, starting transfers between devices, swap_bit(): return lax.ppermute(array, 'dp', [(i, i ^ 1 << bit) for i in range(count)])  52.7 us
    ppermute x23, starting transfers between devices, along(): return lax.ppermute(array, ('section', 'dp'), flat)  51.1 us
    pallas_call x6, Pallas kernels, grad_call(): pl.pallas_call(functools.partial(grad_kernel, unit, at), out_shape=[shape...  41.1 us
    convert_element_type x24, other arithmetic, both(): return (first.astype(F32) + second.astype(F32)).astype(BF16)  21.7 us
    ppermute x23, waiting for transfers between devices, along(): return lax.ppermute(array, ('section', 'dp'), flat)  15.8 us
    ppermute x13, starting transfers between devices, swap_section(): return lax.ppermute(array, 'section', [(0, 1), (1, 0)])  12.9 us
  transfers between devices with their start and end apart: 78, of which 30 were waited for; matrix products, arithmetic and copies ran while one was open for 10% of the time, Pallas kernels for 25%

profile of v7, /device:TPU:1, one launch (start us, length us, event | category | flops | bytes accessed | tf_op | source)
XLA Modules:
  0.0 522.5 jit_solution(2037630289703986672)
XLA Ops:
  10.3 2.2 collective-permute-start.4
  12.5 4.6 collective-permute-start.5
  19.6 2.8 collective-permute-start.6
  22.5 2.5 collective-permute-done.3
  25.2 6.5 %collective-permute-done.6 = bf16[48,3072]{1,0:T(8,128)(2,1)S(1)} collective-permute-done((bf16[48,3072]{1,0:T(8,128)(2,1)S(1)}, bf16[48,3072]{1,0:T(8,128)(2,1)S(1)}, u32[]{:S(2)}, u32[]{:S(2)}) %collective-permute-start.6) | collective-permute-done | bytes 294944 | tf_op jit(solution)/shard_map/ppermute | solution.py:460
  35.4 3.5 collective-permute-start.11
  40.5 13.4 %collective-permute-done.9 = bf16[2,48,3072]{2,1,0:T(8,128)(2,1)S(1)} collective-permute-done((bf16[2,48,3072]{2,1,0:T(8,128)(2,1)S(1)}, bf16[2,48,3072]{2,1,0:T(8,128)(2,1)S(1)}, u32[]{:S(2)}, u32[]{:S(2)}) %collective-permute-start.9) | collective-permute-done | bytes 589856 | tf_op jit(solution)/shard_map/ppermute | solution.py:450
  57.1 9.3 %collective-permute-start.14 = (bf16[4,48,3072]{2,1,0:T(8,128)(2,1)S(1)}, bf16[4,48,3072]{2,1,0:T(8,128)(2,1)S(1)}, u32[]{:S(2)}, u32[]{:S(2)}) collective-permute-start(bf16[4,48,3072]{2,1,0:T(8,128)(2,1)S(1)} %pad_maximum_fusion.2.refs_3_), channel_id=1, source_target_pairs={{0,4},{1,5},{2,6},{3,7},{4,0},{5,1},{6,2},{7,3},{8,12},{9,13},{10,... | collective-permute-start | bytes 3538952 | tf_op jit(solution)/shard_map/ppermute | solution.py:450
  66.5 2.4 collective-permute-start.16
  68.8 2.3 maximum_maximum_fusion
  72.9 12.5 %collective-permute-done.14.refs_4_ = bf16[4,48,3072]{2,1,0:T(8,128)(2,1)S(1)} collective-permute-done((bf16[4,48,3072]{2,1,0:T(8,128)(2,1)S(1)}, bf16[4,48,3072]{2,1,0:T(8,128)(2,1)S(1)}, u32[]{:S(2)}, u32[]{:S(2)}) %collective-permute-start.14) | collective-permute-done | bytes 1179680 | tf_op jit(solution)/shard_map/ppermute | solution.py:450
  87.6 2.3 collective-permute-start.17
  92.3 6.9 %collective-permute-done.20 = bf16[1,48,3072]{2,1,0:T(8,128)(2,1)S(1)} collective-permute-done((bf16[1,48,3072]{2,1,0:T(8,128)(2,1)S(1)}, bf16[1,48,3072]{2,1,0:T(8,128)(2,1)S(1)}, u32[]{:S(2)}, u32[]{:S(2)}) %collective-permute-start.20) | collective-permute-done | bytes 294944 | tf_op jit(solution)/shard_map/ppermute | solution.py:450
  104.0 11.5 %collective-permute-done.24 = bf16[2,48,3072]{2,1,0:T(8,128)(2,1)S(1)} collective-permute-done((bf16[2,48,3072]{2,1,0:T(8,128)(2,1)S(1)}, bf16[2,48,3072]{2,1,0:T(8,128)(2,1)S(1)}, u32[]{:S(2)}, u32[]{:S(2)}) %collective-permute-start.24) | collective-permute-done | bytes 589856 | tf_op jit(solution)/shard_map/ppermute | solution.py:450
  116.6 8.8 %collective-permute-done.23 = bf16[2,48,3072]{2,1,0:T(8,128)(2,1)S(1)} collective-permute-done((bf16[2,48,3072]{2,1,0:T(8,128)(2,1)S(1)}, bf16[2,48,3072]{2,1,0:T(8,128)(2,1)S(1)}, u32[]{:S(2)}, u32[]{:S(2)}) %collective-permute-start.23) | collective-permute-done | bytes 589856 | tf_op jit(solution)/shard_map/ppermute | solution.py:450
  127.8 2.3 maximum_maximum_fusion.1
  137.7 2.3 broadcast_select_fusion.1
  140.0 22.0 %collective-permute-done.27 = bf16[4,2,2,16,128]{4,3,2,1,0:T(8,128)(2,1)S(1)} collective-permute-done((bf16[4,2,2,16,128]{4,3,2,1,0:T(8,128)(2,1)S(1)}, bf16[4,2,2,16,128]{4,3,2,1,0:T(8,128)(2,1)S(1)}, u32[]{:S(2)}, u32[]{:S(2)}) %collective-permute-start.27) | collective-permute-done | bytes 65568 | tf_op jit(solution)/shard_map/ppermute | solution.py:450
  171.0 9.9 %layer_fwd.4 = bf16[1,160,768]{2,1,0:T(8,128)(2,1)S(1)} custom-call(s32[62]{0:T(128)S(1)} %concatenate.123.refs_0_, f32[2,8,768]{2,1,0:T(8,128)S(1)} %constant_dynamic-update-slice_fusion.refs_1_, f32[2,1,3072]{2,1,0:T(1,128)S(1)} %constant_dynamic-update-slice_fusion.2.refs_2_, bf16[4,48,3072]{2,1,0:T(8,128)(2,1)S(1)} %pad_maximum_fusion.2.refs_3_, ...), custom_call_target="tpu_custom_call" | custom-call | flops 1 | bytes 1 | tf_op jit(solution)/shard_map/layer_fwd/pallas_call | solution.py:410
  182.6 10.1 %layer_fwd.5 = bf16[1,160,768]{2,1,0:T(8,128)(2,1)S(1)} custom-call(s32[62]{0:T(128)S(1)} %concatenate.123.refs_0_, f32[2,8,768]{2,1,0:T(8,128)S(1)} %constant_dynamic-update-slice_fusion.refs_1_, f32[2,1,3072]{2,1,0:T(1,128)S(1)} %constant_dynamic-update-slice_fusion.2.refs_2_, bf16[4,48,3072]{2,1,0:T(8,128)(2,1)S(1)} %pad_maximum_fusion.2.refs_3_, ...), custom_call_target="tpu_custom_call" | custom-call | flops 1 | bytes 1 | tf_op jit(solution)/shard_map/layer_fwd/pallas_call | solution.py:410
  194.1 10.1 %layer_fwd.6 = bf16[1,160,768]{2,1,0:T(8,128)(2,1)S(1)} custom-call(s32[62]{0:T(128)S(1)} %concatenate.123.refs_0_, f32[2,8,768]{2,1,0:T(8,128)S(1)} %constant_dynamic-update-slice_fusion.refs_1_, f32[2,1,3072]{2,1,0:T(1,128)S(1)} %constant_dynamic-update-slice_fusion.2.refs_2_, bf16[4,48,3072]{2,1,0:T(8,128)(2,1)S(1)} %pad_maximum_fusion.2.refs_3_, ...), custom_call_target="tpu_custom_call" | custom-call | flops 1 | bytes 1 | tf_op jit(solution)/shard_map/layer_fwd/pallas_call | solution.py:410
  205.5 10.3 %layer_fwd.7 = bf16[1,160,768]{2,1,0:T(8,128)(2,1)S(1)} custom-call(s32[62]{0:T(128)S(1)} %concatenate.123.refs_0_, f32[2,8,768]{2,1,0:T(8,128)S(1)} %constant_dynamic-update-slice_fusion.refs_1_, f32[2,1,3072]{2,1,0:T(1,128)S(1)} %constant_dynamic-update-slice_fusion.2.refs_2_, bf16[4,48,3072]{2,1,0:T(8,128)(2,1)S(1)} %pad_maximum_fusion.2.refs_3_, ...), custom_call_target="tpu_custom_call" | custom-call | flops 1 | bytes 1 | tf_op jit(solution)/shard_map/layer_fwd/pallas_call | solution.py:410
  218.6 4.9 collective-permute-start.39
  223.5 9.8 %layer_back.7 = (bf16[1,160,768]{2,1,0:T(8,128)(2,1)S(1)}, bf16[4,160,768]{2,1,0:T(8,128)(2,1)S(1)}, f32[4,160,768]{2,1,0:T(8,128)}, f32[4,8,768]{2,1,0:T(8,128)...) custom-call(s32[62]{0:T(128)S(1)} %concatenate.123.refs_0_, ...), custom_call_target="tpu_custom_call", output_to_operand_aliasing={{1}: (24, {}), {2}: (25, {}), {3}: (26, {}), {4}: (27, {}),... | custom-call | flops 1 | bytes 1 | tf_op jit(solution)/shard_map/layer_back/pallas_call | solution.py:410
  234.7 19.1 %layer_back.8 = (bf16[1,160,768]{2,1,0:T(8,128)(2,1)}, bf16[4,160,768]{2,1,0:T(8,128)(2,1)S(1)}, f32[4,160,768]{2,1,0:T(8,128)}, f32[4,8,768]{2,1,0:T(8,128)S(1)...) custom-call(s32[62]{0:T(128)S(1)} %concatenate.123.refs_0_, ...), custom_call_target="tpu_custom_call", output_to_operand_aliasing={{1}: (25, {}), {2}: (26, {}), {3}: (27, {}), {4}: (28, {}),... | custom-call | flops 1 | bytes 1 | tf_op jit(solution)/shard_map/layer_back/pallas_call | solution.py:410
  255.1 19.3 %layer_back.9 = (bf16[1,160,768]{2,1,0:T(8,128)(2,1)}, bf16[4,160,768]{2,1,0:T(8,128)(2,1)S(1)}, f32[4,160,768]{2,1,0:T(8,128)}, f32[4,8,768]{2,1,0:T(8,128)S(1)...) custom-call(s32[62]{0:T(128)S(1)} %concatenate.123.refs_0_, ...), custom_call_target="tpu_custom_call", output_to_operand_aliasing={{1}: (25, {}), {2}: (26, {}), {3}: (27, {}), {4}: (28, {}),... | custom-call | flops 1 | bytes 1 | tf_op jit(solution)/shard_map/layer_back/pallas_call | solution.py:410
  276.7 18.8 %layer_back.10 = (bf16[1,160,768]{2,1,0:T(8,128)(2,1)}, bf16[4,160,768]{2,1,0:T(8,128)(2,1)S(1)}, f32[4,160,768]{2,1,0:T(8,128)}, f32[4,8,768]{2,1,0:T(8,128)S(1...) custom-call(s32[62]{0:T(128)S(1)} %concatenate.123.refs_0_, ...), custom_call_target="tpu_custom_call", output_to_operand_aliasing={{1}: (23, {}), {2}: (24, {}), {3}: (25, {}), {4}: (26, {}),... | custom-call | flops 1 | bytes 1 | tf_op jit(solution)/shard_map/layer_back/pallas_call | solution.py:410
  296.2 19.2 %layer_back.11 = (bf16[1,160,768]{2,1,0:T(8,128)(2,1)}, bf16[4,160,768]{2,1,0:T(8,128)(2,1)S(1)}, f32[4,160,768]{2,1,0:T(8,128)}, f32[4,8,768]{2,1,0:T(8,128)S(1...) custom-call(s32[62]{0:T(128)S(1)} %concatenate.123.refs_0_, ...), custom_call_target="tpu_custom_call", output_to_operand_aliasing={{1}: (23, {}), {2}: (24, {}), {3}: (25, {}), {4}: (26, {}),... | custom-call | flops 1 | bytes 1 | tf_op jit(solution)/shard_map/layer_back/pallas_call | solution.py:410
  315.4 7.1 %layer_grad.8 = (bf16[8,48,3072]{2,1,0:T(8,128)(2,1)S(1)}, bf16[8,48,3072]{2,1,0:T(8,128)(2,1)}) custom-call(s32[31]{0:T(128)S(1)} %concatenate.140.meta, bf16[4,4,160,768]{3,2,1,0:T(8,128)(2,1)} %get-tuple-element.244.refs_0_.refs_1_, bf16[4,4,160,768]{3,2,1,0:T(8,128)(2,1)} %get-tuple-element.244.refs_0_.refs_1_, ...), custom_call_target="tpu_custom_call" | custom-call | flops 1 | bytes 1 | tf_op jit(solution)/shard_map/layer_grad/pallas_call | solution.py:431
  324.6 6.6 %layer_grad.7 = (bf16[8,48,3072]{2,1,0:T(8,128)(2,1)S(1)}, bf16[8,48,3072]{2,1,0:T(8,128)(2,1)}) custom-call(s32[31]{0:T(128)S(1)} %concatenate.140.meta, bf16[4,4,160,768]{3,2,1,0:T(8,128)(2,1)} %get-tuple-element.244.refs_0_.refs_1_, bf16[3,4,160,3072]{3,2,1,0:T(8,128)(2,1)} %get-tuple-element.245.refs_1_.refs_2_), custom_call_target="tpu_custom_call" | custom-call | flops 1 | bytes 1 | tf_op jit(solution)/shard_map/layer_grad/pallas_call | solution.py:431
  336.2 6.7 %layer_grad.6 = (bf16[8,48,3072]{2,1,0:T(8,128)(2,1)S(1)}, bf16[8,48,3072]{2,1,0:T(8,128)(2,1)}) custom-call(s32[31]{0:T(128)S(1)} %concatenate.140.meta, bf16[4,4,160,768]{3,2,1,0:T(8,128)(2,1)} %get-tuple-element.244.refs_0_.refs_1_, bf16[3,4,160,3072]{3,2,1,0:T(8,128)(2,1)} %get-tuple-element.245.refs_1_.refs_2_), custom_call_target="tpu_custom_call" | custom-call | flops 1 | bytes 1 | tf_op jit(solution)/shard_map/layer_grad/pallas_call | solution.py:431
  344.3 6.7 %layer_grad.11 = (bf16[8,48,3072]{2,1,0:T(8,128)(2,1)S(1)}, bf16[8,48,3072]{2,1,0:T(8,128)(2,1)}) custom-call(s32[31]{0:T(128)S(1)} %concatenate.140.meta, bf16[4,4,160,768]{3,2,1,0:T(8,128)(2,1)} %get-tuple-element.244.refs_0_.refs_1_, bf16[3,4,160,3072]{3,2,1,0:T(8,128)(2,1)} %get-tuple-element.245.refs_1_.refs_2_), custom_call_target="tpu_custom_call" | custom-call | flops 1 | bytes 1 | tf_op jit(solution)/shard_map/layer_grad/pallas_call | solution.py:431
  361.2 2.7 add_convert_fusion.11
  373.3 6.9 %layer_grad.9 = (bf16[8,48,3072]{2,1,0:T(8,128)(2,1)S(1)}, bf16[8,48,3072]{2,1,0:T(8,128)(2,1)}) custom-call(s32[31]{0:T(128)S(1)} %concatenate.140.meta, bf16[4,4,160,768]{3,2,1,0:T(8,128)(2,1)} %get-tuple-element.244.refs_0_.refs_1_, bf16[3,4,160,3072]{3,2,1,0:T(8,128)(2,1)} %get-tuple-element.245.refs_1_.refs_2_), custom_call_target="tpu_custom_call" | custom-call | flops 1 | bytes 1 | tf_op jit(solution)/shard_map/layer_grad/pallas_call | solution.py:431
  380.2 7.0 %layer_grad.10 = (bf16[8,48,3072]{2,1,0:T(8,128)(2,1)S(1)}, bf16[8,48,3072]{2,1,0:T(8,128)(2,1)}) custom-call(s32[31]{0:T(128)S(1)} %concatenate.140.meta, bf16[4,4,160,768]{3,2,1,0:T(8,128)(2,1)} %get-tuple-element.244.refs_0_.refs_1_, bf16[4,4,160,768]{3,2,1,0:T(8,128)(2,1)} %get-tuple-element.244.refs_0_.refs_1_, ...), custom_call_target="tpu_custom_call" | custom-call | flops 1 | bytes 1 | tf_op jit(solution)/shard_map/layer_grad/pallas_call | solution.py:431
  388.3 3.1 collective-permute-done.49
  397.2 2.2 collective-permute-start.54
  403.5 8.2 %collective-permute-done.54 = bf16[2,48,3072]{2,1,0:T(8,128)(2,1)S(1)} collective-permute-done((bf16[2,48,3072]{2,1,0:T(8,128)(2,1)S(1)}, bf16[2,48,3072]{2,1,0:T(8,128)(2,1)S(1)}, u32[]{:S(2)}, u32[]{:S(2)}) %collective-permute-start.54) | collective-permute-done | bytes 589856 | tf_op jit(solution)/shard_map/ppermute | solution.py:450
  416.3 4.1 collective-permute-start.58
  427.1 5.9 %collective-permute-start.67 = (bf16[48,6144]{1,0:T(8,128)(2,1)S(1)}, bf16[48,6144]{1,0:T(8,128)(2,1)S(1)}, u32[]{:S(2)}, u32[]{:S(2)}) collective-permute-start(bf16[48,6144]{1,0:T(8,128)(2,1)S(1)} %pad_maximum_fusion.16), channel_id=1, source_target_pairs={{8,16},{9,17},{10,18},{11,19},{12,20},{13,21},{14,22},{15,23},{16,... | collective-permute-start | bytes 1769480 | tf_op jit(solution)/shard_map/ppermute | solution.py:460
  434.3 23.5 %collective-permute-done.63 = bf16[4,48,3072]{2,1,0:T(8,128)(2,1)S(1)} collective-permute-done((bf16[4,48,3072]{2,1,0:T(8,128)(2,1)S(1)}, bf16[4,48,3072]{2,1,0:T(8,128)(2,1)S(1)}, u32[]{:S(2)}, u32[]{:S(2)}) %collective-permute-start.63) | collective-permute-done | bytes 1179680 | tf_op jit(solution)/shard_map/ppermute | solution.py:450
  466.3 5.8 %collective-permute-done.68 = bf16[2,48,3072]{2,1,0:T(8,128)(2,1)S(1)} collective-permute-done((bf16[2,48,3072]{2,1,0:T(8,128)(2,1)S(1)}, bf16[2,48,3072]{2,1,0:T(8,128)(2,1)S(1)}, u32[]{:S(2)}, u32[]{:S(2)}) %collective-permute-start.68) | collective-permute-done | bytes 589856 | tf_op jit(solution)/shard_map/ppermute | solution.py:450
  473.7 11.0 %collective-permute-done.70 = bf16[2,48,3072]{2,1,0:T(8,128)(2,1)S(1)} collective-permute-done((bf16[2,48,3072]{2,1,0:T(8,128)(2,1)S(1)}, bf16[2,48,3072]{2,1,0:T(8,128)(2,1)S(1)}, u32[]{:S(2)}, u32[]{:S(2)}) %collective-permute-start.70) | collective-permute-done | bytes 589856 | tf_op jit(solution)/shard_map/ppermute | solution.py:450
  484.9 6.4 %collective-permute-start.74 = (bf16[1,48,3072]{2,1,0:T(8,128)(2,1)S(1)}, bf16[1,48,3072]{2,1,0:T(8,128)(2,1)S(1)}, u32[]{:S(2)}, u32[]{:S(2)}) collective-permute-start(bf16[1,48,3072]{2,1,0:T(8,128)(2,1)S(1)} %add_convert_fusion.28), channel_id=1, source_target_pairs={{0,4},{1,5},{2,6},{3,7},{4,0},{5,1},{6,2},{7,3},{8,12},{9,13},{10,... | collective-permute-start | bytes 884744 | tf_op jit(solution)/shard_map/ppermute | solution.py:450
  492.2 5.6 %collective-permute-start.76 = (bf16[48,3200]{1,0:T(8,128)(2,1)S(1)}, bf16[48,3200]{1,0:T(8,128)(2,1)S(1)}, u32[]{:S(2)}, u32[]{:S(2)}) collective-permute-start(bf16[48,3200]{1,0:T(8,128)(2,1)S(1)} %pad_maximum_fusion.17), channel_id=1, source_target_pairs={{8,16},{9,17},{10,18},{11,19},{12,20},{13,21},{14,22},{15,23},{16,... | collective-permute-start | bytes 921608 | tf_op jit(solution)/shard_map/ppermute | solution.py:460
  500.7 5.0 collective-permute-done.76
  507.0 2.3 select_bitcast_fusion.1
  509.2 2.7 select_bitcast_fusion
  (369 shorter events, 140.6 us)
Async XLA Ops:
  33.9 20.2 %collective-permute-start.8 = (bf16[2,48,3072]{2,1,0:T(8,128)(2,1)S(1)}, bf16[2,48,3072]{2,1,0:T(8,128)(2,1)S(1)}, u32[]{:S(2)}, u32[]{:S(2)}) collective-permute-start(bf16[2,48,3072]{2,1,0:T(8,128)(2,1)S(1)} %pad_maximum_fusion.10), channel_id=1, source_target_pairs={{0,2},{1,3},{2,0},{3,1},{4,6},{5,7},{6,4},{7,5},{8,10},{9,11},{10,... | collective-permute-start | bytes 1769480 | tf_op jit(solution)/shard_map/ppermute | solution.py:450
  34.2 19.8 %collective-permute-start.9 = (bf16[2,48,3072]{2,1,0:T(8,128)(2,1)S(1)}, bf16[2,48,3072]{2,1,0:T(8,128)(2,1)S(1)}, u32[]{:S(2)}, u32[]{:S(2)}) collective-permute-start(bf16[2,48,3072]{2,1,0:T(8,128)(2,1)S(1)} %pad_maximum_fusion.11), channel_id=1, source_target_pairs={{0,4},{1,5},{2,6},{3,7},{4,0},{5,1},{6,2},{7,3},{8,12},{9,13},{10,... | collective-permute-start | bytes 1769480 | tf_op jit(solution)/shard_map/ppermute | solution.py:450
  35.4 19.3 %collective-permute-start.11 = (bf16[48,6144]{1,0:T(8,128)(2,1)S(1)}, bf16[48,6144]{1,0:T(8,128)(2,1)S(1)}, u32[]{:S(2)}, u32[]{:S(2)}) collective-permute-start(bf16[48,6144]{1,0:T(8,128)(2,1)S(1)} %slice.541), channel_id=1, source_target_pairs={{8,16},{9,17},{10,18},{11,19},{12,20},{13,21},{14,22},{15,23},{16,... | collective-permute-start | bytes 1769480 | tf_op jit(solution)/shard_map/ppermute | solution.py:460
  54.8 16.4 %collective-permute-start.12 = (bf16[1,2,2,16,128]{4,3,2,1,0:T(8,128)(2,1)S(1)}, bf16[1,2,2,16,128]{4,3,2,1,0:T(8,128)(2,1)S(1)}, u32[]{:S(2)}, u32[]{:S(2)}) collective-permute-start(bf16[1,2,2,16,128]{4,3,2,1,0:T(8,128)(2,1)S(1)} %maximum_bitcast_fusion.3), channel_id=1, source_target_pairs={{0,1},{1,0},{2,3},{3,2},{4,5},{5,4},{6,7},{7,6},{8,9},{9,8},{10,11... | collective-permute-start | bytes 49160 | tf_op jit(solution)/shard_map/ppermute | solution.py:450
  55.8 16.0 %collective-permute-start.13 = (bf16[48,9216]{1,0:T(8,128)(2,1)S(1)}, bf16[48,9216]{1,0:T(8,128)(2,1)S(1)}, u32[]{:S(2)}, u32[]{:S(2)}) collective-permute-start(bf16[48,9216]{1,0:T(8,128)(2,1)S(1)} %get-tuple-element.172), channel_id=1, source_target_pairs={{8,0},{9,1},{10,2},{11,3},{12,4},{13,5},{14,6},{15,7},{16,24},{17,... | collective-permute-start | bytes 2654216 | tf_op jit(solution)/shard_map/ppermute | solution.py:460
  57.1 28.3 %collective-permute-start.14 = (bf16[4,48,3072]{2,1,0:T(8,128)(2,1)S(1)}, bf16[4,48,3072]{2,1,0:T(8,128)(2,1)S(1)}, u32[]{:S(2)}, u32[]{:S(2)}) collective-permute-start(bf16[4,48,3072]{2,1,0:T(8,128)(2,1)S(1)} %pad_maximum_fusion.2.refs_3_), channel_id=1, source_target_pairs={{0,4},{1,5},{2,6},{3,7},{4,0},{5,1},{6,2},{7,3},{8,12},{9,13},{10,... | collective-permute-start | bytes 3538952 | tf_op jit(solution)/shard_map/ppermute | solution.py:450
  66.4 19.0 %collective-permute-start.15 = (bf16[4,48,3072]{2,1,0:T(8,128)(2,1)S(1)}, bf16[4,48,3072]{2,1,0:T(8,128)(2,1)S(1)}, u32[]{:S(2)}, u32[]{:S(2)}) collective-permute-start(bf16[4,48,3072]{2,1,0:T(8,128)(2,1)S(1)} %pad_maximum_fusion.3.refs_7_), channel_id=1, source_target_pairs={{0,1},{1,0},{2,3},{3,2},{4,5},{5,4},{6,7},{7,6},{8,9},{9,8},{10,11... | collective-permute-start | bytes 3538952 | tf_op jit(solution)/shard_map/ppermute | solution.py:450
  66.5 18.9 %collective-permute-start.16 = (bf16[4,48,3072]{2,1,0:T(8,128)(2,1)S(1)}, bf16[4,48,3072]{2,1,0:T(8,128)(2,1)}, u32[]{:S(2)}, u32[]{:S(2)}) collective-permute-start(bf16[4,48,3072]{2,1,0:T(8,128)(2,1)S(1)} %pad_maximum_fusion.4.refs_11_), channel_id=1, source_target_pairs={{0,2},{1,3},{2,0},{3,1},{4,6},{5,7},{6,4},{7,5},{8,10},{9,11},{10,... | collective-permute-start | bytes 3538952 | tf_op jit(solution)/shard_map/ppermute | solution.py:450
  85.4 14.0 %collective-permute-start.21 = (bf16[4,48,9216]{2,1,0:T(8,128)(2,1)}, bf16[4,48,9216]{2,1,0:T(8,128)(2,1)}, u32[]{:S(2)}, u32[]{:S(2)}) collective-permute-start(bf16[4,48,9216]{2,1,0:T(8,128)(2,1)} %maximum_maximum_fusion), channel_id=1, source_target_pairs={{0,16},{16,0},{1,17},{17,1},{2,18},{18,2},{3,19},{19,3},{4,20},{20... | collective-permute-start | bytes 10616840 | tf_op jit(solution)/shard_map/ppermute | solution.py:454
  99.4 32.8 %collective-permute-start.26 = (bf16[4,48,9216]{2,1,0:T(8,128)(2,1)S(1)}, bf16[4,48,9216]{2,1,0:T(8,128)(2,1)}, u32[]{:S(2)}, u32[]{:S(2)}) collective-permute-start(bf16[4,48,9216]{2,1,0:T(8,128)(2,1)S(1)} %pad_maximum_fusion), channel_id=1, source_target_pairs={{0,16},{16,0},{1,17},{17,1},{2,18},{18,2},{3,19},{19,3},{4,20},{20... | collective-permute-start | bytes 10616840 | tf_op jit(solution)/shard_map/ppermute | solution.py:454
  100.6 14.9 %collective-permute-start.24 = (bf16[2,48,3072]{2,1,0:T(8,128)(2,1)S(1)}, bf16[2,48,3072]{2,1,0:T(8,128)(2,1)S(1)}, u32[]{:S(2)}, u32[]{:S(2)}) collective-permute-start(bf16[2,48,3072]{2,1,0:T(8,128)(2,1)S(1)} %pad_maximum_fusion.15), channel_id=1, source_target_pairs={{0,1},{1,0},{2,3},{3,2},{4,5},{5,4},{6,7},{7,6},{8,9},{9,8},{10,11... | collective-permute-start | bytes 1769480 | tf_op jit(solution)/shard_map/ppermute | solution.py:450
  101.2 24.2 %collective-permute-start.23 = (bf16[2,48,3072]{2,1,0:T(8,128)(2,1)S(1)}, bf16[2,48,3072]{2,1,0:T(8,128)(2,1)S(1)}, u32[]{:S(2)}, u32[]{:S(2)}) collective-permute-start(bf16[2,48,3072]{2,1,0:T(8,128)(2,1)S(1)} %pad_maximum_fusion.14), channel_id=1, source_target_pairs={{0,4},{1,5},{2,6},{3,7},{4,0},{5,1},{6,2},{7,3},{8,12},{9,13},{10,... | collective-permute-start | bytes 1769480 | tf_op jit(solution)/shard_map/ppermute | solution.py:450
  101.3 25.4 %collective-permute-start.22 = (bf16[2,48,3072]{2,1,0:T(8,128)(2,1)S(1)}, bf16[2,48,3072]{2,1,0:T(8,128)(2,1)S(1)}, u32[]{:S(2)}, u32[]{:S(2)}) collective-permute-start(bf16[2,48,3072]{2,1,0:T(8,128)(2,1)S(1)} %pad_maximum_fusion.13), channel_id=1, source_target_pairs={{0,2},{1,3},{2,0},{3,1},{4,6},{5,7},{6,4},{7,5},{8,10},{9,11},{10,... | collective-permute-start | bytes 1769480 | tf_op jit(solution)/shard_map/ppermute | solution.py:450
  102.7 29.5 %collective-permute-start.25 = (bf16[4,160,768]{2,1,0:T(8,128)(2,1)S(1)}, bf16[4,160,768]{2,1,0:T(8,128)(2,1)}, u32[]{:S(2)}, u32[]{:S(2)}) collective-permute-start(bf16[4,160,768]{2,1,0:T(8,128)(2,1)S(1)} %broadcast_select_fusion), channel_id=1, source_target_pairs={{0,8},{1,9},{2,10},{3,11},{4,12},{5,13},{6,14},{7,15},{24,16},{25,... | collective-permute-start | bytes 2949128 | tf_op jit(solution)/shard_map/ppermute | solution.py:460
  132.2 31.8 %collective-permute-start.31 = (bf16[4,48,9216]{2,1,0:T(8,128)(2,1)}, bf16[4,48,9216]{2,1,0:T(8,128)(2,1)}, u32[]{:S(2)}, u32[]{:S(2)}) collective-permute-start(bf16[4,48,9216]{2,1,0:T(8,128)(2,1)} %maximum_maximum_fusion.1), channel_id=1, source_target_pairs={{0,16},{16,0},{1,17},{17,1},{2,18},{18,2},{3,19},{19,3},{4,20},{20... | collective-permute-start | bytes 10616840 | tf_op jit(solution)/shard_map/ppermute | solution.py:454
  132.4 31.5 %collective-permute-start.28 = (bf16[4,48,3072]{2,1,0:T(8,128)(2,1)}, bf16[4,48,3072]{2,1,0:T(8,128)(2,1)}, u32[]{:S(2)}, u32[]{:S(2)}) collective-permute-start(bf16[4,48,3072]{2,1,0:T(8,128)(2,1)} %pad_maximum_fusion.5.refs_5_), channel_id=1, source_target_pairs={{0,4},{1,5},{2,6},{3,7},{4,0},{5,1},{6,2},{7,3},{8,12},{9,13},{10,... | collective-permute-start | bytes 3538952 | tf_op jit(solution)/shard_map/ppermute | solution.py:450
  134.3 29.6 %collective-permute-start.29 = (bf16[4,48,3072]{2,1,0:T(8,128)(2,1)}, bf16[4,48,3072]{2,1,0:T(8,128)(2,1)}, u32[]{:S(2)}, u32[]{:S(2)}) collective-permute-start(bf16[4,48,3072]{2,1,0:T(8,128)(2,1)} %pad_maximum_fusion.6.refs_9_), channel_id=1, source_target_pairs={{0,1},{1,0},{2,3},{3,2},{4,5},{5,4},{6,7},{7,6},{8,9},{9,8},{10,11... | collective-permute-start | bytes 3538952 | tf_op jit(solution)/shard_map/ppermute | solution.py:450
  134.7 29.3 %collective-permute-start.30 = (bf16[4,48,3072]{2,1,0:T(8,128)(2,1)}, bf16[4,48,3072]{2,1,0:T(8,128)(2,1)}, u32[]{:S(2)}, u32[]{:S(2)}) collective-permute-start(bf16[4,48,3072]{2,1,0:T(8,128)(2,1)} %pad_maximum_fusion.7.refs_13_), channel_id=1, source_target_pairs={{0,2},{1,3},{2,0},{3,1},{4,6},{5,7},{6,4},{7,5},{8,10},{9,11},{10,... | collective-permute-start | bytes 3538952 | tf_op jit(solution)/shard_map/ppermute | solution.py:450
  136.2 25.8 %collective-permute-start.27 = (bf16[4,2,2,16,128]{4,3,2,1,0:T(8,128)(2,1)S(1)}, bf16[4,2,2,16,128]{4,3,2,1,0:T(8,128)(2,1)S(1)}, u32[]{:S(2)}, u32[]{:S(2)}) collective-permute-start(bf16[4,2,2,16,128]{4,3,2,1,0:T(8,128)(2,1)S(1)} %pad_maximum_fusion.20), channel_id=1, source_target_pairs={{0,4},{1,5},{2,6},{3,7},{4,0},{5,1},{6,2},{7,3},{8,12},{9,13},{10,... | collective-permute-start | bytes 196616 | tf_op jit(solution)/shard_map/ppermute | solution.py:450
  181.0 34.9 %collective-permute-start.35 = (bf16[1,160,768]{2,1,0:T(8,128)(2,1)S(1)}, bf16[1,160,768]{2,1,0:T(8,128)(2,1)S(1)}, u32[]{:S(2)}, u32[]{:S(2)}) collective-permute-start(bf16[1,160,768]{2,1,0:T(8,128)(2,1)S(1)} %layer_fwd.4), channel_id=1, source_target_pairs={{0,8},{1,9},{2,10},{3,11},{4,12},{5,13},{6,14},{7,15},{16,24},{17,... | collective-permute-start | bytes 737288 | tf_op jit(solution)/shard_map/ppermute | solution.py:460
  192.7 30.8 %collective-permute-start.36 = (bf16[1,160,768]{2,1,0:T(8,128)(2,1)S(1)}, bf16[1,160,768]{2,1,0:T(8,128)(2,1)S(1)}, u32[]{:S(2)}, u32[]{:S(2)}) collective-permute-start(bf16[1,160,768]{2,1,0:T(8,128)(2,1)S(1)} %layer_fwd.5), channel_id=1, source_target_pairs={{0,8},{1,9},{2,10},{3,11},{4,12},{5,13},{6,14},{7,15},{16,24},{17,... | collective-permute-start | bytes 737288 | tf_op jit(solution)/shard_map/ppermute | solution.py:460
  204.2 30.5 %collective-permute-start.37 = (bf16[1,160,768]{2,1,0:T(8,128)(2,1)S(1)}, bf16[1,160,768]{2,1,0:T(8,128)(2,1)S(1)}, u32[]{:S(2)}, u32[]{:S(2)}) collective-permute-start(bf16[1,160,768]{2,1,0:T(8,128)(2,1)S(1)} %layer_fwd.6), channel_id=1, source_target_pairs={{0,8},{1,9},{2,10},{3,11},{4,12},{5,13},{6,14},{7,15},{16,24},{17,... | collective-permute-start | bytes 737288 | tf_op jit(solution)/shard_map/ppermute | solution.py:460
  217.3 17.4 %collective-permute-start.38 = (bf16[1,160,768]{2,1,0:T(8,128)(2,1)S(1)}, bf16[1,160,768]{2,1,0:T(8,128)(2,1)S(1)}, u32[]{:S(2)}, u32[]{:S(2)}) collective-permute-start(bf16[1,160,768]{2,1,0:T(8,128)(2,1)S(1)} %get-tuple-element.198), channel_id=1, source_target_pairs={{8,0},{9,1},{10,2},{11,3},{12,4},{13,5},{14,6},{15,7},{24,16},{25,... | collective-permute-start | bytes 737288 | tf_op jit(solution)/shard_map/ppermute | solution.py:460
  218.6 36.5 %collective-permute-start.39 = (bf16[1,160,768]{2,1,0:T(8,128)(2,1)S(1)}, bf16[1,160,768]{2,1,0:T(8,128)(2,1)S(1)}, u32[]{:S(2)}, u32[]{:S(2)}) collective-permute-start(bf16[1,160,768]{2,1,0:T(8,128)(2,1)S(1)} %layer_fwd.7), channel_id=1, source_target_pairs={{0,8},{1,9},{2,10},{3,11},{4,12},{5,13},{6,14},{7,15},{16,24},{17,... | collective-permute-start | bytes 737288 | tf_op jit(solution)/shard_map/ppermute | solution.py:460
  233.4 21.7 %collective-permute-start.40 = (bf16[1,160,768]{2,1,0:T(8,128)(2,1)S(1)}, bf16[1,160,768]{2,1,0:T(8,128)(2,1)S(1)}, u32[]{:S(2)}, u32[]{:S(2)}) collective-permute-start(bf16[1,160,768]{2,1,0:T(8,128)(2,1)S(1)} %get-tuple-element.207), channel_id=1, source_target_pairs={{8,0},{9,1},{10,2},{11,3},{12,4},{13,5},{14,6},{15,7},{24,16},{25,... | collective-permute-start | bytes 737288 | tf_op jit(solution)/shard_map/ppermute | solution.py:460
  253.8 22.9 %collective-permute-start.42 = (bf16[1,160,768]{2,1,0:T(8,128)(2,1)}, bf16[1,160,768]{2,1,0:T(8,128)(2,1)}, u32[]{:S(2)}, u32[]{:S(2)}) collective-permute-start(bf16[1,160,768]{2,1,0:T(8,128)(2,1)} %get-tuple-element.216), channel_id=1, source_target_pairs={{8,0},{9,1},{10,2},{11,3},{12,4},{13,5},{14,6},{15,7},{24,16},{25,... | collective-permute-start | bytes 737288 | tf_op jit(solution)/shard_map/ppermute | solution.py:460
  274.4 21.8 %collective-permute-start.41 = (bf16[1,160,768]{2,1,0:T(8,128)(2,1)}, bf16[1,160,768]{2,1,0:T(8,128)(2,1)S(1)}, u32[]{:S(2)}, u32[]{:S(2)}) collective-permute-start(bf16[1,160,768]{2,1,0:T(8,128)(2,1)} %get-tuple-element.225), channel_id=1, source_target_pairs={{8,0},{9,1},{10,2},{11,3},{12,4},{13,5},{14,6},{15,7},{24,16},{25,... | collective-permute-start | bytes 737288 | tf_op jit(solution)/shard_map/ppermute | solution.py:460
  323.8 32.7 %collective-permute-start.47 = (bf16[8,48,3072]{2,1,0:T(8,128)(2,1)}, bf16[8,48,3072]{2,1,0:T(8,128)(2,1)}, u32[]{:S(2)}, u32[]{:S(2)}) collective-permute-start(bf16[8,48,3072]{2,1,0:T(8,128)(2,1)} %get-tuple-element.251), channel_id=1, source_target_pairs={{0,16},{16,0},{1,17},{17,1},{2,18},{18,2},{3,19},{19,3},{4,20},{20... | collective-permute-start | bytes 7077896 | tf_op jit(solution)/shard_map/ppermute | solution.py:454
  332.6 26.6 %collective-permute-start.46 = (bf16[8,48,3072]{2,1,0:T(8,128)(2,1)}, bf16[8,48,3072]{2,1,0:T(8,128)(2,1)}, u32[]{:S(2)}, u32[]{:S(2)}) collective-permute-start(bf16[8,48,3072]{2,1,0:T(8,128)(2,1)} %get-tuple-element.249), channel_id=1, source_target_pairs={{0,16},{16,0},{1,17},{17,1},{2,18},{18,2},{3,19},{19,3},{4,20},{20... | collective-permute-start | bytes 7077896 | tf_op jit(solution)/shard_map/ppermute | solution.py:454
  332.8 31.1 %collective-permute-start.44 = (bf16[4,160,768]{2,1,0:T(8,128)(2,1)S(1)}, bf16[4,160,768]{2,1,0:T(8,128)(2,1)}, u32[]{:S(2)}, u32[]{:S(2)}) collective-permute-start(bf16[4,160,768]{2,1,0:T(8,128)(2,1)S(1)} %get-tuple-element.242), channel_id=1, source_target_pairs={{0,16},{16,8},{1,17},{17,9},{2,18},{18,10},{3,19},{19,11},{4,20},{... | collective-permute-start | bytes 2949128 | tf_op jit(solution)/shard_map/ppermute | solution.py:460
  334.7 29.2 %collective-permute-start.43 = (bf16[4,160,768]{2,1,0:T(8,128)(2,1)S(1)}, bf16[4,160,768]{2,1,0:T(8,128)(2,1)}, u32[]{:S(2)}, u32[]{:S(2)}) collective-permute-start(bf16[4,160,768]{2,1,0:T(8,128)(2,1)S(1)} %get-tuple-element.242), channel_id=1, source_target_pairs={{24,8},{8,16},{25,9},{9,17},{26,10},{10,18},{27,11},{11,19},{28,12... | collective-permute-start | bytes 2949128 | tf_op jit(solution)/shard_map/ppermute | solution.py:460
  363.9 23.4 %collective-permute-start.48 = (bf16[8,96,128]{2,1,0:T(8,128)(2,1)S(1)}, bf16[8,96,128]{2,1,0:T(8,128)(2,1)}, u32[]{:S(2)}, u32[]{:S(2)}) collective-permute-start(bf16[8,96,128]{2,1,0:T(8,128)(2,1)S(1)} %bitcast.188), channel_id=1, source_target_pairs={{0,16},{16,0},{1,17},{17,1},{2,18},{18,2},{3,19},{19,3},{4,20},{20... | collective-permute-start | bytes 589832 | tf_op jit(solution)/shard_map/ppermute | solution.py:454
  363.9 27.5 %collective-permute-start.49 = (bf16[4,48,3072]{2,1,0:T(8,128)(2,1)}, bf16[4,48,3072]{2,1,0:T(8,128)(2,1)}, u32[]{:S(2)}, u32[]{:S(2)}) collective-permute-start(bf16[4,48,3072]{2,1,0:T(8,128)(2,1)} %add_convert_fusion.11), channel_id=1, source_target_pairs={{0,1},{1,0},{2,3},{3,2},{4,5},{5,4},{6,7},{7,6},{8,9},{9,8},{10,11... | collective-permute-start | bytes 3538952 | tf_op jit(solution)/shard_map/ppermute | solution.py:450
  364.3 28.7 %collective-permute-start.50 = (bf16[4,48,3072]{2,1,0:T(8,128)(2,1)S(1)}, bf16[4,48,3072]{2,1,0:T(8,128)(2,1)}, u32[]{:S(2)}, u32[]{:S(2)}) collective-permute-start(bf16[4,48,3072]{2,1,0:T(8,128)(2,1)S(1)} %add_convert_fusion.10), channel_id=1, source_target_pairs={{0,2},{1,3},{2,0},{3,1},{4,6},{5,7},{6,4},{7,5},{8,10},{9,11},{10,... | collective-permute-start | bytes 3538952 | tf_op jit(solution)/shard_map/ppermute | solution.py:450
  366.3 28.6 %collective-permute-start.51 = (bf16[4,48,3072]{2,1,0:T(8,128)(2,1)S(1)}, bf16[4,48,3072]{2,1,0:T(8,128)(2,1)}, u32[]{:S(2)}, u32[]{:S(2)}) collective-permute-start(bf16[4,48,3072]{2,1,0:T(8,128)(2,1)S(1)} %add_convert_fusion.9), channel_id=1, source_target_pairs={{0,4},{1,5},{2,6},{3,7},{4,0},{5,1},{6,2},{7,3},{8,12},{9,13},{10,... | collective-permute-start | bytes 3538952 | tf_op jit(solution)/shard_map/ppermute | solution.py:450
  367.0 29.8 %collective-permute-start.52 = (bf16[8,48,3072]{2,1,0:T(8,128)(2,1)}, bf16[8,48,3072]{2,1,0:T(8,128)(2,1)S(1)}, u32[]{:S(2)}, u32[]{:S(2)}) collective-permute-start(bf16[8,48,3072]{2,1,0:T(8,128)(2,1)} %get-tuple-element.268), channel_id=1, source_target_pairs={{0,16},{16,0},{1,17},{17,1},{2,18},{18,2},{3,19},{19,3},{4,20},{20... | collective-permute-start | bytes 7077896 | tf_op jit(solution)/shard_map/ppermute | solution.py:454
  397.2 14.6 %collective-permute-start.54 = (bf16[2,48,3072]{2,1,0:T(8,128)(2,1)S(1)}, bf16[2,48,3072]{2,1,0:T(8,128)(2,1)S(1)}, u32[]{:S(2)}, u32[]{:S(2)}) collective-permute-start(bf16[2,48,3072]{2,1,0:T(8,128)(2,1)S(1)} %get-tuple-element.270), channel_id=1, source_target_pairs={{0,2},{1,3},{2,0},{3,1},{4,6},{5,7},{6,4},{7,5},{8,10},{9,11},{10,... | collective-permute-start | bytes 1769480 | tf_op jit(solution)/shard_map/ppermute | solution.py:450
  399.4 13.3 %collective-permute-start.55 = (bf16[2,48,3072]{2,1,0:T(8,128)(2,1)S(1)}, bf16[2,48,3072]{2,1,0:T(8,128)(2,1)S(1)}, u32[]{:S(2)}, u32[]{:S(2)}) collective-permute-start(bf16[2,48,3072]{2,1,0:T(8,128)(2,1)S(1)} %get-tuple-element.271), channel_id=1, source_target_pairs={{0,4},{1,5},{2,6},{3,7},{4,0},{5,1},{6,2},{7,3},{8,12},{9,13},{10,... | collective-permute-start | bytes 1769480 | tf_op jit(solution)/shard_map/ppermute | solution.py:450
  399.7 13.0 %collective-permute-start.56 = (bf16[2,48,3072]{2,1,0:T(8,128)(2,1)S(1)}, bf16[2,48,3072]{2,1,0:T(8,128)(2,1)S(1)}, u32[]{:S(2)}, u32[]{:S(2)}) collective-permute-start(bf16[2,48,3072]{2,1,0:T(8,128)(2,1)S(1)} %get-tuple-element.272), channel_id=1, source_target_pairs={{0,1},{1,0},{2,3},{3,2},{4,5},{5,4},{6,7},{7,6},{8,9},{9,8},{10,11... | collective-permute-start | bytes 1769480 | tf_op jit(solution)/shard_map/ppermute | solution.py:450
  425.7 32.1 %collective-permute-start.63 = (bf16[4,48,3072]{2,1,0:T(8,128)(2,1)S(1)}, bf16[4,48,3072]{2,1,0:T(8,128)(2,1)S(1)}, u32[]{:S(2)}, u32[]{:S(2)}) collective-permute-start(bf16[4,48,3072]{2,1,0:T(8,128)(2,1)S(1)} %get-tuple-element.281), channel_id=1, source_target_pairs={{0,4},{1,5},{2,6},{3,7},{4,0},{5,1},{6,2},{7,3},{8,12},{9,13},{10,... | collective-permute-start | bytes 3538952 | tf_op jit(solution)/shard_map/ppermute | solution.py:450
  427.1 32.5 %collective-permute-start.67 = (bf16[48,6144]{1,0:T(8,128)(2,1)S(1)}, bf16[48,6144]{1,0:T(8,128)(2,1)S(1)}, u32[]{:S(2)}, u32[]{:S(2)}) collective-permute-start(bf16[48,6144]{1,0:T(8,128)(2,1)S(1)} %pad_maximum_fusion.16), channel_id=1, source_target_pairs={{8,16},{9,17},{10,18},{11,19},{12,20},{13,21},{14,22},{15,23},{16,... | collective-permute-start | bytes 1769480 | tf_op jit(solution)/shard_map/ppermute | solution.py:460
  433.0 25.8 %collective-permute-start.65 = (bf16[4,48,3072]{2,1,0:T(8,128)(2,1)S(1)}, bf16[4,48,3072]{2,1,0:T(8,128)(2,1)S(1)}, u32[]{:S(2)}, u32[]{:S(2)}) collective-permute-start(bf16[4,48,3072]{2,1,0:T(8,128)(2,1)S(1)} %get-tuple-element.283), channel_id=1, source_target_pairs={{0,1},{1,0},{2,3},{3,2},{4,5},{5,4},{6,7},{7,6},{8,9},{9,8},{10,11... | collective-permute-start | bytes 3538952 | tf_op jit(solution)/shard_map/ppermute | solution.py:450
  433.3 26.0 %collective-permute-start.66 = (bf16[4,48,3072]{2,1,0:T(8,128)(2,1)S(1)}, bf16[4,48,3072]{2,1,0:T(8,128)(2,1)S(1)}, u32[]{:S(2)}, u32[]{:S(2)}) collective-permute-start(bf16[4,48,3072]{2,1,0:T(8,128)(2,1)S(1)} %get-tuple-element.284), channel_id=1, source_target_pairs={{0,2},{1,3},{2,0},{3,1},{4,6},{5,7},{6,4},{7,5},{8,10},{9,11},{10,... | collective-permute-start | bytes 3538952 | tf_op jit(solution)/shard_map/ppermute | solution.py:450
  461.0 23.8 %collective-permute-start.71 = (bf16[48,128]{1,0:T(8,128)(2,1)S(1)}, bf16[48,128]{1,0:T(8,128)(2,1)S(1)}, u32[]{:S(2)}, u32[]{:S(2)}) collective-permute-start(bf16[48,128]{1,0:T(8,128)(2,1)S(1)} %get-tuple-element.289), channel_id=1, source_target_pairs={{0,8},{1,9},{2,10},{3,11},{4,12},{5,13},{6,14},{7,15},{24,16},{25,... | collective-permute-start | bytes 36872 | tf_op jit(solution)/shard_map/ppermute | solution.py:460
  463.2 21.6 %collective-permute-start.70 = (bf16[2,48,3072]{2,1,0:T(8,128)(2,1)S(1)}, bf16[2,48,3072]{2,1,0:T(8,128)(2,1)S(1)}, u32[]{:S(2)}, u32[]{:S(2)}) collective-permute-start(bf16[2,48,3072]{2,1,0:T(8,128)(2,1)S(1)} %get-tuple-element.288), channel_id=1, source_target_pairs={{0,4},{1,5},{2,6},{3,7},{4,0},{5,1},{6,2},{7,3},{8,12},{9,13},{10,... | collective-permute-start | bytes 1769480 | tf_op jit(solution)/shard_map/ppermute | solution.py:450
  465.0 19.8 %collective-permute-start.72 = (bf16[48,9216]{1,0:T(8,128)(2,1)S(1)}, bf16[48,9216]{1,0:T(8,128)(2,1)S(1)}, u32[]{:S(2)}, u32[]{:S(2)}) collective-permute-start(bf16[48,9216]{1,0:T(8,128)(2,1)S(1)} %pad_maximum_fusion.9), channel_id=1, source_target_pairs={{0,8},{1,9},{2,10},{3,11},{4,12},{5,13},{6,14},{7,15},{24,16},{25,... | collective-permute-start | bytes 2654216 | tf_op jit(solution)/shard_map/ppermute | solution.py:460
  484.9 13.7 %collective-permute-start.74 = (bf16[1,48,3072]{2,1,0:T(8,128)(2,1)S(1)}, bf16[1,48,3072]{2,1,0:T(8,128)(2,1)S(1)}, u32[]{:S(2)}, u32[]{:S(2)}) collective-permute-start(bf16[1,48,3072]{2,1,0:T(8,128)(2,1)S(1)} %add_convert_fusion.28), channel_id=1, source_target_pairs={{0,4},{1,5},{2,6},{3,7},{4,0},{5,1},{6,2},{7,3},{8,12},{9,13},{10,... | collective-permute-start | bytes 884744 | tf_op jit(solution)/shard_map/ppermute | solution.py:450
  492.2 13.5 %collective-permute-start.76 = (bf16[48,3200]{1,0:T(8,128)(2,1)S(1)}, bf16[48,3200]{1,0:T(8,128)(2,1)S(1)}, u32[]{:S(2)}, u32[]{:S(2)}) collective-permute-start(bf16[48,3200]{1,0:T(8,128)(2,1)S(1)} %pad_maximum_fusion.17), channel_id=1, source_target_pairs={{8,16},{9,17},{10,18},{11,19},{12,20},{13,21},{14,22},{15,23},{16,... | collective-permute-start | bytes 921608 | tf_op jit(solution)/shard_map/ppermute | solution.py:460
  (79 other events, 922.1 us)
